TPU v7x, 32 devices: a whole 2x2x4 slice. The times are simulated.
32 devices in a mesh: enc: 4 (over z), dp: 8 (over y, x, core).
Axes of the slice: x: 2, y: 2, z: 4, core: 2. Of those that a mesh axis runs over, the one named last changes fastest.
Arguments:
- text: bfloat16 [16384, 768], P(('enc', 'dp')), may hold values from -6 to 6
- region_feats: bfloat16 [13312, 2048], P(('enc', 'dp')), may hold values from -6 to 6
- boxes: bfloat16 [4, 13312], P(None, ('enc', 'dp')), may hold values from 0 to 1
- caption_count: int32 [128], P(('enc', 'dp')), may hold values from 8 to 128, as said below
- region_count: int32 [128], P(('enc', 'dp')), may hold values from 36 to 100, as said below
- region_offset: int32 [32], P(('enc', 'dp')), may hold values from 0 to 31
- w_img: bfloat16 [2048, 768], P(('enc', 'dp')), may hold values from -0.125 to 0.125
- w_box: bfloat16 [4, 768], replicated, may hold values from -3 to 3
- b_img: float32 [768], replicated, may hold values from -3 to 3
- g_reg: float32 [768], replicated, may hold values from 0.25 to 1.75
- beta_reg: float32 [768], replicated, may hold values from -1.75 to 1.75
- w_query: bfloat16 [768, 768], P(('enc', 'dp')), may hold values from -0.21875 to 0.21875
- b_query: float32 [768], replicated, may hold values from -1.75 to 1.75
- w_key: bfloat16 [768, 768], P(('enc', 'dp')), may hold values from -0.21875 to 0.21875
- w_value: bfloat16 [768, 768], P(('enc', 'dp')), may hold values from -0.21875 to 0.21875
- b_value: float32 [768], replicated, may hold values from -1.75 to 1.75
- w_out: bfloat16 [768, 768], P(('enc', 'dp')), may hold values from -1.75 to 1.75
- b_out: float32 [768], replicated, may hold values from -1.75 to 1.75
- g_one: float32 [768], replicated, may hold values from 0.25 to 1.75
- beta_one: float32 [768], replicated, may hold values from -1.75 to 1.75
- w_up: bfloat16 [768, 3072], P(('enc', 'dp')), may hold values from -0.21875 to 0.21875
- b_up: float32 [3072], replicated, may hold values from -1.75 to 1.75
- w_down: bfloat16 [3072, 768], P(('enc', 'dp')), may hold values from -0.109375 to 0.109375
- b_down: float32 [768], replicated, may hold values from -1.75 to 1.75
- g_two: float32 [768], replicated, may hold values from 0.25 to 1.75
- beta_two: float32 [768], replicated, may hold values from -1.75 to 1.75
- cotangent: bfloat16 [32768, 768], P(('enc', 'dp'))
Outputs:
- output: bfloat16 [32768, 768], P(('enc', 'dp'))
- grad_text: bfloat16 [16384, 768], P(('enc', 'dp'))
- grad_feats: bfloat16 [13312, 2048], P(('enc', 'dp'))
- grad_boxes: bfloat16 [4, 13312], P(None, ('enc', 'dp'))
- grad_w_img: float32 [2048, 768], replicated
- grad_w_box: float32 [4, 768], replicated
- grad_b_img: float32 [768], replicated
- grad_g_reg: float32 [768], replicated
- grad_beta_reg: float32 [768], replicated
- grad_w_query: float32 [768, 768], replicated
- grad_b_query: float32 [768], replicated
- grad_w_key: float32 [768, 768], replicated
- grad_w_value: float32 [768, 768], replicated
- grad_b_value: float32 [768], replicated
- grad_w_out: float32 [768, 768], replicated
- grad_b_out: float32 [768], replicated
- grad_g_one: float32 [768], replicated
- grad_beta_one: float32 [768], replicated
- grad_w_up: float32 [768, 3072], replicated
- grad_b_up: float32 [3072], replicated
- grad_w_down: float32 [3072, 768], replicated
- grad_b_down: float32 [768], replicated
- grad_g_two: float32 [768], replicated
- grad_beta_two: float32 [768], replicated
Inputs may be any that keep to these rules, and one draw needn't show every extreme that they name: `caption_count`: some sequence has exactly 128 caption tokens. `region_count`: in every draw some holder's 4 sequences all have 100 regions.
All inputs are finite; a program needn't handle non-finite values.
Results may differ from a plain program's by a relative error of at most 0.018.
Values may be sent and summed in bfloat16 or wider, within the bound.
No kernel may reach another device: no remote copies, remote signals or barrier semaphores. Data moves between devices by JAX's collectives and lax.ppermute only.
A program may use at most 192 MiB of HBM per device.

v0:
```python
import jax
import jax.numpy as jnp
from jax import lax
from jax.sharding import PartitionSpec as P

HEADS = 12


epsilon = 1e-05


def normalize(values, gain_vec, shift_vec):
    centered = values - jnp.mean(values, -1, keepdims=True)
    inverse = lax.rsqrt(jnp.mean(centered * centered, -1, keepdims=True) + epsilon)
    normed = centered * inverse
    return (normed * gain_vec + shift_vec, normed, inverse)


def normalize_back(upstream, normed, inverse, gain_vec):
    weighted = upstream * gain_vec
    result = inverse * (
        weighted
        - jnp.mean(weighted, -1, keepdims=True)
        - normed * jnp.mean(weighted * normed, -1, keepdims=True)
    )
    return (result, jnp.sum(upstream * normed, 0), jnp.sum(upstream, 0))


def exact_gelu(values):
    return jax.nn.gelu(values, approximate=False)


def outer_sum(row_data, row_grad):
    return jnp.einsum("ra,rb->ab", row_data, row_grad, preferred_element_type=jnp.float32)


def back_product(row_grad, weight):
    return jnp.einsum("rb,ab->ra", row_grad, weight, preferred_element_type=jnp.float32)


def column_sum(row_grad):
    return jnp.sum(row_grad.astype(jnp.float32), 0)


def body(
    text,
    region_feats,
    boxes,
    caption_count,
    region_count,
    region_offset,
    w_img,
    w_box,
    b_img,
    g_reg,
    beta_reg,
    w_query,
    b_query,
    w_key,
    w_value,
    b_value,
    w_out,
    b_out,
    g_one,
    beta_one,
    w_up,
    b_up,
    w_down,
    b_down,
    g_two,
    beta_two,
    cotangent,
):
    img_full, query_full, key_full, value_full, out_full, up_full, down_full = (
        lax.all_gather(w_img, ("enc", "dp"), axis=0, tiled=True),
        lax.all_gather(w_query, ("enc", "dp"), axis=0, tiled=True),
        lax.all_gather(w_key, ("enc", "dp"), axis=0, tiled=True),
        lax.all_gather(w_value, ("enc", "dp"), axis=0, tiled=True),
        lax.all_gather(w_out, ("enc", "dp"), axis=0, tiled=True),
        lax.all_gather(w_up, ("enc", "dp"), axis=0, tiled=True),
        lax.all_gather(w_down, ("enc", "dp"), axis=0, tiled=True),
    )
    device_count = lax.axis_size(("enc", "dp"))
    seq_count = caption_count.shape[0]
    model_width = text.shape[1]
    text_len = text.shape[0] // seq_count
    seq_len = cotangent.shape[0] // seq_count
    region_len = seq_len - text_len
    sent_rows = region_feats.shape[0]
    per_peer = sent_rows // device_count
    head_dim = model_width // HEADS
    score_scale = head_dim ** (-0.5)
    pre_norm = (
        jnp.dot(region_feats, img_full, preferred_element_type=jnp.float32)
        + jnp.einsum("cr,cd->rd", boxes, w_box, preferred_element_type=jnp.float32)
        + b_img
    )
    encoded, enc_normed, enc_inverse = normalize(pre_norm, g_reg, beta_reg)
    received = lax.all_to_all(
        encoded.astype(jnp.bfloat16), ("enc", "dp"), split_axis=0, concat_axis=0, tiled=True
    )
    position = jnp.arange(sent_rows, dtype=jnp.int32)
    arrival = (
        position % per_peer * device_count
        + (position // per_peer - region_offset[0]) % device_count
    )
    starts = jnp.cumsum(region_count) - region_count
    slot_total = seq_count * region_len
    slot_pos = jnp.arange(slot_total, dtype=jnp.int32) % region_len
    wanted = jnp.repeat(starts, region_len, total_repeat_length=slot_total) + slot_pos
    slot_live = slot_pos < jnp.repeat(region_count, region_len, total_repeat_length=slot_total)
    placement = ((wanted[:, None] == arrival[None, :]) & slot_live[:, None]).astype(jnp.bfloat16)
    regions = jnp.dot(placement, received, preferred_element_type=jnp.float32).astype(jnp.bfloat16)
    hidden_in = jnp.concatenate(
        [
            text.reshape(seq_count, text_len, model_width),
            regions.reshape(seq_count, region_len, model_width),
        ],
        1,
    ).reshape(seq_count * seq_len, model_width)
    key_live = jnp.concatenate(
        [
            jnp.arange(text_len)[None, :] < caption_count[:, None],
            jnp.arange(region_len)[None, :] < region_count[:, None],
        ],
        1,
    )
    row_live = key_live.reshape(-1, 1).astype(jnp.float32)

    def heads_view(tensor):
        return tensor.reshape(seq_count, seq_len, HEADS, head_dim)

    query_heads = heads_view(
        (jnp.dot(hidden_in, query_full, preferred_element_type=jnp.float32) + b_query).astype(
            jnp.bfloat16
        )
    )
    key_heads = heads_view(
        jnp.dot(hidden_in, key_full, preferred_element_type=jnp.float32).astype(jnp.bfloat16)
    )
    value_heads = heads_view(
        (jnp.dot(hidden_in, value_full, preferred_element_type=jnp.float32) + b_value).astype(
            jnp.bfloat16
        )
    )
    scores = (
        jnp.einsum("sqhd,skhd->shqk", query_heads, key_heads, preferred_element_type=jnp.float32)
        * score_scale
    )
    scores = jnp.where(key_live[:, None, None, :], scores, -1e30)
    row_max = jnp.max(scores, -1, keepdims=True)
    exp_scores = jnp.exp(scores - row_max)
    attn_probs = exp_scores / jnp.sum(exp_scores, -1, keepdims=True)
    probs_low = attn_probs.astype(jnp.bfloat16)
    context = (
        jnp.einsum("shqk,skhd->sqhd", probs_low, value_heads, preferred_element_type=jnp.float32)
        .reshape(-1, model_width)
        .astype(jnp.bfloat16)
    )
    mixed = (
        hidden_in.astype(jnp.float32)
        + jnp.dot(context, out_full, preferred_element_type=jnp.float32)
        + b_out
    )
    normed_one, one_normed, one_inverse = normalize(mixed, g_one, beta_one)
    normed_one = normed_one.astype(jnp.bfloat16)
    gate_in = jnp.dot(normed_one, up_full, preferred_element_type=jnp.float32) + b_up
    activated = exact_gelu(gate_in).astype(jnp.bfloat16)
    second_in = (
        normed_one.astype(jnp.float32)
        + jnp.dot(activated, down_full, preferred_element_type=jnp.float32)
        + b_down
    )
    normed_two, two_normed, two_inverse = normalize(second_in, g_two, beta_two)
    output = (normed_two * row_live).astype(jnp.bfloat16)
    grad_second = cotangent.astype(jnp.float32) * row_live
    grad_second_in, grad_g_two, grad_beta_two = normalize_back(
        grad_second, two_normed, two_inverse, g_two
    )
    grad_down_out = grad_second_in.astype(jnp.bfloat16)
    grad_w_down = outer_sum(activated, grad_down_out)
    grad_b_down = column_sum(grad_down_out)
    grad_activated = back_product(grad_down_out, down_full)
    gelu_pull = jax.vjp(exact_gelu, gate_in)[1]
    grad_gate = gelu_pull(grad_activated)[0].astype(jnp.bfloat16)
    grad_w_up = outer_sum(normed_one, grad_gate)
    grad_b_up = column_sum(grad_gate)
    grad_first = back_product(grad_gate, up_full) + grad_second_in
    grad_mixed, grad_g_one, grad_beta_one = normalize_back(
        grad_first, one_normed, one_inverse, g_one
    )
    grad_attn = grad_mixed.astype(jnp.bfloat16)
    grad_w_out = outer_sum(context, grad_attn)
    grad_b_out = column_sum(grad_attn)
    grad_context = heads_view(back_product(grad_attn, out_full).astype(jnp.bfloat16))
    grad_probs = jnp.einsum(
        "sqhd,skhd->shqk", grad_context, value_heads, preferred_element_type=jnp.float32
    )
    grad_values = (
        jnp.einsum("shqk,sqhd->skhd", probs_low, grad_context, preferred_element_type=jnp.float32)
        .reshape(-1, model_width)
        .astype(jnp.bfloat16)
    )
    grad_scores = (
        attn_probs * (grad_probs - jnp.sum(attn_probs * grad_probs, -1, keepdims=True))
    ).astype(jnp.bfloat16)
    grad_query = (
        (
            jnp.einsum(
                "shqk,skhd->sqhd", grad_scores, key_heads, preferred_element_type=jnp.float32
            )
            * score_scale
        )
        .reshape(-1, model_width)
        .astype(jnp.bfloat16)
    )
    grad_keys = (
        (
            jnp.einsum(
                "shqk,sqhd->skhd", grad_scores, query_heads, preferred_element_type=jnp.float32
            )
            * score_scale
        )
        .reshape(-1, model_width)
        .astype(jnp.bfloat16)
    )
    grad_w_query = outer_sum(hidden_in, grad_query)
    grad_b_query = column_sum(grad_query)
    grad_w_key = outer_sum(hidden_in, grad_keys)
    grad_w_value = outer_sum(hidden_in, grad_values)
    grad_b_value = column_sum(grad_values)
    grad_hidden = (
        grad_mixed
        + back_product(grad_query, query_full)
        + back_product(grad_keys, key_full)
        + back_product(grad_values, value_full)
    )
    grad_hidden = grad_hidden.reshape(seq_count, seq_len, model_width)
    grad_text = grad_hidden[:, :text_len].reshape(-1, model_width).astype(jnp.bfloat16)
    grad_slots = grad_hidden[:, text_len:].reshape(-1, model_width).astype(jnp.bfloat16)
    grad_sent = jnp.einsum(
        "tn,td->nd", placement, grad_slots, preferred_element_type=jnp.float32
    ).astype(jnp.bfloat16)
    grad_encoded = lax.all_to_all(
        grad_sent, ("enc", "dp"), split_axis=0, concat_axis=0, tiled=True
    ).astype(jnp.float32)
    grad_pre, grad_g_reg, grad_beta_reg = normalize_back(
        grad_encoded, enc_normed, enc_inverse, g_reg
    )
    grad_pre = grad_pre.astype(jnp.bfloat16)
    grad_w_img = outer_sum(region_feats, grad_pre)
    grad_w_box = jnp.einsum("cr,rd->cd", boxes, grad_pre, preferred_element_type=jnp.float32)
    grad_b_img = column_sum(grad_pre)
    grad_feats = back_product(grad_pre, img_full).astype(jnp.bfloat16)
    grad_boxes = jnp.einsum(
        "cd,rd->cr", w_box, grad_pre, preferred_element_type=jnp.float32
    ).astype(jnp.bfloat16)
    (
        grad_w_img,
        grad_w_box,
        grad_b_img,
        grad_g_reg,
        grad_beta_reg,
        grad_w_query,
        grad_b_query,
        grad_w_key,
        grad_w_value,
        grad_b_value,
        grad_w_out,
        grad_b_out,
        grad_g_one,
        grad_beta_one,
        grad_w_up,
        grad_b_up,
        grad_w_down,
        grad_b_down,
        grad_g_two,
        grad_beta_two,
    ) = lax.psum(
        (
            grad_w_img,
            grad_w_box,
            grad_b_img,
            grad_g_reg,
            grad_beta_reg,
            grad_w_query,
            grad_b_query,
            grad_w_key,
            grad_w_value,
            grad_b_value,
            grad_w_out,
            grad_b_out,
            grad_g_one,
            grad_beta_one,
            grad_w_up,
            grad_b_up,
            grad_w_down,
            grad_b_down,
            grad_g_two,
            grad_beta_two,
        ),
        ("enc", "dp"),
    )
    return (
        output,
        grad_text,
        grad_feats,
        grad_boxes,
        grad_w_img,
        grad_w_box,
        grad_b_img,
        grad_g_reg,
        grad_beta_reg,
        grad_w_query,
        grad_b_query,
        grad_w_key,
        grad_w_value,
        grad_b_value,
        grad_w_out,
        grad_b_out,
        grad_g_one,
        grad_beta_one,
        grad_w_up,
        grad_b_up,
        grad_w_down,
        grad_b_down,
        grad_g_two,
        grad_beta_two,
    )


def solution(mesh):
    return jax.shard_map(
        body,
        mesh=mesh,
        in_specs=(
            P(("enc", "dp"), None),
            P(("enc", "dp"), None),
            P(None, ("enc", "dp")),
            P(("enc", "dp")),
            P(("enc", "dp")),
            P(("enc", "dp")),
            P(("enc", "dp"), None),
            P(),
            P(),
            P(),
            P(),
            P(("enc", "dp"), None),
            P(),
            P(("enc", "dp"), None),
            P(("enc", "dp"), None),
            P(),
            P(("enc", "dp"), None),
            P(),
            P(),
            P(),
            P(("enc", "dp"), None),
            P(),
            P(("enc", "dp"), None),
            P(),
            P(),
            P(),
            P(("enc", "dp"), None),
        ),
        out_specs=(
            P(("enc", "dp"), None),
            P(("enc", "dp"), None),
            P(("enc", "dp"), None),
            P(None, ("enc", "dp")),
            P(),
            P(),
            P(),
            P(),
            P(),
            P(),
            P(),
            P(),
            P(),
            P(),
            P(),
            P(),
            P(),
            P(),
            P(),
            P(),
            P(),
            P(),
            P(),
            P(),
        ),
        check_vma=False,
    )
```

profile of v0, /device:TPU:0, one launch (start us, length us, event | category | flops | bytes accessed | tf_op | source)
XLA Modules:
  0.0 1141.3 jit_solution(5793821062588575223)
XLA Ops:
  11.2 61.4 %all-gather.8.cloned.1.call-done = bf16[2048,768]{1,0:T(8,128)(2,1)} async-done(((bf16[64,768]{1,0:T(8,128)(2,1)}), bf16[2048,768]{1,0:T(8,128)(2,1)}) %all-gather.8.cloned.1.call-update) | async-done | bytes 3145744 | tf_op jit(solution)/shard_map/all_gather | solution.py:75
  72.6 3.4 fusion.82
  79.5 3.4 all-to-all-start
  85.8 2.6 select_compare_fusion
  89.0 2.6 select_add_fusion
  91.7 12.7 %all-to-all-done = bf16[32,13,768]{2,1,0:T(8,128)(2,1)S(1)} async-done(((bf16[32,13,768]{2,1,0:T(8,128)(2,1)}), bf16[32,13,768]{2,1,0:T(8,128)(2,1)S(1)}, u32[]{:S(2)}, u32[]{:S(2)}) %all-to-all-start) | async-done | bytes 639008 | tf_op jit(solution)/shard_map/all_to_all | solution.py:99
  106.5 24.1 %all-gather.14.cloned.1.call-done = bf16[768,768]{1,0:T(8,128)(2,1)} async-done(((bf16[24,768]{1,0:T(8,128)(2,1)}), bf16[768,768]{1,0:T(8,128)(2,1)}) %all-gather.14.cloned.1.call-update) | async-done | bytes 1179664 | tf_op jit(solution)/shard_map/all_gather | solution.py:77
  130.6 3.8 convolution_convert_fusion.2
  134.4 1.7 copy.66
  136.2 2.4 reshape.314
  138.5 48.0 %all-gather.12.cloned.1.call-done = bf16[768,768]{1,0:T(8,128)(2,1)} async-done(((bf16[24,768]{1,0:T(8,128)(2,1)}), bf16[768,768]{1,0:T(8,128)(2,1)}) %all-gather.12.cloned.1.call-update) | async-done | bytes 1179664 | tf_op jit(solution)/shard_map/all_gather | solution.py:76
  186.5 3.1 add_convert_fusion.3
  189.7 1.6 copy.65
  191.3 2.9 reshape.313
  194.2 48.1 %all-gather.10.cloned.1.call-done = bf16[768,768]{1,0:T(8,128)(2,1)} async-done(((bf16[24,768]{1,0:T(8,128)(2,1)}), bf16[768,768]{1,0:T(8,128)(2,1)}) %all-gather.10.cloned.1.call-update) | async-done | bytes 1179664 | tf_op jit(solution)/shard_map/all_gather | solution.py:78
  242.3 4.3 add_convert_fusion.4
  246.6 2.6 copy.64
  249.1 3.9 reshape.312
  253.0 7.8 fusion.39
  260.8 13.1 %fusion.78 = (f32[4,12,256]{2,1,0:T(8,128)S(1)}, f32[4,12,256,256]{2,3,1,0:T(8,128)S(1)}) fusion(f32[4,12,256,256]{2,3,1,0:T(8,128)} %fusion.39, pred[4,256]{1,0:T(4,128)(4,1)S(1)} %get-tuple-element.137), kind=kOutput, calls=%fused_computation.163 | output fusion | flops 18874624 | bytes 25216000 | tf_op jit(solution)/shard_map/sub | solution.py:152
  275.0 3.4 copy-done.8
  279.9 1.5 copy.89
  281.4 16.6 %all-gather.16.cloned.1.call-done = bf16[768,768]{1,0:T(8,128)(2,1)} async-done(((bf16[24,768]{1,0:T(8,128)(2,1)}), bf16[768,768]{1,0:T(8,128)(2,1)}) %all-gather.16.cloned.1.call-update) | async-done | bytes 1179664 | tf_op jit(solution)/shard_map/all_gather | solution.py:79
  298.0 3.4 fusion.79
  301.5 1.6 copy-done.3
  303.7 59.7 %all-gather.18.cloned.1.call-done = bf16[768,3072]{1,0:T(8,128)(2,1)} async-done(((bf16[24,3072]{1,0:T(8,128)(2,1)}), bf16[768,3072]{1,0:T(8,128)(2,1)}) %all-gather.18.cloned.1.call-update) | async-done | bytes 4718608 | tf_op jit(solution)/shard_map/all_gather | solution.py:80
  363.4 38.1 %multiply_convert_fusion.1 = (bf16[1024,3072]{1,0:T(8,128)(2,1)}, f32[1024,3072]{1,0:T(8,128)}, f32[1024,3072]{1,0:T(8,128)}) fusion(f32[3072]{0:T(1024)S(1)} %copy-done.60, bf16[768,3072]{1,0:T(8,128)(2,1)} %all-gather.18.cloned.1.call-done, f32[1024,768]{1,0:T(8,128)} %copy-done.3, f32[768]{0:T(1024)S(1)} %copy-done.34, f32[768]{0:T(1024)S(1)} %copy-done.29, ...), kind=kOutput, calls=%fused_computation.7 | convolution fusion | flops 5043388416 | bytes 39348224 | tf_op jit(solution)/shard_map/dot_general | solution.py:167
  401.5 27.3 %all-gather.20.cloned.1.call-done = bf16[3072,768]{1,0:T(8,128)(2,1)} async-done(((bf16[96,768]{1,0:T(8,128)(2,1)}), bf16[3072,768]{1,0:T(8,128)(2,1)}) %all-gather.20.cloned.1.call-update) | async-done | bytes 4718608 | tf_op jit(solution)/shard_map/all_gather | solution.py:81
  428.8 9.3 fusion.80
  439.5 2.4 multiply_reduce_fusion.1
  442.0 3.5 convert_reduce_fusion.1
  445.5 7.8 fusion.68
  453.3 18.8 %convert_reduce_fusion = (f32[3072]{0:T(1024)S(1)}, bf16[1024,3072]{1,0:T(8,128)(2,1)}) fusion(f32[1024,3072]{1,0:T(8,128)} %get-tuple-element.132, bf16[3072,768]{1,0:T(8,128)(2,1)} %all-gather.20.cloned.1.call-done, f32[1024,768]{1,0:T(8,128)} %copy-done.15, f32[1024,3072]{1,0:T(8,128)} %get-tuple-element.152, f32[3072]{0:T(1024)S(1)} %copy-done.60), kind=kOutput, calls=%fused_computation.3 | convolution fusion | flops 4886098944 | bytes 39346176 | tf_op jit(solution)/shard_map/rb,ab->ra/dot_general | solution.py:38
  472.1 10.1 multiply_reduce_fusion.2
  483.6 2.8 fusion.65
  486.4 2.6 convolution_convert_fusion.1
  489.0 1.7 copy.72
  490.8 2.4 reshape.315
  493.2 7.3 convert_reduce_fusion.3
  500.5 8.9 multiply_reduce_fusion
  509.5 7.1 multiply_convert_fusion
  516.6 2.0 fusion.31
  521.6 2.9 fusion.87
  527.6 2.9 fusion.85
  530.5 2.9 fusion.86
  533.3 1.6 fusion.83
  535.0 1.5 fusion.84
  537.2 1.6 add_convert_fusion.1
  541.6 3.5 all-to-all-start.1
  545.2 11.0 fusion.81
  556.2 9.5 all-to-all-done.1
  565.8 1.5 convert_reduce_fusion.6
  567.4 2.3 reshape.319
  569.7 1.9 multiply_reduce_fusion.9
  572.9 4.5 convolution_bitcast_fusion
  578.8 43.5 %all-reduce = (f32[4,768]{1,0:T(4,128)}, f32[768]{0:T(1024)}, f32[768]{0:T(1024)}, f32[768]{0:T(1024)}, f32[768]{0:T(1024)}, /*index=5*/f32[768]{0:T(1024)}, f32...) all-reduce(f32[4,768]{1,0:T(4,128)S(1)} %convolution_bitcast_fusion, ...), channel_id=1, replica_groups=mesh['enc'=4,'dp'=8] {'enc','dp'}, use_global_device_ids=true, to_apply=%region_17.19 | all-reduce | flops 14592 | bytes 116736 | tf_op jit(solution)/shard_map/psum | solution.py:279
  623.1 4.9 convolution_convert_fusion
  628.0 476.7 %all-reduce.4.cloned.1.call-done = (f32[2048,768]{0,1:T(8,128)}, f32[768,768]{1,0:T(8,128)}, f32[768,768]{1,0:T(8,128)}, f32[768,768]{1,0:T(8,128)}, f32[768,768...) async-done(((f32[2048,768]{0,1:T(8,128)}, f32[768,768]{1,0:T(8,128)}, f32[768,768]{1,0:T(8,128)}, f32[768,768]{1,0:T(8,128)}, f32[768,768]{1,0:T(8,128)}, ...) | async-done | bytes 34603024 | tf_op jit(solution)/shard_map/psum | solution.py:279
  1104.7 6.6 copy.84
  1111.3 3.4 copy.126
  1114.7 1.4 copy.127
  1117.2 1.4 copy.128
  1121.1 9.3 copy.130
  1130.4 3.7 copy.131
  (212 shorter events, 35.1 us)
Async XLA Ops:
  7.2 65.4 %copy-start = (bf16[416,2048]{1,0:T(8,128)(2,1)S(1)}, bf16[416,2048]{1,0:T(8,128)(2,1)}, u32[]{:S(2)}) copy-start(bf16[416,2048]{1,0:T(8,128)(2,1)} %param.34) | copy-start | bytes 5111812
  7.2 65.4 %all-gather.8.cloned.1.call-start = ((), (), s32[]{:S(2)}) async-start(), calls=%async_computation.2 | async-start | bytes 3244032 | tf_op jit(solution)/shard_map/all_gather | solution.py:75
  7.9 122.7 %all-gather.14.cloned.1.call-start = ((), (), s32[]{:S(2)}) async-start(), calls=%async_computation.5 | async-start | bytes 1216512 | tf_op jit(solution)/shard_map/all_gather | solution.py:77
  8.7 177.8 %all-gather.12.cloned.1.call-start = ((), (), s32[]{:S(2)}) async-start(), calls=%async_computation.4 | async-start | bytes 1216512 | tf_op jit(solution)/shard_map/all_gather | solution.py:76
  9.4 232.9 %all-gather.10.cloned.1.call-start = ((), (), s32[]{:S(2)}) async-start(), calls=%async_computation.3 | async-start | bytes 1216512 | tf_op jit(solution)/shard_map/all_gather | solution.py:78
  10.0 288.0 %all-gather.16.cloned.1.call-start = ((), (), s32[]{:S(2)}) async-start(), calls=%async_computation.6 | async-start | bytes 1216512 | tf_op jit(solution)/shard_map/all_gather | solution.py:79
  10.6 352.8 %all-gather.18.cloned.1.call-start = ((), (), s32[]{:S(2)}) async-start(), calls=%async_computation.7 | async-start | bytes 4866048 | tf_op jit(solution)/shard_map/all_gather | solution.py:80
  11.2 64.8 %copy-start.38 = (bf16[4,768]{1,0:T(4,128)(2,1)S(1)}, bf16[4,768]{1,0:T(4,128)(2,1)}, u32[]{:S(2)}) copy-start(bf16[4,768]{1,0:T(4,128)(2,1)} %param.40) | copy-start | bytes 18436
  11.2 64.8 %copy-start.41 = (bf16[4,416]{1,0:T(4,128)(2,1)S(1)}, bf16[4,416]{1,0:T(4,128)(2,1)}, u32[]{:S(2)}) copy-start(bf16[4,416]{1,0:T(4,128)(2,1)} %param.35) | copy-start | bytes 9988
  11.2 64.8 %copy-start.47 = (f32[768]{0:T(1024)S(1)}, f32[768]{0:T(1024)}, u32[]{:S(2)}) copy-start(f32[768]{0:T(1024)} %param.41) | copy-start | bytes 9220
  76.0 2.1 copy-start.30
  76.0 2.1 copy-start.48
  76.5 7.8 copy-start.46
  76.5 7.8 copy-start.56
  79.5 24.9 %all-to-all-start = ((bf16[32,13,768]{2,1,0:T(8,128)(2,1)}), bf16[32,13,768]{2,1,0:T(8,128)(2,1)S(1)}, u32[]{:S(2)}, u32[]{:S(2)}) async-start(bf16[32,13,768]{2,1,0:T(8,128)(2,1)} %all_to_all.14), calls=%async_computation | async-start | bytes 1572864 | tf_op jit(solution)/shard_map/all_to_all | solution.py:99
  82.9 345.9 %all-gather.20.cloned.1.call-start = ((), (), s32[]{:S(2)}) async-start(), calls=%async_computation.8 | async-start | bytes 4866048 | tf_op jit(solution)/shard_map/all_gather | solution.py:81
  88.4 16.9 %copy-start.54 = (pred[512]{0:T(512)(128)(4,1)}, pred[512]{0:T(512)(128)(4,1)S(1)}, u32[]{:S(2)}) copy-start(pred[512]{0:T(512)(128)(4,1)S(1)} %select_compare_fusion) | copy-start | bytes 1540
  88.4 16.8 %copy-start.50 = (s32[416]{0:T(512)}, s32[416]{0:T(512)S(1)}, u32[]{:S(2)}) copy-start(s32[416]{0:T(512)S(1)} %fusion.52) | copy-start | bytes 4996
  91.6 13.6 %copy-start.52 = (s32[512]{0:T(512)}, s32[512]{0:T(512)S(1)}, u32[]{:S(2)}) copy-start(s32[512]{0:T(512)S(1)} %select_add_fusion) | copy-start | bytes 6148
  106.5 24.1 %copy-start.19 = (bf16[4,256,768]{2,1,0:T(8,128)(2,1)}, bf16[4,256,768]{2,1,0:T(8,128)(2,1)S(1)}, u32[]{:S(2)}) copy-start(bf16[4,256,768]{2,1,0:T(8,128)(2,1)S(1)} %pad_maximum_fusion) | copy-start | bytes 4718596
  134.4 52.1 %copy-start.61 = (f32[768]{0:T(1024)S(1)}, f32[768]{0:T(1024)}, u32[]{:S(2)}) copy-start(f32[768]{0:T(1024)} %param.45) | copy-start | bytes 9220
  189.7 52.6 %copy-start.62 = (f32[768]{0:T(1024)S(1)}, f32[768]{0:T(1024)}, u32[]{:S(2)}) copy-start(f32[768]{0:T(1024)} %param.48) | copy-start | bytes 9220
  194.2 58.8 %copy-start.5 = (bf16[4,256,12,64]{1,0,3,2:T(4,128)(2,1)}, bf16[4,256,12,64]{1,0,3,2:T(4,128)(2,1)S(1)}, u32[]{:S(2)}) copy-start(bf16[4,256,12,64]{1,0,3,2:T(4,128)(2,1)S(1)} %reshape.313) | copy-start | bytes 4718596
  260.8 13.1 %copy-start.22 = (bf16[4,256,12,64]{1,0,3,2:T(4,128)(2,1)S(1)}, bf16[4,256,12,64]{1,0,3,2:T(4,128)(2,1)}, u32[]{:S(2)}) copy-start(bf16[4,256,12,64]{1,0,3,2:T(4,128)(2,1)} %reshape.312) | copy-start | bytes 4718596
  273.9 4.5 copy-start.8
  273.9 4.8 copy-start.27
  278.7 19.4 %copy-start.20 = (bf16[4,256,768]{2,1,0:T(8,128)(2,1)S(1)}, bf16[4,256,768]{2,1,0:T(8,128)(2,1)}, u32[]{:S(2)}) copy-start(bf16[4,256,768]{2,1,0:T(8,128)(2,1)} %copy-done.19) | copy-start | bytes 4718596
  278.7 19.4 %copy-start.63 = (f32[768]{0:T(1024)S(1)}, f32[768]{0:T(1024)}, u32[]{:S(2)}) copy-start(f32[768]{0:T(1024)} %param.50) | copy-start | bytes 9220
  301.5 61.9 %copy-start.29 = (f32[768]{0:T(1024)S(1)}, f32[768]{0:T(1024)}, u32[]{:S(2)}) copy-start(f32[768]{0:T(1024)} %param.51) | copy-start | bytes 9220
  301.5 61.9 %copy-start.34 = (f32[768]{0:T(1024)S(1)}, f32[768]{0:T(1024)}, u32[]{:S(2)}) copy-start(f32[768]{0:T(1024)} %param.52) | copy-start | bytes 9220
  301.5 61.9 %copy-start.60 = (f32[3072]{0:T(1024)S(1)}, f32[3072]{0:T(1024)}, u32[]{:S(2)}) copy-start(f32[3072]{0:T(1024)} %param.54) | copy-start | bytes 36868
  303.7 125.1 %copy-start.64 = (f32[768]{0:T(1024)S(1)}, f32[768]{0:T(1024)}, u32[]{:S(2)}) copy-start(f32[768]{0:T(1024)} %param.56) | copy-start | bytes 9220
  438.7 3.3 copy-start.49
  439.5 6.0 slice-start.6
  442.0 3.5 slice-start.7
  445.5 7.8 copy-start.15
  453.3 18.8 %copy-start.4 = (f32[1024,768]{1,0:T(8,128)S(1)}, f32[1024,768]{1,0:T(8,128)}, u32[]{:S(2)}) copy-start(f32[1024,768]{1,0:T(8,128)} %copy-done.3) | copy-start | bytes 9437188
  483.3 3.1 copy-start.9
  483.6 2.8 copy-start.59
  489.0 4.1 copy-start.28
  493.2 7.3 copy-start.23
  493.2 7.4 copy-start.25
  493.2 16.3 %slice-start = ((s8[12582912]{0:T(1024)(128)(4,1)}), s8[4194304]{0:T(1024)(128)(4,1)S(1)}, s32[]{:S(2)}) async-start(s8[12582912]{0:T(1024)(128)(4,1)} %bitcast.136), calls=%async_computation.10 | async-start | bytes 8388608
  493.2 16.3 %slice-start.1 = ((s8[12582912]{0:T(1024)(128)(4,1)}), s8[4194304]{0:T(1024)(128)(4,1)S(1)}, s32[]{:S(2)}) async-start(s8[12582912]{0:T(1024)(128)(4,1)} %bitcast.136), calls=%async_computation.11 | async-start | bytes 8388608
  500.5 8.9 slice-start.2
  509.5 7.2 copy-start.6
  516.6 2.0 copy-start.7
  530.4 2.9 copy-start.58
  535.0 1.9 copy-start.10
  535.0 2.2 copy-start.26
  541.6 24.1 %all-to-all-start.1 = ((bf16[32,13,768]{2,1,0:T(8,128)(2,1)}), bf16[32,13,768]{2,1,0:T(8,128)(2,1)}, u32[]{:S(2)}, u32[]{:S(2)}) async-start(bf16[32,13,768]{2,1,0:T(8,128)(2,1)} %all_to_all.17), calls=%async_computation.1 | async-start | bytes 1572864 | tf_op jit(solution)/shard_map/all_to_all | solution.py:244
  545.2 20.6 %copy-start.31 = (f32[768]{0:T(1024)S(1)}, f32[768]{0:T(1024)}, u32[]{:S(2)}) copy-start(f32[768]{0:T(1024)} %param.42) | copy-start | bytes 9220
  545.2 24.5 %copy-start.33 = (f32[416]{0:T(512)S(1)}, f32[416]{0:T(512)}, u32[]{:S(2)}) copy-start(f32[416]{0:T(512)} %copy-done.32) | copy-start | bytes 4996
  545.2 24.5 %copy-start.37 = (f32[416]{0:T(512)S(1)}, f32[416]{0:T(512)}, u32[]{:S(2)}) copy-start(f32[416]{0:T(512)} %copy-done.36) | copy-start | bytes 4996
  545.2 559.5 %all-reduce.4.cloned.1.call-start = ((), (), s32[]{:S(2)}) async-start(), calls=%async_computation.9 | async-start | bytes 69206016 | tf_op jit(solution)/shard_map/psum | solution.py:279
  556.2 13.5 %copy-start.2 = (f32[416,768]{1,0:T(8,128)S(1)}, f32[416,768]{1,0:T(8,128)}, u32[]{:S(2)}) copy-start(f32[416,768]{1,0:T(8,128)} %copy-done.1) | copy-start | bytes 3833860
  569.7 1.9 copy-start.11
  577.5 44.8 %copy-start.39 = (bf16[4,768]{1,0:T(4,128)(2,1)S(1)}, bf16[4,768]{1,0:T(4,128)(2,1)}, u32[]{:S(2)}) copy-start(bf16[4,768]{1,0:T(4,128)(2,1)} %param.40) | copy-start | bytes 18436
  1111.3 3.4 copy-start.18
  1114.7 2.5 copy-start.17
  1117.2 2.5 copy-start.16
  1119.7 10.7 slice-start.3
  1121.1 9.3 slice-start.4
  1121.1 9.3 slice-start.5
  (19 other events, 23.0 us)
Sparse Core Ops, SparseCore 0:
  10.9 61.6 all-gather.7
  75.5 55.1 all-gather.13
  133.5 52.9 all-gather.11
  189.3 52.9 all-gather.9
  245.0 52.9 all-gather.15
  300.8 62.5 all-gather.17
  366.3 62.4 all-gather.19
  577.6 527.0 all-reduce.3
where the time goes:
time: 1150 us; the launch traced here: 1140 us
  waiting for transfers between devices  788 us (69%)
  matrix products  172 us (15%)
  local copies, waits for them, and re-layouts  74.1 us (6%)
  blocking collectives  43.5 us (4%)
  other arithmetic  39.6 us (3%)
  between operations  15.9 us (1%)
    psum x1, waiting for transfers between devices, body(): lax.psum((grad_w_img, grad_w_box, grad_b_img, grad_g_reg, grad_beta_reg,...  477 us
    all_gather x1, waiting for transfers between devices, body(): lax.all_gather(w_img, ('enc', 'dp'), axis=0, tiled=True)  61.4 us
    all_gather x1, waiting for transfers between devices, body(): lax.all_gather(w_up, ('enc', 'dp'), axis=0, tiled=True)  59.7 us
    all_gather x1, waiting for transfers between devices, body(): lax.all_gather(w_value, ('enc', 'dp'), axis=0, tiled=True)  48.1 us
    all_gather x1, waiting for transfers between devices, body(): lax.all_gather(w_query, ('enc', 'dp'), axis=0, tiled=True)  48 us
    psum x1, blocking collectives, body(): lax.psum((grad_w_img, grad_w_box, grad_b_img, grad_g_reg, grad_beta_reg,...  43.5 us
    unnamed x158, local copies, waits for them, and re-layouts  43 us
    dot_general x7, matrix products, back_product(): jnp.einsum('rb,ab->ra', row_grad, weight, preferred_element_type=jnp.floa...  41 us
  transfers between devices with their start and end apart: 10, of which 10 were waited for; matrix products, arithmetic and copies ran while one was open for 11% of the time, Pallas kernels for 0%

commit v1 on v0

--- a/solution.py
+++ b/solution.py
@@ -40,6 +40,47 @@
 
 def column_sum(row_grad):
     return jnp.sum(row_grad.astype(jnp.float32), 0)
+
+
+def axis_bits(name):
+    size = lax.axis_size(name)
+    bits = []
+    step = 1
+    while step < size:
+        bits.append((name, step))
+        step *= 2
+    return bits
+
+
+def swap_bit(tensor, bit):
+    name, step = bit
+    size = lax.axis_size(name)
+    return lax.ppermute(tensor, name, [(i, i ^ step) for i in range(size)])
+
+
+def stage_orders():
+    dp_bits, enc_bits = axis_bits("dp"), axis_bits("enc")
+    near, middle = dp_bits[:1], dp_bits[1:]
+    half = len(middle) // 2
+    return (
+        near + middle + enc_bits,
+        near + middle[half:] + middle[:half] + enc_bits,
+    )
+
+
+def scatter_sum(parts, order):
+    dp_bits, enc_bits = axis_bits("dp"), axis_bits("enc")
+    layout = enc_bits[::-1] + dp_bits[::-1]
+    value = parts.reshape((2,) * len(layout) + parts.shape[1:])
+    for bit in order:
+        axis = layout.index(bit)
+        layout = layout[:axis] + layout[axis + 1 :]
+        mine = (lax.axis_index(bit[0]) // bit[1]) % 2
+        away = lax.dynamic_index_in_dim(value, 1 - mine, axis, keepdims=False)
+        kept = lax.dynamic_index_in_dim(value, mine, axis, keepdims=False)
+        came = swap_bit(away, bit)
+        value = (kept.astype(jnp.float32) + came.astype(jnp.float32)).astype(jnp.bfloat16)
+    return value
 
 
 def body(
@@ -71,15 +112,19 @@
     beta_two,
     cotangent,
 ):
-    img_full, query_full, key_full, value_full, out_full, up_full, down_full = (
-        lax.all_gather(w_img, ("enc", "dp"), axis=0, tiled=True),
-        lax.all_gather(w_query, ("enc", "dp"), axis=0, tiled=True),
-        lax.all_gather(w_key, ("enc", "dp"), axis=0, tiled=True),
-        lax.all_gather(w_value, ("enc", "dp"), axis=0, tiled=True),
-        lax.all_gather(w_out, ("enc", "dp"), axis=0, tiled=True),
-        lax.all_gather(w_up, ("enc", "dp"), axis=0, tiled=True),
-        lax.all_gather(w_down, ("enc", "dp"), axis=0, tiled=True),
-    )
+    axes = ("enc", "dp")
+    first = lax.all_gather(
+        jnp.concatenate([w_img, w_query, w_key, w_value, w_out], 0), axes, axis=0
+    )
+    up_full = lax.all_gather(w_up, axes, axis=0, tiled=True)
+    down_full = lax.all_gather(w_down, axes, axis=0, tiled=True)
+    cuts = []
+    at = 0
+    for weight in (w_img, w_query, w_key, w_value, w_out):
+        rows = weight.shape[0]
+        cuts.append(first[:, at : at + rows].reshape(-1, weight.shape[1]))
+        at += rows
+    img_full, query_full, key_full, value_full, out_full = cuts
     device_count = lax.axis_size(("enc", "dp"))
     seq_count = caption_count.shape[0]
     model_width = text.shape[1]
@@ -255,52 +300,77 @@
     grad_boxes = jnp.einsum(
         "cd,rd->cr", w_box, grad_pre, preferred_element_type=jnp.float32
     ).astype(jnp.bfloat16)
+    orders = stage_orders()
+    width = model_width
+    ff_blocks = w_up.shape[1] // width
+
+    def parts_of(grad):
+        return grad.astype(jnp.bfloat16).reshape(device_count, -1, grad.shape[-1])
+
+    up_cols = jnp.stack(
+        [grad_w_up[:, j * width : (j + 1) * width] for j in range(ff_blocks)], 0
+    ).reshape(-1, width)
+    small = [
+        grad_w_box,
+        grad_b_img[None],
+        grad_g_reg[None],
+        grad_beta_reg[None],
+        grad_b_query[None],
+        grad_b_value[None],
+        grad_b_out[None],
+        grad_g_one[None],
+        grad_beta_one[None],
+        grad_b_up.reshape(-1, width),
+        grad_b_down[None],
+        grad_g_two[None],
+        grad_beta_two[None],
+    ]
+    small = jnp.concatenate(small, 0)
+    small_rows = small.shape[0]
+    per_small = -(-small_rows // device_count)
+    small = jnp.pad(small, ((0, per_small * device_count - small_rows), (0, 0)))
+    ff_sum = jnp.concatenate(
+        [
+            scatter_sum(parts_of(grad_w_down), orders[0]),
+            scatter_sum(parts_of(up_cols), orders[1]),
+        ],
+        0,
+    )
+    ff_all = lax.all_gather(ff_sum, axes, axis=0)
+    qkv_parts = jnp.concatenate(
+        [parts_of(g) for g in (grad_w_query, grad_w_key, grad_w_value, grad_w_out)], 1
+    )
+    img_parts = jnp.concatenate([parts_of(grad_w_img), parts_of(small)], 1)
+    rest_sum = jnp.concatenate(
+        [scatter_sum(qkv_parts, orders[0]), scatter_sum(img_parts, orders[1])], 0
+    )
+    rest_all = lax.all_gather(rest_sum, axes, axis=0)
+
+    down_rows = w_down.shape[0]
+    grad_w_down = ff_all[:, :down_rows].reshape(-1, width).astype(jnp.float32)
+    up_cols = ff_all[:, down_rows:].reshape(ff_blocks, -1, width).astype(jnp.float32)
+    grad_w_up = jnp.concatenate([up_cols[j] for j in range(ff_blocks)], 1)
+    at = 0
+    pieces = []
+    for rows in [w_query.shape[0]] * 4 + [w_img.shape[0], per_small]:
+        pieces.append(rest_all[:, at : at + rows].reshape(-1, width).astype(jnp.float32))
+        at += rows
+    grad_w_query, grad_w_key, grad_w_value, grad_w_out, grad_w_img, small = pieces
+    box_rows = grad_w_box.shape[0]
+    grad_w_box = small[:box_rows]
+    singles = small[box_rows:small_rows]
     (
-        grad_w_img,
-        grad_w_box,
         grad_b_img,
         grad_g_reg,
         grad_beta_reg,
-        grad_w_query,
         grad_b_query,
-        grad_w_key,
-        grad_w_value,
         grad_b_value,
-        grad_w_out,
         grad_b_out,
         grad_g_one,
         grad_beta_one,
-        grad_w_up,
-        grad_b_up,
-        grad_w_down,
-        grad_b_down,
-        grad_g_two,
-        grad_beta_two,
-    ) = lax.psum(
-        (
-            grad_w_img,
-            grad_w_box,
-            grad_b_img,
-            grad_g_reg,
-            grad_beta_reg,
-            grad_w_query,
-            grad_b_query,
-            grad_w_key,
-            grad_w_value,
-            grad_b_value,
-            grad_w_out,
-            grad_b_out,
-            grad_g_one,
-            grad_beta_one,
-            grad_w_up,
-            grad_b_up,
-            grad_w_down,
-            grad_b_down,
-            grad_g_two,
-            grad_beta_two,
-        ),
-        ("enc", "dp"),
-    )
+    ) = [singles[i] for i in range(8)]
+    grad_b_up = singles[8 : 8 + ff_blocks].reshape(-1)
+    grad_b_down, grad_g_two, grad_beta_two = [singles[8 + ff_blocks + i] for i in range(3)]
     return (
         output,
         grad_text,

time: 1150 us -> 681 us (0.59)
  waiting for transfers between devices: 788 us -> 291 us
  other arithmetic: 39.6 us -> 89.8 us
  blocking collectives: 43.5 us -> 0 us
  starting transfers between devices: 7.43 us -> 24.9 us
  local copies, waits for them, and re-layouts: 74.1 us -> 87.3 us
    psum x1 -> x0, waiting for transfers between devices: 477 us -> none  [body(): lax.psum((grad_w_img, grad_w_box, grad_b_img, grad_g_reg, grad_beta_reg,...]
    all_gather x7 -> x5, waiting for transfers between devices: 285 us -> 134 us  [the longest x1 74.4 us: body(): lax.all_gather(jnp.concatenate([w_img, w_query, w_key, w_value, w_out], 0...]
    ppermute x0 -> x20, waiting for transfers between devices: none -> 133 us  [swap_bit(): return lax.ppermute(tensor, name, [(i, i ^ step) for i in range(size)])]
    psum x1 -> x0, blocking collectives: 43.5 us -> none  [body(): lax.psum((grad_w_img, grad_w_box, grad_b_img, grad_g_reg, grad_beta_reg,...]
    convert_element_type x0 -> x27, other arithmetic: none -> 29.8 us  [the longest x20 14 us: scatter_sum(): (kept.astype(jnp.float32) + came.astype(jnp.float32)).astype(jnp.bfloat16)]
    unnamed x158 -> x163, local copies, waits for them, and re-layouts: 43 us -> 22.5 us
    ppermute x0 -> x20, starting transfers between devices: none -> 18 us  [swap_bit(): return lax.ppermute(tensor, name, [(i, i ^ step) for i in range(size)])]
    slice x0 -> x8, local copies, waits for them, and re-layouts: none -> 15.6 us  [the longest x2 6.86 us: body(): cuts.append(first[:, at:at + rows].reshape(-1, weight.shape[1]))]
  transfers between devices with their start and end apart: 10 -> 27, of which waited for: 10 -> 17; matrix products, arithmetic and copies ran while one was open for 11% -> 29% of each run, Pallas kernels for 0% -> 0%
where the time goes in v1:
time: 681 us; the launch traced here: 676 us
  waiting for transfers between devices  291 us (43%)
  matrix products  167 us (25%)
  other arithmetic  89.8 us (13%)
  local copies, waits for them, and re-layouts  87.3 us (13%)
  starting transfers between devices  24.9 us (4%)
  between operations  16.4 us (2%)
    ppermute x20, waiting for transfers between devices, swap_bit(): return lax.ppermute(tensor, name, [(i, i ^ step) for i in range(size)])  133 us
    all_gather x1, waiting for transfers between devices, body(): lax.all_gather(jnp.concatenate([w_img, w_query, w_key, w_value, w_out], 0...  74.4 us
    all_gather x1, waiting for transfers between devices, body(): ff_all = lax.all_gather(ff_sum, axes, axis=0)  59.1 us
    dot_general x7, matrix products, back_product(): jnp.einsum('rb,ab->ra', row_grad, weight, preferred_element_type=jnp.floa...  40.7 us
    dot_general x1, matrix products, body(): jnp.dot(normed_one, up_full, preferred_element_type=jnp.float32) + b_up  38.1 us
    dot_general x7, matrix products, outer_sum(): jnp.einsum('ra,rb->ab', row_data, row_grad, preferred_element_type=jnp.fl...  30.9 us
    unnamed x163, local copies, waits for them, and re-layouts  22.5 us
    ppermute x20, starting transfers between devices, swap_bit(): return lax.ppermute(tensor, name, [(i, i ^ step) for i in range(size)])  18 us
  transfers between devices with their start and end apart: 27, of which 17 were waited for; matrix products, arithmetic and copies ran while one was open for 29% of the time, Pallas kernels for 0%

profile of v1, /device:TPU:0, one launch (start us, length us, event | category | flops | bytes accessed | tf_op | source)
XLA Modules:
  0.0 676.5 jit_solution(7776403684317768918)
XLA Ops:
  15.8 74.4 %all-gather.14.cloned.1.call-done = bf16[5120,768]{1,0:T(8,128)(2,1)} async-done(((bf16[160,768]{1,0:T(8,128)(2,1)}), bf16[5120,768]{1,0:T(8,128)(2,1)}) %all-gather.14.cloned.1.call-update) | async-done | bytes 7864336 | tf_op jit(solution)/shard_map/all_gather | solution.py:116
  90.2 2.2 slice.224
  97.5 3.4 all-to-all-start
  102.1 2.6 select_compare_fusion
  105.4 2.6 select_add_fusion
  108.0 4.6 fusion.101
  112.6 11.7 %all-to-all-done = bf16[32,13,768]{2,1,0:T(8,128)(2,1)S(1)} async-done(((bf16[32,13,768]{2,1,0:T(8,128)(2,1)}), bf16[32,13,768]{2,1,0:T(8,128)(2,1)S(1)}, u32[]{:S(2)}, u32[]{:S(2)}) %all-to-all-start) | async-done | bytes 639008 | tf_op jit(solution)/shard_map/all_to_all | solution.py:144
  125.4 1.8 convolution_convert_fusion.10
  131.6 2.9 reshape.459
  134.5 4.8 convolution_convert_fusion.5
  139.3 2.8 copy.135
  142.1 3.9 reshape.461
  146.0 4.3 add_convert_fusion.4
  150.2 2.6 copy.133
  152.8 3.9 reshape.457
  156.7 7.8 %fusion.51 = f32[4,12,256,256]{2,3,1,0:T(8,128)} fusion(bf16[4,256,12,64]{1,0,3,2:T(4,128)(2,1)} %reshape.461, bf16[4,256,12,64]{1,0,3,2:T(4,128)(2,1)S(1)} %reshape.459), kind=kOutput, calls=%fused_computation.120 | convolution fusion | flops 402653184 | bytes 15728640 | tf_op jit(solution)/shard_map/sqhd,skhd->shqk/dot_general | solution.py:192
  164.4 13.0 %fusion.107 = (f32[4,12,256]{2,1,0:T(8,128)S(1)}, f32[4,12,256,256]{2,3,1,0:T(8,128)S(1)}) fusion(f32[4,12,256,256]{2,3,1,0:T(8,128)} %fusion.51, pred[4,256]{1,0:T(4,128)(4,1)S(1)} %get-tuple-element.102), kind=kOutput, calls=%fused_computation.279 | output fusion | flops 18874624 | bytes 25216000 | tf_op jit(solution)/shard_map/sub | solution.py:197
  178.6 3.4 copy-done.10
  188.0 38.1 %multiply_convert_fusion.1 = (bf16[1024,3072]{1,0:T(8,128)(2,1)}, f32[1024,3072]{1,0:T(8,128)}, f32[1024,3072]{1,0:T(8,128)}) fusion(f32[3072]{0:T(1024)S(1)} %copy-done.66, bf16[768,3072]{1,0:T(8,128)(2,1)} %all-gather.10.cloned.1.call-done, f32[1024,768]{1,0:T(8,128)} %copy-done.7, f32[768]{0:T(1024)S(1)} %copy-done.71, f32[768]{0:T(1024)S(1)} %copy-done.56, ...), kind=kOutput, calls=%fused_computation.6 | convolution fusion | flops 5043388416 | bytes 39348224 | tf_op jit(solution)/shard_map/dot_general | solution.py:212
  226.0 9.3 %fusion.109 = (f32[1024]{0:T(1024)S(1)}, f32[1024,768]{1,0:T(8,128)S(1)}) fusion(f32[768]{0:T(1024)S(1)} %copy-done.70, bf16[1024,3072]{1,0:T(8,128)(2,1)} %get-tuple-element.72, bf16[3072,768]{1,0:T(8,128)(2,1)} %all-gather.12.cloned.1.call-done, f32[768]{0:T(1024)S(1)} %copy-done.71, f32[768]{0:T(1024)S(1)} %copy-done.56, f32[1024]{0:T(1024)S(1)} %add_rsqrt_fusion.1, ...), kind=kOutput, calls=%fused_computation.281 | convolution fusion | flops 4838915072 | bytes 17323008 | tf_op jit(solution)/shard_map/dot_general | solution.py:216
  236.8 3.0 multiply_reduce_fusion.1
  239.8 2.6 convert_reduce_fusion.1
  242.5 18.8 %fusion.112 = (bf16[3072]{0:T(1024)(128)(2,1)S(1)}, bf16[1024,3072]{1,0:T(8,128)(2,1)}) fusion(f32[1024,3072]{1,0:T(8,128)} %get-tuple-element.73, bf16[3072,768]{1,0:T(8,128)(2,1)} %all-gather.12.cloned.1.call-done, f32[1024,768]{1,0:T(8,128)} %get-tuple-element.67, f32[1024,3072]{1,0:T(8,128)} %get-tuple-element.117, f32[3072]{0:T(1024)S(1)} %copy-done.66), kind=kOutput, calls=%fused_computation.284 | convolution fusion | flops 4882953216 | bytes 39340032 | tf_op jit(solution)/shard_map/rb,ab->ra/dot_general | solution.py:38
  261.2 10.1 %multiply_reduce_fusion.2 = (bf16[768]{0:T(1024)(128)(2,1)S(1)}, f32[1024]{0:T(1024)S(1)}, f32[1024]{0:T(1024)S(1)}, bf16[768]{0:T(1024)(128)(2,1)S(1)}, f32[1024,768]{1,0:T(8,128)S(1)}) fusion(f32[1024,768]{1,0:T(8,128)S(1)} %copy-done.8, f32[1024]{0:T(1024)S(1)} %add_rsqrt_fusion.1, f32[1024]{0:T(1024)S(1)} %broadcast_multiply_fusion.6, ...), kind=kOutput, calls=%fused_computation.49 | convolution fusion | flops 4839698432 | bytes 20469760 | tf_op jit(solution)/shard_map/rb,ab->ra/dot_general | solution.py:38
  274.2 2.6 convolution_convert_fusion.4
  278.5 2.4 reshape.463
  280.9 7.3 %fusion.111 = (bf16[12,64]{1,0:T(8,128)(2,1)S(1)}, bf16[4,256,12,64]{1,3,2,0:T(8,128)(2,1)S(1)}) fusion(f32[4,12,256,256]{2,3,1,0:T(8,128)} %copy-done.10, f32[4,12,256]{2,1,0:T(8,128)S(1)} %copy-done.42, bf16[4,256,12,64]{1,0,3,2:T(4,128)(2,1)} %reshape.463), kind=kOutput, calls=%fused_computation.283 | convolution fusion | flops 410516736 | bytes 15779328 | tf_op jit(solution)/shard_map/shqk,sqhd->skhd/dot_general | solution.py:245
  288.3 8.9 %multiply_reduce_fusion = (f32[4,12,256]{2,1,0:T(8,128)S(1)}, f32[4,12,256,256]{2,3,1,0:T(8,128)}) fusion(f32[4,12,256,256]{2,3,1,0:T(8,128)} %copy-done.10, f32[4,12,256]{2,1,0:T(8,128)S(1)} %copy-done.42, bf16[4,256,12,64]{1,0,3,2:T(4,128)(2,1)S(1)} %copy-done.27, bf16[4,256,12,64]{1,0,3,2:T(4,128)(2,1)S(1)} %copy-done.29), kind=kOutput, calls=%fused_computation.4 | convolution fusion | flops 412078080 | bytes 28409856 | tf_op jit(solution)/shard_map/sqhd,skhd->shqk/dot_general | solution.py:241
  297.2 7.1 %multiply_convert_fusion = bf16[4,12,256,256]{2,3,1,0:T(8,128)(2,1)S(1)} fusion(f32[4,12,256,256]{2,3,1,0:T(8,128)} %get-tuple-element.122, f32[4,12,256]{2,1,0:T(8,128)S(1)} %get-tuple-element.121, f32[4,12,256,256]{2,3,1,0:T(8,128)S(1)} %bitcast.302, f32[4,12,256]{2,1,0:T(8,128)S(1)} %copy-done.42), kind=kLoop, calls=%fused_computation.3 | loop fusion | flops 12582912 | bytes 31555584 | tf_op jit(solution)/shard_map/convert_element_type | solution.py:251
  305.8 2.0 fusion.43
  309.4 2.5 convolution_convert_fusion.9
  314.9 2.5 convolution_convert_fusion.7
  326.5 2.1 all_to_all.17
  328.6 3.4 all-to-all-start.1
  332.0 3.0 convolution_convert_fusion.8
  340.9 11.6 %all-to-all-done.1 = bf16[32,13,768]{2,1,0:T(8,128)(2,1)} async-done(((bf16[32,13,768]{2,1,0:T(8,128)(2,1)}), bf16[32,13,768]{2,1,0:T(8,128)(2,1)}, u32[]{:S(2)}, u32[]{:S(2)}) %all-to-all-start.1) | async-done | bytes 639008 | tf_op jit(solution)/shard_map/all_to_all | solution.py:289
  352.6 2.3 reshape.469
  358.1 2.6 fusion.96
  363.5 4.6 fusion.22
  368.1 4.7 copy.157
  375.8 3.2 fusion.13
  379.2 2.5 fusion.14
  387.4 16.4 %collective-permute-done.6 = bf16[2,2,2,65,768]{4,2,3,1,0:T(2,128)(2,1)} collective-permute-done((bf16[2,2,2,65,768]{4,2,3,1,0:T(2,128)(2,1)}, bf16[2,2,2,65,768]{4,2,3,1,0:T(2,128)(2,1)}, u32[]{:S(2)}, u32[]{:S(2)}) %collective-permute-start.6) | collective-permute-done | bytes 798752 | tf_op jit(solution)/shard_map/ppermute | solution.py:58
  407.4 7.6 %collective-permute-done.1 = bf16[2,2,2,96,768]{4,3,0,1,2:T(8,128)(2,1)} collective-permute-done((bf16[2,2,2,96,768]{4,3,0,1,2:T(8,128)(2,1)}, bf16[2,2,2,96,768]{4,3,0,1,2:T(8,128)(2,1)}, u32[]{:S(2)}, u32[]{:S(2)}) %collective-permute-start.1) | collective-permute-done | bytes 1179680 | tf_op jit(solution)/shard_map/ppermute | solution.py:58
  417.3 6.5 collective-permute-done.7
  425.9 4.7 collective-permute-done.2
  434.1 6.8 %collective-permute-done.3 = bf16[2,96,768]{2,1,0:T(8,128)(2,1)S(1)} collective-permute-done((bf16[2,96,768]{2,1,0:T(8,128)(2,1)S(1)}, bf16[2,96,768]{2,1,0:T(8,128)(2,1)S(1)}, u32[]{:S(2)}, u32[]{:S(2)}) %collective-permute-start.3) | collective-permute-done | bytes 294944 | tf_op jit(solution)/shard_map/ppermute | solution.py:58
  441.1 6.6 collective-permute-done.4
  448.6 8.4 %convolution_convert_fusion.1 = bf16[3072,768]{1,0:T(8,128)(2,1)S(1)} fusion(bf16[1024,3072]{1,0:T(8,128)(2,1)} %get-tuple-element.72, f32[1024,768]{1,0:T(8,128)} %get-tuple-element.67), kind=kOutput, calls=%fused_computation.29 | convolution fusion | flops 4834983936 | bytes 14155776 | tf_op jit(solution)/shard_map/ra,rb->ab/dot_general | solution.py:34
  458.9 8.5 %convolution_convert_fusion = bf16[768,3072]{1,0:T(8,128)(2,1)S(1)} fusion(bf16[1024,3072]{1,0:T(8,128)(2,1)} %get-tuple-element.128, f32[1024,768]{1,0:T(8,128)S(1)} %copy-done.9, f32[768]{0:T(1024)S(1)} %copy-done.72, f32[768]{0:T(1024)S(1)} %copy-done.56, f32[1024]{0:T(1024)S(1)} %add_rsqrt_fusion.1, f32[1024]{0:T(1024)S(1)} %broadcast_multiply_fusion.6), kind=kOutput, calls=%fused_computation.28 | convolution fusion | flops 4838129664 | bytes 14170112 | tf_op jit(solution)/shard_map/ra,rb->ab/dot_general | solution.py:34
  471.7 2.2 collective-permute-done.15
  476.2 31.9 %collective-permute-done.11 = bf16[2,2,2,96,768]{4,3,2,1,0:T(8,128)(2,1)S(1)} collective-permute-done((bf16[2,2,2,96,768]{4,3,2,1,0:T(8,128)(2,1)S(1)}, bf16[2,2,2,96,768]{4,3,2,1,0:T(8,128)(2,1)S(1)}, u32[]{:S(2)}, u32[]{:S(2)}) %collective-permute-start.11) | collective-permute-done | bytes 1179680 | tf_op jit(solution)/shard_map/ppermute | solution.py:58
  511.4 20.6 %collective-permute-done.12 = bf16[2,2,96,768]{3,2,1,0:T(8,128)(2,1)S(1)} collective-permute-done((bf16[2,2,96,768]{3,2,1,0:T(8,128)(2,1)S(1)}, bf16[2,2,96,768]{3,2,1,0:T(8,128)(2,1)S(1)}, u32[]{:S(2)}, u32[]{:S(2)}) %collective-permute-start.12) | collective-permute-done | bytes 589856 | tf_op jit(solution)/shard_map/ppermute | solution.py:58
  534.6 13.6 %collective-permute-done.13 = bf16[2,96,768]{2,1,0:T(8,128)(2,1)S(1)} collective-permute-done((bf16[2,96,768]{2,1,0:T(8,128)(2,1)S(1)}, bf16[2,96,768]{2,1,0:T(8,128)(2,1)S(1)}, u32[]{:S(2)}, u32[]{:S(2)}) %collective-permute-start.13) | collective-permute-done | bytes 294944 | tf_op jit(solution)/shard_map/ppermute | solution.py:58
  550.0 7.1 %collective-permute-done.18 = bf16[2,96,768]{2,1,0:T(8,128)(2,1)S(1)} collective-permute-done((bf16[2,96,768]{2,1,0:T(8,128)(2,1)S(1)}, bf16[2,96,768]{2,1,0:T(8,128)(2,1)S(1)}, u32[]{:S(2)}, u32[]{:S(2)}) %collective-permute-start.18) | collective-permute-done | bytes 294944 | tf_op jit(solution)/shard_map/ppermute | solution.py:58
  557.4 8.4 %collective-permute-done.19 = bf16[96,768]{1,0:T(8,128)(2,1)S(1)} collective-permute-done((bf16[96,768]{1,0:T(8,128)(2,1)S(1)}, bf16[96,768]{1,0:T(8,128)(2,1)S(1)}, u32[]{:S(2)}, u32[]{:S(2)}) %collective-permute-start.19) | collective-permute-done | bytes 147488 | tf_op jit(solution)/shard_map/ppermute | solution.py:58
  567.5 4.6 convolution_convert_fusion.3
  575.1 2.7 fusion.100
  584.3 3.4 bitcast_convert_fusion.1
  587.7 59.1 %all-gather.16.cloned.1.call-done = bf16[6144,768]{1,0:T(8,128)(2,1)} async-done(((bf16[192,768]{1,0:T(8,128)(2,1)}), bf16[6144,768]{1,0:T(8,128)(2,1)}) %all-gather.16.cloned.1.call-update) | async-done | bytes 9437200 | tf_op jit(solution)/shard_map/all_gather | solution.py:339
  646.9 8.9 %fusion.98 = (bf16[32,96,768]{2,1,0:T(8,128)(2,1)S(1)}, f32[32,96,768]{2,1,0:T(8,128)}) fusion(bf16[32,192,768]{2,1,0:T(8,128)(2,1)} %bitcast.307), kind=kLoop, calls=%fused_computation.270 | loop fusion | flops 2359296 | bytes 23592960 | tf_op jit(solution)/shard_map/slice | solution.py:350
  655.7 4.8 fusion.99
  660.5 4.8 bitcast_convert_fusion
  665.3 4.2 pad_maximum_fusion
  (326 shorter events, 108.7 us)
Async XLA Ops:
  7.2 85.2 %copy-start = (bf16[416,2048]{1,0:T(8,128)(2,1)S(1)}, bf16[416,2048]{1,0:T(8,128)(2,1)}, u32[]{:S(2)}) copy-start(bf16[416,2048]{1,0:T(8,128)(2,1)} %param.34) | copy-start | bytes 5111812
  7.2 83.0 %all-gather.14.cloned.1.call-start = ((), (), s32[]{:S(2)}) async-start(), calls=%async_computation.4 | async-start | bytes 8110080 | tf_op jit(solution)/shard_map/all_gather | solution.py:116
  12.1 175.9 %all-gather.10.cloned.1.call-start = ((), (), s32[]{:S(2)}) async-start(), calls=%async_computation.2 | async-start | bytes 4866048 | tf_op jit(solution)/shard_map/all_gather | solution.py:119
  12.8 213.2 %all-gather.12.cloned.1.call-start = ((), (), s32[]{:S(2)}) async-start(), calls=%async_computation.3 | async-start | bytes 4866048 | tf_op jit(solution)/shard_map/all_gather | solution.py:120
  94.6 7.0 %copy-start.55 = (s32[4]{0:T(128)S(1)}, s32[4]{0:T(128)}, u32[]{:S(2)}) copy-start(s32[4]{0:T(128)} %param.37) | copy-start | bytes 52
  97.5 26.8 %all-to-all-start = ((bf16[32,13,768]{2,1,0:T(8,128)(2,1)}), bf16[32,13,768]{2,1,0:T(8,128)(2,1)S(1)}, u32[]{:S(2)}, u32[]{:S(2)}) async-start(bf16[32,13,768]{2,1,0:T(8,128)(2,1)} %all_to_all.14), calls=%async_computation | async-start | bytes 1572864 | tf_op jit(solution)/shard_map/all_to_all | solution.py:144
  104.7 20.7 %copy-start.64 = (pred[512]{0:T(512)(128)(4,1)}, pred[512]{0:T(512)(128)(4,1)S(1)}, u32[]{:S(2)}) copy-start(pred[512]{0:T(512)(128)(4,1)S(1)} %select_compare_fusion) | copy-start | bytes 1540
  104.8 20.6 %copy-start.60 = (s32[416]{0:T(512)}, s32[416]{0:T(512)S(1)}, u32[]{:S(2)}) copy-start(s32[416]{0:T(512)S(1)} %fusion.77) | copy-start | bytes 4996
  108.0 17.4 %copy-start.62 = (s32[512]{0:T(512)}, s32[512]{0:T(512)S(1)}, u32[]{:S(2)}) copy-start(s32[512]{0:T(512)S(1)} %select_add_fusion) | copy-start | bytes 6148
  112.6 14.6 %copy-start.39 = (bf16[512,768]{1,0:T(8,128)(2,1)S(1)}, bf16[512,768]{1,0:T(8,128)(2,1)}, u32[]{:S(2)}) copy-start(bf16[512,768]{1,0:T(8,128)(2,1)} %param.33) | copy-start | bytes 2359300
  112.6 15.9 %copy-start.67 = (f32[768]{0:T(1024)S(1)}, f32[768]{0:T(1024)}, u32[]{:S(2)}) copy-start(f32[768]{0:T(1024)} %param.45) | copy-start | bytes 9220
  125.4 3.1 copy-start.31
  134.4 22.2 %copy-start.4 = (bf16[4,256,12,64]{1,0,3,2:T(4,128)(2,1)}, bf16[4,256,12,64]{1,0,3,2:T(4,128)(2,1)S(1)}, u32[]{:S(2)}) copy-start(bf16[4,256,12,64]{1,0,3,2:T(4,128)(2,1)S(1)} %reshape.459) | copy-start | bytes 4718596
  139.3 6.7 copy-start.68
  164.4 13.1 %copy-start.26 = (bf16[4,256,12,64]{1,0,3,2:T(4,128)(2,1)S(1)}, bf16[4,256,12,64]{1,0,3,2:T(4,128)(2,1)}, u32[]{:S(2)}) copy-start(bf16[4,256,12,64]{1,0,3,2:T(4,128)(2,1)} %reshape.457) | copy-start | bytes 4718596
  177.5 4.5 copy-start.10
  177.5 4.8 copy-start.41
  187.9 38.1 %copy-start.70 = (f32[768]{0:T(1024)S(1)}, f32[768]{0:T(1024)}, u32[]{:S(2)}) copy-start(f32[768]{0:T(1024)} %param.56) | copy-start | bytes 9220
  242.4 18.8 %copy-start.8 = (f32[1024,768]{1,0:T(8,128)S(1)}, f32[1024,768]{1,0:T(8,128)}, u32[]{:S(2)}) copy-start(f32[1024,768]{1,0:T(8,128)} %copy-done.7) | copy-start | bytes 9437188
  276.8 4.1 copy-start.42
  280.9 7.3 %copy-start.27 = (bf16[4,256,12,64]{1,0,3,2:T(4,128)(2,1)S(1)}, bf16[4,256,12,64]{1,0,3,2:T(4,128)(2,1)}, u32[]{:S(2)}) copy-start(bf16[4,256,12,64]{1,0,3,2:T(4,128)(2,1)} %reshape.457) | copy-start | bytes 4718596
  280.9 7.4 %copy-start.29 = (bf16[4,256,12,64]{1,0,3,2:T(4,128)(2,1)S(1)}, bf16[4,256,12,64]{1,0,3,2:T(4,128)(2,1)}, u32[]{:S(2)}) copy-start(bf16[4,256,12,64]{1,0,3,2:T(4,128)(2,1)} %reshape.463) | copy-start | bytes 4718596
  280.9 16.3 %slice-start.1 = ((s8[12582912]{0:T(1024)(128)(4,1)}), s8[4194304]{0:T(1024)(128)(4,1)S(1)}, s32[]{:S(2)}) async-start(s8[12582912]{0:T(1024)(128)(4,1)} %bitcast.301), calls=%async_computation.8 | async-start | bytes 8388608
  280.9 16.3 %slice-start.2 = ((s8[12582912]{0:T(1024)(128)(4,1)}), s8[4194304]{0:T(1024)(128)(4,1)S(1)}, s32[]{:S(2)}) async-start(s8[12582912]{0:T(1024)(128)(4,1)} %bitcast.301), calls=%async_computation.9 | async-start | bytes 8388608
  288.2 8.9 %slice-start.3 = ((s8[12582912]{0:T(1024)(128)(4,1)}), s8[4194304]{0:T(1024)(128)(4,1)S(1)}, s32[]{:S(2)}) async-start(s8[12582912]{0:T(1024)(128)(4,1)} %bitcast.301), calls=%async_computation.10 | async-start | bytes 8388608
  297.2 7.2 %copy-start.6 = (bf16[4,256,12,64]{1,0,3,2:T(4,128)(2,1)S(1)}, bf16[4,256,12,64]{1,0,3,2:T(4,128)(2,1)}, u32[]{:S(2)}) copy-start(bf16[4,256,12,64]{1,0,3,2:T(4,128)(2,1)} %reshape.461) | copy-start | bytes 4718596
  328.6 24.0 %all-to-all-start.1 = ((bf16[32,13,768]{2,1,0:T(8,128)(2,1)}), bf16[32,13,768]{2,1,0:T(8,128)(2,1)}, u32[]{:S(2)}, u32[]{:S(2)}) async-start(bf16[32,13,768]{2,1,0:T(8,128)(2,1)} %all_to_all.17), calls=%async_computation.1 | async-start | bytes 1572864 | tf_op jit(solution)/shard_map/all_to_all | solution.py:289
  331.9 240.2 %all-gather.18.cloned.1.call-start = ((), (), s32[]{:S(2)}) async-start(), calls=%async_computation.6 | async-start | bytes 8515584 | tf_op jit(solution)/shard_map/all_gather | solution.py:347
  332.0 3.0 copy-start.13
  332.0 3.0 copy-start.25
  338.9 15.9 %copy-start.2 = (f32[416,768]{1,0:T(8,128)S(1)}, f32[416,768]{1,0:T(8,128)}, u32[]{:S(2)}) copy-start(f32[416,768]{1,0:T(8,128)} %copy-done.1) | copy-start | bytes 3833860
  338.9 15.9 %copy-start.44 = (f32[768]{0:T(1024)S(1)}, f32[768]{0:T(1024)}, u32[]{:S(2)}) copy-start(f32[768]{0:T(1024)} %param.42) | copy-start | bytes 9220
  338.9 15.9 %copy-start.46 = (f32[416]{0:T(512)S(1)}, f32[416]{0:T(512)}, u32[]{:S(2)}) copy-start(f32[416]{0:T(512)} %copy-done.45) | copy-start | bytes 4996
  338.9 15.9 %copy-start.49 = (f32[416]{0:T(512)S(1)}, f32[416]{0:T(512)}, u32[]{:S(2)}) copy-start(f32[416]{0:T(512)} %copy-done.48) | copy-start | bytes 4996
  340.5 35.3 %collective-permute-start = (bf16[2,2,2,2,96,768]{5,4,0,1,2,3:T(8,128)(2,1)}, bf16[2,2,2,2,96,768]{5,4,0,1,2,3:T(8,128)(2,1)}, u32[]{:S(2)}, u32[]{:S(2)}) collective-permute-start(bf16[2,2,2,2,96,768]{5,4,0,1,2,3:T(8,128)(2,1)} %bitcast.292), channel_id=1, source_target_pairs={{0,1},{1,0},{2,3},{3,2},{4,5},{5,4},{6,7},{7,6},{8,9},{9,8},{10,11... | collective-permute-start | bytes 7077896 | tf_op jit(solution)/shard_map/ppermute | solution.py:58
  354.8 7.2 %copy-start.54 = (bf16[4,416]{1,0:T(4,128)(2,1)S(1)}, bf16[4,416]{1,0:T(4,128)(2,1)}, u32[]{:S(2)}) copy-start(bf16[4,416]{1,0:T(4,128)(2,1)} %param.35) | copy-start | bytes 9988
  363.5 9.3 %copy-start.37 = (bf16[2,2,2,2,2,1,768]{6,5,4,3,2,1,0:T(2,128)(2,1)}, bf16[2,2,2,2,2,1,768]{6,5,4,3,2,1,0:T(2,128)(2,1)S(1)}, u32[]{:S(2)}) copy-start(bf16[2,2,2,2,2,1,768]{6,5,4,3,2,1,0:T(2,128)(2,1)S(1)} %concatenate.64) | copy-start | bytes 147460
  375.6 3.6 collective-permute-start.5
  375.7 3.5 copy-start.3
  375.8 3.5 copy-start.38
  379.0 5.8 copy-start.14
  383.3 20.5 %collective-permute-start.6 = (bf16[2,2,2,65,768]{4,2,3,1,0:T(2,128)(2,1)}, bf16[2,2,2,65,768]{4,2,3,1,0:T(2,128)(2,1)}, u32[]{:S(2)}, u32[]{:S(2)}) collective-permute-start(bf16[2,2,2,65,768]{4,2,3,1,0:T(2,128)(2,1)} %bitcast.295), channel_id=1, source_target_pairs={{0,4},{1,5},{2,6},{3,7},{4,0},{5,1},{6,2},{7,3},{8,12},{9,13},{10,... | collective-permute-start | bytes 2396168 | tf_op jit(solution)/shard_map/ppermute | solution.py:58
  385.9 29.1 %collective-permute-start.1 = (bf16[2,2,2,96,768]{4,3,0,1,2:T(8,128)(2,1)}, bf16[2,2,2,96,768]{4,3,0,1,2:T(8,128)(2,1)}, u32[]{:S(2)}, u32[]{:S(2)}) collective-permute-start(bf16[2,2,2,96,768]{4,3,0,1,2:T(8,128)(2,1)} %dynamic-slice_bitcast_fusion.3), channel_id=1, source_target_pairs={{0,2},{1,3},{2,0},{3,1},{4,6},{5,7},{6,4},{7,5},{8,10},{9,11},{10,... | collective-permute-start | bytes 3538952 | tf_op jit(solution)/shard_map/ppermute | solution.py:58
  387.4 27.7 %copy-start.15 = (bf16[2,2,2,2,96,768]{5,4,0,1,2,3:T(8,128)(2,1)S(1)}, bf16[2,2,2,2,96,768]{5,4,0,1,2,3:T(8,128)(2,1)}, u32[]{:S(2)}) copy-start(bf16[2,2,2,2,96,768]{5,4,0,1,2,3:T(8,128)(2,1)} %copy-done.14) | copy-start | bytes 7077892
  406.0 17.8 %collective-permute-start.7 = (bf16[2,2,65,768]{3,2,1,0:T(8,128)(2,1)}, bf16[2,2,65,768]{3,2,1,0:T(8,128)(2,1)}, u32[]{:S(2)}, u32[]{:S(2)}) collective-permute-start(bf16[2,2,65,768]{3,2,1,0:T(8,128)(2,1)} %dynamic-slice_bitcast_fusion.7), channel_id=1, source_target_pairs={{0,2},{1,3},{2,0},{3,1},{4,6},{5,7},{6,4},{7,5},{8,10},{9,11},{10,... | collective-permute-start | bytes 1198088 | tf_op jit(solution)/shard_map/ppermute | solution.py:58
  416.7 14.0 %collective-permute-start.2 = (bf16[2,2,96,768]{3,2,0,1:T(8,128)(2,1)S(1)}, bf16[2,2,96,768]{3,2,0,1:T(8,128)(2,1)}, u32[]{:S(2)}, u32[]{:S(2)}) collective-permute-start(bf16[2,2,96,768]{3,2,0,1:T(8,128)(2,1)S(1)} %dynamic-slice_bitcast_fusion.6), channel_id=1, source_target_pairs={{0,4},{1,5},{2,6},{3,7},{4,0},{5,1},{6,2},{7,3},{8,12},{9,13},{10,... | collective-permute-start | bytes 1769480 | tf_op jit(solution)/shard_map/ppermute | solution.py:58
  425.0 7.7 %collective-permute-start.8 = (bf16[2,65,768]{2,1,0:T(8,128)(2,1)S(1)}, bf16[2,65,768]{2,1,0:T(8,128)(2,1)S(1)}, u32[]{:S(2)}, u32[]{:S(2)}) collective-permute-start(bf16[2,65,768]{2,1,0:T(8,128)(2,1)S(1)} %dynamic-slice_bitcast_fusion.11), channel_id=1, source_target_pairs={{0,8},{8,0},{16,24},{24,16},{1,9},{9,1},{17,25},{25,17},{2,10},{10... | collective-permute-start | bytes 599048 | tf_op jit(solution)/shard_map/ppermute | solution.py:58
  431.9 9.0 %collective-permute-start.3 = (bf16[2,96,768]{2,1,0:T(8,128)(2,1)S(1)}, bf16[2,96,768]{2,1,0:T(8,128)(2,1)S(1)}, u32[]{:S(2)}, u32[]{:S(2)}) collective-permute-start(bf16[2,96,768]{2,1,0:T(8,128)(2,1)S(1)} %dynamic-slice_bitcast_fusion.10), channel_id=1, source_target_pairs={{0,8},{8,0},{16,24},{24,16},{1,9},{9,1},{17,25},{25,17},{2,10},{10... | collective-permute-start | bytes 884744 | tf_op jit(solution)/shard_map/ppermute | solution.py:58
  432.9 8.2 %collective-permute-start.9 = (bf16[65,768]{1,0:T(8,128)(2,1)S(1)}, bf16[65,768]{1,0:T(8,128)(2,1)S(1)}, u32[]{:S(2)}, u32[]{:S(2)}) collective-permute-start(bf16[65,768]{1,0:T(8,128)(2,1)S(1)} %dynamic-slice_bitcast_fusion.15), channel_id=1, source_target_pairs={{0,16},{8,24},{16,0},{24,8},{1,17},{9,25},{17,1},{25,9},{2,18},{10... | collective-permute-start | bytes 299528 | tf_op jit(solution)/shard_map/ppermute | solution.py:58
  441.0 6.8 collective-permute-start.4
  448.5 198.3 %all-gather.16.cloned.1.call-start = ((), (), s32[]{:S(2)}) async-start(), calls=%async_computation.5 | async-start | bytes 9732096 | tf_op jit(solution)/shard_map/all_gather | solution.py:339
  457.3 12.1 %collective-permute-start.10 = (bf16[2,2,2,2,96,768]{5,4,3,2,1,0:T(8,128)(2,1)S(1)}, bf16[2,2,2,2,96,768]{5,4,3,2,1,0:T(8,128)(2,1)S(1)}, u32[]{:S(2)}, u32[]{:S(2)}) collective-permute-start(bf16[2,2,2,2,96,768]{5,4,3,2,1,0:T(8,128)(2,1)S(1)} %dynamic-slice_bitcast_fusion), channel_id=1, source_target_pairs={{0,1},{1,0},{2,3},{3,2},{4,5},{5,4},{6,7},{7,6},{8,9},{9,8},{10,11... | collective-permute-start | bytes 7077896 | tf_op jit(solution)/shard_map/ppermute | solution.py:58
  469.3 4.6 collective-permute-start.15
  470.2 37.9 %collective-permute-start.11 = (bf16[2,2,2,96,768]{4,3,2,1,0:T(8,128)(2,1)S(1)}, bf16[2,2,2,96,768]{4,3,2,1,0:T(8,128)(2,1)S(1)}, u32[]{:S(2)}, u32[]{:S(2)}) collective-permute-start(bf16[2,2,2,96,768]{4,3,2,1,0:T(8,128)(2,1)S(1)} %dynamic-slice_bitcast_fusion.2), channel_id=1, source_target_pairs={{0,2},{1,3},{2,0},{3,1},{4,6},{5,7},{6,4},{7,5},{8,10},{9,11},{10,... | collective-permute-start | bytes 3538952 | tf_op jit(solution)/shard_map/ppermute | solution.py:58
  474.7 35.3 %collective-permute-start.16 = (bf16[2,2,2,96,768]{4,3,0,1,2:T(8,128)(2,1)S(1)}, bf16[2,2,2,96,768]{4,3,0,1,2:T(8,128)(2,1)S(1)}, u32[]{:S(2)}, u32[]{:S(2)}) collective-permute-start(bf16[2,2,2,96,768]{4,3,0,1,2:T(8,128)(2,1)S(1)} %dynamic-slice_bitcast_fusion.1), channel_id=1, source_target_pairs={{0,4},{1,5},{2,6},{3,7},{4,0},{5,1},{6,2},{7,3},{8,12},{9,13},{10,... | collective-permute-start | bytes 3538952 | tf_op jit(solution)/shard_map/ppermute | solution.py:58
  508.5 23.5 %collective-permute-start.12 = (bf16[2,2,96,768]{3,2,1,0:T(8,128)(2,1)S(1)}, bf16[2,2,96,768]{3,2,1,0:T(8,128)(2,1)S(1)}, u32[]{:S(2)}, u32[]{:S(2)}) collective-permute-start(bf16[2,2,96,768]{3,2,1,0:T(8,128)(2,1)S(1)} %dynamic-slice_bitcast_fusion.5), channel_id=1, source_target_pairs={{0,4},{1,5},{2,6},{3,7},{4,0},{5,1},{6,2},{7,3},{8,12},{9,13},{10,... | collective-permute-start | bytes 1769480 | tf_op jit(solution)/shard_map/ppermute | solution.py:58
  510.4 23.2 %collective-permute-start.17 = (bf16[2,2,96,768]{3,2,0,1:T(8,128)(2,1)S(1)}, bf16[2,2,96,768]{3,2,0,1:T(8,128)(2,1)S(1)}, u32[]{:S(2)}, u32[]{:S(2)}) collective-permute-start(bf16[2,2,96,768]{3,2,0,1:T(8,128)(2,1)S(1)} %dynamic-slice_bitcast_fusion.4), channel_id=1, source_target_pairs={{0,2},{1,3},{2,0},{3,1},{4,6},{5,7},{6,4},{7,5},{8,10},{9,11},{10,... | collective-permute-start | bytes 1769480 | tf_op jit(solution)/shard_map/ppermute | solution.py:58
  532.2 34.4 %copy-start.17 = (bf16[416,768]{1,0:T(8,128)(2,1)S(1)}, bf16[416,768]{1,0:T(8,128)(2,1)}, u32[]{:S(2)}) copy-start(bf16[416,768]{1,0:T(8,128)(2,1)} %get-tuple-element.71) | copy-start | bytes 1916932
  532.2 34.4 %copy-start.51 = (bf16[4,768]{1,0:T(4,128)(2,1)S(1)}, bf16[4,768]{1,0:T(4,128)(2,1)}, u32[]{:S(2)}) copy-start(bf16[4,768]{1,0:T(4,128)(2,1)} %param.40) | copy-start | bytes 18436
  532.2 15.9 %collective-permute-start.13 = (bf16[2,96,768]{2,1,0:T(8,128)(2,1)S(1)}, bf16[2,96,768]{2,1,0:T(8,128)(2,1)S(1)}, u32[]{:S(2)}, u32[]{:S(2)}) collective-permute-start(bf16[2,96,768]{2,1,0:T(8,128)(2,1)S(1)} %dynamic-slice_bitcast_fusion.9), channel_id=1, source_target_pairs={{0,8},{8,0},{16,24},{24,16},{1,9},{9,1},{17,25},{25,17},{2,10},{10... | collective-permute-start | bytes 884744 | tf_op jit(solution)/shard_map/ppermute | solution.py:58
  533.7 23.4 %collective-permute-start.18 = (bf16[2,96,768]{2,1,0:T(8,128)(2,1)S(1)}, bf16[2,96,768]{2,1,0:T(8,128)(2,1)S(1)}, u32[]{:S(2)}, u32[]{:S(2)}) collective-permute-start(bf16[2,96,768]{2,1,0:T(8,128)(2,1)S(1)} %dynamic-slice_bitcast_fusion.8), channel_id=1, source_target_pairs={{0,8},{8,0},{16,24},{24,16},{1,9},{9,1},{17,25},{25,17},{2,10},{10... | collective-permute-start | bytes 884744 | tf_op jit(solution)/shard_map/ppermute | solution.py:58
  548.2 9.1 %collective-permute-start.14 = (bf16[96,768]{1,0:T(8,128)(2,1)S(1)}, bf16[96,768]{1,0:T(8,128)(2,1)S(1)}, u32[]{:S(2)}, u32[]{:S(2)}) collective-permute-start(bf16[96,768]{1,0:T(8,128)(2,1)S(1)} %dynamic-slice_bitcast_fusion.13), channel_id=1, source_target_pairs={{0,16},{8,24},{16,0},{24,8},{1,17},{9,25},{17,1},{25,9},{2,18},{10... | collective-permute-start | bytes 442376 | tf_op jit(solution)/shard_map/ppermute | solution.py:58
  557.3 8.5 %collective-permute-start.19 = (bf16[96,768]{1,0:T(8,128)(2,1)S(1)}, bf16[96,768]{1,0:T(8,128)(2,1)S(1)}, u32[]{:S(2)}, u32[]{:S(2)}) collective-permute-start(bf16[96,768]{1,0:T(8,128)(2,1)S(1)} %dynamic-slice_bitcast_fusion.12), channel_id=1, source_target_pairs={{0,16},{8,24},{16,0},{24,8},{1,17},{9,25},{17,1},{25,9},{2,18},{10... | collective-permute-start | bytes 442376 | tf_op jit(solution)/shard_map/ppermute | solution.py:58
  581.0 3.3 slice-start
  (40 other events, 66.2 us)
Sparse Core Ops, SparseCore 0:
  12.2 77.9 all-gather.13
  93.1 66.8 all-gather.9
  162.9 62.4 all-gather.11
  448.7 98.3 all-gather.17
  566.7 80.0 all-gather.15

commit v2 on v0

v2 whole, which is shorter than its diff:
```python
import functools
import math

import jax
import jax.numpy as jnp
from jax import lax
from jax.experimental import pallas as pl
from jax.experimental.pallas import tpu as pltpu
from jax.sharding import PartitionSpec as P

HEADS = 12
epsilon = 1e-05
f32, bf16 = jnp.float32, jnp.bfloat16

ERFC_P = 0.35
ERFC_C = (
    0.19567911,
    0.22612264,
    0.02080242,
    0.63768037,
    -0.6386366,
    0.75239514,
    -0.19404308,
)


def nn(a, b):
    return lax.dot_general(a, b, (((1,), (0,)), ((), ())), preferred_element_type=f32)


def nt(a, b):
    return lax.dot_general(a, b, (((1,), (1,)), ((), ())), preferred_element_type=f32)


def tn(a, b):
    return lax.dot_general(a, b, (((0,), (0,)), ((), ())), preferred_element_type=f32)


def norm_parts(values):
    centered = values - jnp.mean(values, -1, keepdims=True)
    inverse = lax.rsqrt(jnp.mean(centered * centered, -1, keepdims=True) + epsilon)
    return centered * inverse, inverse


def norm_back(upstream, normed, inverse, gain):
    weighted = upstream * gain
    return inverse * (
        weighted
        - jnp.mean(weighted, -1, keepdims=True)
        - normed * jnp.mean(weighted * normed, -1, keepdims=True)
    )


def gelu_parts(x):
    e = jnp.exp(-0.5 * x * x)
    t = 1.0 / (1.0 + (ERFC_P * math.sqrt(0.5)) * jnp.abs(x))
    acc = jnp.full_like(t, 0.5 * ERFC_C[-1])
    for c in ERFC_C[-2::-1]:
        acc = acc * t + 0.5 * c
    tail = acc * t * e
    phi = jnp.where(x >= 0, 1.0 - tail, tail)
    return x * phi, phi + x * (e * (1.0 / math.sqrt(2.0 * math.pi)))


def one_hot(wanted, live, rows, pad, sent, devices, offset):
    row = lax.broadcasted_iota(jnp.int32, (1, rows), 1)
    shift = pad.bit_length() - 1
    turn = lax.shift_right_logical(row, shift) - offset
    turn = jnp.where(turn < 0, turn + devices, turn)
    inside = jnp.bitwise_and(row, pad - 1)
    arrival = jnp.where(inside < sent, inside * devices + turn, -1)
    return ((wanted == arrival) & live).astype(bf16)


def spread(pad, sent, rows, padded):
    to = lax.broadcasted_iota(jnp.int32, (padded, 1), 0)
    shift = pad.bit_length() - 1
    inside = jnp.bitwise_and(to, pad - 1)
    source = jnp.where(inside < sent, lax.shift_right_logical(to, shift) * sent + inside, -1)
    return (source == lax.broadcasted_iota(jnp.int32, (1, rows), 1)).astype(bf16)


def image_encode(
    pad, sent, x_ref, box_ref, wi_ref, wb_ref, bi_ref, gr_ref, betar_ref, pre_ref, enc_ref
):
    pre = nn(x_ref[...], wi_ref[...]) + tn(box_ref[...], wb_ref[...]) + bi_ref[...]
    pre_ref[...] = pre
    normed, _ = norm_parts(pre)
    encoded = (normed * gr_ref[...] + betar_ref[...]).astype(bf16)
    enc_ref[...] = nn(spread(pad, sent, x_ref.shape[0], enc_ref.shape[0]), encoded).astype(bf16)


def attention_forward(
    pad, sent, devices,
    captions, counts, offset,
    enc_ref, text_ref,
    wq_ref, wk_ref, wv_ref, wo_ref, bq_ref, bv_ref, bo_ref, g_ref, beta_ref,
    h_ref, q_ref, k_ref, v_ref, p_ref, c_ref, mixed_ref, n_ref,
):
    s = pl.program_id(0)
    text_len = text_ref.shape[0]
    rows, width = h_ref.shape
    hd = width // HEADS
    start = jnp.int32(0)
    for i in range(captions.shape[0]):
        start = start + jnp.where(s > i, counts[i], 0)
    slot = lax.broadcasted_iota(jnp.int32, (rows - text_len, 1), 0)
    taken = one_hot(
        slot + start, slot < counts[s], enc_ref.shape[0], pad, sent, devices, offset[0]
    )
    h_ref[:text_len, :] = text_ref[...]
    h_ref[text_len:, :] = nn(taken, enc_ref[...]).astype(bf16)
    h = h_ref[...]
    q = (nn(h, wq_ref[...]) + bq_ref[...]).astype(bf16)
    k = nn(h, wk_ref[...]).astype(bf16)
    v = (nn(h, wv_ref[...]) + bv_ref[...]).astype(bf16)
    q_ref[...] = q
    k_ref[...] = k
    v_ref[...] = v
    row = lax.broadcasted_iota(jnp.int32, (rows, 1), 0)
    live = (row < captions[s]) | ((row >= text_len) & (row < text_len + counts[s]))
    lane = lax.broadcasted_iota(jnp.int32, (1, 2 * hd), 1)
    masks = [(lane < hd).astype(bf16), (lane >= hd).astype(bf16)]
    scaled = q * jnp.asarray(hd**-0.5, bf16)
    for pair in range(HEADS // 2):
        cols = slice(pair * 2 * hd, (pair + 1) * 2 * hd)
        context = None
        for j in range(2):
            scores = nt(k[:, cols], scaled[:, cols] * masks[j])
            scores = jnp.where(live, scores, -1e30)
            top = jnp.max(scores, 0, keepdims=True)
            e = jnp.exp(scores - top)
            p = (e * (1.0 / jnp.sum(e, 0, keepdims=True))).astype(bf16)
            p_ref[0, 2 * pair + j] = p
            part = tn(p, v[:, cols] * masks[j])
            context = part if context is None else context + part
        c_ref[:, cols] = context.astype(bf16)
    mixed = h.astype(f32) + nn(c_ref[...], wo_ref[...]) + bo_ref[...]
    mixed_ref[...] = mixed
    normed, _ = norm_parts(mixed)
    n_ref[...] = (normed * g_ref[...] + beta_ref[...]).astype(bf16)


def image_backward(
    pad, sent, core_ref,
    x_ref, box_ref, wi_ref, pre_ref, back_ref, gr_ref, sums_ref, attn_sums_ref, bu_ref,
    gp_ref, gx_ref, away_ref, kept_ref, acc_ref,
):
    rows, feat = x_ref.shape
    width = pre_ref.shape[1]
    grad = tn(spread(pad, sent, rows, back_ref.shape[0]), back_ref[...])
    normed, inverse = norm_parts(pre_ref[...])
    gp = norm_back(grad, normed, inverse, gr_ref[...]).astype(bf16)
    gp_ref[...] = gp
    acc_ref[:feat, :] = tn(x_ref[...], gp)
    acc_ref[feat:, :] = jnp.zeros((acc_ref.shape[0] - feat, width), f32)
    acc_ref[feat : feat + box_ref.shape[0], :] = nn(box_ref[...], gp)
    at = feat + 8
    acc_ref[at : at + 1, :] = jnp.sum(gp.astype(f32), 0, keepdims=True)
    acc_ref[at + 1 : at + 2, :] = jnp.sum(grad * normed, 0, keepdims=True)
    acc_ref[at + 2 : at + 3, :] = jnp.sum(grad, 0, keepdims=True)
    acc_ref[at + 8 : at + 16, :] = sums_ref[...]
    acc_ref[at + 16 : at + 24, :] = attn_sums_ref[...]
    acc_ref[at + 24 : at + 24 + bu_ref.shape[0], :] = bu_ref[...]
    core = core_ref[0]
    pairs, chunk, _ = away_ref.shape
    for i in range(pairs):
        first = pl.multiple_of((2 * i + 1 - core) * chunk, 8)
        away_ref[i] = acc_ref[pl.ds(first, chunk), :].astype(bf16)
        first = pl.multiple_of((2 * i + core) * chunk, 8)
        kept_ref[i] = acc_ref[pl.ds(first, chunk), :].astype(bf16)
    gx_ref[...] = nt(gp, wi_ref[...]).astype(bf16)


def feed_forward(
    captions, counts, n_ref, mixed_ref, cot_ref, wd_ref, *refs,
):
    blocks = len(refs) - 17
    up_refs = refs[:blocks]
    wu_ref = refs[-1]

    @pl.when(pl.program_id(0) == 0)
    def _():
        for j in range(blocks):
            wu_ref[j] = up_refs[j][...].astype(f32).reshape(wu_ref.shape[1:]).astype(bf16)

    feed_forward_rows(captions, counts, n_ref, mixed_ref, cot_ref, wu_ref, wd_ref, *refs[blocks:-1])


def feed_forward_rows(
    captions, counts, n_ref, mixed_ref, cot_ref, wu_ref, wd_ref, wo_ref, bu_ref, bd_ref, g1_ref, g2_ref, beta2_ref,
    out_ref, act_ref, gdo_ref, gg_ref, gm_ref, ga_ref, gc_ref, sums_ref, bu_sum_ref, d_ref,
):
    s = pl.program_id(0)
    n1 = n_ref[...]
    rows, width = n1.shape
    ff = act_ref.shape[1]
    step = width
    per = wd_ref.shape[0] * step // ff

    def down_rows(j):
        return wd_ref[j // step * per : (j // step + 1) * per].reshape(step, width)

    @pl.when(s == 0)
    def _():
        sums_ref[...] = jnp.zeros_like(sums_ref)
        bu_sum_ref[...] = jnp.zeros_like(bu_sum_ref)

    second = n1.astype(f32) + bd_ref[...]
    for j in range(0, ff, step):
        cols = slice(j, j + step)
        gate = nn(n1, wu_ref[j // step]) + bu_ref[cols]
        act, d = gelu_parts(gate)
        act = act.astype(bf16)
        act_ref[:, cols] = act
        d_ref[:, cols] = d
        second = second + nn(act, down_rows(j))
    normed, inverse = norm_parts(second)
    text_len = rows // 2
    row = lax.broadcasted_iota(jnp.int32, (rows, 1), 0)
    live = (row < captions[s]) | ((row >= text_len) & (row < text_len + counts[s]))
    live = live.astype(f32)
    out_ref[...] = ((normed * g2_ref[...] + beta2_ref[...]) * live).astype(bf16)
    up = cot_ref[...].astype(f32) * live

    def add(i, value):
        sums_ref[i : i + 1, :] += jnp.sum(value, 0, keepdims=True)

    add(0, up * normed)
    add(1, up)
    gsi = norm_back(up, normed, inverse, g2_ref[...])
    gdo = gsi.astype(bf16)
    gdo_ref[...] = gdo
    add(2, gdo.astype(f32))
    first = gsi
    for j in range(0, ff, step):
        cols = slice(j, j + step)
        gg = (nt(gdo, down_rows(j)) * d_ref[:, cols]).astype(bf16)
        gg_ref[:, cols] = gg
        bu_sum_ref[:, cols] += jnp.sum(gg.astype(f32), 0, keepdims=True)
        first = first + nt(gg, wu_ref[j // step])
    normed, inverse = norm_parts(mixed_ref[...])
    add(3, first * normed)
    add(4, first)
    gm = norm_back(first, normed, inverse, g1_ref[...])
    gm_ref[...] = gm
    ga = gm.astype(bf16)
    ga_ref[...] = ga
    add(5, ga.astype(f32))
    gc_ref[...] = nt(ga, wo_ref[...]).astype(bf16)


def attention_backward(
    pad, sent, devices,
    counts, offset,
    q_ref, k_ref, v_ref, p_ref, gc_ref, gm_ref, wq_ref, wk_ref, wv_ref,
    gq_ref, gk_ref, gv_ref, gt_ref, gs_ref, sums_ref, acc_ref,
):
    s = pl.program_id(0)
    rows, width = q_ref.shape
    hd = width // HEADS
    scale = hd**-0.5

    @pl.when(s == 0)
    def _():
        sums_ref[...] = jnp.zeros_like(sums_ref)

    lane = lax.broadcasted_iota(jnp.int32, (1, 2 * hd), 1)
    masks = [(lane < hd).astype(bf16), (lane >= hd).astype(bf16)]
    for pair in range(HEADS // 2):
        cols = slice(pair * 2 * hd, (pair + 1) * 2 * hd)
        gq = gk = gv = None
        for j in range(2):
            p = p_ref[0, 2 * pair + j]
            gc = gc_ref[:, cols] * masks[j]
            gp = nt(v_ref[:, cols], gc)
            part = nn(p, gc)
            gv = part if gv is None else gv + part
            pf = p.astype(f32)
            weighted = pf * gp
            gs = (weighted - pf * jnp.sum(weighted, 0, keepdims=True)).astype(bf16)
            part = tn(gs, k_ref[:, cols] * masks[j])
            gq = part if gq is None else gq + part
            part = nn(gs, q_ref[:, cols] * masks[j])
            gk = part if gk is None else gk + part
        gq_ref[:, cols] = (gq * scale).astype(bf16)
        gk_ref[:, cols] = (gk * scale).astype(bf16)
        gv_ref[:, cols] = gv.astype(bf16)
    gq, gk, gv = gq_ref[...], gk_ref[...], gv_ref[...]
    sums_ref[0:1, :] += jnp.sum(gq.astype(f32), 0, keepdims=True)
    sums_ref[1:2, :] += jnp.sum(gv.astype(f32), 0, keepdims=True)
    hidden = gm_ref[...] + nt(gq, wq_ref[...]) + nt(gk, wk_ref[...]) + nt(gv, wv_ref[...])
    text_len = gt_ref.shape[0]
    gt_ref[...] = hidden[:text_len].astype(bf16)
    start = jnp.int32(0)
    for i in range(counts.shape[0]):
        start = start + jnp.where(s > i, counts[i], 0)
    slot = lax.broadcasted_iota(jnp.int32, (rows - text_len, 1), 0)
    taken = one_hot(
        slot + start, slot < counts[s], acc_ref.shape[0], pad, sent, devices, offset[0]
    )
    part = tn(taken, hidden[text_len:].astype(bf16))

    @pl.when(s == 0)
    def _():
        acc_ref[...] = part

    @pl.when(s > 0)
    def _():
        acc_ref[...] += part

    @pl.when(s == pl.num_programs(0) - 1)
    def _():
        gs_ref[...] = acc_ref[...].astype(bf16)


def whole(shape):
    return pl.BlockSpec(shape, lambda s, *_: (0,) * len(shape), pipeline_mode=pl.Buffered(1))


def tile(shape):
    return pl.BlockSpec(shape, lambda s, *_: (s,) + (0,) * (len(shape) - 1))


def still(shape):
    return pl.BlockSpec(shape, lambda s, *_: (0,) * len(shape))


LIMIT = 60 * 1024 * 1024


def cost(flops, moved, exps=0):
    return pl.CostEstimate(flops=int(flops), bytes_accessed=int(moved), transcendentals=int(exps))


def run_image_encode(geometry, x, boxes, wi, wb, bi, gr, betar):
    pad, sent, devices = geometry
    rows, feat = x.shape
    d = wi.shape[1]
    operands = (x, boxes, wi, wb, bi, gr, betar)
    shapes = [jax.ShapeDtypeStruct((rows, d), f32), jax.ShapeDtypeStruct((pad * devices, d), bf16)]
    return pl.pallas_call(
        functools.partial(image_encode, pad, sent),
        out_shape=shapes,
        compiler_params=pltpu.CompilerParams(vmem_limit_bytes=LIMIT),
        cost_estimate=cost(2 * rows * d * feat, x.size * 2 + wi.size * 2 + rows * d * 6),
        name="image_encode",
    )(*operands)


def run_attention_forward(
    geometry, captions, counts, offset, enc, text, wq, wk, wv, wo, bq, bv, bo, g1, beta1
):
    seqs = captions.shape[0]
    text_rows, d = text.shape
    total = 2 * text_rows
    L = total // seqs
    row = tile((L, d))
    vec = whole((d,))
    mat = whole((d, d))
    shapes = (
        [jax.ShapeDtypeStruct((total, d), bf16)] * 4
        + [
            jax.ShapeDtypeStruct((seqs, HEADS, L, L), bf16),
            jax.ShapeDtypeStruct((total, d), bf16),
            jax.ShapeDtypeStruct((total, d), f32),
            jax.ShapeDtypeStruct((total, d), bf16),
        ]
    )
    return pl.pallas_call(
        functools.partial(attention_forward, *geometry),
        out_shape=shapes,
        grid_spec=pltpu.PrefetchScalarGridSpec(
            num_scalar_prefetch=3,
            grid=(seqs,),
            in_specs=[whole(enc.shape), tile((L // 2, d))] + [mat] * 4 + [vec] * 5,
            out_specs=[row] * 4 + [tile((1, HEADS, L, L))] + [row] * 3,
        ),
        compiler_params=pltpu.CompilerParams(
            dimension_semantics=("arbitrary",), vmem_limit_bytes=LIMIT
        ),
        cost_estimate=cost(
            2 * total * d * (4 * d + 2 * L * 4),
            total * d * 18 + seqs * HEADS * L * L * 2,
            seqs * HEADS * L * L,
        ),
        name="attention_forward",
    )(
        captions, counts, offset, enc, text,
        wq, wk, wv, wo, bq, bv, bo, g1, beta1,
    )


def run_image_backward(geometry, chunk, core, x, boxes, wi, pre, back, gr, sums, attn_sums, bu):
    pad, sent, devices = geometry
    rows, feat = x.shape
    d = pre.shape[1]
    half = jax.ShapeDtypeStruct((devices // 2, chunk, d), bf16)
    operands = (x, boxes, wi, pre, back, gr, sums, attn_sums, bu)
    return pl.pallas_call(
        functools.partial(image_backward, pad, sent),
        out_shape=[
            jax.ShapeDtypeStruct((rows, d), bf16),
            jax.ShapeDtypeStruct((rows, feat), bf16),
            half,
            half,
        ],
        grid_spec=pltpu.PrefetchScalarGridSpec(
            num_scalar_prefetch=1,
            grid=(1,),
            in_specs=[whole(o.shape) for o in operands],
            out_specs=[whole((rows, d)), whole((rows, feat)), whole(half.shape), whole(half.shape)],
            scratch_shapes=[pltpu.VMEM((devices * chunk, d), f32)],
        ),
        compiler_params=pltpu.CompilerParams(
            dimension_semantics=("arbitrary",), vmem_limit_bytes=LIMIT
        ),
        cost_estimate=cost(4 * rows * d * feat, x.size * 4 + wi.size * 2 + devices * chunk * d * 2),
        name="image_backward",
    )(core, *operands)


def join_kernel(core_ref, *refs):
    core = core_ref[0]
    out_ref = refs[-1]
    groups = list(zip(refs[:-1:2], refs[1:-1:2]))
    at = 0
    for i in range(groups[0][0].shape[0]):
        for first in (0, 1):
            for own_ref, came_ref in groups:
                own, came = own_ref[i].astype(f32), came_ref[i].astype(f32)
                rows = own.shape[0]
                out_ref[at : at + rows, :] = jnp.where(core == first, own, came)
                at += rows


def join_square(core, halves, index):
    width = halves[0].shape[2]
    per = width // (2 * sum(t.shape[1] for t in halves[::2]))
    return pl.pallas_call(
        join_kernel,
        out_shape=jax.ShapeDtypeStruct((width, width), f32),
        grid_spec=pltpu.PrefetchScalarGridSpec(
            num_scalar_prefetch=1,
            grid=(1,),
            in_specs=[
                pl.BlockSpec((per,) + t.shape[1:], lambda s, *_: (index, 0, 0)) for t in halves
            ],
            out_specs=pl.BlockSpec((width, width), lambda s, *_: (0, 0)),
        ),
        cost_estimate=cost(0, width * width * 8),
        name="join_square",
    )(core, *halves)


def join_image_kernel(feat, core_ref, *refs):
    out_ref, small_ref, acc_ref = refs[-3:]
    join_kernel(core_ref, *refs[:-3], acc_ref)
    out_ref[...] = acc_ref[:feat, :]
    small_ref[...] = acc_ref[feat : feat + small_ref.shape[0], :]


def join_image(core, halves, feat, small_rows):
    width = halves[0].shape[2]
    rows = sum(t.shape[0] * t.shape[1] for t in halves)
    return pl.pallas_call(
        functools.partial(join_image_kernel, feat),
        out_shape=[
            jax.ShapeDtypeStruct((feat, width), f32),
            jax.ShapeDtypeStruct((small_rows, width), f32),
        ],
        grid_spec=pltpu.PrefetchScalarGridSpec(
            num_scalar_prefetch=1,
            grid=(1,),
            in_specs=[whole(t.shape) for t in halves],
            out_specs=[whole((feat, width)), whole((small_rows, width))],
            scratch_shapes=[pltpu.VMEM((rows, width), f32)],
        ),
        compiler_params=pltpu.CompilerParams(vmem_limit_bytes=LIMIT),
        cost_estimate=cost(0, feat * width * 8),
        name="join_image",
    )(core, *halves)


def widen_ff_kernel(down_in, up_in, down_ref, up_ref):
    down_ref[...] = down_in[...].reshape(down_ref.shape).astype(f32)
    up_ref[...] = up_in[...].reshape(up_ref.shape).astype(f32)


def widen_ff(parts, width, blocks):
    devices, rows, _ = parts.shape
    per = devices // blocks
    return pl.pallas_call(
        widen_ff_kernel,
        out_shape=[
            jax.ShapeDtypeStruct((blocks * width, width), f32),
            jax.ShapeDtypeStruct((width, blocks * width), f32),
        ],
        grid=(blocks,),
        in_specs=[
            pl.BlockSpec((per, rows // 2, width), lambda t: (t, 0, 0)),
            pl.BlockSpec((per, rows // 2, width), lambda t: (t, 1, 0)),
        ],
        out_specs=[
            pl.BlockSpec((width, width), lambda t: (t, 0)),
            pl.BlockSpec((width, width), lambda t: (0, t)),
        ],
        cost_estimate=cost(0, parts.size * 6),
        name="widen_ff",
    )(parts, parts)


def run_feed_forward(captions, counts, n1, mixed, cot, weights, cut, wo, bu, bd, g1, g2, beta2):
    seqs = captions.shape[0]
    total, d = n1.shape
    devices = weights.shape[0]
    down = weights.shape[1] // 2
    ff = devices * down
    blocks = ff // d

    def part(rows, index):
        return pl.BlockSpec(
            (devices, rows, d), lambda s, *_: (0, index, 0), pipeline_mode=pl.Buffered(1)
        )

    if cut % 8 == 0:
        ups = [part(cut, blocks + j) for j in range(blocks)]
        up_weights = [weights] * blocks
    else:
        ups = [whole((d, d))] * blocks
        up_weights = [
            weights[:, down + j * cut : down + (j + 1) * cut].reshape(d, d) for j in range(blocks)
        ]

    L = total // seqs
    row = tile((L, d))
    wide = tile((L, ff))
    vec = whole((d,))
    shapes = [
        jax.ShapeDtypeStruct((total, d), bf16),
        jax.ShapeDtypeStruct((total, ff), bf16),
        jax.ShapeDtypeStruct((total, d), bf16),
        jax.ShapeDtypeStruct((total, ff), bf16),
        jax.ShapeDtypeStruct((total, d), f32),
        jax.ShapeDtypeStruct((total, d), bf16),
        jax.ShapeDtypeStruct((total, d), bf16),
        jax.ShapeDtypeStruct((8, d), f32),
        jax.ShapeDtypeStruct((1, ff), f32),
    ]
    return pl.pallas_call(
        feed_forward,
        out_shape=shapes,
        grid_spec=pltpu.PrefetchScalarGridSpec(
            num_scalar_prefetch=2,
            grid=(seqs,),
            in_specs=[row, row, row, part(down, 0)]
            + ups
            + [whole((d, d)), whole((ff,)), vec, vec, vec, vec],
            out_specs=[row, wide, row, wide, row, row, row, still((8, d)), still((1, ff))],
            scratch_shapes=[pltpu.VMEM((L, ff), f32), pltpu.VMEM((blocks, d, d), bf16)],
        ),
        compiler_params=pltpu.CompilerParams(
            dimension_semantics=("arbitrary",), vmem_limit_bytes=LIMIT
        ),
        cost_estimate=cost(2 * total * d * (4 * ff + d), total * (ff * 4 + d * 18) + d * ff * 4, total * ff),
        name="feed_forward",
    )(captions, counts, n1, mixed, cot, weights, *up_weights, wo, bu, bd, g1, g2, beta2)


def run_attention_backward(geometry, counts, offset, q, k, v, p, gc, gm, wq, wk, wv):
    seqs, _, L, _ = p.shape
    total, d = q.shape
    row = tile((L, d))
    half = tile((L // 2, d))
    mat = whole((d, d))
    received = geometry[0] * geometry[2]
    shapes = [jax.ShapeDtypeStruct((total, d), bf16)] * 3 + [
        jax.ShapeDtypeStruct((total // 2, d), bf16),
        jax.ShapeDtypeStruct((received, d), bf16),
        jax.ShapeDtypeStruct((8, d), f32),
    ]
    return pl.pallas_call(
        functools.partial(attention_backward, *geometry),
        out_shape=shapes,
        grid_spec=pltpu.PrefetchScalarGridSpec(
            num_scalar_prefetch=2,
            grid=(seqs,),
            in_specs=[row, row, row, tile((1, HEADS, L, L)), row, row, mat, mat, mat],
            out_specs=[row, row, row, half, still((received, d)), still((8, d))],
            scratch_shapes=[pltpu.VMEM((received, d), f32)],
        ),
        compiler_params=pltpu.CompilerParams(
            dimension_semantics=("arbitrary",), vmem_limit_bytes=LIMIT
        ),
        cost_estimate=cost(2 * total * d * (3 * d + 4 * L * 4), total * d * 20 + seqs * HEADS * L * L * 2),
        name="attention_backward",
    )(counts, offset, q, k, v, p, gc, gm, wq, wk, wv)


def weight_grad_kernel(lhs_of, rhs_of, core_ref, *refs):
    lhs_refs = refs[: max(lhs_of) + 1]
    rhs_refs = refs[len(lhs_refs) : len(lhs_refs) + max(rhs_of) + 1]
    away_ref, kept_ref, acc_ref = refs[-3:]
    step = pl.program_id(0)
    core = core_ref[0]
    pairs = away_ref.shape[0]
    kinds = {}
    for i, kind in enumerate(zip(lhs_of, rhs_of)):
        kinds.setdefault(kind, []).append(i)
    for (a, b), steps in kinds.items():

        @pl.when((step >= steps[0]) & (step <= steps[-1]))
        def _(a=a, b=b):
            value = tn(lhs_refs[a][...], rhs_refs[b][...]).astype(bf16)
            acc_ref[...] = value.reshape(acc_ref.shape)

    for i in range(pairs):
        away_ref[i] = acc_ref[2 * i + 1 - core]
        kept_ref[i] = acc_ref[2 * i + core]


def weight_grads(core, devices, lhs, rhs, lhs_of, rhs_of, lhs_maps, rhs_maps, out_width, name):
    steps = len(lhs_of)
    total = lhs[0].shape[0]
    width = out_width
    rows = steps * width // devices
    per = width // rows
    half = jax.ShapeDtypeStruct((devices // 2, rows, width), bf16)
    out = pl.BlockSpec((per // 2, rows, width), lambda s, *_: (s, 0, 0))
    specs = [pl.BlockSpec((total, width), m) for m in lhs_maps + rhs_maps]
    return pl.pallas_call(
        functools.partial(weight_grad_kernel, lhs_of, rhs_of),
        out_shape=[half, half],
        grid_spec=pltpu.PrefetchScalarGridSpec(
            num_scalar_prefetch=1,
            grid=(steps,),
            in_specs=specs,
            out_specs=[out, out],
            scratch_shapes=[pltpu.VMEM((per, rows, width), bf16)],
        ),
        compiler_params=pltpu.CompilerParams(
            dimension_semantics=("arbitrary",), vmem_limit_bytes=LIMIT
        ),
        cost_estimate=cost(2 * total * width * width * steps, steps * width * (total + width) * 2),
        name=name,
    )(core, *lhs, *rhs)


def axis_bits(name):
    size = lax.axis_size(name)
    bits = []
    step = 1
    while step < size:
        bits.append((name, step))
        step *= 2
    return bits


def bit_layout():
    return axis_bits("enc")[::-1] + axis_bits("dp")[::-1]


def my_bit(bit):
    return (lax.axis_index(bit[0]) // bit[1]) % 2


def swap_bit(tensor, bit):
    name, step = bit
    size = lax.axis_size(name)
    return lax.ppermute(tensor, name, [(i, i ^ step) for i in range(size)])


def stage_orders():
    dp_bits, enc_bits = axis_bits("dp"), axis_bits("enc")
    near, middle = dp_bits[:1], dp_bits[1:]
    half = len(middle) // 2
    return (
        near + middle + enc_bits,
        near + middle[half:] + middle[:half] + enc_bits,
    )


def add_low(kept, came):
    return (kept.astype(f32) + came.astype(f32)).astype(bf16)


class Scatter:
    def __init__(self, away, kept, order):
        self.order = list(order)
        self.layout = bit_layout()
        self.value = (away, kept)
        self.fresh = True

    def stage(self):
        bit = self.order.pop(0)
        axis = self.layout.index(bit)
        self.layout.remove(bit)
        if self.fresh:
            away, kept = self.value
            self.fresh = False
        else:
            mine = my_bit(bit)
            away, kept = [
                add_low(*[lax.dynamic_index_in_dim(t, i, axis, keepdims=False) for t in self.value])
                for i in (1 - mine, mine)
            ]
        shape = (2,) * len(self.layout) + kept.shape[-2:]
        self.value = (kept.reshape(shape), swap_bit(away, bit).reshape(shape))
        return away

    def total(self):
        return add_low(*self.value)

    def split(self, at, orders):
        parts = []
        for rows, order in zip((slice(None, at), slice(at, None)), orders):
            part = Scatter(*[t[..., rows, :] for t in self.value], ())
            part.order = [b for b in order if b in self.layout]
            part.layout = list(self.layout)
            part.fresh = False
            parts.append(part)
        return parts

    def merge(self, parts):
        self.value = tuple(jnp.concatenate(t, -2) for t in zip(*[p.value for p in parts]))
        self.layout = list(parts[0].layout)
        self.order = list(parts[0].order)


class Gather:
    def __init__(self, rows, order, layout=()):
        self.order = list(order)[::-1]
        self.layout = list(layout)
        self.value = rows

    def stage(self):
        bit = self.order.pop(0)
        sent = self.value
        came = swap_bit(sent, bit)
        self.layout = [b for b in bit_layout() if b in self.layout or b == bit]
        axis = self.layout.index(bit)
        shape = sent.shape[:axis] + (2,) + sent.shape[axis:]
        at = lax.broadcasted_iota(jnp.int32, shape, axis)
        self.value = jnp.where(
            at == my_bit(bit), jnp.expand_dims(sent, axis), jnp.expand_dims(came, axis)
        )
        return sent

    def rows(self):
        return self.value.reshape((-1,) + self.value.shape[-2:])

    def halves(self):
        (bit,) = self.order
        came = swap_bit(self.value, bit)
        shape = (-1,) + came.shape[-2:]
        return self.value.reshape(shape), came.reshape(shape)

    def split(self, at, orders):
        values = (self.value[..., :at, :], self.value[..., at:, :])
        return [
            Gather(value, [b for b in order if b not in self.layout], self.layout)
            for value, order in zip(values, orders)
        ]


def fence(movers, *values):
    leaves, tree = jax.tree.flatten(([m.value for m in movers], values))
    held, values = jax.tree.unflatten(tree, lax.optimization_barrier(leaves))
    for mover, value in zip(movers, held):
        mover.value = value
    return values


class Sum:
    def __init__(self, away, kept, orders):
        self.movers = [Scatter(away, kept, orders[0])]
        self.orders = orders
        self.at = 8 * (-(-away.shape[1] // 16))
        far = len(axis_bits("enc"))
        middle = len(orders[0]) - 1 - far
        self.steps = (
            [self.near]
            + [self.run] * middle
            + [self.far]
            + [self.run] * (far - 1)
            + [self.turn]
            + [self.run] * (far - 1)
            + [self.part]
            + [self.run] * (middle - 1)
        )

    @property
    def value(self):
        return [m.value for m in self.movers]

    @value.setter
    def value(self, values):
        for mover, value in zip(self.movers, values):
            mover.value = value

    def stage(self):
        self.steps.pop(0)()

    def run(self):
        for mover in self.movers:
            mover.stage()

    def near(self):
        self.run()
        self.whole = self.movers[0]
        self.movers = self.whole.split(self.at, self.orders)

    def far(self):
        self.whole.merge(self.movers)
        self.movers = [self.whole]
        self.run()

    def turn(self):
        self.movers = [Gather(self.whole.total(), axis_bits("enc"))]
        self.run()

    def part(self):
        self.movers = self.movers[0].split(self.at, self.orders)
        self.run()

    def halves(self):
        return [t for mover in self.movers for t in mover.halves()]


def body(
    text,
    region_feats,
    boxes,
    caption_count,
    region_count,
    region_offset,
    w_img,
    w_box,
    b_img,
    g_reg,
    beta_reg,
    w_query,
    b_query,
    w_key,
    w_value,
    b_value,
    w_out,
    b_out,
    g_one,
    beta_one,
    w_up,
    b_up,
    w_down,
    b_down,
    g_two,
    beta_two,
    cotangent,
):
    axes = ("enc", "dp")
    orders = stage_orders()
    model_width = text.shape[1]
    ff_blocks = w_up.shape[1] // model_width
    cut = w_query.shape[0]
    far = axis_bits("enc")

    middle = len(orders[0]) - 1 - len(far)
    core = (lax.axis_index("dp") % 2).astype(jnp.int32).reshape(1)

    up_blocks = w_up.reshape(cut, ff_blocks, model_width).transpose(1, 0, 2)
    ff_shard = jnp.concatenate([w_down, up_blocks.reshape(ff_blocks * cut, model_width)], 0)
    ff_weights = lax.all_gather(ff_shard, axes, axis=0)
    rows_up = cut
    img = Gather(w_img, far)
    attn = Gather(jnp.concatenate([w_query, w_key, w_value, w_out], 0), far)
    img.stage()
    fence([img, attn])
    while img.order:
        img.stage()
        attn.stage()
        fence([img, attn])
    img = img.split(w_img.shape[0] // 2, orders)
    attn.stage()
    for _ in range(middle):
        for part in img:
            part.stage()
        fence([*img, attn])
    attn = attn.split(2 * cut, orders)
    for part in (*img, *attn):
        part.stage()
    img_full = jnp.concatenate([t.rows() for t in img], 1).reshape(-1, model_width)
    device_count = lax.axis_size(axes)
    seq_count = caption_count.shape[0]
    sent_rows, feat = region_feats.shape
    per_peer = sent_rows // device_count
    pad = 8 * (-(-per_peer // 8))
    pad = 1 << (pad - 1).bit_length()
    box_count = boxes.shape[0]
    geometry = (pad, per_peer, device_count)
    pre_norm, encoded = run_image_encode(
        geometry, region_feats, boxes, img_full, w_box, b_img, g_reg, beta_reg
    )
    (encoded,) = fence(attn, encoded)
    received = lax.all_to_all(encoded, axes, split_axis=0, concat_axis=0, tiled=True)
    for _ in range(middle - 1):
        for part in attn:
            part.stage()
        (received,) = fence(attn, received)
    for part in attn:
        part.stage()
    query_full, key_full, value_full, out_full = [
        t.reshape(-1, model_width)
        for part in attn
        for t in (part.rows()[:, :cut], part.rows()[:, cut:])
    ]
    (
        hidden_in,
        queries,
        keys,
        values,
        probs,
        context,
        mixed,
        normed_one,
    ) = run_attention_forward(
        geometry,
        caption_count,
        region_count,
        region_offset,
        received,
        text,
        query_full,
        key_full,
        value_full,
        out_full,
        b_query,
        b_value,
        b_out,
        g_one,
        beta_one,
    )
    (
        output,
        activated,
        grad_down_out,
        grad_gate,
        grad_mixed,
        grad_attn,
        grad_context,
        sums,
        grad_b_up,
    ) = run_feed_forward(
        caption_count,
        region_count,
        normed_one,
        mixed,
        cotangent,
        ff_weights,
        rows_up,
        out_full,
        b_up,
        b_down,
        g_one,
        g_two,
        beta_two,
    )
    fixed = lambda s, *_: (0, 0)
    moving = lambda s, *_: (0, s)
    down_away, down_kept = weight_grads(
        core,
        device_count,
        [activated],
        [grad_down_out],
        [0] * ff_blocks,
        [0] * ff_blocks,
        [moving],
        [fixed],
        model_width,
        "grad_w_down",
    )
    up_away, up_kept = weight_grads(
        core,
        device_count,
        [normed_one],
        [grad_gate],
        [0] * ff_blocks,
        [0] * ff_blocks,
        [fixed],
        [moving],
        model_width,
        "grad_w_up",
    )
    down = Scatter(down_away, down_kept, orders[0])
    up = Scatter(up_away, up_kept, orders[1])
    down.stage()
    up.stage()
    (grad_context,) = fence([down, up], grad_context)
    down.stage()
    up.stage()
    grad_query, grad_keys, grad_values, grad_text, grad_slots, attn_sums = run_attention_backward(
        geometry,
        region_count,
        region_offset,
        queries,
        keys,
        values,
        probs,
        grad_context,
        grad_mixed,
        query_full,
        key_full,
        value_full,
    )
    grad_query, grad_keys, grad_values, grad_slots, attn_sums = fence(
        [down, up], grad_query, grad_keys, grad_values, grad_slots, attn_sums
    )
    back = lax.all_to_all(grad_slots, axes, split_axis=0, concat_axis=0, tiled=True)
    down.stage()
    up.stage()
    attn_away, attn_kept = weight_grads(
        core,
        device_count,
        [hidden_in, context],
        [grad_query, grad_keys, grad_values, grad_attn],
        [0, 0, 0, 1],
        [0, 1, 2, 3],
        [fixed] * 2,
        [fixed] * 4,
        model_width,
        "grad_w_attn",
    )
    attn = Sum(attn_away, attn_kept, orders)
    (back,) = fence([down, up, attn], back)
    while len(down.order) > len(far):
        down.stage()
        up.stage()
        fence([down, up])
    down.stage()
    up.stage()
    attn.stage()
    small_rows = 40
    chunk = 8 * (-(-(feat + small_rows) // (8 * device_count)))
    grad_pre, grad_feats, img_away, img_kept = run_image_backward(
        geometry,
        chunk,
        core,
        region_feats,
        boxes,
        img_full,
        pre_norm,
        back,
        g_reg,
        sums,
        attn_sums,
        grad_b_up.reshape(ff_blocks, model_width),
    )
    img = Sum(img_away, img_kept, orders)
    fence([down, up, attn, img])
    while down.order:
        down.stage()
        up.stage()
        if not down.order:
            attn.stage()
            img.stage()
        fence([down, up, attn, img])
    ff_shard = jnp.concatenate([down.total(), up.total()], 0)
    ff_all = lax.all_gather(ff_shard, axes, axis=0)
    while attn.steps:
        attn.stage()
        img.stage()
        if len(attn.steps) == 0:
            grad_w_down, grad_w_up = widen_ff(ff_all, model_width, ff_blocks)
            grad_w_down, grad_w_up = fence([attn, img], grad_w_down, grad_w_up)
        else:
            fence([attn, img])
    attn_halves = attn.halves()
    img.stage()
    fence([img], *attn_halves)
    img_halves = img.halves()
    grad_w_query, grad_w_key, grad_w_value, grad_w_out = [
        join_square(core, attn_halves, j) for j in range(4)
    ]
    grad_boxes = jnp.einsum("cd,rd->cr", w_box, grad_pre, preferred_element_type=f32).astype(bf16)
    grad_w_img, small = join_image(core, img_halves, feat, small_rows)
    grad_w_box = small[:box_count]
    grad_b_img, grad_g_reg, grad_beta_reg = [small[8 + i] for i in range(3)]
    grad_g_two, grad_beta_two, grad_b_down, grad_g_one, grad_beta_one, grad_b_out = [
        small[16 + i] for i in range(6)
    ]
    grad_b_query, grad_b_value = small[24], small[25]
    grad_b_up = small[32 : 32 + ff_blocks].reshape(-1)
    return (
        output,
        grad_text,
        grad_feats,
        grad_boxes,
        grad_w_img,
        grad_w_box,
        grad_b_img,
        grad_g_reg,
        grad_beta_reg,
        grad_w_query,
        grad_b_query,
        grad_w_key,
        grad_w_value,
        grad_b_value,
        grad_w_out,
        grad_b_out,
        grad_g_one,
        grad_beta_one,
        grad_w_up,
        grad_b_up,
        grad_w_down,
        grad_b_down,
        grad_g_two,
        grad_beta_two,
    )


def solution(mesh):
    return jax.shard_map(
        body,
        mesh=mesh,
        in_specs=(
            P(("enc", "dp"), None),
            P(("enc", "dp"), None),
            P(None, ("enc", "dp")),
            P(("enc", "dp")),
            P(("enc", "dp")),
            P(("enc", "dp")),
            P(("enc", "dp"), None),
            P(),
            P(),
            P(),
            P(),
            P(("enc", "dp"), None),
            P(),
            P(("enc", "dp"), None),
            P(("enc", "dp"), None),
            P(),
            P(("enc", "dp"), None),
            P(),
            P(),
            P(),
            P(("enc", "dp"), None),
            P(),
            P(("enc", "dp"), None),
            P(),
            P(),
            P(),
            P(("enc", "dp"), None),
        ),
        out_specs=(
            P(("enc", "dp"), None),
            P(("enc", "dp"), None),
            P(("enc", "dp"), None),
            P(None, ("enc", "dp")),
            P(),
            P(),
            P(),
            P(),
            P(),
            P(),
            P(),
            P(),
            P(),
            P(),
            P(),
            P(),
            P(),
            P(),
            P(),
            P(),
            P(),
            P(),
            P(),
            P(),
        ),
        check_vma=False,
    )
```

time: 1150 us -> 515 us (0.45)
  waiting for transfers between devices: 788 us -> 203 us
  matrix products: 172 us -> 0.89 us
  Pallas kernels: 0 us -> 161 us
  starting transfers between devices: 7.43 us -> 70.4 us
  local copies, waits for them, and re-layouts: 74.1 us -> 19.7 us
  blocking collectives: 43.5 us -> 0 us
    psum x1 -> x0, waiting for transfers between devices: 477 us -> none  [body(): lax.psum((grad_w_img, grad_w_box, grad_b_img, grad_g_reg, grad_beta_reg,...]
    all_gather x7 -> x2, waiting for transfers between devices: 285 us -> 0.04 us  [the longest x1 0.02 us: body(): ff_all = lax.all_gather(ff_shard, axes, axis=0)]
    ppermute x0 -> x56, waiting for transfers between devices: none -> 197 us  [swap_bit(): return lax.ppermute(tensor, name, [(i, i ^ step) for i in range(size)])]
    dot_general x32 -> x1, matrix products: 172 us -> 0.89 us  [body(): jnp.einsum('cd,rd->cr', w_box, grad_pre, preferred_element_type=f32)]
    pallas_call x0 -> x14, Pallas kernels: none -> 161 us  [the longest x1 41.8 us: run_feed_forward(): pl.pallas_call(feed_forward, out_shape=shapes, grid_spec=pltpu.PrefetchSc...]
    ppermute x0 -> x56, starting transfers between devices: none -> 62.8 us  [swap_bit(): return lax.ppermute(tensor, name, [(i, i ^ step) for i in range(size)])]
    psum x1 -> x0, blocking collectives: 43.5 us -> none  [body(): lax.psum((grad_w_img, grad_w_box, grad_b_img, grad_g_reg, grad_beta_reg,...]
    unnamed x158 -> x60, local copies, waits for them, and re-layouts: 43 us -> 2.44 us
  transfers between devices with their start and end apart: 10 -> 60, of which waited for: 10 -> 37; matrix products, arithmetic and copies ran while one was open for 11% -> 9% of each run, Pallas kernels for 0% -> 19%
where the time goes in v2:
time: 515 us; the launch traced here: 507 us
  waiting for transfers between devices  203 us (39%)
  Pallas kernels  161 us (31%)
  starting transfers between devices  70.4 us (14%)
  other arithmetic  36.3 us (7%)
  local copies, waits for them, and re-layouts  19.7 us (4%)
  between operations  15.8 us (3%)
    ppermute x56, waiting for transfers between devices, swap_bit(): return lax.ppermute(tensor, name, [(i, i ^ step) for i in range(size)])  197 us
    ppermute x56, starting transfers between devices, swap_bit(): return lax.ppermute(tensor, name, [(i, i ^ step) for i in range(size)])  62.8 us
    pallas_call x1, Pallas kernels, run_feed_forward(): pl.pallas_call(feed_forward, out_shape=shapes, grid_spec=pltpu.PrefetchSc...  41.8 us
    pallas_call x3, Pallas kernels, weight_grads(): pl.pallas_call(functools.partial(weight_grad_kernel, lhs_of, rhs_of), out...  30.5 us
    pallas_call x1, Pallas kernels, run_attention_backward(): pl.pallas_call(functools.partial(attention_backward, *geometry), out_shap...  23.6 us
    pallas_call x1, Pallas kernels, run_attention_forward(): pl.pallas_call(functools.partial(attention_forward, *geometry), out_shape...  21.5 us
    convert_element_type x31, other arithmetic, add_low(): return (kept.astype(f32) + came.astype(f32)).astype(bf16)  21.4 us
    pallas_call x4, Pallas kernels, join_square(): pl.pallas_call(join_kernel, out_shape=jax.ShapeDtypeStruct((width, width)...  11.5 us
  transfers between devices with their start and end apart: 60, of which 37 were waited for; matrix products, arithmetic and copies ran while one was open for 9% of the time, Pallas kernels for 19%

profile of v2, /device:TPU:0, one launch (start us, length us, event | category | flops | bytes accessed | tf_op | source)
XLA Modules:
  0.0 506.9 jit_solution(7233492505641710970)
XLA Ops:
  9.9 4.1 collective-permute-start
  14.1 4.9 collective-permute-done
  19.7 3.5 collective-permute-start.1
  23.2 6.7 %collective-permute-done.2 = bf16[96,768]{1,0:T(8,128)(2,1)S(1)} collective-permute-done((bf16[96,768]{1,0:T(8,128)(2,1)S(1)}, bf16[96,768]{1,0:T(8,128)(2,1)S(1)}, u32[]{:S(2)}, u32[]{:S(2)}) %collective-permute-start.2) | collective-permute-done | bytes 147488 | tf_op jit(solution)/shard_map/ppermute | solution.py:670
  30.0 3.1 collective-permute-done.1
  36.5 2.4 collective-permute-done.4
  40.7 2.7 collective-permute-done.5
  46.3 11.3 %collective-permute-done.7 = bf16[2,2,2,32,768]{4,3,2,1,0:T(8,128)(2,1)S(1)} collective-permute-done((bf16[2,2,2,32,768]{4,3,2,1,0:T(8,128)(2,1)S(1)}, bf16[2,2,2,32,768]{4,3,2,1,0:T(8,128)(2,1)S(1)}, u32[]{:S(2)}, u32[]{:S(2)}) %collective-permute-start.7) | collective-permute-done | bytes 393248 | tf_op jit(solution)/shard_map/ppermute | solution.py:670
  57.7 5.2 %collective-permute-done.6 = bf16[2,2,2,32,768]{4,3,2,1,0:T(8,128)(2,1)S(1)} collective-permute-done((bf16[2,2,2,32,768]{4,3,2,1,0:T(8,128)(2,1)S(1)}, bf16[2,2,2,32,768]{4,3,2,1,0:T(8,128)(2,1)S(1)}, u32[]{:S(2)}, u32[]{:S(2)}) %collective-permute-start.6) | collective-permute-done | bytes 393248 | tf_op jit(solution)/shard_map/ppermute | solution.py:670
  66.4 5.0 collective-permute-done.9
  73.1 2.1 bitcast_select_fusion.3
  75.2 2.0 pad_maximum_fusion
  77.2 6.6 %image_encode.1 = (f32[416,768]{1,0:T(8,128)}, bf16[512,768]{1,0:T(8,128)(2,1)}) custom-call(bf16[416,2048]{1,0:T(8,128)(2,1)} %x_ref.3, bf16[4,416]{1,0:T(4,128)(2,1)} %box_ref.3, bf16[2048,768]{1,0:T(8,128)(2,1)} %bitcast.166, bf16[4,768]{1,0:T(4,128)(2,1)} %wb_ref.1, f32[768]{0:T(1024)} %bi_ref.1, f32[768]{0:T(1024)} %gr_ref.3, f32[768]{0:T(1024)} %betar_ref.1), custom_call_target="tpu_custom_call" | custom-call | flops 1308622848 | bytes 6766592 | tf_op jit(solution)/shard_map/image_encode/pallas_call | solution.py:342
  83.8 4.2 all-to-all-start
  88.0 1.8 collective-permute-start.13
  91.2 21.7 %collective-permute-done.13 = bf16[2,2,2,48,768]{4,3,2,1,0:T(8,128)(2,1)S(1)} collective-permute-done((bf16[2,2,2,48,768]{4,3,2,1,0:T(8,128)(2,1)S(1)}, bf16[2,2,2,48,768]{4,3,2,1,0:T(8,128)(2,1)S(1)}, u32[]{:S(2)}, u32[]{:S(2)}) %collective-permute-start.13) | collective-permute-done | bytes 589856 | tf_op jit(solution)/shard_map/ppermute | solution.py:670
  113.3 5.8 %all-to-all-done = bf16[32,16,768]{2,1,0:T(8,128)(2,1)} async-done(((bf16[32,16,768]{2,1,0:T(8,128)(2,1)}), bf16[32,16,768]{2,1,0:T(8,128)(2,1)}, u32[]{:S(2)}, u32[]{:S(2)}) %all-to-all-start) | async-done | bytes 786464 | tf_op jit(solution)/shard_map/all_to_all | solution.py:903
  124.1 2.3 fusion.50
  126.4 21.5 %attention_forward.1 = (bf16[1024,768]{1,0:T(8,128)(2,1)}, bf16[1024,768]{1,0:T(8,128)(2,1)}, bf16[1024,768]{1,0:T(8,128)(2,1)}, bf16[1024,768]{1,0:T(8,128)(2,1...) custom-call(s32[4]{0:T(128)} %captions.3, ...), custom_call_target="tpu_custom_call" | custom-call | flops 8053063680 | bytes 20447232 | tf_op jit(solution)/shard_map/attention_forward/pallas_call | solution.py:370
  147.9 41.8 %feed_forward.1 = (bf16[1024,768]{1,0:T(8,128)(2,1)}, bf16[1024,3072]{1,0:T(8,128)(2,1)}, bf16[1024,768]{1,0:T(8,128)(2,1)}, bf16[1024,3072]{1,0:T(8,128)(2,1)},...) custom-call(s32[4]{0:T(128)} %captions.3, ...), custom_call_target="tpu_custom_call" | custom-call | flops 20535312384 | bytes 36175872 | tf_op jit(solution)/shard_map/feed_forward/pallas_call | solution.py:550
  189.8 9.4 %grad_w_up.1 = (bf16[16,96,768]{2,1,0:T(8,128)(2,1)}, bf16[16,96,768]{2,1,0:T(8,128)(2,1)}) custom-call(s32[1]{0:T(128)} %bitcast.18.core_ref, bf16[1024,768]{1,0:T(8,128)(2,1)} %get-tuple-element.173.n_ref.refs_0_, bf16[1024,3072]{1,0:T(8,128)(2,1)} %get-tuple-element.184.refs_1_), custom_call_target="tpu_custom_call" | custom-call | flops 4831838208 | bytes 11010048 | tf_op jit(solution)/shard_map/grad_w_up/pallas_call | solution.py:631
  199.3 10.0 %grad_w_down.1 = (bf16[16,96,768]{2,1,0:T(8,128)(2,1)}, bf16[16,96,768]{2,1,0:T(8,128)(2,1)}) custom-call(s32[1]{0:T(128)} %bitcast.18.core_ref, bf16[1024,3072]{1,0:T(8,128)(2,1)} %get-tuple-element.180.refs_0_, bf16[1024,768]{1,0:T(8,128)(2,1)} %get-tuple-element.181.refs_1_), custom_call_target="tpu_custom_call" | custom-call | flops 4831838208 | bytes 11010048 | tf_op jit(solution)/shard_map/grad_w_down/pallas_call | solution.py:631
  209.8 4.5 collective-permute-done.16
  214.3 3.5 fusion.3
  219.3 3.3 fusion.1
  223.8 23.6 %attention_backward.1 = (bf16[1024,768]{1,0:T(8,128)(2,1)}, bf16[1024,768]{1,0:T(8,128)(2,1)}, bf16[1024,768]{1,0:T(8,128)(2,1)}, bf16[512,768]{1,0:T(8,128)(2,1...) custom-call(s32[4]{0:T(128)} %counts.5, s32[1]{0:T(128)S(6)} %copy.135.offset, ...), custom_call_target="tpu_custom_call" | custom-call | flops 10066329600 | bytes 22020096 | tf_op jit(solution)/shard_map/attention_backward/pallas_call | solution.py:582
  247.5 3.4 collective-permute-done.18
  250.9 3.3 all-to-all-start.1
  257.4 2.3 fusion.9
  261.3 11.1 %grad_w_attn.1 = (bf16[16,96,768]{2,1,0:T(8,128)(2,1)}, bf16[16,96,768]{2,1,0:T(8,128)(2,1)}) custom-call(s32[1]{0:T(128)} %bitcast.18.core_ref, bf16[1024,768]{1,0:T(8,128)(2,1)} %get-tuple-element.205.refs_0_, bf16[1024,768]{1,0:T(8,128)(2,1)} %get-tuple-element.206.refs_1_, bf16[1024,768]{1,0:T(8,128)(2,1)} %get-tuple-element.207.refs_2_, ...), custom_call_target="tpu_custom_call" | custom-call | flops 4831838208 | bytes 11010048 | tf_op jit(solution)/shard_map/grad_w_attn/pallas_call | solution.py:631
  272.4 5.5 %collective-permute-done.21 = bf16[2,2,96,768]{3,2,0,1:T(8,128)(2,1)S(1)} collective-permute-done((bf16[2,2,96,768]{3,2,0,1:T(8,128)(2,1)S(1)}, bf16[2,2,96,768]{3,2,0,1:T(8,128)(2,1)S(1)}, u32[]{:S(2)}, u32[]{:S(2)}) %collective-permute-start.21) | collective-permute-done | bytes 589856 | tf_op jit(solution)/shard_map/ppermute | solution.py:670
  285.7 9.4 %image_backward.1 = (bf16[416,768]{1,0:T(8,128)(2,1)}, bf16[416,2048]{1,0:T(8,128)(2,1)}, bf16[16,72,768]{2,1,0:T(8,128)(2,1)}, bf16[16,72,768]{2,1,0:T(8,128)(2,1)}) custom-call(s32[1]{0:T(128)} %bitcast.18.core_ref, bf16[416,2048]{1,0:T(8,128)(2,1)} %x_ref.3, bf16[4,416]{1,0:T(4,128)(2,1)} %box_ref.3, bf16[2048,768]{1,0:T(8,128)(2,1)} %bitcast.167, ...), custom_call_target="tpu_custom_call" | custom-call | flops 2617245696 | bytes 10092544 | tf_op jit(solution)/shard_map/image_backward/pallas_call | solution.py:400
  295.1 1.8 fusion.48
  303.3 2.1 slice.142
  305.5 2.6 collective-permute-start.26
  313.2 6.3 %collective-permute-done.26 = bf16[96,768]{1,0:T(8,128)(2,1)S(1)} collective-permute-done((bf16[96,768]{1,0:T(8,128)(2,1)S(1)}, bf16[96,768]{1,0:T(8,128)(2,1)S(1)}, u32[]{:S(2)}, u32[]{:S(2)}) %collective-permute-start.26) | collective-permute-done | bytes 147488 | tf_op jit(solution)/shard_map/ppermute | solution.py:670
  319.5 2.1 collective-permute-done.25
  324.0 1.7 collective-permute-start.32
  330.6 13.9 %collective-permute-done.31 = bf16[2,2,48,768]{3,2,1,0:T(8,128)(2,1)S(1)} collective-permute-done((bf16[2,2,48,768]{3,2,1,0:T(8,128)(2,1)S(1)}, bf16[2,2,48,768]{3,2,1,0:T(8,128)(2,1)S(1)}, u32[]{:S(2)}, u32[]{:S(2)}) %collective-permute-start.31) | collective-permute-done | bytes 294944 | tf_op jit(solution)/shard_map/ppermute | solution.py:670
  346.2 1.8 collective-permute-start.36
  348.1 3.9 collective-permute-done.36
  354.0 3.1 collective-permute-start.37
  357.1 12.2 %collective-permute-done.37 = bf16[96,768]{1,0:T(8,128)(2,1)S(1)} collective-permute-done((bf16[96,768]{1,0:T(8,128)(2,1)S(1)}, bf16[96,768]{1,0:T(8,128)(2,1)S(1)}, u32[]{:S(2)}, u32[]{:S(2)}) %collective-permute-start.37) | collective-permute-done | bytes 147488 | tf_op jit(solution)/shard_map/ppermute | solution.py:670
  369.3 2.1 collective-permute-done.38
  371.5 2.7 collective-permute-start.39
  374.6 11.1 %collective-permute-done.39 = bf16[96,768]{1,0:T(8,128)(2,1)S(1)} collective-permute-done((bf16[96,768]{1,0:T(8,128)(2,1)S(1)}, bf16[96,768]{1,0:T(8,128)(2,1)S(1)}, u32[]{:S(2)}, u32[]{:S(2)}) %collective-permute-start.39) | collective-permute-done | bytes 147488 | tf_op jit(solution)/shard_map/ppermute | solution.py:670
  385.8 8.3 %collective-permute-done.40 = bf16[72,768]{1,0:T(8,128)(2,1)S(1)} collective-permute-done((bf16[72,768]{1,0:T(8,128)(2,1)S(1)}, bf16[72,768]{1,0:T(8,128)(2,1)S(1)}, u32[]{:S(2)}, u32[]{:S(2)}) %collective-permute-start.40) | collective-permute-done | bytes 110624 | tf_op jit(solution)/shard_map/ppermute | solution.py:670
  394.3 3.2 collective-permute-start.41
  397.5 7.7 %collective-permute-done.42 = bf16[72,768]{1,0:T(8,128)(2,1)S(1)} collective-permute-done((bf16[72,768]{1,0:T(8,128)(2,1)S(1)}, bf16[72,768]{1,0:T(8,128)(2,1)S(1)}, u32[]{:S(2)}, u32[]{:S(2)}) %collective-permute-start.42) | collective-permute-done | bytes 110624 | tf_op jit(solution)/shard_map/ppermute | solution.py:670
  405.4 14.1 %collective-permute-done.41 = bf16[2,96,768]{2,1,0:T(8,128)(2,1)S(1)} collective-permute-done((bf16[2,96,768]{2,1,0:T(8,128)(2,1)S(1)}, bf16[2,96,768]{2,1,0:T(8,128)(2,1)S(1)}, u32[]{:S(2)}, u32[]{:S(2)}) %collective-permute-start.41) | collective-permute-done | bytes 294944 | tf_op jit(solution)/shard_map/ppermute | solution.py:670
  419.7 1.9 collective-permute-start.44
  421.6 1.9 collective-permute-start.43
  423.5 2.1 collective-permute-done.45
  432.6 3.7 collective-permute-done.49
  437.2 9.7 %collective-permute-done.48 = bf16[2,2,40,768]{3,2,1,0:T(8,128)(2,1)S(1)} collective-permute-done((bf16[2,2,40,768]{3,2,1,0:T(8,128)(2,1)S(1)}, bf16[2,2,40,768]{3,2,1,0:T(8,128)(2,1)S(1)}, u32[]{:S(2)}, u32[]{:S(2)}) %collective-permute-start.48) | collective-permute-done | bytes 245792 | tf_op jit(solution)/shard_map/ppermute | solution.py:670
  448.2 10.8 %widen_ff.1 = (f32[3072,768]{1,0:T(8,128)}, f32[768,3072]{1,0:T(8,128)}) custom-call(bf16[32,192,768]{2,1,0:T(8,128)(2,1)} %bitcast.148, bf16[32,192,768]{2,1,0:T(8,128)(2,1)} %bitcast.149), custom_call_target="tpu_custom_call" | custom-call | bytes 28311552 | tf_op jit(solution)/shard_map/widen_ff/pallas_call | solution.py:493
  462.0 8.9 %collective-permute-done.51 = bf16[2,2,2,32,768]{4,3,2,1,0:T(8,128)(2,1)S(1)} collective-permute-done((bf16[2,2,2,32,768]{4,3,2,1,0:T(8,128)(2,1)}, bf16[2,2,2,32,768]{4,3,2,1,0:T(8,128)(2,1)S(1)}, u32[]{:S(2)}, u32[]{:S(2)}) %collective-permute-start.51) | collective-permute-done | bytes 393248 | tf_op jit(solution)/shard_map/ppermute | solution.py:670
  470.9 2.0 broadcast_select_fusion.5
  478.0 2.9 join_square.7
  480.9 2.9 join_square.6
  483.8 2.9 join_square.5
  486.7 2.9 join_square.4
  490.7 5.3 %join_image.1 = (f32[2048,768]{1,0:T(8,128)}, f32[40,768]{1,0:T(8,128)}) custom-call(s32[1]{0:T(128)} %bitcast.18.core_ref, bf16[16,40,768]{2,1,0:T(8,128)(2,1)} %bitcast.78.refs_0_, bf16[16,40,768]{2,1,0:T(8,128)(2,1)} %bitcast.181, bf16[16,32,768]{2,1,0:T(8,128)(2,1)} %bitcast.80.refs_2_, bf16[16,32,768]{2,1,0:T(8,128)(2,1)} %bitcast.184), custom_call_target="tpu_custom_call" | custom-call | bytes 12582912 | tf_op jit(solution)/shard_map/join_image/pallas_call | solution.py:466
  496.0 1.8 slice_reduce_fusion
  (229 shorter events, 82.4 us)
Async XLA Ops:
  7.2 140.7 %all-gather.5.cloned.1.call-start = ((), (), s32[]{:S(2)}) async-start(), calls=%async_computation.2 | async-start | bytes 9732096 | tf_op jit(solution)/shard_map/all_gather | solution.py:871
  9.9 9.0 %collective-permute-start = (bf16[64,768]{1,0:T(8,128)(2,1)S(1)}, bf16[64,768]{1,0:T(8,128)(2,1)S(1)}, u32[]{:S(2)}, u32[]{:S(2)}) collective-permute-start(bf16[64,768]{1,0:T(8,128)(2,1)S(1)} %copy-done.19), channel_id=1, source_target_pairs={{0,16},{8,24},{16,0},{24,8},{1,17},{9,25},{17,1},{25,9},{2,18},{10... | collective-permute-start | bytes 294920 | tf_op jit(solution)/shard_map/ppermute | solution.py:670
  19.0 10.8 %collective-permute-start.2 = (bf16[96,768]{1,0:T(8,128)(2,1)S(1)}, bf16[96,768]{1,0:T(8,128)(2,1)S(1)}, u32[]{:S(2)}, u32[]{:S(2)}) collective-permute-start(bf16[96,768]{1,0:T(8,128)(2,1)S(1)} %pad_maximum_fusion.3), channel_id=1, source_target_pairs={{0,16},{8,24},{16,0},{24,8},{1,17},{9,25},{17,1},{25,9},{2,18},{10... | collective-permute-start | bytes 442376 | tf_op jit(solution)/shard_map/ppermute | solution.py:670
  19.7 13.3 %collective-permute-start.1 = (bf16[2,64,768]{2,1,0:T(8,128)(2,1)S(1)}, bf16[2,64,768]{2,1,0:T(8,128)(2,1)S(1)}, u32[]{:S(2)}, u32[]{:S(2)}) collective-permute-start(bf16[2,64,768]{2,1,0:T(8,128)(2,1)S(1)} %broadcast_select_fusion.23), channel_id=1, source_target_pairs={{0,8},{8,0},{16,24},{24,16},{1,9},{9,1},{17,25},{25,17},{2,10},{10... | collective-permute-start | bytes 589832 | tf_op jit(solution)/shard_map/ppermute | solution.py:670
  33.1 5.7 %collective-permute-start.4 = (bf16[2,2,32,768]{3,2,1,0:T(8,128)(2,1)S(1)}, bf16[2,2,32,768]{3,2,1,0:T(8,128)(2,1)S(1)}, u32[]{:S(2)}, u32[]{:S(2)}) collective-permute-start(bf16[2,2,32,768]{3,2,1,0:T(8,128)(2,1)S(1)} %get-tuple-element.337), channel_id=1, source_target_pairs={{0,2},{1,3},{2,0},{3,1},{4,6},{5,7},{6,4},{7,5},{8,10},{9,11},{10,... | collective-permute-start | bytes 589832 | tf_op jit(solution)/shard_map/ppermute | solution.py:670
  34.8 8.7 %collective-permute-start.5 = (bf16[2,96,768]{2,1,0:T(8,128)(2,1)S(1)}, bf16[2,96,768]{2,1,0:T(8,128)(2,1)S(1)}, u32[]{:S(2)}, u32[]{:S(2)}) collective-permute-start(bf16[2,96,768]{2,1,0:T(8,128)(2,1)S(1)} %broadcast_select_fusion.21), channel_id=1, source_target_pairs={{0,8},{8,0},{16,24},{24,16},{1,9},{9,1},{17,25},{25,17},{2,10},{10... | collective-permute-start | bytes 884744 | tf_op jit(solution)/shard_map/ppermute | solution.py:670
  34.9 5.7 %collective-permute-start.3 = (bf16[2,2,32,768]{3,2,1,0:T(8,128)(2,1)S(1)}, bf16[2,2,32,768]{3,2,1,0:T(8,128)(2,1)S(1)}, u32[]{:S(2)}, u32[]{:S(2)}) collective-permute-start(bf16[2,2,32,768]{3,2,1,0:T(8,128)(2,1)S(1)} %get-tuple-element.338), channel_id=1, source_target_pairs={{0,4},{1,5},{2,6},{3,7},{4,0},{5,1},{6,2},{7,3},{8,12},{9,13},{10,... | collective-permute-start | bytes 589832 | tf_op jit(solution)/shard_map/ppermute | solution.py:670
  43.6 14.0 %collective-permute-start.7 = (bf16[2,2,2,32,768]{4,3,2,1,0:T(8,128)(2,1)S(1)}, bf16[2,2,2,32,768]{4,3,2,1,0:T(8,128)(2,1)S(1)}, u32[]{:S(2)}, u32[]{:S(2)}) collective-permute-start(bf16[2,2,2,32,768]{4,3,2,1,0:T(8,128)(2,1)S(1)} %broadcast_select_fusion.17), channel_id=1, source_target_pairs={{0,4},{1,5},{2,6},{3,7},{4,0},{5,1},{6,2},{7,3},{8,12},{9,13},{10,... | collective-permute-start | bytes 1179656 | tf_op jit(solution)/shard_map/ppermute | solution.py:670
  45.2 17.8 %collective-permute-start.6 = (bf16[2,2,2,32,768]{4,3,2,1,0:T(8,128)(2,1)S(1)}, bf16[2,2,2,32,768]{4,3,2,1,0:T(8,128)(2,1)S(1)}, u32[]{:S(2)}, u32[]{:S(2)}) collective-permute-start(bf16[2,2,2,32,768]{4,3,2,1,0:T(8,128)(2,1)S(1)} %broadcast_select_fusion.19), channel_id=1, source_target_pairs={{0,2},{1,3},{2,0},{3,1},{4,6},{5,7},{6,4},{7,5},{8,10},{9,11},{10,... | collective-permute-start | bytes 1179656 | tf_op jit(solution)/shard_map/ppermute | solution.py:670
  63.1 8.3 %collective-permute-start.9 = (bf16[2,2,48,768]{3,2,1,0:T(8,128)(2,1)S(1)}, bf16[2,2,48,768]{3,2,1,0:T(8,128)(2,1)S(1)}, u32[]{:S(2)}, u32[]{:S(2)}) collective-permute-start(bf16[2,2,48,768]{3,2,1,0:T(8,128)(2,1)S(1)} %get-tuple-element.333), channel_id=1, source_target_pairs={{0,2},{1,3},{2,0},{3,1},{4,6},{5,7},{6,4},{7,5},{8,10},{9,11},{10,... | collective-permute-start | bytes 884744 | tf_op jit(solution)/shard_map/ppermute | solution.py:670
  63.5 9.5 %collective-permute-start.10 = (bf16[2,2,2,2,32,768]{5,4,3,2,1,0:T(8,128)(2,1)S(1)}, bf16[2,2,2,2,32,768]{5,4,3,2,1,0:T(8,128)(2,1)}, u32[]{:S(2)}, u32[]{:S(2)}) collective-permute-start(bf16[2,2,2,2,32,768]{5,4,3,2,1,0:T(8,128)(2,1)S(1)} %broadcast_select_fusion.7), channel_id=1, source_target_pairs={{0,1},{1,0},{2,3},{3,2},{4,5},{5,4},{6,7},{7,6},{8,9},{9,8},{10,11... | collective-permute-start | bytes 2359304 | tf_op jit(solution)/shard_map/ppermute | solution.py:670
  63.5 9.6 %collective-permute-start.11 = (bf16[2,2,2,2,32,768]{5,4,3,2,1,0:T(8,128)(2,1)S(1)}, bf16[2,2,2,2,32,768]{5,4,3,2,1,0:T(8,128)(2,1)}, u32[]{:S(2)}, u32[]{:S(2)}) collective-permute-start(bf16[2,2,2,2,32,768]{5,4,3,2,1,0:T(8,128)(2,1)S(1)} %broadcast_select_fusion.6), channel_id=1, source_target_pairs={{0,1},{1,0},{2,3},{3,2},{4,5},{5,4},{6,7},{7,6},{8,9},{9,8},{10,11... | collective-permute-start | bytes 2359304 | tf_op jit(solution)/shard_map/ppermute | solution.py:670
  64.0 8.9 %collective-permute-start.8 = (bf16[2,2,48,768]{3,2,1,0:T(8,128)(2,1)S(1)}, bf16[2,2,48,768]{3,2,1,0:T(8,128)(2,1)S(1)}, u32[]{:S(2)}, u32[]{:S(2)}) collective-permute-start(bf16[2,2,48,768]{3,2,1,0:T(8,128)(2,1)S(1)} %get-tuple-element.334), channel_id=1, source_target_pairs={{0,4},{1,5},{2,6},{3,7},{4,0},{5,1},{6,2},{7,3},{8,12},{9,13},{10,... | collective-permute-start | bytes 884744 | tf_op jit(solution)/shard_map/ppermute | solution.py:670
  83.8 35.3 %all-to-all-start = ((bf16[32,16,768]{2,1,0:T(8,128)(2,1)}), bf16[32,16,768]{2,1,0:T(8,128)(2,1)}, u32[]{:S(2)}, u32[]{:S(2)}) async-start(bf16[32,16,768]{2,1,0:T(8,128)(2,1)} %bitcast.183), calls=%async_computation | async-start | bytes 1572864 | tf_op jit(solution)/shard_map/all_to_all | solution.py:903
  88.0 25.0 %collective-permute-start.13 = (bf16[2,2,2,48,768]{4,3,2,1,0:T(8,128)(2,1)S(1)}, bf16[2,2,2,48,768]{4,3,2,1,0:T(8,128)(2,1)S(1)}, u32[]{:S(2)}, u32[]{:S(2)}) collective-permute-start(bf16[2,2,2,48,768]{4,3,2,1,0:T(8,128)(2,1)S(1)} %broadcast_select_fusion.9), channel_id=1, source_target_pairs={{0,4},{1,5},{2,6},{3,7},{4,0},{5,1},{6,2},{7,3},{8,12},{9,13},{10,... | collective-permute-start | bytes 1769480 | tf_op jit(solution)/shard_map/ppermute | solution.py:670
  89.8 23.4 %collective-permute-start.12 = (bf16[2,2,2,48,768]{4,3,2,1,0:T(8,128)(2,1)S(1)}, bf16[2,2,2,48,768]{4,3,2,1,0:T(8,128)(2,1)S(1)}, u32[]{:S(2)}, u32[]{:S(2)}) collective-permute-start(bf16[2,2,2,48,768]{4,3,2,1,0:T(8,128)(2,1)S(1)} %broadcast_select_fusion.13), channel_id=1, source_target_pairs={{0,2},{1,3},{2,0},{3,1},{4,6},{5,7},{6,4},{7,5},{8,10},{9,11},{10,... | collective-permute-start | bytes 1769480 | tf_op jit(solution)/shard_map/ppermute | solution.py:670
  119.1 2.8 collective-permute-start.14
  119.1 4.5 collective-permute-start.15
  199.2 10.6 %collective-permute-start.17 = (bf16[16,96,768]{2,1,0:T(8,128)(2,1)}, bf16[16,96,768]{2,1,0:T(8,128)(2,1)}, u32[]{:S(2)}, u32[]{:S(2)}) collective-permute-start(bf16[16,96,768]{2,1,0:T(8,128)(2,1)} %get-tuple-element.186), channel_id=1, source_target_pairs={{0,1},{1,0},{2,3},{3,2},{4,5},{5,4},{6,7},{7,6},{8,9},{9,8},{10,11... | collective-permute-start | bytes 7077896 | tf_op jit(solution)/shard_map/ppermute | solution.py:670
  199.3 15.0 %copy-start.8 = (bf16[16,96,768]{2,1,0:T(8,128)(2,1)S(1)}, bf16[16,96,768]{2,1,0:T(8,128)(2,1)}, u32[]{:S(2)}) copy-start(bf16[16,96,768]{2,1,0:T(8,128)(2,1)} %get-tuple-element.185) | copy-start | bytes 7077892
  209.3 4.9 collective-permute-start.16
  217.8 29.7 %collective-permute-start.19 = (bf16[2,2,2,96,768]{4,3,0,1,2:T(8,128)(2,1)}, bf16[2,2,2,96,768]{4,3,0,1,2:T(8,128)(2,1)S(1)}, u32[]{:S(2)}, u32[]{:S(2)}) collective-permute-start(bf16[2,2,2,96,768]{4,3,0,1,2:T(8,128)(2,1)} %get-tuple-element.299), channel_id=1, source_target_pairs={{0,4},{1,5},{2,6},{3,7},{4,0},{5,1},{6,2},{7,3},{8,12},{9,13},{10,... | collective-permute-start | bytes 3538952 | tf_op jit(solution)/shard_map/ppermute | solution.py:670
  222.6 28.3 %collective-permute-start.18 = (bf16[2,2,2,96,768]{4,3,0,1,2:T(8,128)(2,1)}, bf16[2,2,2,96,768]{4,3,0,1,2:T(8,128)(2,1)}, u32[]{:S(2)}, u32[]{:S(2)}) collective-permute-start(bf16[2,2,2,96,768]{4,3,0,1,2:T(8,128)(2,1)} %get-tuple-element.301), channel_id=1, source_target_pairs={{0,2},{1,3},{2,0},{3,1},{4,6},{5,7},{6,4},{7,5},{8,10},{9,11},{10,... | collective-permute-start | bytes 3538952 | tf_op jit(solution)/shard_map/ppermute | solution.py:670
  250.9 28.8 %all-to-all-start.1 = ((bf16[32,16,768]{2,1,0:T(8,128)(2,1)}), bf16[32,16,768]{2,1,0:T(8,128)(2,1)}, u32[]{:S(2)}, u32[]{:S(2)}) async-start(bf16[32,16,768]{2,1,0:T(8,128)(2,1)} %bitcast.182), calls=%async_computation.1 | async-start | bytes 1572864 | tf_op jit(solution)/shard_map/all_to_all | solution.py:1016
  254.2 193.9 %all-gather.7.cloned.1.call-start = ((), (), s32[]{:S(2)}) async-start(), calls=%async_computation.3 | async-start | bytes 9732096 | tf_op jit(solution)/shard_map/all_gather | solution.py:1066
  255.8 22.1 %collective-permute-start.21 = (bf16[2,2,96,768]{3,2,0,1:T(8,128)(2,1)S(1)}, bf16[2,2,96,768]{3,2,0,1:T(8,128)(2,1)S(1)}, u32[]{:S(2)}, u32[]{:S(2)}) collective-permute-start(bf16[2,2,96,768]{3,2,0,1:T(8,128)(2,1)S(1)} %get-tuple-element.309), channel_id=1, source_target_pairs={{0,2},{1,3},{2,0},{3,1},{4,6},{5,7},{6,4},{7,5},{8,10},{9,11},{10,... | collective-permute-start | bytes 1769480 | tf_op jit(solution)/shard_map/ppermute | solution.py:670
  259.8 19.9 %collective-permute-start.20 = (bf16[2,2,96,768]{3,2,0,1:T(8,128)(2,1)}, bf16[2,2,96,768]{3,2,0,1:T(8,128)(2,1)S(1)}, u32[]{:S(2)}, u32[]{:S(2)}) collective-permute-start(bf16[2,2,96,768]{3,2,0,1:T(8,128)(2,1)} %get-tuple-element.311), channel_id=1, source_target_pairs={{0,4},{1,5},{2,6},{3,7},{4,0},{5,1},{6,2},{7,3},{8,12},{9,13},{10,... | collective-permute-start | bytes 1769480 | tf_op jit(solution)/shard_map/ppermute | solution.py:670
  261.3 18.9 %copy-start.25 = (f32[1,3072]{1,0:T(1,128)S(1)}, f32[1,3072]{1,0:T(1,128)}, u32[]{:S(2)}) copy-start(f32[1,3072]{1,0:T(1,128)} %get-tuple-element.217) | copy-start | bytes 36868
  279.6 15.4 %collective-permute-start.24 = (bf16[16,96,768]{2,1,0:T(8,128)(2,1)}, bf16[16,96,768]{2,1,0:T(8,128)(2,1)}, u32[]{:S(2)}, u32[]{:S(2)}) collective-permute-start(bf16[16,96,768]{2,1,0:T(8,128)(2,1)} %get-tuple-element.225), channel_id=1, source_target_pairs={{0,1},{1,0},{2,3},{3,2},{4,5},{5,4},{6,7},{7,6},{8,9},{9,8},{10,11... | collective-permute-start | bytes 7077896 | tf_op jit(solution)/shard_map/ppermute | solution.py:670
  282.4 14.7 %collective-permute-start.23 = (bf16[2,96,768]{2,1,0:T(8,128)(2,1)}, bf16[2,96,768]{2,1,0:T(8,128)(2,1)S(1)}, u32[]{:S(2)}, u32[]{:S(2)}) collective-permute-start(bf16[2,96,768]{2,1,0:T(8,128)(2,1)} %get-tuple-element.319), channel_id=1, source_target_pairs={{0,8},{8,0},{16,24},{24,16},{1,9},{9,1},{17,25},{25,17},{2,10},{10... | collective-permute-start | bytes 884744 | tf_op jit(solution)/shard_map/ppermute | solution.py:670
  284.8 13.6 %collective-permute-start.22 = (bf16[2,96,768]{2,1,0:T(8,128)(2,1)}, bf16[2,96,768]{2,1,0:T(8,128)(2,1)}, u32[]{:S(2)}, u32[]{:S(2)}) collective-permute-start(bf16[2,96,768]{2,1,0:T(8,128)(2,1)} %get-tuple-element.321), channel_id=1, source_target_pairs={{0,8},{8,0},{16,24},{24,16},{1,9},{9,1},{17,25},{25,17},{2,10},{10... | collective-permute-start | bytes 884744 | tf_op jit(solution)/shard_map/ppermute | solution.py:670
  298.5 12.1 %collective-permute-start.29 = (bf16[16,72,768]{2,1,0:T(8,128)(2,1)}, bf16[16,72,768]{2,1,0:T(8,128)(2,1)}, u32[]{:S(2)}, u32[]{:S(2)}) collective-permute-start(bf16[16,72,768]{2,1,0:T(8,128)(2,1)} %get-tuple-element.237), channel_id=1, source_target_pairs={{0,1},{1,0},{2,3},{3,2},{4,5},{5,4},{6,7},{7,6},{8,9},{9,8},{10,11... | collective-permute-start | bytes 5308424 | tf_op jit(solution)/shard_map/ppermute | solution.py:670
  299.4 22.2 %collective-permute-start.28 = (bf16[2,2,2,48,768]{4,3,2,1,0:T(8,128)(2,1)}, bf16[2,2,2,48,768]{4,3,2,1,0:T(8,128)(2,1)}, u32[]{:S(2)}, u32[]{:S(2)}) collective-permute-start(bf16[2,2,2,48,768]{4,3,2,1,0:T(8,128)(2,1)} %fusion.15), channel_id=1, source_target_pairs={{0,4},{1,5},{2,6},{3,7},{4,0},{5,1},{6,2},{7,3},{8,12},{9,13},{10,... | collective-permute-start | bytes 1769480 | tf_op jit(solution)/shard_map/ppermute | solution.py:670
  301.5 20.2 %collective-permute-start.27 = (bf16[2,2,2,48,768]{4,3,0,1,2:T(8,128)(2,1)}, bf16[2,2,2,48,768]{4,3,0,1,2:T(8,128)(2,1)}, u32[]{:S(2)}, u32[]{:S(2)}) collective-permute-start(bf16[2,2,2,48,768]{4,3,0,1,2:T(8,128)(2,1)} %get-tuple-element.303), channel_id=1, source_target_pairs={{0,2},{1,3},{2,0},{3,1},{4,6},{5,7},{6,4},{7,5},{8,10},{9,11},{10,... | collective-permute-start | bytes 1769480 | tf_op jit(solution)/shard_map/ppermute | solution.py:670
  305.5 14.0 %collective-permute-start.26 = (bf16[96,768]{1,0:T(8,128)(2,1)S(1)}, bf16[96,768]{1,0:T(8,128)(2,1)S(1)}, u32[]{:S(2)}, u32[]{:S(2)}) collective-permute-start(bf16[96,768]{1,0:T(8,128)(2,1)S(1)} %get-tuple-element.329), channel_id=1, source_target_pairs={{0,16},{8,24},{16,0},{24,8},{1,17},{9,25},{17,1},{25,9},{2,18},{10... | collective-permute-start | bytes 442376 | tf_op jit(solution)/shard_map/ppermute | solution.py:670
  309.1 12.5 %collective-permute-start.25 = (bf16[96,768]{1,0:T(8,128)(2,1)S(1)}, bf16[96,768]{1,0:T(8,128)(2,1)S(1)}, u32[]{:S(2)}, u32[]{:S(2)}) collective-permute-start(bf16[96,768]{1,0:T(8,128)(2,1)S(1)} %get-tuple-element.331), channel_id=1, source_target_pairs={{0,16},{8,24},{16,0},{24,8},{1,17},{9,25},{17,1},{25,9},{2,18},{10... | collective-permute-start | bytes 442376 | tf_op jit(solution)/shard_map/ppermute | solution.py:670
  322.6 21.8 %collective-permute-start.33 = (bf16[2,2,2,32,768]{4,3,2,1,0:T(8,128)(2,1)S(1)}, bf16[2,2,2,32,768]{4,3,2,1,0:T(8,128)(2,1)S(1)}, u32[]{:S(2)}, u32[]{:S(2)}) collective-permute-start(bf16[2,2,2,32,768]{4,3,2,1,0:T(8,128)(2,1)S(1)} %fusion.23), channel_id=1, source_target_pairs={{0,4},{1,5},{2,6},{3,7},{4,0},{5,1},{6,2},{7,3},{8,12},{9,13},{10,... | collective-permute-start | bytes 1179656 | tf_op jit(solution)/shard_map/ppermute | solution.py:670
  324.0 20.5 %collective-permute-start.32 = (bf16[2,2,2,40,768]{4,3,2,1,0:T(8,128)(2,1)S(1)}, bf16[2,2,2,40,768]{4,3,2,1,0:T(8,128)(2,1)S(1)}, u32[]{:S(2)}, u32[]{:S(2)}) collective-permute-start(bf16[2,2,2,40,768]{4,3,2,1,0:T(8,128)(2,1)S(1)} %fusion.19), channel_id=1, source_target_pairs={{0,2},{1,3},{2,0},{3,1},{4,6},{5,7},{6,4},{7,5},{8,10},{9,11},{10,... | collective-permute-start | bytes 1474568 | tf_op jit(solution)/shard_map/ppermute | solution.py:670
  326.8 17.7 %collective-permute-start.31 = (bf16[2,2,48,768]{3,2,1,0:T(8,128)(2,1)S(1)}, bf16[2,2,48,768]{3,2,1,0:T(8,128)(2,1)S(1)}, u32[]{:S(2)}, u32[]{:S(2)}) collective-permute-start(bf16[2,2,48,768]{3,2,1,0:T(8,128)(2,1)S(1)} %fusion.32), channel_id=1, source_target_pairs={{0,2},{1,3},{2,0},{3,1},{4,6},{5,7},{6,4},{7,5},{8,10},{9,11},{10,... | collective-permute-start | bytes 884744 | tf_op jit(solution)/shard_map/ppermute | solution.py:670
  328.5 16.0 %collective-permute-start.30 = (bf16[2,2,48,768]{3,2,0,1:T(8,128)(2,1)S(1)}, bf16[2,2,48,768]{3,2,0,1:T(8,128)(2,1)S(1)}, u32[]{:S(2)}, u32[]{:S(2)}) collective-permute-start(bf16[2,2,48,768]{3,2,0,1:T(8,128)(2,1)S(1)} %get-tuple-element.317), channel_id=1, source_target_pairs={{0,4},{1,5},{2,6},{3,7},{4,0},{5,1},{6,2},{7,3},{8,12},{9,13},{10,... | collective-permute-start | bytes 884744 | tf_op jit(solution)/shard_map/ppermute | solution.py:670
  344.6 7.4 %collective-permute-start.35 = (bf16[2,2,40,768]{3,2,1,0:T(8,128)(2,1)S(1)}, bf16[2,2,40,768]{3,2,1,0:T(8,128)(2,1)S(1)}, u32[]{:S(2)}, u32[]{:S(2)}) collective-permute-start(bf16[2,2,40,768]{3,2,1,0:T(8,128)(2,1)S(1)} %fusion.35), channel_id=1, source_target_pairs={{0,4},{1,5},{2,6},{3,7},{4,0},{5,1},{6,2},{7,3},{8,12},{9,13},{10,... | collective-permute-start | bytes 737288 | tf_op jit(solution)/shard_map/ppermute | solution.py:670
  345.7 7.0 %collective-permute-start.34 = (bf16[2,96,768]{2,1,0:T(8,128)(2,1)S(1)}, bf16[2,96,768]{2,1,0:T(8,128)(2,1)S(1)}, u32[]{:S(2)}, u32[]{:S(2)}) collective-permute-start(bf16[2,96,768]{2,1,0:T(8,128)(2,1)S(1)} %fusion.33), channel_id=1, source_target_pairs={{0,8},{8,0},{16,24},{24,16},{1,9},{9,1},{17,25},{25,17},{2,10},{10... | collective-permute-start | bytes 884744 | tf_op jit(solution)/shard_map/ppermute | solution.py:670
  346.2 5.7 %collective-permute-start.36 = (bf16[2,2,32,768]{3,2,1,0:T(8,128)(2,1)S(1)}, bf16[2,2,32,768]{3,2,1,0:T(8,128)(2,1)S(1)}, u32[]{:S(2)}, u32[]{:S(2)}) collective-permute-start(bf16[2,2,32,768]{3,2,1,0:T(8,128)(2,1)S(1)} %get-tuple-element.323), channel_id=1, source_target_pairs={{0,2},{1,3},{2,0},{3,1},{4,6},{5,7},{6,4},{7,5},{8,10},{9,11},{10,... | collective-permute-start | bytes 589832 | tf_op jit(solution)/shard_map/ppermute | solution.py:670
  352.8 18.6 %collective-permute-start.38 = (bf16[2,72,768]{2,1,0:T(8,128)(2,1)S(1)}, bf16[2,72,768]{2,1,0:T(8,128)(2,1)S(1)}, u32[]{:S(2)}, u32[]{:S(2)}) collective-permute-start(bf16[2,72,768]{2,1,0:T(8,128)(2,1)S(1)} %fusion.37), channel_id=1, source_target_pairs={{0,8},{8,0},{16,24},{24,16},{1,9},{9,1},{17,25},{25,17},{2,10},{10... | collective-permute-start | bytes 663560 | tf_op jit(solution)/shard_map/ppermute | solution.py:670
  354.0 15.4 %collective-permute-start.37 = (bf16[96,768]{1,0:T(8,128)(2,1)S(1)}, bf16[96,768]{1,0:T(8,128)(2,1)S(1)}, u32[]{:S(2)}, u32[]{:S(2)}) collective-permute-start(bf16[96,768]{1,0:T(8,128)(2,1)S(1)} %get-tuple-element.327), channel_id=1, source_target_pairs={{0,16},{8,24},{16,0},{24,8},{1,17},{9,25},{17,1},{25,9},{2,18},{10... | collective-permute-start | bytes 442376 | tf_op jit(solution)/shard_map/ppermute | solution.py:670
  371.5 14.2 %collective-permute-start.39 = (bf16[96,768]{1,0:T(8,128)(2,1)S(1)}, bf16[96,768]{1,0:T(8,128)(2,1)S(1)}, u32[]{:S(2)}, u32[]{:S(2)}) collective-permute-start(bf16[96,768]{1,0:T(8,128)(2,1)S(1)} %add_convert_fusion.27), channel_id=1, source_target_pairs={{0,16},{8,24},{16,0},{24,8},{1,17},{9,25},{17,1},{25,9},{2,18},{10... | collective-permute-start | bytes 442376 | tf_op jit(solution)/shard_map/ppermute | solution.py:670
  374.3 19.9 %collective-permute-start.40 = (bf16[72,768]{1,0:T(8,128)(2,1)S(1)}, bf16[72,768]{1,0:T(8,128)(2,1)S(1)}, u32[]{:S(2)}, u32[]{:S(2)}) collective-permute-start(bf16[72,768]{1,0:T(8,128)(2,1)S(1)} %get-tuple-element.335), channel_id=1, source_target_pairs={{0,16},{8,24},{16,0},{24,8},{1,17},{9,25},{17,1},{25,9},{2,18},{10... | collective-permute-start | bytes 331784 | tf_op jit(solution)/shard_map/ppermute | solution.py:670
  394.2 11.1 %collective-permute-start.42 = (bf16[72,768]{1,0:T(8,128)(2,1)S(1)}, bf16[72,768]{1,0:T(8,128)(2,1)S(1)}, u32[]{:S(2)}, u32[]{:S(2)}) collective-permute-start(bf16[72,768]{1,0:T(8,128)(2,1)S(1)} %add_convert_fusion.34), channel_id=1, source_target_pairs={{0,16},{8,24},{16,0},{24,8},{1,17},{9,25},{17,1},{25,9},{2,18},{10... | collective-permute-start | bytes 331784 | tf_op jit(solution)/shard_map/ppermute | solution.py:670
  394.3 25.1 %collective-permute-start.41 = (bf16[2,96,768]{2,1,0:T(8,128)(2,1)S(1)}, bf16[2,96,768]{2,1,0:T(8,128)(2,1)S(1)}, u32[]{:S(2)}, u32[]{:S(2)}) collective-permute-start(bf16[2,96,768]{2,1,0:T(8,128)(2,1)S(1)} %broadcast_select_fusion.20), channel_id=1, source_target_pairs={{0,8},{8,0},{16,24},{24,16},{1,9},{9,1},{17,25},{25,17},{2,10},{10... | collective-permute-start | bytes 884744 | tf_op jit(solution)/shard_map/ppermute | solution.py:670
  419.5 6.0 %collective-permute-start.45 = (bf16[2,72,768]{2,1,0:T(8,128)(2,1)S(1)}, bf16[2,72,768]{2,1,0:T(8,128)(2,1)S(1)}, u32[]{:S(2)}, u32[]{:S(2)}) collective-permute-start(bf16[2,72,768]{2,1,0:T(8,128)(2,1)S(1)} %broadcast_select_fusion.22), channel_id=1, source_target_pairs={{0,8},{8,0},{16,24},{24,16},{1,9},{9,1},{17,25},{25,17},{2,10},{10... | collective-permute-start | bytes 663560 | tf_op jit(solution)/shard_map/ppermute | solution.py:670
  419.7 7.6 %collective-permute-start.44 = (bf16[2,2,48,768]{3,2,1,0:T(8,128)(2,1)S(1)}, bf16[2,2,48,768]{3,2,1,0:T(8,128)(2,1)S(1)}, u32[]{:S(2)}, u32[]{:S(2)}) collective-permute-start(bf16[2,2,48,768]{3,2,1,0:T(8,128)(2,1)S(1)} %get-tuple-element.325), channel_id=1, source_target_pairs={{0,2},{1,3},{2,0},{3,1},{4,6},{5,7},{6,4},{7,5},{8,10},{9,11},{10,... | collective-permute-start | bytes 884744 | tf_op jit(solution)/shard_map/ppermute | solution.py:670
  421.6 6.7 %collective-permute-start.43 = (bf16[2,2,48,768]{3,2,1,0:T(8,128)(2,1)S(1)}, bf16[2,2,48,768]{3,2,1,0:T(8,128)(2,1)S(1)}, u32[]{:S(2)}, u32[]{:S(2)}) collective-permute-start(bf16[2,2,48,768]{3,2,1,0:T(8,128)(2,1)S(1)} %get-tuple-element.326), channel_id=1, source_target_pairs={{0,4},{1,5},{2,6},{3,7},{4,0},{5,1},{6,2},{7,3},{8,12},{9,13},{10,... | collective-permute-start | bytes 884744 | tf_op jit(solution)/shard_map/ppermute | solution.py:670
  428.4 7.9 %collective-permute-start.49 = (bf16[2,2,32,768]{3,2,1,0:T(8,128)(2,1)S(1)}, bf16[2,2,32,768]{3,2,1,0:T(8,128)(2,1)S(1)}, u32[]{:S(2)}, u32[]{:S(2)}) collective-permute-start(bf16[2,2,32,768]{3,2,1,0:T(8,128)(2,1)S(1)} %slice.118), channel_id=1, source_target_pairs={{0,2},{1,3},{2,0},{3,1},{4,6},{5,7},{6,4},{7,5},{8,10},{9,11},{10,... | collective-permute-start | bytes 589832 | tf_op jit(solution)/shard_map/ppermute | solution.py:670
  429.2 18.5 %collective-permute-start.47 = (bf16[2,2,2,48,768]{4,3,2,1,0:T(8,128)(2,1)S(1)}, bf16[2,2,2,48,768]{4,3,2,1,0:T(8,128)(2,1)S(1)}, u32[]{:S(2)}, u32[]{:S(2)}) collective-permute-start(bf16[2,2,2,48,768]{4,3,2,1,0:T(8,128)(2,1)S(1)} %broadcast_select_fusion.8), channel_id=1, source_target_pairs={{0,4},{1,5},{2,6},{3,7},{4,0},{5,1},{6,2},{7,3},{8,12},{9,13},{10,... | collective-permute-start | bytes 1769480 | tf_op jit(solution)/shard_map/ppermute | solution.py:670
  431.0 15.9 %collective-permute-start.48 = (bf16[2,2,40,768]{3,2,1,0:T(8,128)(2,1)S(1)}, bf16[2,2,40,768]{3,2,1,0:T(8,128)(2,1)S(1)}, u32[]{:S(2)}, u32[]{:S(2)}) collective-permute-start(bf16[2,2,40,768]{3,2,1,0:T(8,128)(2,1)S(1)} %slice.117), channel_id=1, source_target_pairs={{0,4},{1,5},{2,6},{3,7},{4,0},{5,1},{6,2},{7,3},{8,12},{9,13},{10,... | collective-permute-start | bytes 737288 | tf_op jit(solution)/shard_map/ppermute | solution.py:670
  431.3 16.6 %collective-permute-start.46 = (bf16[2,2,2,48,768]{4,3,2,1,0:T(8,128)(2,1)S(1)}, bf16[2,2,2,48,768]{4,3,2,1,0:T(8,128)(2,1)S(1)}, u32[]{:S(2)}, u32[]{:S(2)}) collective-permute-start(bf16[2,2,2,48,768]{4,3,2,1,0:T(8,128)(2,1)S(1)} %broadcast_select_fusion.12), channel_id=1, source_target_pairs={{0,2},{1,3},{2,0},{3,1},{4,6},{5,7},{6,4},{7,5},{8,10},{9,11},{10,... | collective-permute-start | bytes 1769480 | tf_op jit(solution)/shard_map/ppermute | solution.py:670
  447.9 11.2 %copy-start = (bf16[2,2,2,2,48,768]{5,4,3,2,1,0:T(8,128)(2,1)}, bf16[2,2,2,2,48,768]{5,4,3,2,1,0:T(8,128)(2,1)S(1)}, u32[]{:S(2)}) copy-start(bf16[2,2,2,2,48,768]{5,4,3,2,1,0:T(8,128)(2,1)S(1)} %broadcast_select_fusion) | copy-start | bytes 3538948
  459.0 15.4 %copy-start.10 = (bf16[2,2,2,40,768]{4,3,2,1,0:T(8,128)(2,1)S(1)}, bf16[2,2,2,40,768]{4,3,2,1,0:T(8,128)(2,1)}, u32[]{:S(2)}) copy-start(bf16[2,2,2,40,768]{4,3,2,1,0:T(8,128)(2,1)} %broadcast_select_fusion.14) | copy-start | bytes 1474564
  459.0 16.5 %collective-permute-start.52 = (bf16[2,2,2,2,48,768]{5,4,3,2,1,0:T(8,128)(2,1)S(1)}, bf16[2,2,2,2,48,768]{5,4,3,2,1,0:T(8,128)(2,1)S(1)}, u32[]{:S(2)}, u32[]{:S(2)}) collective-permute-start(bf16[2,2,2,2,48,768]{5,4,3,2,1,0:T(8,128)(2,1)S(1)} %broadcast_select_fusion.2), channel_id=1, source_target_pairs={{0,1},{1,0},{2,3},{3,2},{4,5},{5,4},{6,7},{7,6},{8,9},{9,8},{10,11... | collective-permute-start | bytes 3538952 | tf_op jit(solution)/shard_map/ppermute | solution.py:670
  459.1 16.4 %collective-permute-start.53 = (bf16[2,2,2,2,48,768]{5,4,3,2,1,0:T(8,128)(2,1)S(1)}, bf16[2,2,2,2,48,768]{5,4,3,2,1,0:T(8,128)(2,1)S(1)}, u32[]{:S(2)}, u32[]{:S(2)}) collective-permute-start(bf16[2,2,2,2,48,768]{5,4,3,2,1,0:T(8,128)(2,1)S(1)} %broadcast_select_fusion), channel_id=1, source_target_pairs={{0,1},{1,0},{2,3},{3,2},{4,5},{5,4},{6,7},{7,6},{8,9},{9,8},{10,11... | collective-permute-start | bytes 3538952 | tf_op jit(solution)/shard_map/ppermute | solution.py:670
  459.6 11.3 %collective-permute-start.51 = (bf16[2,2,2,32,768]{4,3,2,1,0:T(8,128)(2,1)}, bf16[2,2,2,32,768]{4,3,2,1,0:T(8,128)(2,1)S(1)}, u32[]{:S(2)}, u32[]{:S(2)}) collective-permute-start(bf16[2,2,2,32,768]{4,3,2,1,0:T(8,128)(2,1)} %broadcast_select_fusion.16), channel_id=1, source_target_pairs={{0,4},{1,5},{2,6},{3,7},{4,0},{5,1},{6,2},{7,3},{8,12},{9,13},{10,... | collective-permute-start | bytes 1179656 | tf_op jit(solution)/shard_map/ppermute | solution.py:670
  461.3 13.1 %collective-permute-start.50 = (bf16[2,2,2,40,768]{4,3,2,1,0:T(8,128)(2,1)}, bf16[2,2,2,40,768]{4,3,2,1,0:T(8,128)(2,1)S(1)}, u32[]{:S(2)}, u32[]{:S(2)}) collective-permute-start(bf16[2,2,2,40,768]{4,3,2,1,0:T(8,128)(2,1)} %broadcast_select_fusion.14), channel_id=1, source_target_pairs={{0,2},{1,3},{2,0},{3,1},{4,6},{5,7},{6,4},{7,5},{8,10},{9,11},{10,... | collective-permute-start | bytes 1474568 | tf_op jit(solution)/shard_map/ppermute | solution.py:670
  476.6 12.9 %collective-permute-start.54 = (bf16[2,2,2,2,40,768]{5,4,3,2,1,0:T(8,128)(2,1)}, bf16[2,2,2,2,40,768]{5,4,3,2,1,0:T(8,128)(2,1)S(1)}, u32[]{:S(2)}, u32[]{:S(2)}) collective-permute-start(bf16[2,2,2,2,40,768]{5,4,3,2,1,0:T(8,128)(2,1)} %broadcast_select_fusion.4), channel_id=1, source_target_pairs={{0,1},{1,0},{2,3},{3,2},{4,5},{5,4},{6,7},{7,6},{8,9},{9,8},{10,11... | collective-permute-start | bytes 2949128 | tf_op jit(solution)/shard_map/ppermute | solution.py:670
  476.6 12.9 %collective-permute-start.55 = (bf16[2,2,2,2,32,768]{5,4,3,2,1,0:T(8,128)(2,1)}, bf16[2,2,2,2,32,768]{5,4,3,2,1,0:T(8,128)(2,1)S(1)}, u32[]{:S(2)}, u32[]{:S(2)}) collective-permute-start(bf16[2,2,2,2,32,768]{5,4,3,2,1,0:T(8,128)(2,1)} %broadcast_select_fusion.5), channel_id=1, source_target_pairs={{0,1},{1,0},{2,3},{3,2},{4,5},{5,4},{6,7},{7,6},{8,9},{9,8},{10,11... | collective-permute-start | bytes 2359304 | tf_op jit(solution)/shard_map/ppermute | solution.py:670
  (24 other events, 117.0 us)
Sparse Core Ops, SparseCore 0:
  11.6 108.3 all-gather.4
  322.6 98.4 all-gather.6

commit v3 on v2

--- a/solution.py
+++ b/solution.py
@@ -144,8 +144,9 @@
 def image_backward(
     pad, sent, core_ref,
     x_ref, box_ref, wi_ref, pre_ref, back_ref, gr_ref, sums_ref, attn_sums_ref, bu_ref,
-    gp_ref, gx_ref, away_ref, kept_ref, acc_ref,
+    gp_ref, gx_ref, *outs,
 ):
+    *outs, acc_ref = outs
     rows, feat = x_ref.shape
     width = pre_ref.shape[1]
     grad = tn(spread(pad, sent, rows, back_ref.shape[0]), back_ref[...])
@@ -163,12 +164,15 @@
     acc_ref[at + 16 : at + 24, :] = attn_sums_ref[...]
     acc_ref[at + 24 : at + 24 + bu_ref.shape[0], :] = bu_ref[...]
     core = core_ref[0]
-    pairs, chunk, _ = away_ref.shape
-    for i in range(pairs):
-        first = pl.multiple_of((2 * i + 1 - core) * chunk, 8)
-        away_ref[i] = acc_ref[pl.ds(first, chunk), :].astype(bf16)
-        first = pl.multiple_of((2 * i + core) * chunk, 8)
-        kept_ref[i] = acc_ref[pl.ds(first, chunk), :].astype(bf16)
+    half = len(outs) // 2
+    chunk = sum(ref.shape[1] for ref in outs[:half])
+    for i in range(outs[0].shape[0]):
+        for side in (0, 1):
+            at = (2 * i + (1 - core if side == 0 else core)) * chunk
+            for ref in outs[side * half : (side + 1) * half]:
+                rows_here = ref.shape[1]
+                ref[i] = acc_ref[pl.ds(pl.multiple_of(at, 8), rows_here), :].astype(bf16)
+                at = at + rows_here
     gx_ref[...] = nt(gp, wi_ref[...]).astype(bf16)
 
 
@@ -395,21 +399,23 @@
     pad, sent, devices = geometry
     rows, feat = x.shape
     d = pre.shape[1]
-    half = jax.ShapeDtypeStruct((devices // 2, chunk, d), bf16)
+    first = 8 * (-(-chunk // 16))
+    parts = [
+        jax.ShapeDtypeStruct((devices // 2, r, d), bf16) for r in (first, chunk - first) * 2
+    ]
     operands = (x, boxes, wi, pre, back, gr, sums, attn_sums, bu)
-    return pl.pallas_call(
+    gp, gx, *out = pl.pallas_call(
         functools.partial(image_backward, pad, sent),
         out_shape=[
             jax.ShapeDtypeStruct((rows, d), bf16),
             jax.ShapeDtypeStruct((rows, feat), bf16),
-            half,
-            half,
+            *parts,
         ],
         grid_spec=pltpu.PrefetchScalarGridSpec(
             num_scalar_prefetch=1,
             grid=(1,),
             in_specs=[whole(o.shape) for o in operands],
-            out_specs=[whole((rows, d)), whole((rows, feat)), whole(half.shape), whole(half.shape)],
+            out_specs=[whole((rows, d)), whole((rows, feat))] + [whole(p.shape) for p in parts],
             scratch_shapes=[pltpu.VMEM((devices * chunk, d), f32)],
         ),
         compiler_params=pltpu.CompilerParams(
@@ -418,6 +424,7 @@
         cost_estimate=cost(4 * rows * d * feat, x.size * 4 + wi.size * 2 + devices * chunk * d * 2),
         name="image_backward",
     )(core, *operands)
+    return gp, gx, list(zip(out[:2], out[2:]))
 
 
 def join_kernel(core_ref, *refs):
@@ -434,80 +441,57 @@
                 at += rows
 
 
-def join_square(core, halves, index):
-    width = halves[0].shape[2]
-    per = width // (2 * sum(t.shape[1] for t in halves[::2]))
+def join_blocks(core, halves, shape, step):
+    pairs, rows, width = halves[0].shape
+    per = width // (2 * rows)
+    down, right = step
+    block = pl.BlockSpec((per, rows, width), lambda s, *_: (s, 0, 0))
     return pl.pallas_call(
         join_kernel,
-        out_shape=jax.ShapeDtypeStruct((width, width), f32),
+        out_shape=jax.ShapeDtypeStruct(shape, f32),
         grid_spec=pltpu.PrefetchScalarGridSpec(
             num_scalar_prefetch=1,
-            grid=(1,),
-            in_specs=[
-                pl.BlockSpec((per,) + t.shape[1:], lambda s, *_: (index, 0, 0)) for t in halves
-            ],
-            out_specs=pl.BlockSpec((width, width), lambda s, *_: (0, 0)),
-        ),
-        cost_estimate=cost(0, width * width * 8),
-        name="join_square",
+            grid=(pairs // per,),
+            in_specs=[block, block],
+            out_specs=pl.BlockSpec((width, width), lambda s, *_: (s * down, s * right)),
+        ),
+        cost_estimate=cost(0, pairs * rows * width * 12),
+        name="join_blocks",
     )(core, *halves)
 
 
-def join_image_kernel(feat, core_ref, *refs):
-    out_ref, small_ref, acc_ref = refs[-3:]
-    join_kernel(core_ref, *refs[:-3], acc_ref)
-    out_ref[...] = acc_ref[:feat, :]
-    small_ref[...] = acc_ref[feat : feat + small_ref.shape[0], :]
-
-
-def join_image(core, halves, feat, small_rows):
-    width = halves[0].shape[2]
-    rows = sum(t.shape[0] * t.shape[1] for t in halves)
+def widen_rest_kernel(attn_rows, img_rows, parts_ref, *outs):
+    *squares, img_ref, small_ref = outs
+    devices = parts_ref.shape[0]
+    width = img_ref.shape[1]
+    per = width // attn_rows
+    feat = img_ref.shape[0]
+    for j, out_ref in enumerate(squares):
+        for i in range(per):
+            value = parts_ref[j * per + i, :attn_rows, :]
+            out_ref[i * attn_rows : (i + 1) * attn_rows, :] = value.astype(f32)
+    for i in range(devices):
+        value = parts_ref[i, attn_rows:, :].astype(f32)
+        at = i * img_rows
+        inside = min(max(feat - at, 0), img_rows)
+        if inside:
+            img_ref[at : at + inside, :] = value[:inside]
+        last = min(feat + small_ref.shape[0] - at, img_rows)
+        if last > inside:
+            first = at + inside - feat
+            small_ref[first : first + last - inside, :] = value[inside:last]
+
+
+def widen_rest(parts, attn_rows, feat, small_rows):
+    devices, rows, width = parts.shape
+    shapes = [(width, width)] * 4 + [(feat, width), (small_rows, width)]
     return pl.pallas_call(
-        functools.partial(join_image_kernel, feat),
-        out_shape=[
-            jax.ShapeDtypeStruct((feat, width), f32),
-            jax.ShapeDtypeStruct((small_rows, width), f32),
-        ],
-        grid_spec=pltpu.PrefetchScalarGridSpec(
-            num_scalar_prefetch=1,
-            grid=(1,),
-            in_specs=[whole(t.shape) for t in halves],
-            out_specs=[whole((feat, width)), whole((small_rows, width))],
-            scratch_shapes=[pltpu.VMEM((rows, width), f32)],
-        ),
+        functools.partial(widen_rest_kernel, attn_rows, rows - attn_rows),
+        out_shape=[jax.ShapeDtypeStruct(t, f32) for t in shapes],
         compiler_params=pltpu.CompilerParams(vmem_limit_bytes=LIMIT),
-        cost_estimate=cost(0, feat * width * 8),
-        name="join_image",
-    )(core, *halves)
-
-
-def widen_ff_kernel(down_in, up_in, down_ref, up_ref):
-    down_ref[...] = down_in[...].reshape(down_ref.shape).astype(f32)
-    up_ref[...] = up_in[...].reshape(up_ref.shape).astype(f32)
-
-
-def widen_ff(parts, width, blocks):
-    devices, rows, _ = parts.shape
-    per = devices // blocks
-    return pl.pallas_call(
-        widen_ff_kernel,
-        out_shape=[
-            jax.ShapeDtypeStruct((blocks * width, width), f32),
-            jax.ShapeDtypeStruct((width, blocks * width), f32),
-        ],
-        grid=(blocks,),
-        in_specs=[
-            pl.BlockSpec((per, rows // 2, width), lambda t: (t, 0, 0)),
-            pl.BlockSpec((per, rows // 2, width), lambda t: (t, 1, 0)),
-        ],
-        out_specs=[
-            pl.BlockSpec((width, width), lambda t: (t, 0)),
-            pl.BlockSpec((width, width), lambda t: (0, t)),
-        ],
         cost_estimate=cost(0, parts.size * 6),
-        name="widen_ff",
-    )(parts, parts)
+        name="widen_rest",
+    )(parts)
 
 
 def run_feed_forward(captions, counts, n1, mixed, cot, weights, cut, wo, bu, bd, g1, g2, beta2):
@@ -597,13 +581,13 @@
     )(counts, offset, q, k, v, p, gc, gm, wq, wk, wv)
 
 
-def weight_grad_kernel(lhs_of, rhs_of, core_ref, *refs):
+def weight_grad_kernel(lhs_of, rhs_of, groups, core_ref, *refs):
     lhs_refs = refs[: max(lhs_of) + 1]
     rhs_refs = refs[len(lhs_refs) : len(lhs_refs) + max(rhs_of) + 1]
-    away_ref, kept_ref, acc_ref = refs[-3:]
+    outs = refs[len(lhs_refs) + len(rhs_refs) : -1]
+    acc_ref = refs[-1]
     step = pl.program_id(0)
     core = core_ref[0]
-    pairs = away_ref.shape[0]
     kinds = {}
     for i, kind in enumerate(zip(lhs_of, rhs_of)):
         kinds.setdefault(kind, []).append(i)
@@ -614,28 +598,30 @@
             value = tn(lhs_refs[a][...], rhs_refs[b][...]).astype(bf16)
             acc_ref[...] = value.reshape(acc_ref.shape)
 
-    for i in range(pairs):
-        away_ref[i] = acc_ref[2 * i + 1 - core]
-        kept_ref[i] = acc_ref[2 * i + core]
-
-
-def weight_grads(core, devices, lhs, rhs, lhs_of, rhs_of, lhs_maps, rhs_maps, out_width, name):
+    for i in range(outs[0].shape[0]):
+        for side in (0, 1):
+            at = 0
+            for ref in outs[side * groups : (side + 1) * groups]:
+                rows = ref.shape[1]
+                ref[i] = acc_ref[2 * i + (1 - core if side == 0 else core), at : at + rows, :]
+                at += rows
+
+
+def weight_grads(core, devices, lhs, rhs, lhs_of, rhs_of, lhs_maps, rhs_maps, width, groups, name):
     steps = len(lhs_of)
     total = lhs[0].shape[0]
-    width = out_width
     rows = steps * width // devices
     per = width // rows
-    half = jax.ShapeDtypeStruct((devices // 2, rows, width), bf16)
-    out = pl.BlockSpec((per // 2, rows, width), lambda s, *_: (s, 0, 0))
+    outs = [rows // groups] * (2 * groups)
     specs = [pl.BlockSpec((total, width), m) for m in lhs_maps + rhs_maps]
-    return pl.pallas_call(
-        functools.partial(weight_grad_kernel, lhs_of, rhs_of),
-        out_shape=[half, half],
+    out = pl.pallas_call(
+        functools.partial(weight_grad_kernel, lhs_of, rhs_of, groups),
+        out_shape=[jax.ShapeDtypeStruct((devices // 2, r, width), bf16) for r in outs],
         grid_spec=pltpu.PrefetchScalarGridSpec(
             num_scalar_prefetch=1,
             grid=(steps,),
             in_specs=specs,
-            out_specs=[out, out],
+            out_specs=[pl.BlockSpec((per // 2, r, width), lambda s, *_: (s, 0, 0)) for r in outs],
             scratch_shapes=[pltpu.VMEM((per, rows, width), bf16)],
         ),
         compiler_params=pltpu.CompilerParams(
@@ -644,6 +630,7 @@
         cost_estimate=cost(2 * total * width * width * steps, steps * width * (total + width) * 2),
         name=name,
     )(core, *lhs, *rhs)
+    return list(zip(out[:groups], out[groups:]))
 
 
 def axis_bits(name):
@@ -711,21 +698,6 @@
     def total(self):
         return add_low(*self.value)
 
-    def split(self, at, orders):
-        parts = []
-        for rows, order in zip((slice(None, at), slice(at, None)), orders):
-            part = Scatter(*[t[..., rows, :] for t in self.value], ())
-            part.order = [b for b in order if b in self.layout]
-            part.layout = list(self.layout)
-            part.fresh = False
-            parts.append(part)
-        return parts
-
-    def merge(self, parts):
-        self.value = tuple(jnp.concatenate(t, -2) for t in zip(*[p.value for p in parts]))
-        self.layout = list(parts[0].layout)
-        self.order = list(parts[0].order)
-
 
 class Gather:
     def __init__(self, rows, order, layout=()):
@@ -772,22 +744,10 @@
 
 
 class Sum:
-    def __init__(self, away, kept, orders):
-        self.movers = [Scatter(away, kept, orders[0])]
-        self.orders = orders
-        self.at = 8 * (-(-away.shape[1] // 16))
+    def __init__(self, parts, orders):
         far = len(axis_bits("enc"))
-        middle = len(orders[0]) - 1 - far
-        self.steps = (
-            [self.near]
-            + [self.run] * middle
-            + [self.far]
-            + [self.run] * (far - 1)
-            + [self.turn]
-            + [self.run] * (far - 1)
-            + [self.part]
-            + [self.run] * (middle - 1)
-        )
+        self.movers = [Scatter(*part, order) for part, order in zip(parts, orders)]
+        self.steps = [self.run] * (len(orders[0]) - far) + [self.merge] + [self.run] * (far - 1)
 
     @property
     def value(self):
@@ -799,32 +759,21 @@
             mover.value = value
 
     def stage(self):
-        self.steps.pop(0)()
+        if self.steps:
+            self.steps.pop(0)()
 
     def run(self):
         for mover in self.movers:
             mover.stage()
 
-    def near(self):
+    def merge(self):
+        first = self.movers[0]
+        first.value = tuple(jnp.concatenate(t, -2) for t in zip(*[m.value for m in self.movers]))
+        self.movers = [first]
         self.run()
-        self.whole = self.movers[0]
-        self.movers = self.whole.split(self.at, self.orders)
-
-    def far(self):
-        self.whole.merge(self.movers)
-        self.movers = [self.whole]
-        self.run()
-
-    def turn(self):
-        self.movers = [Gather(self.whole.total(), axis_bits("enc"))]
-        self.run()
-
-    def part(self):
-        self.movers = self.movers[0].split(self.at, self.orders)
-        self.run()
-
-    def halves(self):
-        return [t for mover in self.movers for t in mover.halves()]
+
+    def total(self):
+        return self.movers[0].total()
 
 
 def body(
@@ -868,12 +817,12 @@
 
     up_blocks = w_up.reshape(cut, ff_blocks, model_width).transpose(1, 0, 2)
     ff_shard = jnp.concatenate([w_down, up_blocks.reshape(ff_blocks * cut, model_width)], 0)
-    ff_weights = lax.all_gather(ff_shard, axes, axis=0)
     rows_up = cut
     img = Gather(w_img, far)
     attn = Gather(jnp.concatenate([w_query, w_key, w_value, w_out], 0), far)
     img.stage()
-    fence([img, attn])
+    (ff_shard,) = fence([img, attn], ff_shard)
+    ff_weights = lax.all_gather(ff_shard, axes, axis=0)
     while img.order:
         img.stage()
         attn.stage()
@@ -965,7 +914,7 @@
     )
     fixed = lambda s, *_: (0, 0)
     moving = lambda s, *_: (0, s)
-    down_away, down_kept = weight_grads(
+    (down,) = weight_grads(
         core,
         device_count,
         [activated],
@@ -975,9 +924,10 @@
         [moving],
         [fixed],
         model_width,
+        1,
         "grad_w_down",
     )
-    up_away, up_kept = weight_grads(
+    (up,) = weight_grads(
         core,
         device_count,
         [normed_one],
@@ -987,15 +937,13 @@
         [fixed],
         [moving],
         model_width,
+        1,
         "grad_w_up",
     )
-    down = Scatter(down_away, down_kept, orders[0])
-    up = Scatter(up_away, up_kept, orders[1])
-    down.stage()
-    up.stage()
-    (grad_context,) = fence([down, up], grad_context)
-    down.stage()
-    up.stage()
+    ff = Sum([down, up], orders)
+    ff.stage()
+    (grad_context,) = fence([ff], grad_context)
+    ff.stage()
     grad_query, grad_keys, grad_values, grad_text, grad_slots, attn_sums = run_attention_backward(
         geometry,
         region_count,
@@ -1011,12 +959,11 @@
         value_full,
     )
     grad_query, grad_keys, grad_values, grad_slots, attn_sums = fence(
-        [down, up], grad_query, grad_keys, grad_values, grad_slots, attn_sums
+        [ff], grad_query, grad_keys, grad_values, grad_slots, attn_sums
     )
     back = lax.all_to_all(grad_slots, axes, split_axis=0, concat_axis=0, tiled=True)
-    down.stage()
-    up.stage()
-    attn_away, attn_kept = weight_grads(
+    ff.stage()
+    attn_parts = weight_grads(
         core,
         device_count,
         [hidden_in, context],
@@ -1026,20 +973,19 @@
         [fixed] * 2,
         [fixed] * 4,
         model_width,
+        2,
         "grad_w_attn",
     )
-    attn = Sum(attn_away, attn_kept, orders)
-    (back,) = fence([down, up, attn], back)
-    while len(down.order) > len(far):
-        down.stage()
-        up.stage()
-        fence([down, up])
-    down.stage()
-    up.stage()
+    attn = Sum(attn_parts, orders)
+    (back,) = fence([ff, attn], back)
+    while len(ff.steps) > len(far):
+        ff.stage()
+        fence([ff])
+    ff.stage()
     attn.stage()
     small_rows = 40
     chunk = 8 * (-(-(feat + small_rows) // (8 * device_count)))
-    grad_pre, grad_feats, img_away, img_kept = run_image_backward(
+    grad_pre, grad_feats, img_parts = run_image_backward(
         geometry,
         chunk,
         core,
@@ -1053,34 +999,40 @@
         attn_sums,
         grad_b_up.reshape(ff_blocks, model_width),
     )
-    img = Sum(img_away, img_kept, orders)
-    fence([down, up, attn, img])
-    while down.order:
+    img = Sum(img_parts, orders)
+    fence([ff, attn, img])
+    while ff.steps:
+        ff.stage()
+        if not ff.steps:
+            attn.stage()
+            img.stage()
+        fence([ff, attn, img])
+    ff = Gather(ff.total(), far)
+    ff.stage()
+    while img.steps:
+        attn.stage()
+        img.stage()
+        fence([attn, img, ff])
+    rest = jnp.concatenate([attn.total(), img.total()], 0)
+    rest_all = lax.all_gather(rest, axes, axis=0)
+    fence([ff], rest)
+    while ff.order:
+        ff.stage()
+        fence([ff])
+    down, up = ff.split(w_down.shape[0], orders)
+    while len(down.order) > 1:
         down.stage()
         up.stage()
-        if not down.order:
-            attn.stage()
-            img.stage()
-        fence([down, up, attn, img])
-    ff_shard = jnp.concatenate([down.total(), up.total()], 0)
-    ff_all = lax.all_gather(ff_shard, axes, axis=0)
-    while attn.steps:
-        attn.stage()
-        img.stage()
-        if len(attn.steps) == 0:
-            grad_w_down, grad_w_up = widen_ff(ff_all, model_width, ff_blocks)
-            grad_w_down, grad_w_up = fence([attn, img], grad_w_down, grad_w_up)
-        else:
-            fence([attn, img])
-    attn_halves = attn.halves()
-    img.stage()
-    fence([img], *attn_halves)
-    img_halves = img.halves()
-    grad_w_query, grad_w_key, grad_w_value, grad_w_out = [
-        join_square(core, attn_halves, j) for j in range(4)
-    ]
+        fence([down, up])
+    down_halves, up_halves = down.halves(), up.halves()
+    grad_w_down = join_blocks(
+        core, down_halves, (ff_blocks * model_width, model_width), (1, 0)
+    )
+    grad_w_up = join_blocks(core, up_halves, (model_width, ff_blocks * model_width), (0, 1))
     grad_boxes = jnp.einsum("cd,rd->cr", w_box, grad_pre, preferred_element_type=f32).astype(bf16)
-    grad_w_img, small = join_image(core, img_halves, feat, small_rows)
+    grad_w_query, grad_w_key, grad_w_value, grad_w_out, grad_w_img, small = widen_rest(
+        rest_all, 4 * cut, feat, small_rows
+    )
     grad_w_box = small[:box_count]
     grad_b_img, grad_g_reg, grad_beta_reg = [small[8 + i] for i in range(3)]
     grad_g_two, grad_beta_two, grad_b_down, grad_g_one, grad_beta_one, grad_b_out = [

time: 515 us -> 488 us (0.948)
  starting transfers between devices: 70.4 us -> 61.4 us
  local copies, waits for them, and re-layouts: 19.7 us -> 11.9 us
    ppermute x56 -> x48, starting transfers between devices: 62.8 us -> 54.7 us  [swap_bit(): return lax.ppermute(tensor, name, [(i, i ^ step) for i in range(size)])]
    slice x6 -> x0, local copies, waits for them, and re-layouts: 7.88 us -> none  [split(): part = Scatter(*[t[..., rows, :] for t in self.value], ())]
    ppermute x56 -> x48, waiting for transfers between devices: 197 us -> 190 us  [swap_bit(): return lax.ppermute(tensor, name, [(i, i ^ step) for i in range(size)])]
    all_gather x1, waiting for transfers between devices: 0.02 us -> 5.54 us  [body(): rest_all = lax.all_gather(rest, axes, axis=0)]
    pallas_call x9 -> x6, Pallas kernels: 58.2 us -> 52.7 us  [the longest x3 30.4 us: weight_grads(): pl.pallas_call(functools.partial(weight_grad_kernel, lhs_of, rhs_of, grou...]
    select_n x26 -> x20, other arithmetic: 9.76 us -> 4.58 us  [stage(): jnp.where(at == my_bit(bit), jnp.expand_dims(sent, axis), jnp.expand_dims...]
    convert_element_type x31 -> x24, other arithmetic: 21.4 us -> 23.7 us  [add_low(): return (kept.astype(f32) + came.astype(f32)).astype(bf16)]
  transfers between devices with their start and end apart: 60 -> 52, of which waited for: 37 -> 31; matrix products, arithmetic and copies ran while one was open for 9% -> 8% of each run, Pallas kernels for 19% -> 20%
where the time goes in v3:
time: 488 us; the launch traced here: 480 us
  waiting for transfers between devices  200 us (41%)
  Pallas kernels  156 us (32%)
  starting transfers between devices  61.4 us (13%)
  other arithmetic  34.5 us (7%)
  between operations  15.8 us (3%)
  local copies, waits for them, and re-layouts  11.9 us (2%)
    ppermute x48, waiting for transfers between devices, swap_bit(): return lax.ppermute(tensor, name, [(i, i ^ step) for i in range(size)])  190 us
    ppermute x48, starting transfers between devices, swap_bit(): return lax.ppermute(tensor, name, [(i, i ^ step) for i in range(size)])  54.7 us
    pallas_call x1, Pallas kernels, run_feed_forward(): pl.pallas_call(feed_forward, out_shape=shapes, grid_spec=pltpu.PrefetchSc...  41.7 us
    pallas_call x3, Pallas kernels, weight_grads(): pl.pallas_call(functools.partial(weight_grad_kernel, lhs_of, rhs_of, grou...  30.4 us
    convert_element_type x24, other arithmetic, add_low(): return (kept.astype(f32) + came.astype(f32)).astype(bf16)  23.7 us
    pallas_call x1, Pallas kernels, run_attention_backward(): pl.pallas_call(functools.partial(attention_backward, *geometry), out_shap...  23.6 us
    pallas_call x1, Pallas kernels, run_attention_forward(): pl.pallas_call(functools.partial(attention_forward, *geometry), out_shape...  21.5 us
    pallas_call x2, Pallas kernels, join_blocks(): pl.pallas_call(join_kernel, out_shape=jax.ShapeDtypeStruct(shape, f32), g...  13.2 us
  transfers between devices with their start and end apart: 52, of which 31 were waited for; matrix products, arithmetic and copies ran while one was open for 8% of the time, Pallas kernels for 20%

profile of v3, /device:TPU:0, one launch (start us, length us, event | category | flops | bytes accessed | tf_op | source)
XLA Modules:
  0.0 479.7 jit_solution(774852399881552517)
XLA Ops:
  7.2 4.1 collective-permute-start
  12.3 1.6 pad_maximum_fusion.1
  14.8 1.7 collective-permute-done
  17.3 3.5 collective-permute-start.1
  20.8 5.1 %collective-permute-done.2 = bf16[96,768]{1,0:T(8,128)(2,1)S(1)} collective-permute-done((bf16[96,768]{1,0:T(8,128)(2,1)S(1)}, bf16[96,768]{1,0:T(8,128)(2,1)S(1)}, u32[]{:S(2)}, u32[]{:S(2)}) %collective-permute-start.2) | collective-permute-done | bytes 147488 | tf_op jit(solution)/shard_map/ppermute | solution.py:657
  27.3 1.6 collective-permute-start.4
  30.6 4.8 %collective-permute-done.4 = bf16[2,2,32,768]{3,2,1,0:T(8,128)(2,1)S(1)} collective-permute-done((bf16[2,2,32,768]{3,2,1,0:T(8,128)(2,1)S(1)}, bf16[2,2,32,768]{3,2,1,0:T(8,128)(2,1)S(1)}, u32[]{:S(2)}, u32[]{:S(2)}) %collective-permute-start.4) | collective-permute-done | bytes 196640 | tf_op jit(solution)/shard_map/ppermute | solution.py:657
  35.7 6.4 %collective-permute-done.5 = bf16[2,96,768]{2,1,0:T(8,128)(2,1)S(1)} collective-permute-done((bf16[2,96,768]{2,1,0:T(8,128)(2,1)S(1)}, bf16[2,96,768]{2,1,0:T(8,128)(2,1)S(1)}, u32[]{:S(2)}, u32[]{:S(2)}) %collective-permute-start.5) | collective-permute-done | bytes 294944 | tf_op jit(solution)/shard_map/ppermute | solution.py:657
  45.2 11.3 %collective-permute-done.7 = bf16[2,2,2,32,768]{4,3,2,1,0:T(8,128)(2,1)S(1)} collective-permute-done((bf16[2,2,2,32,768]{4,3,2,1,0:T(8,128)(2,1)S(1)}, bf16[2,2,2,32,768]{4,3,2,1,0:T(8,128)(2,1)S(1)}, u32[]{:S(2)}, u32[]{:S(2)}) %collective-permute-start.7) | collective-permute-done | bytes 393248 | tf_op jit(solution)/shard_map/ppermute | solution.py:657
  56.6 4.6 collective-permute-done.6
  61.4 2.5 collective-permute-start.9
  64.6 4.4 collective-permute-done.9
  69.0 4.3 collective-permute-done.8
  73.5 1.6 bitcast_select_fusion.3
  75.2 2.4 pad_maximum_fusion
  77.5 6.6 %image_encode.1 = (f32[416,768]{1,0:T(8,128)}, bf16[512,768]{1,0:T(8,128)(2,1)}) custom-call(bf16[416,2048]{1,0:T(8,128)(2,1)} %x_ref.3, bf16[4,416]{1,0:T(4,128)(2,1)} %box_ref.3, bf16[2048,768]{1,0:T(8,128)(2,1)} %bitcast.132, bf16[4,768]{1,0:T(4,128)(2,1)} %wb_ref.1, f32[768]{0:T(1024)} %bi_ref.1, f32[768]{0:T(1024)} %gr_ref.3, f32[768]{0:T(1024)} %betar_ref.1), custom_call_target="tpu_custom_call" | custom-call | flops 1308622848 | bytes 6766592 | tf_op jit(solution)/shard_map/image_encode/pallas_call | solution.py:346
  84.1 3.3 all-to-all-start
  87.5 1.7 collective-permute-start.13
  90.6 25.2 %collective-permute-done.13 = bf16[2,2,2,48,768]{4,3,2,1,0:T(8,128)(2,1)S(1)} collective-permute-done((bf16[2,2,2,48,768]{4,3,2,1,0:T(8,128)(2,1)S(1)}, bf16[2,2,2,48,768]{4,3,2,1,0:T(8,128)(2,1)S(1)}, u32[]{:S(2)}, u32[]{:S(2)}) %collective-permute-start.13) | collective-permute-done | bytes 589856 | tf_op jit(solution)/shard_map/ppermute | solution.py:657
  116.2 4.3 all-to-all-done
  121.7 2.6 collective-permute-done.14
  124.2 1.7 collective-permute-done.15
  126.3 2.3 fusion.39
  128.6 21.5 %attention_forward.1 = (bf16[1024,768]{1,0:T(8,128)(2,1)}, bf16[1024,768]{1,0:T(8,128)(2,1)}, bf16[1024,768]{1,0:T(8,128)(2,1)}, bf16[1024,768]{1,0:T(8,128)(2,1...) custom-call(s32[4]{0:T(128)} %captions.3, ...), custom_call_target="tpu_custom_call" | custom-call | flops 8053063680 | bytes 20447232 | tf_op jit(solution)/shard_map/attention_forward/pallas_call | solution.py:374
  150.2 41.7 %feed_forward.1 = (bf16[1024,768]{1,0:T(8,128)(2,1)}, bf16[1024,3072]{1,0:T(8,128)(2,1)}, bf16[1024,768]{1,0:T(8,128)(2,1)}, bf16[1024,3072]{1,0:T(8,128)(2,1)},...) custom-call(s32[4]{0:T(128)} %captions.3, ...), custom_call_target="tpu_custom_call" | custom-call | flops 20535312384 | bytes 36175872 | tf_op jit(solution)/shard_map/feed_forward/pallas_call | solution.py:534
  191.9 9.4 %grad_w_up.1 = (bf16[16,96,768]{2,1,0:T(8,128)(2,1)}, bf16[16,96,768]{2,1,0:T(8,128)(2,1)}) custom-call(s32[1]{0:T(128)} %bitcast.18.core_ref, bf16[1024,768]{1,0:T(8,128)(2,1)} %get-tuple-element.177.n_ref.refs_0_, bf16[1024,3072]{1,0:T(8,128)(2,1)} %get-tuple-element.189.refs_1_), custom_call_target="tpu_custom_call" | custom-call | flops 4831838208 | bytes 11010048 | tf_op jit(solution)/shard_map/grad_w_up/pallas_call | solution.py:617
  201.7 9.7 %grad_w_down.1 = (bf16[16,96,768]{2,1,0:T(8,128)(2,1)}, bf16[16,96,768]{2,1,0:T(8,128)(2,1)}) custom-call(s32[1]{0:T(128)} %bitcast.18.core_ref, bf16[1024,3072]{1,0:T(8,128)(2,1)} %get-tuple-element.185.refs_0_, bf16[1024,768]{1,0:T(8,128)(2,1)} %get-tuple-element.186.refs_1_), custom_call_target="tpu_custom_call" | custom-call | flops 4831838208 | bytes 11010048 | tf_op jit(solution)/shard_map/grad_w_down/pallas_call | solution.py:617
  211.6 4.7 collective-permute-done.16
  216.3 2.7 fusion.3
  220.6 3.3 fusion.1
  226.9 23.6 %attention_backward.1 = (bf16[1024,768]{1,0:T(8,128)(2,1)}, bf16[1024,768]{1,0:T(8,128)(2,1)}, bf16[1024,768]{1,0:T(8,128)(2,1)}, bf16[512,768]{1,0:T(8,128)(2,1...) custom-call(s32[4]{0:T(128)} %counts.5, s32[1]{0:T(128)S(6)} %copy.121.offset, ...), custom_call_target="tpu_custom_call" | custom-call | flops 10066329600 | bytes 22020096 | tf_op jit(solution)/shard_map/attention_backward/pallas_call | solution.py:566
  250.6 1.6 collective-permute-done.18
  252.1 3.4 all-to-all-start.1
  256.5 1.6 collective-permute-start.21
  258.1 2.4 fusion.8
  262.2 11.2 %grad_w_attn.1 = (bf16[16,48,768]{2,1,0:T(8,128)(2,1)}, bf16[16,48,768]{2,1,0:T(8,128)(2,1)}, bf16[16,48,768]{2,1,0:T(8,128)(2,1)}, bf16[16,48,768]{2,1,0:T(8,128)(2,1)}) custom-call(s32[1]{0:T(128)} %bitcast.18.core_ref, bf16[1024,768]{1,0:T(8,128)(2,1)} %get-tuple-element.210.refs_0_, bf16[1024,768]{1,0:T(8,128)(2,1)} %get-tuple-element.211.refs_1_, ...), custom_call_target="tpu_custom_call" | custom-call | flops 4831838208 | bytes 11010048 | tf_op jit(solution)/shard_map/grad_w_attn/pallas_call | solution.py:617
  273.4 5.8 %collective-permute-done.21 = bf16[2,2,96,768]{3,2,1,0:T(8,128)(2,1)} collective-permute-done((bf16[2,2,96,768]{3,2,1,0:T(8,128)(2,1)}, bf16[2,2,96,768]{3,2,1,0:T(8,128)(2,1)}, u32[]{:S(2)}, u32[]{:S(2)}) %collective-permute-start.21) | collective-permute-done | bytes 589856 | tf_op jit(solution)/shard_map/ppermute | solution.py:657
  286.7 9.4 %image_backward.1 = (bf16[416,768]{1,0:T(8,128)(2,1)}, bf16[416,2048]{1,0:T(8,128)(2,1)}, bf16[16,40,768]{2,1,0:T(8,128)(2,1)}, bf16[16,32,768]{2,1,0:T(8,128)(2...) custom-call(s32[1]{0:T(128)} %bitcast.18.core_ref, bf16[416,2048]{1,0:T(8,128)(2,1)} %x_ref.3, ...), custom_call_target="tpu_custom_call" | custom-call | flops 2617245696 | bytes 10092544 | tf_op jit(solution)/shard_map/image_backward/pallas_call | solution.py:407
  296.2 2.8 collective-permute-done.22
  299.1 3.0 fusion.14
  302.8 2.4 fusion.12
  306.9 2.5 collective-permute-start.25
  309.5 13.9 %collective-permute-done.25 = bf16[192,768]{1,0:T(8,128)(2,1)S(1)} collective-permute-done((bf16[192,768]{1,0:T(8,128)(2,1)S(1)}, bf16[192,768]{1,0:T(8,128)(2,1)S(1)}, u32[]{:S(2)}, u32[]{:S(2)}) %collective-permute-start.25) | collective-permute-done | bytes 294944 | tf_op jit(solution)/shard_map/ppermute | solution.py:657
  332.5 6.6 %collective-permute-done.34 = bf16[192,768]{1,0:T(8,128)(2,1)S(1)} collective-permute-done((bf16[192,768]{1,0:T(8,128)(2,1)S(1)}, bf16[192,768]{1,0:T(8,128)(2,1)S(1)}, u32[]{:S(2)}, u32[]{:S(2)}) %collective-permute-start.34) | collective-permute-done | bytes 294944 | tf_op jit(solution)/shard_map/ppermute | solution.py:657
  339.2 7.4 %collective-permute-done.31 = bf16[2,2,48,768]{3,2,0,1:T(8,128)(2,1)S(1)} collective-permute-done((bf16[2,2,48,768]{3,2,0,1:T(8,128)(2,1)S(1)}, bf16[2,2,48,768]{3,2,0,1:T(8,128)(2,1)S(1)}, u32[]{:S(2)}, u32[]{:S(2)}) %collective-permute-start.31) | collective-permute-done | bytes 294944 | tf_op jit(solution)/shard_map/ppermute | solution.py:657
  348.0 2.9 collective-permute-start.35
  351.0 1.8 collective-permute-start.37
  352.8 3.9 collective-permute-done.37
  359.0 9.2 %collective-permute-done.38 = bf16[96,768]{1,0:T(8,128)(2,1)S(1)} collective-permute-done((bf16[96,768]{1,0:T(8,128)(2,1)S(1)}, bf16[96,768]{1,0:T(8,128)(2,1)S(1)}, u32[]{:S(2)}, u32[]{:S(2)}) %collective-permute-start.38) | collective-permute-done | bytes 147488 | tf_op jit(solution)/shard_map/ppermute | solution.py:657
  368.4 5.7 %collective-permute-done.40 = bf16[72,768]{1,0:T(8,128)(2,1)S(1)} collective-permute-done((bf16[72,768]{1,0:T(8,128)(2,1)S(1)}, bf16[72,768]{1,0:T(8,128)(2,1)S(1)}, u32[]{:S(2)}, u32[]{:S(2)}) %collective-permute-start.40) | collective-permute-done | bytes 110624 | tf_op jit(solution)/shard_map/ppermute | solution.py:657
  375.0 10.7 %collective-permute-done.41 = bf16[2,192,768]{2,1,0:T(8,128)(2,1)S(1)} collective-permute-done((bf16[2,192,768]{2,1,0:T(8,128)(2,1)S(1)}, bf16[2,192,768]{2,1,0:T(8,128)(2,1)S(1)}, u32[]{:S(2)}, u32[]{:S(2)}) %collective-permute-start.41) | collective-permute-done | bytes 589856 | tf_op jit(solution)/shard_map/ppermute | solution.py:657
  386.0 3.4 collective-permute-start.43
  389.4 1.9 collective-permute-start.42
  391.3 7.2 %collective-permute-done.43 = bf16[2,2,96,768]{3,2,1,0:T(8,128)(2,1)S(1)} collective-permute-done((bf16[2,2,96,768]{3,2,1,0:T(8,128)(2,1)S(1)}, bf16[2,2,96,768]{3,2,1,0:T(8,128)(2,1)S(1)}, u32[]{:S(2)}, u32[]{:S(2)}) %collective-permute-start.43) | collective-permute-done | bytes 589856 | tf_op jit(solution)/shard_map/ppermute | solution.py:657
  398.7 5.8 %collective-permute-done.42 = bf16[2,2,96,768]{3,2,1,0:T(8,128)(2,1)S(1)} collective-permute-done((bf16[2,2,96,768]{3,2,1,0:T(8,128)(2,1)S(1)}, bf16[2,2,96,768]{3,2,1,0:T(8,128)(2,1)S(1)}, u32[]{:S(2)}, u32[]{:S(2)}) %collective-permute-start.42) | collective-permute-done | bytes 589856 | tf_op jit(solution)/shard_map/ppermute | solution.py:657
  404.6 2.5 collective-permute-start.45
  407.2 21.1 %collective-permute-done.45 = bf16[2,2,2,96,768]{4,3,2,1,0:T(8,128)(2,1)S(1)} collective-permute-done((bf16[2,2,2,96,768]{4,3,2,1,0:T(8,128)(2,1)S(1)}, bf16[2,2,2,96,768]{4,3,2,1,0:T(8,128)(2,1)S(1)}, u32[]{:S(2)}, u32[]{:S(2)}) %collective-permute-start.45) | collective-permute-done | bytes 1179680 | tf_op jit(solution)/shard_map/ppermute | solution.py:657
  428.6 1.7 collective-permute-done.44
  432.8 6.7 %collective-permute-done.47 = bf16[2,2,2,2,96,768]{5,4,3,2,1,0:T(8,128)(2,1)S(1)} collective-permute-done((bf16[2,2,2,2,96,768]{5,4,3,2,1,0:T(8,128)(2,1)S(1)}, bf16[2,2,2,2,96,768]{5,4,3,2,1,0:T(8,128)(2,1)S(1)}, u32[]{:S(2)}, u32[]{:S(2)}) %collective-permute-start.47) | collective-permute-done | bytes 2359328 | tf_op jit(solution)/shard_map/ppermute | solution.py:657
  440.8 6.5 %join_blocks.3 = f32[3072,768]{1,0:T(8,128)} custom-call(s32[1]{0:T(128)} %bitcast.18.core_ref, bf16[16,96,768]{2,1,0:T(8,128)(2,1)} %bitcast.135, bf16[16,96,768]{2,1,0:T(8,128)(2,1)} %bitcast.140), custom_call_target="tpu_custom_call" | custom-call | bytes 14155776 | tf_op jit(solution)/shard_map/join_blocks/pallas_call | solution.py:449
  447.4 6.6 %join_blocks.2 = f32[768,3072]{1,0:T(8,128)} custom-call(s32[1]{0:T(128)} %bitcast.18.core_ref, bf16[16,96,768]{2,1,0:T(8,128)(2,1)} %bitcast.134, bf16[16,96,768]{2,1,0:T(8,128)(2,1)} %bitcast.73.refs_1_), custom_call_target="tpu_custom_call" | custom-call | bytes 14155776 | tf_op jit(solution)/shard_map/join_blocks/pallas_call | solution.py:449
  454.0 5.5 %all-gather.7.cloned.1.call-done = bf16[5376,768]{1,0:T(8,128)(2,1)} async-done(((bf16[168,768]{1,0:T(8,128)(2,1)}), bf16[5376,768]{1,0:T(8,128)(2,1)}) %all-gather.7.cloned.1.call-update) | async-done | bytes 8257552 | tf_op jit(solution)/shard_map/all_gather | solution.py:1017
  459.6 9.2 %widen_rest.1 = (f32[768,768]{1,0:T(8,128)}, f32[768,768]{1,0:T(8,128)}, f32[768,768]{1,0:T(8,128)}, f32[768,768]{1,0:T(8,128)}, f32[2048,768]{1,0:T(8,128)}, /*index=5*/f32[40,768]{1,0:T(8,128)}) custom-call(bf16[32,168,768]{2,1,0:T(8,128)(2,1)} %bitcast.136), custom_call_target="tpu_custom_call" | custom-call | bytes 24772608 | tf_op jit(solution)/shard_map/widen_rest/pallas_call | solution.py:488
  468.7 1.7 slice_reduce_fusion
  (168 shorter events, 51.3 us)
Async XLA Ops:
  7.2 9.3 %copy-start.13 = (bf16[64,768]{1,0:T(8,128)(2,1)S(1)}, bf16[64,768]{1,0:T(8,128)(2,1)}, u32[]{:S(2)}) copy-start(bf16[64,768]{1,0:T(8,128)(2,1)} %param.33) | copy-start | bytes 294916
  7.2 143.0 %all-gather.5.cloned.1.call-start = ((), (), s32[]{:S(2)}) async-start(), calls=%async_computation.2 | async-start | bytes 9732096 | tf_op jit(solution)/shard_map/all_gather | solution.py:825
  7.2 9.2 %collective-permute-start = (bf16[64,768]{1,0:T(8,128)(2,1)}, bf16[64,768]{1,0:T(8,128)(2,1)S(1)}, u32[]{:S(2)}, u32[]{:S(2)}) collective-permute-start(bf16[64,768]{1,0:T(8,128)(2,1)} %param.33), channel_id=1, source_target_pairs={{0,16},{8,24},{16,0},{24,8},{1,17},{9,25},{17,1},{25,9},{2,18},{10... | collective-permute-start | bytes 294920 | tf_op jit(solution)/shard_map/ppermute | solution.py:657
  14.8 12.5 %copy-start.16 = (pred[2]{0:T(512)(128)(4,1)}, pred[2]{0:T(512)(128)(4,1)S(1)}, u32[]{:S(2)}) copy-start(pred[2]{0:T(512)(128)(4,1)S(1)} %iota_compare_fusion.1) | copy-start | bytes 10
  16.6 9.3 %collective-permute-start.2 = (bf16[96,768]{1,0:T(8,128)(2,1)S(1)}, bf16[96,768]{1,0:T(8,128)(2,1)S(1)}, u32[]{:S(2)}, u32[]{:S(2)}) collective-permute-start(bf16[96,768]{1,0:T(8,128)(2,1)S(1)} %pad_maximum_fusion.3), channel_id=1, source_target_pairs={{0,16},{8,24},{16,0},{24,8},{1,17},{9,25},{17,1},{25,9},{2,18},{10... | collective-permute-start | bytes 442376 | tf_op jit(solution)/shard_map/ppermute | solution.py:657
  17.3 9.8 %collective-permute-start.1 = (bf16[2,64,768]{2,1,0:T(8,128)(2,1)S(1)}, bf16[2,64,768]{2,1,0:T(8,128)(2,1)S(1)}, u32[]{:S(2)}, u32[]{:S(2)}) collective-permute-start(bf16[2,64,768]{2,1,0:T(8,128)(2,1)S(1)} %broadcast_select_fusion.17), channel_id=1, source_target_pairs={{0,8},{8,0},{16,24},{24,16},{1,9},{9,1},{17,25},{25,17},{2,10},{10... | collective-permute-start | bytes 589832 | tf_op jit(solution)/shard_map/ppermute | solution.py:657
  27.3 8.2 %collective-permute-start.4 = (bf16[2,2,32,768]{3,2,1,0:T(8,128)(2,1)S(1)}, bf16[2,2,32,768]{3,2,1,0:T(8,128)(2,1)S(1)}, u32[]{:S(2)}, u32[]{:S(2)}) collective-permute-start(bf16[2,2,32,768]{3,2,1,0:T(8,128)(2,1)S(1)} %get-tuple-element.345), channel_id=1, source_target_pairs={{0,2},{1,3},{2,0},{3,1},{4,6},{5,7},{6,4},{7,5},{8,10},{9,11},{10,... | collective-permute-start | bytes 589832 | tf_op jit(solution)/shard_map/ppermute | solution.py:657
  28.8 13.3 %collective-permute-start.5 = (bf16[2,96,768]{2,1,0:T(8,128)(2,1)S(1)}, bf16[2,96,768]{2,1,0:T(8,128)(2,1)S(1)}, u32[]{:S(2)}, u32[]{:S(2)}) collective-permute-start(bf16[2,96,768]{2,1,0:T(8,128)(2,1)S(1)} %broadcast_select_fusion.16), channel_id=1, source_target_pairs={{0,8},{8,0},{16,24},{24,16},{1,9},{9,1},{17,25},{25,17},{2,10},{10... | collective-permute-start | bytes 884744 | tf_op jit(solution)/shard_map/ppermute | solution.py:657
  29.1 6.5 %collective-permute-start.3 = (bf16[2,2,32,768]{3,2,1,0:T(8,128)(2,1)S(1)}, bf16[2,2,32,768]{3,2,1,0:T(8,128)(2,1)S(1)}, u32[]{:S(2)}, u32[]{:S(2)}) collective-permute-start(bf16[2,2,32,768]{3,2,1,0:T(8,128)(2,1)S(1)} %get-tuple-element.346), channel_id=1, source_target_pairs={{0,4},{1,5},{2,6},{3,7},{4,0},{5,1},{6,2},{7,3},{8,12},{9,13},{10,... | collective-permute-start | bytes 589832 | tf_op jit(solution)/shard_map/ppermute | solution.py:657
  42.2 14.3 %collective-permute-start.7 = (bf16[2,2,2,32,768]{4,3,2,1,0:T(8,128)(2,1)S(1)}, bf16[2,2,2,32,768]{4,3,2,1,0:T(8,128)(2,1)S(1)}, u32[]{:S(2)}, u32[]{:S(2)}) collective-permute-start(bf16[2,2,2,32,768]{4,3,2,1,0:T(8,128)(2,1)S(1)} %broadcast_select_fusion.13), channel_id=1, source_target_pairs={{0,4},{1,5},{2,6},{3,7},{4,0},{5,1},{6,2},{7,3},{8,12},{9,13},{10,... | collective-permute-start | bytes 1179656 | tf_op jit(solution)/shard_map/ppermute | solution.py:657
  43.8 17.4 %collective-permute-start.6 = (bf16[2,2,2,32,768]{4,3,2,1,0:T(8,128)(2,1)S(1)}, bf16[2,2,2,32,768]{4,3,2,1,0:T(8,128)(2,1)S(1)}, u32[]{:S(2)}, u32[]{:S(2)}) collective-permute-start(bf16[2,2,2,32,768]{4,3,2,1,0:T(8,128)(2,1)S(1)} %broadcast_select_fusion.15), channel_id=1, source_target_pairs={{0,2},{1,3},{2,0},{3,1},{4,6},{5,7},{6,4},{7,5},{8,10},{9,11},{10,... | collective-permute-start | bytes 1179656 | tf_op jit(solution)/shard_map/ppermute | solution.py:657
  61.4 7.5 %collective-permute-start.9 = (bf16[2,2,48,768]{3,2,1,0:T(8,128)(2,1)S(1)}, bf16[2,2,48,768]{3,2,1,0:T(8,128)(2,1)S(1)}, u32[]{:S(2)}, u32[]{:S(2)}) collective-permute-start(bf16[2,2,48,768]{3,2,1,0:T(8,128)(2,1)S(1)} %get-tuple-element.341), channel_id=1, source_target_pairs={{0,2},{1,3},{2,0},{3,1},{4,6},{5,7},{6,4},{7,5},{8,10},{9,11},{10,... | collective-permute-start | bytes 884744 | tf_op jit(solution)/shard_map/ppermute | solution.py:657
  63.9 9.5 %collective-permute-start.10 = (bf16[2,2,2,2,32,768]{5,4,3,2,1,0:T(8,128)(2,1)S(1)}, bf16[2,2,2,2,32,768]{5,4,3,2,1,0:T(8,128)(2,1)}, u32[]{:S(2)}, u32[]{:S(2)}) collective-permute-start(bf16[2,2,2,2,32,768]{5,4,3,2,1,0:T(8,128)(2,1)S(1)} %broadcast_select_fusion.8), channel_id=1, source_target_pairs={{0,1},{1,0},{2,3},{3,2},{4,5},{5,4},{6,7},{7,6},{8,9},{9,8},{10,11... | collective-permute-start | bytes 2359304 | tf_op jit(solution)/shard_map/ppermute | solution.py:657
  63.9 9.6 %collective-permute-start.11 = (bf16[2,2,2,2,32,768]{5,4,3,2,1,0:T(8,128)(2,1)S(1)}, bf16[2,2,2,2,32,768]{5,4,3,2,1,0:T(8,128)(2,1)}, u32[]{:S(2)}, u32[]{:S(2)}) collective-permute-start(bf16[2,2,2,2,32,768]{5,4,3,2,1,0:T(8,128)(2,1)S(1)} %broadcast_select_fusion.7), channel_id=1, source_target_pairs={{0,1},{1,0},{2,3},{3,2},{4,5},{5,4},{6,7},{7,6},{8,9},{9,8},{10,11... | collective-permute-start | bytes 2359304 | tf_op jit(solution)/shard_map/ppermute | solution.py:657
  64.4 8.9 %collective-permute-start.8 = (bf16[2,2,48,768]{3,2,1,0:T(8,128)(2,1)S(1)}, bf16[2,2,48,768]{3,2,1,0:T(8,128)(2,1)S(1)}, u32[]{:S(2)}, u32[]{:S(2)}) collective-permute-start(bf16[2,2,48,768]{3,2,1,0:T(8,128)(2,1)S(1)} %get-tuple-element.342), channel_id=1, source_target_pairs={{0,4},{1,5},{2,6},{3,7},{4,0},{5,1},{6,2},{7,3},{8,12},{9,13},{10,... | collective-permute-start | bytes 884744 | tf_op jit(solution)/shard_map/ppermute | solution.py:657
  84.1 36.3 %all-to-all-start = ((bf16[32,16,768]{2,1,0:T(8,128)(2,1)}), bf16[32,16,768]{2,1,0:T(8,128)(2,1)}, u32[]{:S(2)}, u32[]{:S(2)}) async-start(bf16[32,16,768]{2,1,0:T(8,128)(2,1)} %bitcast.153), calls=%async_computation | async-start | bytes 1572864 | tf_op jit(solution)/shard_map/all_to_all | solution.py:852
  87.5 28.3 %collective-permute-start.13 = (bf16[2,2,2,48,768]{4,3,2,1,0:T(8,128)(2,1)S(1)}, bf16[2,2,2,48,768]{4,3,2,1,0:T(8,128)(2,1)S(1)}, u32[]{:S(2)}, u32[]{:S(2)}) collective-permute-start(bf16[2,2,2,48,768]{4,3,2,1,0:T(8,128)(2,1)S(1)} %broadcast_select_fusion.10), channel_id=1, source_target_pairs={{0,4},{1,5},{2,6},{3,7},{4,0},{5,1},{6,2},{7,3},{8,12},{9,13},{10,... | collective-permute-start | bytes 1769480 | tf_op jit(solution)/shard_map/ppermute | solution.py:657
  89.2 26.9 %collective-permute-start.12 = (bf16[2,2,2,48,768]{4,3,2,1,0:T(8,128)(2,1)S(1)}, bf16[2,2,2,48,768]{4,3,2,1,0:T(8,128)(2,1)S(1)}, u32[]{:S(2)}, u32[]{:S(2)}) collective-permute-start(bf16[2,2,2,48,768]{4,3,2,1,0:T(8,128)(2,1)S(1)} %broadcast_select_fusion.12), channel_id=1, source_target_pairs={{0,2},{1,3},{2,0},{3,1},{4,6},{5,7},{6,4},{7,5},{8,10},{9,11},{10,... | collective-permute-start | bytes 1769480 | tf_op jit(solution)/shard_map/ppermute | solution.py:657
  120.5 3.7 collective-permute-start.14
  120.6 5.3 %collective-permute-start.15 = (bf16[2,2,2,2,48,768]{5,4,3,2,1,0:T(8,128)(2,1)S(1)}, bf16[2,2,2,2,48,768]{5,4,3,2,1,0:T(8,128)(2,1)S(1)}, u32[]{:S(2)}, u32[]{:S(2)}) collective-permute-start(bf16[2,2,2,2,48,768]{5,4,3,2,1,0:T(8,128)(2,1)S(1)} %broadcast_select_fusion.5), channel_id=1, source_target_pairs={{0,1},{1,0},{2,3},{3,2},{4,5},{5,4},{6,7},{7,6},{8,9},{9,8},{10,11... | collective-permute-start | bytes 3538952 | tf_op jit(solution)/shard_map/ppermute | solution.py:657
  201.3 10.3 %collective-permute-start.17 = (bf16[16,96,768]{2,1,0:T(8,128)(2,1)}, bf16[16,96,768]{2,1,0:T(8,128)(2,1)}, u32[]{:S(2)}, u32[]{:S(2)}) collective-permute-start(bf16[16,96,768]{2,1,0:T(8,128)(2,1)} %get-tuple-element.191), channel_id=1, source_target_pairs={{0,1},{1,0},{2,3},{3,2},{4,5},{5,4},{6,7},{7,6},{8,9},{9,8},{10,11... | collective-permute-start | bytes 7077896 | tf_op jit(solution)/shard_map/ppermute | solution.py:657
  201.7 14.7 %copy-start.2 = (bf16[16,96,768]{2,1,0:T(8,128)(2,1)S(1)}, bf16[16,96,768]{2,1,0:T(8,128)(2,1)}, u32[]{:S(2)}) copy-start(bf16[16,96,768]{2,1,0:T(8,128)(2,1)} %get-tuple-element.190) | copy-start | bytes 7077892
  211.4 4.9 %collective-permute-start.16 = (bf16[16,96,768]{2,1,0:T(8,128)(2,1)}, bf16[16,96,768]{2,1,0:T(8,128)(2,1)}, u32[]{:S(2)}, u32[]{:S(2)}) collective-permute-start(bf16[16,96,768]{2,1,0:T(8,128)(2,1)} %get-tuple-element.188), channel_id=1, source_target_pairs={{0,1},{1,0},{2,3},{3,2},{4,5},{5,4},{6,7},{7,6},{8,9},{9,8},{10,11... | collective-permute-start | bytes 7077896 | tf_op jit(solution)/shard_map/ppermute | solution.py:657
  216.3 4.3 copy-start.4
  219.0 6.3 %copy-start.3 = (bf16[16,96,768]{2,1,0:T(8,128)(2,1)S(1)}, bf16[16,96,768]{2,1,0:T(8,128)(2,1)}, u32[]{:S(2)}) copy-start(bf16[16,96,768]{2,1,0:T(8,128)(2,1)} %get-tuple-element.190) | copy-start | bytes 7077892
  219.0 31.5 %collective-permute-start.19 = (bf16[2,2,2,96,768]{4,3,2,1,0:T(8,128)(2,1)}, bf16[2,2,2,96,768]{4,3,2,1,0:T(8,128)(2,1)S(1)}, u32[]{:S(2)}, u32[]{:S(2)}) collective-permute-start(bf16[2,2,2,96,768]{4,3,2,1,0:T(8,128)(2,1)} %fusion.3), channel_id=1, source_target_pairs={{0,4},{1,5},{2,6},{3,7},{4,0},{5,1},{6,2},{7,3},{8,12},{9,13},{10,... | collective-permute-start | bytes 3538952 | tf_op jit(solution)/shard_map/ppermute | solution.py:657
  223.9 28.2 %collective-permute-start.18 = (bf16[2,2,2,96,768]{4,3,0,1,2:T(8,128)(2,1)}, bf16[2,2,2,96,768]{4,3,0,1,2:T(8,128)(2,1)}, u32[]{:S(2)}, u32[]{:S(2)}) collective-permute-start(bf16[2,2,2,96,768]{4,3,0,1,2:T(8,128)(2,1)} %get-tuple-element.307), channel_id=1, source_target_pairs={{0,2},{1,3},{2,0},{3,1},{4,6},{5,7},{6,4},{7,5},{8,10},{9,11},{10,... | collective-permute-start | bytes 3538952 | tf_op jit(solution)/shard_map/ppermute | solution.py:657
  250.5 6.0 %copy-start.6 = (bf16[2,2,2,96,768]{4,3,2,1,0:T(8,128)(2,1)}, bf16[2,2,2,96,768]{4,3,2,1,0:T(8,128)(2,1)S(1)}, u32[]{:S(2)}) copy-start(bf16[2,2,2,96,768]{4,3,2,1,0:T(8,128)(2,1)S(1)} %collective-permute-done.19) | copy-start | bytes 3538948
  252.1 28.5 %all-to-all-start.1 = ((bf16[32,16,768]{2,1,0:T(8,128)(2,1)}), bf16[32,16,768]{2,1,0:T(8,128)(2,1)}, u32[]{:S(2)}, u32[]{:S(2)}) async-start(bf16[32,16,768]{2,1,0:T(8,128)(2,1)} %bitcast.152), calls=%async_computation.1 | async-start | bytes 1572864 | tf_op jit(solution)/shard_map/all_to_all | solution.py:964
  255.5 204.1 %all-gather.7.cloned.1.call-start = ((), (), s32[]{:S(2)}) async-start(), calls=%async_computation.3 | async-start | bytes 8515584 | tf_op jit(solution)/shard_map/all_gather | solution.py:1017
  256.5 22.7 %collective-permute-start.21 = (bf16[2,2,96,768]{3,2,1,0:T(8,128)(2,1)}, bf16[2,2,96,768]{3,2,1,0:T(8,128)(2,1)}, u32[]{:S(2)}, u32[]{:S(2)}) collective-permute-start(bf16[2,2,96,768]{3,2,1,0:T(8,128)(2,1)} %fusion.15), channel_id=1, source_target_pairs={{0,2},{1,3},{2,0},{3,1},{4,6},{5,7},{6,4},{7,5},{8,10},{9,11},{10,... | collective-permute-start | bytes 1769480 | tf_op jit(solution)/shard_map/ppermute | solution.py:657
  258.1 3.9 copy-start.7
  260.5 20.1 %collective-permute-start.20 = (bf16[2,2,96,768]{3,2,0,1:T(8,128)(2,1)}, bf16[2,2,96,768]{3,2,0,1:T(8,128)(2,1)S(1)}, u32[]{:S(2)}, u32[]{:S(2)}) collective-permute-start(bf16[2,2,96,768]{3,2,0,1:T(8,128)(2,1)} %get-tuple-element.313), channel_id=1, source_target_pairs={{0,4},{1,5},{2,6},{3,7},{4,0},{5,1},{6,2},{7,3},{8,12},{9,13},{10,... | collective-permute-start | bytes 1769480 | tf_op jit(solution)/shard_map/ppermute | solution.py:657
  280.7 18.3 %collective-permute-start.23 = (bf16[16,48,768]{2,1,0:T(8,128)(2,1)}, bf16[16,48,768]{2,1,0:T(8,128)(2,1)}, u32[]{:S(2)}, u32[]{:S(2)}) collective-permute-start(bf16[16,48,768]{2,1,0:T(8,128)(2,1)} %get-tuple-element.232), channel_id=1, source_target_pairs={{0,1},{1,0},{2,3},{3,2},{4,5},{5,4},{6,7},{7,6},{8,9},{9,8},{10,11... | collective-permute-start | bytes 3538952 | tf_op jit(solution)/shard_map/ppermute | solution.py:657
  280.8 18.2 %collective-permute-start.24 = (bf16[16,48,768]{2,1,0:T(8,128)(2,1)}, bf16[16,48,768]{2,1,0:T(8,128)(2,1)}, u32[]{:S(2)}, u32[]{:S(2)}) collective-permute-start(bf16[16,48,768]{2,1,0:T(8,128)(2,1)} %get-tuple-element.234), channel_id=1, source_target_pairs={{0,1},{1,0},{2,3},{3,2},{4,5},{5,4},{6,7},{7,6},{8,9},{9,8},{10,11... | collective-permute-start | bytes 3538952 | tf_op jit(solution)/shard_map/ppermute | solution.py:657
  283.5 15.5 %collective-permute-start.22 = (bf16[2,192,768]{2,1,0:T(8,128)(2,1)}, bf16[2,192,768]{2,1,0:T(8,128)(2,1)S(1)}, u32[]{:S(2)}, u32[]{:S(2)}) collective-permute-start(bf16[2,192,768]{2,1,0:T(8,128)(2,1)} %fusion.16), channel_id=1, source_target_pairs={{0,8},{8,0},{16,24},{24,16},{1,9},{9,1},{17,25},{25,17},{2,10},{10... | collective-permute-start | bytes 1769480 | tf_op jit(solution)/shard_map/ppermute | solution.py:657
  299.0 3.8 copy-start.8
  299.0 24.4 %collective-permute-start.28 = (bf16[16,40,768]{2,1,0:T(8,128)(2,1)}, bf16[16,40,768]{2,1,0:T(8,128)(2,1)}, u32[]{:S(2)}, u32[]{:S(2)}) collective-permute-start(bf16[16,40,768]{2,1,0:T(8,128)(2,1)} %get-tuple-element.246), channel_id=1, source_target_pairs={{0,1},{1,0},{2,3},{3,2},{4,5},{5,4},{6,7},{7,6},{8,9},{9,8},{10,11... | collective-permute-start | bytes 2949128 | tf_op jit(solution)/shard_map/ppermute | solution.py:657
  302.1 21.3 %collective-permute-start.27 = (bf16[2,2,2,48,768]{4,3,0,1,2:T(8,128)(2,1)}, bf16[2,2,2,48,768]{4,3,0,1,2:T(8,128)(2,1)S(1)}, u32[]{:S(2)}, u32[]{:S(2)}) collective-permute-start(bf16[2,2,2,48,768]{4,3,0,1,2:T(8,128)(2,1)} %get-tuple-element.309), channel_id=1, source_target_pairs={{0,4},{1,5},{2,6},{3,7},{4,0},{5,1},{6,2},{7,3},{8,12},{9,13},{10,... | collective-permute-start | bytes 1769480 | tf_op jit(solution)/shard_map/ppermute | solution.py:657
  302.8 20.5 %collective-permute-start.29 = (bf16[16,32,768]{2,1,0:T(8,128)(2,1)}, bf16[16,32,768]{2,1,0:T(8,128)(2,1)}, u32[]{:S(2)}, u32[]{:S(2)}) collective-permute-start(bf16[16,32,768]{2,1,0:T(8,128)(2,1)} %get-tuple-element.248), channel_id=1, source_target_pairs={{0,1},{1,0},{2,3},{3,2},{4,5},{5,4},{6,7},{7,6},{8,9},{9,8},{10,11... | collective-permute-start | bytes 2359304 | tf_op jit(solution)/shard_map/ppermute | solution.py:657
  305.2 18.2 %collective-permute-start.26 = (bf16[2,2,2,48,768]{4,3,0,1,2:T(8,128)(2,1)}, bf16[2,2,2,48,768]{4,3,0,1,2:T(8,128)(2,1)}, u32[]{:S(2)}, u32[]{:S(2)}) collective-permute-start(bf16[2,2,2,48,768]{4,3,0,1,2:T(8,128)(2,1)} %get-tuple-element.311), channel_id=1, source_target_pairs={{0,2},{1,3},{2,0},{3,1},{4,6},{5,7},{6,4},{7,5},{8,10},{9,11},{10,... | collective-permute-start | bytes 1769480 | tf_op jit(solution)/shard_map/ppermute | solution.py:657
  305.7 18.4 %copy-start.10 = (bf16[16,32,768]{2,1,0:T(8,128)(2,1)S(1)}, bf16[16,32,768]{2,1,0:T(8,128)(2,1)}, u32[]{:S(2)}) copy-start(bf16[16,32,768]{2,1,0:T(8,128)(2,1)} %get-tuple-element.247) | copy-start | bytes 2359300
  306.9 16.4 %collective-permute-start.25 = (bf16[192,768]{1,0:T(8,128)(2,1)S(1)}, bf16[192,768]{1,0:T(8,128)(2,1)S(1)}, u32[]{:S(2)}, u32[]{:S(2)}) collective-permute-start(bf16[192,768]{1,0:T(8,128)(2,1)S(1)} %get-tuple-element.331), channel_id=1, source_target_pairs={{0,16},{8,24},{16,0},{24,8},{1,17},{9,25},{17,1},{25,9},{2,18},{10... | collective-permute-start | bytes 884744 | tf_op jit(solution)/shard_map/ppermute | solution.py:657
  323.5 15.6 %collective-permute-start.34 = (bf16[192,768]{1,0:T(8,128)(2,1)S(1)}, bf16[192,768]{1,0:T(8,128)(2,1)S(1)}, u32[]{:S(2)}, u32[]{:S(2)}) collective-permute-start(bf16[192,768]{1,0:T(8,128)(2,1)S(1)} %add_convert_fusion.18), channel_id=1, source_target_pairs={{0,16},{8,24},{16,0},{24,8},{1,17},{9,25},{17,1},{25,9},{2,18},{10... | collective-permute-start | bytes 884744 | tf_op jit(solution)/shard_map/ppermute | solution.py:657
  325.4 21.3 %collective-permute-start.33 = (bf16[2,2,2,32,768]{4,3,0,1,2:T(8,128)(2,1)S(1)}, bf16[2,2,2,32,768]{4,3,0,1,2:T(8,128)(2,1)S(1)}, u32[]{:S(2)}, u32[]{:S(2)}) collective-permute-start(bf16[2,2,2,32,768]{4,3,0,1,2:T(8,128)(2,1)S(1)} %get-tuple-element.321), channel_id=1, source_target_pairs={{0,4},{1,5},{2,6},{3,7},{4,0},{5,1},{6,2},{7,3},{8,12},{9,13},{10,... | collective-permute-start | bytes 1179656 | tf_op jit(solution)/shard_map/ppermute | solution.py:657
  327.9 18.7 %collective-permute-start.32 = (bf16[2,2,2,40,768]{4,3,0,1,2:T(8,128)(2,1)S(1)}, bf16[2,2,2,40,768]{4,3,0,1,2:T(8,128)(2,1)S(1)}, u32[]{:S(2)}, u32[]{:S(2)}) collective-permute-start(bf16[2,2,2,40,768]{4,3,0,1,2:T(8,128)(2,1)S(1)} %get-tuple-element.319), channel_id=1, source_target_pairs={{0,2},{1,3},{2,0},{3,1},{4,6},{5,7},{6,4},{7,5},{8,10},{9,11},{10,... | collective-permute-start | bytes 1474568 | tf_op jit(solution)/shard_map/ppermute | solution.py:657
  329.5 9.6 %copy-start.17 = (pred[2]{0:T(512)(128)(4,1)S(1)}, pred[2]{0:T(512)(128)(4,1)}, u32[]{:S(2)}) copy-start(pred[2]{0:T(512)(128)(4,1)} %copy-done.16) | copy-start | bytes 10
  329.5 17.1 %collective-permute-start.31 = (bf16[2,2,48,768]{3,2,0,1:T(8,128)(2,1)S(1)}, bf16[2,2,48,768]{3,2,0,1:T(8,128)(2,1)S(1)}, u32[]{:S(2)}, u32[]{:S(2)}) collective-permute-start(bf16[2,2,48,768]{3,2,0,1:T(8,128)(2,1)S(1)} %get-tuple-element.327), channel_id=1, source_target_pairs={{0,2},{1,3},{2,0},{3,1},{4,6},{5,7},{6,4},{7,5},{8,10},{9,11},{10,... | collective-permute-start | bytes 884744 | tf_op jit(solution)/shard_map/ppermute | solution.py:657
  331.4 15.2 %collective-permute-start.30 = (bf16[2,2,48,768]{3,2,0,1:T(8,128)(2,1)S(1)}, bf16[2,2,48,768]{3,2,0,1:T(8,128)(2,1)S(1)}, u32[]{:S(2)}, u32[]{:S(2)}) collective-permute-start(bf16[2,2,48,768]{3,2,0,1:T(8,128)(2,1)S(1)} %get-tuple-element.329), channel_id=1, source_target_pairs={{0,4},{1,5},{2,6},{3,7},{4,0},{5,1},{6,2},{7,3},{8,12},{9,13},{10,... | collective-permute-start | bytes 884744 | tf_op jit(solution)/shard_map/ppermute | solution.py:657
  346.8 10.0 %collective-permute-start.36 = (bf16[2,2,40,768]{3,2,0,1:T(8,128)(2,1)S(1)}, bf16[2,2,40,768]{3,2,0,1:T(8,128)(2,1)S(1)}, u32[]{:S(2)}, u32[]{:S(2)}) collective-permute-start(bf16[2,2,40,768]{3,2,0,1:T(8,128)(2,1)S(1)} %get-tuple-element.333), channel_id=1, source_target_pairs={{0,4},{1,5},{2,6},{3,7},{4,0},{5,1},{6,2},{7,3},{8,12},{9,13},{10,... | collective-permute-start | bytes 737288 | tf_op jit(solution)/shard_map/ppermute | solution.py:657
  348.0 8.7 %collective-permute-start.35 = (bf16[2,96,768]{2,1,0:T(8,128)(2,1)S(1)}, bf16[2,96,768]{2,1,0:T(8,128)(2,1)S(1)}, u32[]{:S(2)}, u32[]{:S(2)}) collective-permute-start(bf16[2,96,768]{2,1,0:T(8,128)(2,1)S(1)} %get-tuple-element.325), channel_id=1, source_target_pairs={{0,8},{8,0},{16,24},{24,16},{1,9},{9,1},{17,25},{25,17},{2,10},{10... | collective-permute-start | bytes 884744 | tf_op jit(solution)/shard_map/ppermute | solution.py:657
  351.0 5.7 %collective-permute-start.37 = (bf16[2,2,32,768]{3,2,0,1:T(8,128)(2,1)S(1)}, bf16[2,2,32,768]{3,2,0,1:T(8,128)(2,1)S(1)}, u32[]{:S(2)}, u32[]{:S(2)}) collective-permute-start(bf16[2,2,32,768]{3,2,0,1:T(8,128)(2,1)S(1)} %get-tuple-element.337), channel_id=1, source_target_pairs={{0,2},{1,3},{2,0},{3,1},{4,6},{5,7},{6,4},{7,5},{8,10},{9,11},{10,... | collective-permute-start | bytes 589832 | tf_op jit(solution)/shard_map/ppermute | solution.py:657
  357.0 11.3 %collective-permute-start.39 = (bf16[2,72,768]{2,1,0:T(8,128)(2,1)S(1)}, bf16[2,72,768]{2,1,0:T(8,128)(2,1)S(1)}, u32[]{:S(2)}, u32[]{:S(2)}) collective-permute-start(bf16[2,72,768]{2,1,0:T(8,128)(2,1)S(1)} %get-tuple-element.335), channel_id=1, source_target_pairs={{0,8},{8,0},{16,24},{24,16},{1,9},{9,1},{17,25},{25,17},{2,10},{10... | collective-permute-start | bytes 663560 | tf_op jit(solution)/shard_map/ppermute | solution.py:657
  358.3 10.0 %collective-permute-start.38 = (bf16[96,768]{1,0:T(8,128)(2,1)S(1)}, bf16[96,768]{1,0:T(8,128)(2,1)S(1)}, u32[]{:S(2)}, u32[]{:S(2)}) collective-permute-start(bf16[96,768]{1,0:T(8,128)(2,1)S(1)} %get-tuple-element.339), channel_id=1, source_target_pairs={{0,16},{8,24},{16,0},{24,8},{1,17},{9,25},{17,1},{25,9},{2,18},{10... | collective-permute-start | bytes 442376 | tf_op jit(solution)/shard_map/ppermute | solution.py:657
  368.3 5.8 %collective-permute-start.40 = (bf16[72,768]{1,0:T(8,128)(2,1)S(1)}, bf16[72,768]{1,0:T(8,128)(2,1)S(1)}, u32[]{:S(2)}, u32[]{:S(2)}) collective-permute-start(bf16[72,768]{1,0:T(8,128)(2,1)S(1)} %get-tuple-element.343), channel_id=1, source_target_pairs={{0,16},{8,24},{16,0},{24,8},{1,17},{9,25},{17,1},{25,9},{2,18},{10... | collective-permute-start | bytes 331784 | tf_op jit(solution)/shard_map/ppermute | solution.py:657
  375.0 10.8 %collective-permute-start.41 = (bf16[2,192,768]{2,1,0:T(8,128)(2,1)S(1)}, bf16[2,192,768]{2,1,0:T(8,128)(2,1)S(1)}, u32[]{:S(2)}, u32[]{:S(2)}) collective-permute-start(bf16[2,192,768]{2,1,0:T(8,128)(2,1)S(1)} %broadcast_select_fusion.9), channel_id=1, source_target_pairs={{0,8},{8,0},{16,24},{24,16},{1,9},{9,1},{17,25},{25,17},{2,10},{10... | collective-permute-start | bytes 1769480 | tf_op jit(solution)/shard_map/ppermute | solution.py:657
  386.0 12.5 %collective-permute-start.43 = (bf16[2,2,96,768]{3,2,1,0:T(8,128)(2,1)S(1)}, bf16[2,2,96,768]{3,2,1,0:T(8,128)(2,1)S(1)}, u32[]{:S(2)}, u32[]{:S(2)}) collective-permute-start(bf16[2,2,96,768]{3,2,1,0:T(8,128)(2,1)S(1)} %get-tuple-element.323), channel_id=1, source_target_pairs={{0,2},{1,3},{2,0},{3,1},{4,6},{5,7},{6,4},{7,5},{8,10},{9,11},{10,... | collective-permute-start | bytes 1769480 | tf_op jit(solution)/shard_map/ppermute | solution.py:657
  389.4 15.1 %collective-permute-start.42 = (bf16[2,2,96,768]{3,2,1,0:T(8,128)(2,1)S(1)}, bf16[2,2,96,768]{3,2,1,0:T(8,128)(2,1)S(1)}, u32[]{:S(2)}, u32[]{:S(2)}) collective-permute-start(bf16[2,2,96,768]{3,2,1,0:T(8,128)(2,1)S(1)} %get-tuple-element.324), channel_id=1, source_target_pairs={{0,4},{1,5},{2,6},{3,7},{4,0},{5,1},{6,2},{7,3},{8,12},{9,13},{10,... | collective-permute-start | bytes 1769480 | tf_op jit(solution)/shard_map/ppermute | solution.py:657
  404.6 23.6 %collective-permute-start.45 = (bf16[2,2,2,96,768]{4,3,2,1,0:T(8,128)(2,1)S(1)}, bf16[2,2,2,96,768]{4,3,2,1,0:T(8,128)(2,1)S(1)}, u32[]{:S(2)}, u32[]{:S(2)}) collective-permute-start(bf16[2,2,2,96,768]{4,3,2,1,0:T(8,128)(2,1)S(1)} %broadcast_select_fusion.2), channel_id=1, source_target_pairs={{0,4},{1,5},{2,6},{3,7},{4,0},{5,1},{6,2},{7,3},{8,12},{9,13},{10,... | collective-permute-start | bytes 3538952 | tf_op jit(solution)/shard_map/ppermute | solution.py:657
  407.2 23.0 %collective-permute-start.44 = (bf16[2,2,2,96,768]{4,3,2,1,0:T(8,128)(2,1)S(1)}, bf16[2,2,2,96,768]{4,3,2,1,0:T(8,128)(2,1)S(1)}, u32[]{:S(2)}, u32[]{:S(2)}) collective-permute-start(bf16[2,2,2,96,768]{4,3,2,1,0:T(8,128)(2,1)S(1)} %broadcast_select_fusion.4), channel_id=1, source_target_pairs={{0,2},{1,3},{2,0},{3,1},{4,6},{5,7},{6,4},{7,5},{8,10},{9,11},{10,... | collective-permute-start | bytes 3538952 | tf_op jit(solution)/shard_map/ppermute | solution.py:657
  428.5 3.3 copy-start.11
  428.6 3.3 copy-start.14
  430.5 9.0 %collective-permute-start.47 = (bf16[2,2,2,2,96,768]{5,4,3,2,1,0:T(8,128)(2,1)S(1)}, bf16[2,2,2,2,96,768]{5,4,3,2,1,0:T(8,128)(2,1)S(1)}, u32[]{:S(2)}, u32[]{:S(2)}) collective-permute-start(bf16[2,2,2,2,96,768]{5,4,3,2,1,0:T(8,128)(2,1)S(1)} %broadcast_select_fusion.1), channel_id=1, source_target_pairs={{0,1},{1,0},{2,3},{3,2},{4,5},{5,4},{6,7},{7,6},{8,9},{9,8},{10,11... | collective-permute-start | bytes 7077896 | tf_op jit(solution)/shard_map/ppermute | solution.py:657
  430.6 16.8 %collective-permute-start.46 = (bf16[2,2,2,2,96,768]{5,4,3,2,1,0:T(8,128)(2,1)S(1)}, bf16[2,2,2,2,96,768]{5,4,3,2,1,0:T(8,128)(2,1)}, u32[]{:S(2)}, u32[]{:S(2)}) collective-permute-start(bf16[2,2,2,2,96,768]{5,4,3,2,1,0:T(8,128)(2,1)S(1)} %broadcast_select_fusion), channel_id=1, source_target_pairs={{0,1},{1,0},{2,3},{3,2},{4,5},{5,4},{6,7},{7,6},{8,9},{9,8},{10,11... | collective-permute-start | bytes 7077896 | tf_op jit(solution)/shard_map/ppermute | solution.py:657
  (6 other events, 13.8 us)
Sparse Core Ops, SparseCore 0:
  16.7 108.1 all-gather.4
  375.1 84.4 all-gather.6

commit v4 on v3

--- a/solution.py
+++ b/solution.py
@@ -81,9 +81,20 @@
 
 
 def image_encode(
-    pad, sent, x_ref, box_ref, wi_ref, wb_ref, bi_ref, gr_ref, betar_ref, pre_ref, enc_ref
+    pad, sent, core_ref,
+    x_ref, box_ref, wb_ref, bi_ref, gr_ref, betar_ref, *refs,
 ):
-    pre = nn(x_ref[...], wi_ref[...]) + tn(box_ref[...], wb_ref[...]) + bi_ref[...]
+    *halves, pre_ref, enc_ref, wi_ref = refs
+    core = core_ref[0]
+    at = 0
+    for own_ref, came_ref in zip(halves[::2], halves[1::2]):
+        pairs, rows, _ = own_ref.shape
+        for i in range(pairs):
+            wi_ref[2 * i + core, at : at + rows, :] = own_ref[i]
+            wi_ref[2 * i + 1 - core, at : at + rows, :] = came_ref[i]
+        at += rows
+    weight = wi_ref[...].reshape(x_ref.shape[1], wi_ref.shape[2])
+    pre = nn(x_ref[...], weight) + tn(box_ref[...], wb_ref[...]) + bi_ref[...]
     pre_ref[...] = pre
     normed, _ = norm_parts(pre)
     encoded = (normed * gr_ref[...] + betar_ref[...]).astype(bf16)
@@ -337,19 +348,29 @@
     return pl.CostEstimate(flops=int(flops), bytes_accessed=int(moved), transcendentals=int(exps))
 
 
-def run_image_encode(geometry, x, boxes, wi, wb, bi, gr, betar):
+def run_image_encode(geometry, core, x, boxes, halves, wb, bi, gr, betar):
     pad, sent, devices = geometry
     rows, feat = x.shape
-    d = wi.shape[1]
-    operands = (x, boxes, wi, wb, bi, gr, betar)
-    shapes = [jax.ShapeDtypeStruct((rows, d), f32), jax.ShapeDtypeStruct((pad * devices, d), bf16)]
+    d = wb.shape[1]
+    operands = (x, boxes, wb, bi, gr, betar, *halves)
+    shapes = [
+        jax.ShapeDtypeStruct((rows, d), f32),
+        jax.ShapeDtypeStruct((pad * devices, d), bf16),
+        jax.ShapeDtypeStruct((devices, feat // devices, d), bf16),
+    ]
     return pl.pallas_call(
         functools.partial(image_encode, pad, sent),
         out_shape=shapes,
+        grid_spec=pltpu.PrefetchScalarGridSpec(
+            num_scalar_prefetch=1,
+            grid=(1,),
+            in_specs=[whole(t.shape) for t in operands],
+            out_specs=[whole(t.shape) for t in shapes],
+        ),
         compiler_params=pltpu.CompilerParams(vmem_limit_bytes=LIMIT),
-        cost_estimate=cost(2 * rows * d * feat, x.size * 2 + wi.size * 2 + rows * d * 6),
+        cost_estimate=cost(2 * rows * d * feat, x.size * 2 + feat * d * 4 + rows * d * 6),
         name="image_encode",
-    )(*operands)
+    )(core, *operands)
 
 
 def run_attention_forward(
@@ -460,34 +481,69 @@
     )(core, *halves)
 
 
-def widen_rest_kernel(attn_rows, img_rows, parts_ref, *outs):
-    *squares, img_ref, small_ref = outs
-    devices = parts_ref.shape[0]
-    width = img_ref.shape[1]
-    per = width // attn_rows
-    feat = img_ref.shape[0]
-    for j, out_ref in enumerate(squares):
+def widen_rest_kernel(
+    attn_rows, feat, picks, parts_ref, *refs
+):
+    squares, refs = refs[:4], refs[4:]
+    img_ref, box_ref, refs = refs[0], refs[1], refs[2:]
+    vectors, long_ref, refs = refs[: len(picks)], refs[len(picks)], refs[len(picks) + 1 :]
+    in_buf, square_buf, img_buf, in_sem, out_sem = refs
+    devices, rows, width = in_buf.shape
+    img_rows = rows - attn_rows
+    per = devices // 4
+    loads = [
+        pltpu.make_async_copy(
+            parts_ref.at[j * per : (j + 1) * per], in_buf.at[j * per : (j + 1) * per], in_sem.at[j]
+        )
+        for j in range(4)
+    ]
+    for copy in loads:
+        copy.start()
+    stores = []
+
+    def store(source, target):
+        copy = pltpu.make_async_copy(source, target, out_sem.at[len(stores)])
+        copy.start()
+        stores.append(copy)
+
+    for j in range(4):
+        loads[j].wait()
         for i in range(per):
-            value = parts_ref[j * per + i, :attn_rows, :]
-            out_ref[i * attn_rows : (i + 1) * attn_rows, :] = value.astype(f32)
-    for i in range(devices):
-        value = parts_ref[i, attn_rows:, :].astype(f32)
-        at = i * img_rows
-        inside = min(max(feat - at, 0), img_rows)
-        if inside:
-            img_ref[at : at + inside, :] = value[:inside]
-        last = min(feat + small_ref.shape[0] - at, img_rows)
-        if last > inside:
-            first = at + inside - feat
-            small_ref[first : first + last - inside, :] = value[inside:last]
-
-
-def widen_rest(parts, attn_rows, feat, small_rows):
+            value = in_buf[j * per + i, :attn_rows, :].astype(f32)
+            square_buf[j, i * attn_rows : (i + 1) * attn_rows, :] = value
+        store(square_buf.at[j], squares[j])
+        for i in range(j * per, (j + 1) * per):
+            value = in_buf[i, attn_rows:, :].astype(f32)
+            img_buf[i * img_rows : (i + 1) * img_rows, :] = value
+        first, last = [min(t * per * img_rows, feat) for t in (j, j + 1)]
+        if last > first:
+            store(img_buf.at[first:last], img_ref.at[first:last])
+    box_ref[...] = img_buf[feat : feat + box_ref.shape[0], :]
+    for pick, ref in zip(picks, vectors):
+        ref[...] = img_buf[feat + pick, :]
+    for i in range(long_ref.shape[0] // width):
+        long_ref[i * width : (i + 1) * width] = img_buf[feat + 32 + i, :]
+    for copy in stores:
+        copy.wait()
+
+
+def widen_rest(parts, attn_rows, feat, boxes, long, picks):
     devices, rows, width = parts.shape
-    shapes = [(width, width)] * 4 + [(feat, width), (small_rows, width)]
+    shapes = [(width, width)] * 4 + [(feat, width), (boxes, width)]
+    shapes += [(width,)] * len(picks) + [(long,)]
     return pl.pallas_call(
-        functools.partial(widen_rest_kernel, attn_rows, rows - attn_rows),
+        functools.partial(widen_rest_kernel, attn_rows, feat, picks),
         out_shape=[jax.ShapeDtypeStruct(t, f32) for t in shapes],
+        in_specs=[pl.BlockSpec(memory_space=pl.ANY)],
+        out_specs=[pl.BlockSpec(memory_space=pl.ANY)] * 5
+        + [pl.BlockSpec(memory_space=pltpu.VMEM)] * (len(picks) + 2),
+        scratch_shapes=[
+            pltpu.VMEM((devices, rows, width), bf16),
+            pltpu.VMEM((4, width, width), f32),
+            pltpu.VMEM((devices * (rows - attn_rows), width), f32),
+            pltpu.SemaphoreType.DMA((4,)),
+            pltpu.SemaphoreType.DMA((8,)),
+        ],
         compiler_params=pltpu.CompilerParams(vmem_limit_bytes=LIMIT),
         cost_estimate=cost(0, parts.size * 6),
         name="widen_rest",
@@ -743,6 +799,13 @@
     return values
 
 
+def in_turn(*movers):
+    sent = []
+    for mover in movers:
+        fence([mover], sent)
+        sent = mover.stage()
+
+
 class Sum:
     def __init__(self, parts, orders):
         far = len(axis_bits("enc"))
@@ -759,18 +822,16 @@
             mover.value = value
 
     def stage(self):
-        if self.steps:
-            self.steps.pop(0)()
+        return self.steps.pop(0)() if self.steps else []
 
     def run(self):
-        for mover in self.movers:
-            mover.stage()
+        return [mover.stage() for mover in self.movers]
 
     def merge(self):
         first = self.movers[0]
         first.value = tuple(jnp.concatenate(t, -2) for t in zip(*[m.value for m in self.movers]))
         self.movers = [first]
-        self.run()
+        return self.run()
 
     def total(self):
         return self.movers[0].total()
@@ -821,12 +882,12 @@
     img = Gather(w_img, far)
     attn = Gather(jnp.concatenate([w_query, w_key, w_value, w_out], 0), far)
     img.stage()
-    (ff_shard,) = fence([img, attn], ff_shard)
-    ff_weights = lax.all_gather(ff_shard, axes, axis=0)
+    fence([img, attn])
     while img.order:
         img.stage()
         attn.stage()
-        fence([img, attn])
+        (ff_shard,) = fence([img, attn], ff_shard)
+    ff_weights = lax.all_gather(ff_shard, axes, axis=0)
     img = img.split(w_img.shape[0] // 2, orders)
     attn.stage()
     for _ in range(middle):
@@ -834,9 +895,9 @@
             part.stage()
         fence([*img, attn])
     attn = attn.split(2 * cut, orders)
-    for part in (*img, *attn):
+    img_halves = [t for part in img for t in part.halves()]
+    for part in attn:
         part.stage()
-    img_full = jnp.concatenate([t.rows() for t in img], 1).reshape(-1, model_width)
     device_count = lax.axis_size(axes)
     seq_count = caption_count.shape[0]
     sent_rows, feat = region_feats.shape
@@ -845,9 +906,10 @@
     pad = 1 << (pad - 1).bit_length()
     box_count = boxes.shape[0]
     geometry = (pad, per_peer, device_count)
-    pre_norm, encoded = run_image_encode(
-        geometry, region_feats, boxes, img_full, w_box, b_img, g_reg, beta_reg
-    )
+    pre_norm, encoded, img_full = run_image_encode(
+        geometry, core, region_feats, boxes, img_halves, w_box, b_img, g_reg, beta_reg
+    )
+    img_full = img_full.reshape(feat, model_width)
     (encoded,) = fence(attn, encoded)
     received = lax.all_to_all(encoded, axes, split_axis=0, concat_axis=0, tiled=True)
     for _ in range(middle - 1):
@@ -942,8 +1004,8 @@
     )
     ff = Sum([down, up], orders)
     ff.stage()
-    (grad_context,) = fence([ff], grad_context)
-    ff.stage()
+    sent = ff.stage()
+    grad_context, _ = fence([], grad_context, sent)
     grad_query, grad_keys, grad_values, grad_text, grad_slots, attn_sums = run_attention_backward(
         geometry,
         region_count,
@@ -962,7 +1024,6 @@
         [ff], grad_query, grad_keys, grad_values, grad_slots, attn_sums
     )
     back = lax.all_to_all(grad_slots, axes, split_axis=0, concat_axis=0, tiled=True)
-    ff.stage()
     attn_parts = weight_grads(
         core,
         device_count,
@@ -978,11 +1039,7 @@
     )
     attn = Sum(attn_parts, orders)
     (back,) = fence([ff, attn], back)
-    while len(ff.steps) > len(far):
-        ff.stage()
-        fence([ff])
-    ff.stage()
-    attn.stage()
+    in_turn(ff, attn)
     small_rows = 40
     chunk = 8 * (-(-(feat + small_rows) // (8 * device_count)))
     grad_pre, grad_feats, img_parts = run_image_backward(
@@ -1002,17 +1059,12 @@
     img = Sum(img_parts, orders)
     fence([ff, attn, img])
     while ff.steps:
-        ff.stage()
-        if not ff.steps:
-            attn.stage()
-            img.stage()
+        in_turn(ff, attn, img)
         fence([ff, attn, img])
+    while img.steps:
+        in_turn(attn, img)
+        fence([attn, img])
     ff = Gather(ff.total(), far)
-    ff.stage()
-    while img.steps:
-        attn.stage()
-        img.stage()
-        fence([attn, img, ff])
     rest = jnp.concatenate([attn.total(), img.total()], 0)
     rest_all = lax.all_gather(rest, axes, axis=0)
     fence([ff], rest)
@@ -1030,16 +1082,33 @@
     )
     grad_w_up = join_blocks(core, up_halves, (model_width, ff_blocks * model_width), (0, 1))
     grad_boxes = jnp.einsum("cd,rd->cr", w_box, grad_pre, preferred_element_type=f32).astype(bf16)
-    grad_w_query, grad_w_key, grad_w_value, grad_w_out, grad_w_img, small = widen_rest(
-        rest_all, 4 * cut, feat, small_rows
-    )
-    grad_w_box = small[:box_count]
-    grad_b_img, grad_g_reg, grad_beta_reg = [small[8 + i] for i in range(3)]
-    grad_g_two, grad_beta_two, grad_b_down, grad_g_one, grad_beta_one, grad_b_out = [
-        small[16 + i] for i in range(6)
-    ]
-    grad_b_query, grad_b_value = small[24], small[25]
-    grad_b_up = small[32 : 32 + ff_blocks].reshape(-1)
+    (
+        grad_w_query,
+        grad_w_key,
+        grad_w_value,
+        grad_w_out,
+        grad_w_img,
+        grad_w_box,
+        grad_b_img,
+        grad_g_reg,
+        grad_beta_reg,
+        grad_g_two,
+        grad_beta_two,
+        grad_b_down,
+        grad_g_one,
+        grad_beta_one,
+        grad_b_out,
+        grad_b_query,
+        grad_b_value,
+        grad_b_up,
+    ) = widen_rest(
+        rest_all,
+        4 * cut,
+        feat,
+        box_count,
+        b_up.shape[0],
+        (8, 9, 10, 16, 17, 18, 19, 20, 21, 24, 25),
+    )
     return (
         output,
         grad_text,

time: 488 us -> 511 us (1.047)
  waiting for transfers between devices: 200 us -> 227 us
    ppermute x48, waiting for transfers between devices: 190 us -> 218 us  [swap_bit(): return lax.ppermute(tensor, name, [(i, i ^ step) for i in range(size)])]
    all_to_all x1, waiting for transfers between devices: 0.01 us -> 9.33 us  [body(): lax.all_to_all(grad_slots, axes, split_axis=0, concat_axis=0, tiled=True)]
    ppermute x48, starting transfers between devices: 54.7 us -> 47.3 us  [swap_bit(): return lax.ppermute(tensor, name, [(i, i ^ step) for i in range(size)])]
    all_gather x1, waiting for transfers between devices: 5.54 us -> 0.01 us  [body(): rest_all = lax.all_gather(rest, axes, axis=0)]
    convert_element_type x24 -> x25, other arithmetic: 23.7 us -> 22.4 us  [add_low(): return (kept.astype(f32) + came.astype(f32)).astype(bf16)]
  transfers between devices with their start and end apart: 52 -> 52, of which waited for: 31 -> 37; matrix products, arithmetic and copies ran while one was open for 8% -> 4% of each run, Pallas kernels for 20% -> 19%
where the time goes in v4:
time: 511 us; the launch traced here: 502 us
  waiting for transfers between devices  227 us (44%)
  Pallas kernels  156 us (31%)
  starting transfers between devices  57.8 us (11%)
  other arithmetic  32.1 us (6%)
  between operations  15.8 us (3%)
  local copies, waits for them, and re-layouts  12.7 us (2%)
    ppermute x48, waiting for transfers between devices, swap_bit(): return lax.ppermute(tensor, name, [(i, i ^ step) for i in range(size)])  218 us
    ppermute x48, starting transfers between devices, swap_bit(): return lax.ppermute(tensor, name, [(i, i ^ step) for i in range(size)])  47.3 us
    pallas_call x1, Pallas kernels, run_feed_forward(): pl.pallas_call(feed_forward, out_shape=shapes, grid_spec=pltpu.PrefetchSc...  41.7 us
    pallas_call x3, Pallas kernels, weight_grads(): pl.pallas_call(functools.partial(weight_grad_kernel, lhs_of, rhs_of, grou...  30.2 us
    pallas_call x1, Pallas kernels, run_attention_backward(): pl.pallas_call(functools.partial(attention_backward, *geometry), out_shap...  23.6 us
    convert_element_type x25, other arithmetic, add_low(): return (kept.astype(f32) + came.astype(f32)).astype(bf16)  22.4 us
    pallas_call x1, Pallas kernels, run_attention_forward(): pl.pallas_call(functools.partial(attention_forward, *geometry), out_shape...  21.7 us
    pallas_call x2, Pallas kernels, join_blocks(): pl.pallas_call(join_kernel, out_shape=jax.ShapeDtypeStruct(shape, f32), g...  13.1 us
  transfers between devices with their start and end apart: 52, of which 37 were waited for; matrix products, arithmetic and copies ran while one was open for 4% of the time, Pallas kernels for 19%

profile of v4, /device:TPU:0, one launch (start us, length us, event | category | flops | bytes accessed | tf_op | source)
XLA Modules:
  0.0 502.2 jit_solution(10291334337007894828)
XLA Ops:
  7.2 4.1 collective-permute-start
  12.2 4.3 collective-permute-done
  19.1 1.6 pad_maximum_fusion
  20.7 3.5 collective-permute-start.1
  24.2 2.6 collective-permute-done.2
  26.9 3.6 collective-permute-done.1
  30.6 1.6 collective-permute-start.4
  32.6 1.5 collective-permute-start.3
  34.1 3.0 collective-permute-done.4
  38.6 1.9 collective-permute-done.5
  40.7 1.6 collective-permute-start.7
  42.8 9.4 %collective-permute-done.7 = bf16[2,2,2,32,768]{4,3,2,1,0:T(8,128)(2,1)S(1)} collective-permute-done((bf16[2,2,2,32,768]{4,3,2,1,0:T(8,128)(2,1)S(1)}, bf16[2,2,2,32,768]{4,3,2,1,0:T(8,128)(2,1)S(1)}, u32[]{:S(2)}, u32[]{:S(2)}) %collective-permute-start.7) | collective-permute-done | bytes 393248 | tf_op jit(solution)/shard_map/ppermute | solution.py:713
  53.7 1.4 collective-permute-start.8
  55.2 5.8 %collective-permute-done.9 = bf16[2,2,48,768]{3,2,1,0:T(8,128)(2,1)S(1)} collective-permute-done((bf16[2,2,48,768]{3,2,1,0:T(8,128)(2,1)S(1)}, bf16[2,2,48,768]{3,2,1,0:T(8,128)(2,1)S(1)}, u32[]{:S(2)}, u32[]{:S(2)}) %collective-permute-start.9) | collective-permute-done | bytes 294944 | tf_op jit(solution)/shard_map/ppermute | solution.py:713
  61.1 4.4 collective-permute-done.8
  65.6 7.8 %image_encode.1 = (f32[416,768]{1,0:T(8,128)}, bf16[512,768]{1,0:T(8,128)(2,1)}, bf16[32,64,768]{2,1,0:T(8,128)(2,1)}) custom-call(s32[1]{0:T(128)} %bitcast.2.core_ref, bf16[416,2048]{1,0:T(8,128)(2,1)} %x_ref.3, bf16[4,416]{1,0:T(4,128)(2,1)} %box_ref.3, bf16[4,768]{1,0:T(4,128)(2,1)} %wb_ref.1, f32[768]{0:T(1024)} %bi_ref.1, f32[768]{0:T(1024)} %gr_ref.3, ...), custom_call_target="tpu_custom_call" | custom-call | flops 1308622848 | bytes 9912320 | tf_op jit(solution)/shard_map/image_encode/pallas_call | solution.py:361
  73.3 5.8 %all-to-all-start = ((bf16[32,16,768]{2,1,0:T(8,128)(2,1)}), bf16[32,16,768]{2,1,0:T(8,128)(2,1)}, u32[]{:S(2)}, u32[]{:S(2)}) async-start(bf16[32,16,768]{2,1,0:T(8,128)(2,1)} %bitcast.152), calls=%async_computation | async-start | bytes 1572864 | tf_op jit(solution)/shard_map/all_to_all | solution.py:914
  79.2 1.8 collective-permute-start.13
  80.9 1.5 collective-permute-start.12
  82.4 33.5 %collective-permute-done.13 = bf16[2,2,2,48,768]{4,3,2,1,0:T(8,128)(2,1)S(1)} collective-permute-done((bf16[2,2,2,48,768]{4,3,2,1,0:T(8,128)(2,1)S(1)}, bf16[2,2,2,48,768]{4,3,2,1,0:T(8,128)(2,1)S(1)}, u32[]{:S(2)}, u32[]{:S(2)}) %collective-permute-start.13) | collective-permute-done | bytes 589856 | tf_op jit(solution)/shard_map/ppermute | solution.py:713
  118.5 2.5 collective-permute-done.14
  121.9 1.7 bitcast_select_fusion
  123.6 2.2 fusion.39
  125.8 21.7 %attention_forward.1 = (bf16[1024,768]{1,0:T(8,128)(2,1)}, bf16[1024,768]{1,0:T(8,128)(2,1)}, bf16[1024,768]{1,0:T(8,128)(2,1)}, bf16[1024,768]{1,0:T(8,128)(2,1...) custom-call(s32[4]{0:T(128)} %captions.3, ...), custom_call_target="tpu_custom_call" | custom-call | flops 8053063680 | bytes 20447232 | tf_op jit(solution)/shard_map/attention_forward/pallas_call | solution.py:395
  147.5 41.7 %feed_forward.1 = (bf16[1024,768]{1,0:T(8,128)(2,1)}, bf16[1024,3072]{1,0:T(8,128)(2,1)}, bf16[1024,768]{1,0:T(8,128)(2,1)}, bf16[1024,3072]{1,0:T(8,128)(2,1)},...) custom-call(s32[4]{0:T(128)} %captions.3, ...), custom_call_target="tpu_custom_call" | custom-call | flops 20535312384 | bytes 36175872 | tf_op jit(solution)/shard_map/feed_forward/pallas_call | solution.py:590
  189.3 9.4 %grad_w_down.1 = (bf16[16,96,768]{2,1,0:T(8,128)(2,1)}, bf16[16,96,768]{2,1,0:T(8,128)(2,1)}) custom-call(s32[1]{0:T(128)} %bitcast.2.core_ref, bf16[1024,3072]{1,0:T(8,128)(2,1)} %get-tuple-element.243.refs_0_, bf16[1024,768]{1,0:T(8,128)(2,1)} %get-tuple-element.244.refs_1_), custom_call_target="tpu_custom_call" | custom-call | flops 4831838208 | bytes 11010048 | tf_op jit(solution)/shard_map/grad_w_down/pallas_call | solution.py:673
  198.8 9.6 %grad_w_up.1 = (bf16[16,96,768]{2,1,0:T(8,128)(2,1)}, bf16[16,96,768]{2,1,0:T(8,128)(2,1)}) custom-call(s32[1]{0:T(128)} %bitcast.2.core_ref, bf16[1024,768]{1,0:T(8,128)(2,1)} %get-tuple-element.234.n_ref.refs_0_, bf16[1024,3072]{1,0:T(8,128)(2,1)} %get-tuple-element.247.refs_1_), custom_call_target="tpu_custom_call" | custom-call | flops 4831838208 | bytes 11010048 | tf_op jit(solution)/shard_map/grad_w_up/pallas_call | solution.py:673
  208.8 1.8 constant_dynamic-slice_fusion.1
  210.8 2.5 collective-permute-done.17
  213.3 1.6 fusion.3
  214.9 2.6 fusion.1
  217.5 1.5 collective-permute-start.19
  220.3 23.6 %attention_backward.1 = (bf16[1024,768]{1,0:T(8,128)(2,1)}, bf16[1024,768]{1,0:T(8,128)(2,1)}, bf16[1024,768]{1,0:T(8,128)(2,1)}, bf16[512,768]{1,0:T(8,128)(2,1...) custom-call(s32[4]{0:T(128)} %counts.5, s32[1]{0:T(128)S(6)} %copy.125.offset, ...), custom_call_target="tpu_custom_call" | custom-call | flops 10066329600 | bytes 22020096 | tf_op jit(solution)/shard_map/attention_backward/pallas_call | solution.py:622
  243.9 2.2 collective-permute-done.19
  247.4 4.6 all-to-all-start.1
  252.1 11.2 %grad_w_attn.1 = (bf16[16,48,768]{2,1,0:T(8,128)(2,1)}, bf16[16,48,768]{2,1,0:T(8,128)(2,1)}, bf16[16,48,768]{2,1,0:T(8,128)(2,1)}, bf16[16,48,768]{2,1,0:T(8,128)(2,1)}) custom-call(s32[1]{0:T(128)} %bitcast.2.core_ref, bf16[1024,768]{1,0:T(8,128)(2,1)} %get-tuple-element.264.refs_0_, bf16[1024,768]{1,0:T(8,128)(2,1)} %get-tuple-element.265.refs_1_, ...), custom_call_target="tpu_custom_call" | custom-call | flops 4831838208 | bytes 11010048 | tf_op jit(solution)/shard_map/grad_w_attn/pallas_call | solution.py:673
  263.4 9.3 %all-to-all-done.1 = bf16[32,16,768]{2,1,0:T(8,128)(2,1)S(1)} async-done(((bf16[32,16,768]{2,1,0:T(8,128)(2,1)}), bf16[32,16,768]{2,1,0:T(8,128)(2,1)S(1)}, u32[]{:S(2)}, u32[]{:S(2)}) %all-to-all-start.1) | async-done | bytes 786464 | tf_op jit(solution)/shard_map/all_to_all | solution.py:1026
  273.6 2.0 fusion.15
  275.6 2.3 fusion.8
  278.4 1.5 collective-permute-start.21
  279.9 1.5 collective-permute-start.20
  281.9 1.4 reduce.3
  283.9 9.4 %image_backward.1 = (bf16[416,768]{1,0:T(8,128)(2,1)}, bf16[416,2048]{1,0:T(8,128)(2,1)}, bf16[16,40,768]{2,1,0:T(8,128)(2,1)}, bf16[16,32,768]{2,1,0:T(8,128)(2...) custom-call(s32[1]{0:T(128)} %bitcast.2.core_ref, bf16[416,2048]{1,0:T(8,128)(2,1)} %x_ref.3, ...), custom_call_target="tpu_custom_call" | custom-call | flops 2617245696 | bytes 10092544 | tf_op jit(solution)/shard_map/image_backward/pallas_call | solution.py:428
  299.1 2.5 fusion.14
  306.2 12.7 %collective-permute-done.26 = bf16[2,2,2,48,768]{4,3,0,1,2:T(8,128)(2,1)} collective-permute-done((bf16[2,2,2,48,768]{4,3,0,1,2:T(8,128)(2,1)}, bf16[2,2,2,48,768]{4,3,0,1,2:T(8,128)(2,1)}, u32[]{:S(2)}, u32[]{:S(2)}) %collective-permute-start.26) | collective-permute-done | bytes 589856 | tf_op jit(solution)/shard_map/ppermute | solution.py:713
  324.0 1.5 fusion.18
  325.5 1.5 collective-permute-start.32
  329.5 1.5 collective-permute-start.30
  331.5 12.1 %collective-permute-done.31 = bf16[2,2,48,768]{3,2,0,1:T(8,128)(2,1)S(1)} collective-permute-done((bf16[2,2,48,768]{3,2,0,1:T(8,128)(2,1)S(1)}, bf16[2,2,48,768]{3,2,0,1:T(8,128)(2,1)S(1)}, u32[]{:S(2)}, u32[]{:S(2)}) %collective-permute-start.31) | collective-permute-done | bytes 294944 | tf_op jit(solution)/shard_map/ppermute | solution.py:713
  347.4 4.5 collective-permute-done.36
  355.9 5.8 %collective-permute-done.37 = bf16[96,768]{1,0:T(8,128)(2,1)S(1)} collective-permute-done((bf16[96,768]{1,0:T(8,128)(2,1)S(1)}, bf16[96,768]{1,0:T(8,128)(2,1)S(1)}, u32[]{:S(2)}, u32[]{:S(2)}) %collective-permute-start.37) | collective-permute-done | bytes 147488 | tf_op jit(solution)/shard_map/ppermute | solution.py:713
  361.7 1.4 collective-permute-done.38
  363.1 1.6 collective-permute-start.39
  364.7 5.3 %collective-permute-done.39 = bf16[72,768]{1,0:T(8,128)(2,1)S(1)} collective-permute-done((bf16[72,768]{1,0:T(8,128)(2,1)S(1)}, bf16[72,768]{1,0:T(8,128)(2,1)S(1)}, u32[]{:S(2)}, u32[]{:S(2)}) %collective-permute-start.39) | collective-permute-done | bytes 110624 | tf_op jit(solution)/shard_map/ppermute | solution.py:713
  371.4 13.7 %collective-permute-done.40 = bf16[192,768]{1,0:T(8,128)(2,1)S(1)} collective-permute-done((bf16[192,768]{1,0:T(8,128)(2,1)S(1)}, bf16[192,768]{1,0:T(8,128)(2,1)S(1)}, u32[]{:S(2)}, u32[]{:S(2)}) %collective-permute-start.40) | collective-permute-done | bytes 294944 | tf_op jit(solution)/shard_map/ppermute | solution.py:713
  385.3 21.1 %collective-permute-done.41 = bf16[2,192,768]{2,1,0:T(8,128)(2,1)S(1)} collective-permute-done((bf16[2,192,768]{2,1,0:T(8,128)(2,1)S(1)}, bf16[2,192,768]{2,1,0:T(8,128)(2,1)S(1)}, u32[]{:S(2)}, u32[]{:S(2)}) %collective-permute-start.41) | collective-permute-done | bytes 589856 | tf_op jit(solution)/shard_map/ppermute | solution.py:713
  406.7 4.0 collective-permute-start.43
  410.6 9.5 %collective-permute-done.43 = bf16[2,2,96,768]{3,2,1,0:T(8,128)(2,1)S(1)} collective-permute-done((bf16[2,2,96,768]{3,2,1,0:T(8,128)(2,1)S(1)}, bf16[2,2,96,768]{3,2,1,0:T(8,128)(2,1)S(1)}, u32[]{:S(2)}, u32[]{:S(2)}) %collective-permute-start.43) | collective-permute-done | bytes 589856 | tf_op jit(solution)/shard_map/ppermute | solution.py:713
  422.6 39.6 %collective-permute-done.45 = bf16[2,2,2,96,768]{4,3,2,1,0:T(8,128)(2,1)S(1)} collective-permute-done((bf16[2,2,2,96,768]{4,3,2,1,0:T(8,128)(2,1)S(1)}, bf16[2,2,2,96,768]{4,3,2,1,0:T(8,128)(2,1)S(1)}, u32[]{:S(2)}, u32[]{:S(2)}) %collective-permute-start.45) | collective-permute-done | bytes 1179680 | tf_op jit(solution)/shard_map/ppermute | solution.py:713
  466.2 6.0 %collective-permute-done.47 = bf16[2,2,2,2,96,768]{5,4,3,2,1,0:T(8,128)(2,1)S(1)} collective-permute-done((bf16[2,2,2,2,96,768]{5,4,3,2,1,0:T(8,128)(2,1)S(1)}, bf16[2,2,2,2,96,768]{5,4,3,2,1,0:T(8,128)(2,1)S(1)}, u32[]{:S(2)}, u32[]{:S(2)}) %collective-permute-start.47) | collective-permute-done | bytes 2359328 | tf_op jit(solution)/shard_map/ppermute | solution.py:713
  472.2 1.4 copy-done.5
  473.6 6.5 %join_blocks.3 = f32[3072,768]{1,0:T(8,128)} custom-call(s32[1]{0:T(128)} %bitcast.2.core_ref, bf16[16,96,768]{2,1,0:T(8,128)(2,1)} %bitcast.129, bf16[16,96,768]{2,1,0:T(8,128)(2,1)} %bitcast.137), custom_call_target="tpu_custom_call" | custom-call | bytes 14155776 | tf_op jit(solution)/shard_map/join_blocks/pallas_call | solution.py:470
  480.1 6.5 %join_blocks.2 = f32[768,3072]{1,0:T(8,128)} custom-call(s32[1]{0:T(128)} %bitcast.2.core_ref, bf16[16,96,768]{2,1,0:T(8,128)(2,1)} %bitcast.128, bf16[16,96,768]{2,1,0:T(8,128)(2,1)} %bitcast.73.refs_1_), custom_call_target="tpu_custom_call" | custom-call | bytes 14155776 | tf_op jit(solution)/shard_map/join_blocks/pallas_call | solution.py:470
  486.6 8.2 %widen_rest.1 = (f32[768,768]{1,0:T(8,128)}, f32[768,768]{1,0:T(8,128)}, f32[768,768]{1,0:T(8,128)}, f32[768,768]{1,0:T(8,128)}, f32[2048,768]{1,0:T(8,128)}, /*...) custom-call(bf16[32,168,768]{2,1,0:T(8,128)(2,1)} %bitcast.130), custom_call_target="tpu_custom_call" | custom-call | bytes 24772608 | tf_op jit(solution)/shard_map/widen_rest/pallas_call | solution.py:534
  (172 shorter events, 51.0 us)
Async XLA Ops:
  7.2 140.3 %all-gather.5.cloned.1.call-start = ((), (), s32[]{:S(2)}) async-start(), calls=%async_computation.2 | async-start | bytes 9732096 | tf_op jit(solution)/shard_map/all_gather | solution.py:890
  7.2 9.2 %collective-permute-start = (bf16[64,768]{1,0:T(8,128)(2,1)}, bf16[64,768]{1,0:T(8,128)(2,1)S(1)}, u32[]{:S(2)}, u32[]{:S(2)}) collective-permute-start(bf16[64,768]{1,0:T(8,128)(2,1)} %param.33), channel_id=1, source_target_pairs={{0,16},{8,24},{16,0},{24,8},{1,17},{9,25},{17,1},{25,9},{2,18},{10... | collective-permute-start | bytes 294920 | tf_op jit(solution)/shard_map/ppermute | solution.py:713
  12.2 14.7 %copy-start.19 = (pred[2]{0:T(512)(128)(4,1)}, pred[2]{0:T(512)(128)(4,1)S(1)}, u32[]{:S(2)}) copy-start(pred[2]{0:T(512)(128)(4,1)S(1)} %iota_compare_fusion.1) | copy-start | bytes 10
  17.4 9.3 %collective-permute-start.2 = (bf16[96,768]{1,0:T(8,128)(2,1)S(1)}, bf16[96,768]{1,0:T(8,128)(2,1)S(1)}, u32[]{:S(2)}, u32[]{:S(2)}) collective-permute-start(bf16[96,768]{1,0:T(8,128)(2,1)S(1)} %pad_maximum_fusion.2), channel_id=1, source_target_pairs={{0,16},{8,24},{16,0},{24,8},{1,17},{9,25},{17,1},{25,9},{2,18},{10... | collective-permute-start | bytes 442376 | tf_op jit(solution)/shard_map/ppermute | solution.py:713
  18.1 22.4 %copy-start.17 = (pred[2]{0:T(512)(128)(4,1)}, pred[2]{0:T(512)(128)(4,1)S(1)}, u32[]{:S(2)}) copy-start(pred[2]{0:T(512)(128)(4,1)S(1)} %iota_compare_fusion.2) | copy-start | bytes 10
  20.7 9.7 %collective-permute-start.1 = (bf16[2,64,768]{2,1,0:T(8,128)(2,1)S(1)}, bf16[2,64,768]{2,1,0:T(8,128)(2,1)S(1)}, u32[]{:S(2)}, u32[]{:S(2)}) collective-permute-start(bf16[2,64,768]{2,1,0:T(8,128)(2,1)S(1)} %broadcast_select_fusion.17), channel_id=1, source_target_pairs={{0,8},{8,0},{16,24},{24,16},{1,9},{9,1},{17,25},{25,17},{2,10},{10... | collective-permute-start | bytes 589832 | tf_op jit(solution)/shard_map/ppermute | solution.py:713
  30.6 6.5 %collective-permute-start.4 = (bf16[2,2,32,768]{3,2,1,0:T(8,128)(2,1)S(1)}, bf16[2,2,32,768]{3,2,1,0:T(8,128)(2,1)S(1)}, u32[]{:S(2)}, u32[]{:S(2)}) collective-permute-start(bf16[2,2,32,768]{3,2,1,0:T(8,128)(2,1)S(1)} %get-tuple-element.450), channel_id=1, source_target_pairs={{0,2},{1,3},{2,0},{3,1},{4,6},{5,7},{6,4},{7,5},{8,10},{9,11},{10,... | collective-permute-start | bytes 589832 | tf_op jit(solution)/shard_map/ppermute | solution.py:713
  32.2 83.7 %copy-start.15 = (pred[2]{0:T(512)(128)(4,1)}, pred[2]{0:T(512)(128)(4,1)S(1)}, u32[]{:S(2)}) copy-start(pred[2]{0:T(512)(128)(4,1)S(1)} %iota_compare_fusion.3) | copy-start | bytes 10
  32.2 8.3 %collective-permute-start.5 = (bf16[2,96,768]{2,1,0:T(8,128)(2,1)S(1)}, bf16[2,96,768]{2,1,0:T(8,128)(2,1)S(1)}, u32[]{:S(2)}, u32[]{:S(2)}) collective-permute-start(bf16[2,96,768]{2,1,0:T(8,128)(2,1)S(1)} %broadcast_select_fusion.16), channel_id=1, source_target_pairs={{0,8},{8,0},{16,24},{24,16},{1,9},{9,1},{17,25},{25,17},{2,10},{10... | collective-permute-start | bytes 884744 | tf_op jit(solution)/shard_map/ppermute | solution.py:713
  32.6 5.9 %collective-permute-start.3 = (bf16[2,2,32,768]{3,2,1,0:T(8,128)(2,1)S(1)}, bf16[2,2,32,768]{3,2,1,0:T(8,128)(2,1)S(1)}, u32[]{:S(2)}, u32[]{:S(2)}) collective-permute-start(bf16[2,2,32,768]{3,2,1,0:T(8,128)(2,1)S(1)} %get-tuple-element.451), channel_id=1, source_target_pairs={{0,4},{1,5},{2,6},{3,7},{4,0},{5,1},{6,2},{7,3},{8,12},{9,13},{10,... | collective-permute-start | bytes 589832 | tf_op jit(solution)/shard_map/ppermute | solution.py:713
  40.7 11.6 %collective-permute-start.7 = (bf16[2,2,2,32,768]{4,3,2,1,0:T(8,128)(2,1)S(1)}, bf16[2,2,2,32,768]{4,3,2,1,0:T(8,128)(2,1)S(1)}, u32[]{:S(2)}, u32[]{:S(2)}) collective-permute-start(bf16[2,2,2,32,768]{4,3,2,1,0:T(8,128)(2,1)S(1)} %broadcast_select_fusion.13), channel_id=1, source_target_pairs={{0,4},{1,5},{2,6},{3,7},{4,0},{5,1},{6,2},{7,3},{8,12},{9,13},{10,... | collective-permute-start | bytes 1179656 | tf_op jit(solution)/shard_map/ppermute | solution.py:713
  42.3 10.1 %collective-permute-start.6 = (bf16[2,2,2,32,768]{4,3,2,1,0:T(8,128)(2,1)S(1)}, bf16[2,2,2,32,768]{4,3,2,1,0:T(8,128)(2,1)S(1)}, u32[]{:S(2)}, u32[]{:S(2)}) collective-permute-start(bf16[2,2,2,32,768]{4,3,2,1,0:T(8,128)(2,1)S(1)} %broadcast_select_fusion.15), channel_id=1, source_target_pairs={{0,2},{1,3},{2,0},{3,1},{4,6},{5,7},{6,4},{7,5},{8,10},{9,11},{10,... | collective-permute-start | bytes 1179656 | tf_op jit(solution)/shard_map/ppermute | solution.py:713
  52.5 8.5 %copy-start.3 = (bf16[2,2,2,2,32,768]{5,4,3,2,1,0:T(8,128)(2,1)}, bf16[2,2,2,2,32,768]{5,4,3,2,1,0:T(8,128)(2,1)S(1)}, u32[]{:S(2)}) copy-start(bf16[2,2,2,2,32,768]{5,4,3,2,1,0:T(8,128)(2,1)S(1)} %broadcast_select_fusion.8) | copy-start | bytes 2359300
  52.6 8.4 %collective-permute-start.9 = (bf16[2,2,48,768]{3,2,1,0:T(8,128)(2,1)S(1)}, bf16[2,2,48,768]{3,2,1,0:T(8,128)(2,1)S(1)}, u32[]{:S(2)}, u32[]{:S(2)}) collective-permute-start(bf16[2,2,48,768]{3,2,1,0:T(8,128)(2,1)S(1)} %get-tuple-element.446), channel_id=1, source_target_pairs={{0,2},{1,3},{2,0},{3,1},{4,6},{5,7},{6,4},{7,5},{8,10},{9,11},{10,... | collective-permute-start | bytes 884744 | tf_op jit(solution)/shard_map/ppermute | solution.py:713
  53.2 12.3 %collective-permute-start.10 = (bf16[2,2,2,2,32,768]{5,4,3,2,1,0:T(8,128)(2,1)S(1)}, bf16[2,2,2,2,32,768]{5,4,3,2,1,0:T(8,128)(2,1)}, u32[]{:S(2)}, u32[]{:S(2)}) collective-permute-start(bf16[2,2,2,2,32,768]{5,4,3,2,1,0:T(8,128)(2,1)S(1)} %broadcast_select_fusion.8), channel_id=1, source_target_pairs={{0,1},{1,0},{2,3},{3,2},{4,5},{5,4},{6,7},{7,6},{8,9},{9,8},{10,11... | collective-permute-start | bytes 2359304 | tf_op jit(solution)/shard_map/ppermute | solution.py:713
  53.2 12.3 %collective-permute-start.11 = (bf16[2,2,2,2,32,768]{5,4,3,2,1,0:T(8,128)(2,1)S(1)}, bf16[2,2,2,2,32,768]{5,4,3,2,1,0:T(8,128)(2,1)}, u32[]{:S(2)}, u32[]{:S(2)}) collective-permute-start(bf16[2,2,2,2,32,768]{5,4,3,2,1,0:T(8,128)(2,1)S(1)} %broadcast_select_fusion.7), channel_id=1, source_target_pairs={{0,1},{1,0},{2,3},{3,2},{4,5},{5,4},{6,7},{7,6},{8,9},{9,8},{10,11... | collective-permute-start | bytes 2359304 | tf_op jit(solution)/shard_map/ppermute | solution.py:713
  53.7 11.7 %collective-permute-start.8 = (bf16[2,2,48,768]{3,2,1,0:T(8,128)(2,1)S(1)}, bf16[2,2,48,768]{3,2,1,0:T(8,128)(2,1)S(1)}, u32[]{:S(2)}, u32[]{:S(2)}) collective-permute-start(bf16[2,2,48,768]{3,2,1,0:T(8,128)(2,1)S(1)} %get-tuple-element.447), channel_id=1, source_target_pairs={{0,4},{1,5},{2,6},{3,7},{4,0},{5,1},{6,2},{7,3},{8,12},{9,13},{10,... | collective-permute-start | bytes 884744 | tf_op jit(solution)/shard_map/ppermute | solution.py:713
  73.3 43.8 %all-to-all-start = ((bf16[32,16,768]{2,1,0:T(8,128)(2,1)}), bf16[32,16,768]{2,1,0:T(8,128)(2,1)}, u32[]{:S(2)}, u32[]{:S(2)}) async-start(bf16[32,16,768]{2,1,0:T(8,128)(2,1)} %bitcast.152), calls=%async_computation | async-start | bytes 1572864 | tf_op jit(solution)/shard_map/all_to_all | solution.py:914
  79.2 36.8 %collective-permute-start.13 = (bf16[2,2,2,48,768]{4,3,2,1,0:T(8,128)(2,1)S(1)}, bf16[2,2,2,48,768]{4,3,2,1,0:T(8,128)(2,1)S(1)}, u32[]{:S(2)}, u32[]{:S(2)}) collective-permute-start(bf16[2,2,2,48,768]{4,3,2,1,0:T(8,128)(2,1)S(1)} %broadcast_select_fusion.10), channel_id=1, source_target_pairs={{0,4},{1,5},{2,6},{3,7},{4,0},{5,1},{6,2},{7,3},{8,12},{9,13},{10,... | collective-permute-start | bytes 1769480 | tf_op jit(solution)/shard_map/ppermute | solution.py:713
  80.9 36.1 %collective-permute-start.12 = (bf16[2,2,2,48,768]{4,3,2,1,0:T(8,128)(2,1)S(1)}, bf16[2,2,2,48,768]{4,3,2,1,0:T(8,128)(2,1)S(1)}, u32[]{:S(2)}, u32[]{:S(2)}) collective-permute-start(bf16[2,2,2,48,768]{4,3,2,1,0:T(8,128)(2,1)S(1)} %broadcast_select_fusion.12), channel_id=1, source_target_pairs={{0,2},{1,3},{2,0},{3,1},{4,6},{5,7},{6,4},{7,5},{8,10},{9,11},{10,... | collective-permute-start | bytes 1769480 | tf_op jit(solution)/shard_map/ppermute | solution.py:713
  117.2 3.8 collective-permute-start.14
  117.2 4.7 collective-permute-start.15
  198.7 11.9 %collective-permute-start.16 = (bf16[16,96,768]{2,1,0:T(8,128)(2,1)}, bf16[16,96,768]{2,1,0:T(8,128)(2,1)S(1)}, u32[]{:S(2)}, u32[]{:S(2)}) collective-permute-start(bf16[16,96,768]{2,1,0:T(8,128)(2,1)} %get-tuple-element.246), channel_id=1, source_target_pairs={{0,1},{1,0},{2,3},{3,2},{4,5},{5,4},{6,7},{7,6},{8,9},{9,8},{10,11... | collective-permute-start | bytes 7077896 | tf_op jit(solution)/shard_map/ppermute | solution.py:713
  208.4 5.0 collective-permute-start.17
  210.6 2.7 copy-start.4
  217.5 28.6 %collective-permute-start.19 = (bf16[2,2,2,96,768]{4,3,0,1,2:T(8,128)(2,1)}, bf16[2,2,2,96,768]{4,3,0,1,2:T(8,128)(2,1)}, u32[]{:S(2)}, u32[]{:S(2)}) collective-permute-start(bf16[2,2,2,96,768]{4,3,0,1,2:T(8,128)(2,1)} %fusion.1), channel_id=1, source_target_pairs={{0,4},{1,5},{2,6},{3,7},{4,0},{5,1},{6,2},{7,3},{8,12},{9,13},{10,... | collective-permute-start | bytes 3538952 | tf_op jit(solution)/shard_map/ppermute | solution.py:713
  219.3 28.1 %collective-permute-start.18 = (bf16[2,2,2,96,768]{4,3,0,1,2:T(8,128)(2,1)S(1)}, bf16[2,2,2,96,768]{4,3,0,1,2:T(8,128)(2,1)}, u32[]{:S(2)}, u32[]{:S(2)}) collective-permute-start(bf16[2,2,2,96,768]{4,3,0,1,2:T(8,128)(2,1)S(1)} %fusion), channel_id=1, source_target_pairs={{0,2},{1,3},{2,0},{3,1},{4,6},{5,7},{6,4},{7,5},{8,10},{9,11},{10,... | collective-permute-start | bytes 3538952 | tf_op jit(solution)/shard_map/ppermute | solution.py:713
  247.4 25.2 %all-to-all-start.1 = ((bf16[32,16,768]{2,1,0:T(8,128)(2,1)}), bf16[32,16,768]{2,1,0:T(8,128)(2,1)S(1)}, u32[]{:S(2)}, u32[]{:S(2)}) async-start(bf16[32,16,768]{2,1,0:T(8,128)(2,1)} %bitcast.151), calls=%async_computation.1 | async-start | bytes 1572864 | tf_op jit(solution)/shard_map/all_to_all | solution.py:1026
  252.1 234.6 %all-gather.7.cloned.1.call-start = ((), (), s32[]{:S(2)}) async-start(), calls=%async_computation.3 | async-start | bytes 8515584 | tf_op jit(solution)/shard_map/all_gather | solution.py:1069
  277.9 17.4 %collective-permute-start.22 = (bf16[16,48,768]{2,1,0:T(8,128)(2,1)}, bf16[16,48,768]{2,1,0:T(8,128)(2,1)S(1)}, u32[]{:S(2)}, u32[]{:S(2)}) collective-permute-start(bf16[16,48,768]{2,1,0:T(8,128)(2,1)} %get-tuple-element.294), channel_id=1, source_target_pairs={{0,1},{1,0},{2,3},{3,2},{4,5},{5,4},{6,7},{7,6},{8,9},{9,8},{10,11... | collective-permute-start | bytes 3538952 | tf_op jit(solution)/shard_map/ppermute | solution.py:713
  277.9 17.4 %collective-permute-start.23 = (bf16[16,48,768]{2,1,0:T(8,128)(2,1)}, bf16[16,48,768]{2,1,0:T(8,128)(2,1)}, u32[]{:S(2)}, u32[]{:S(2)}) collective-permute-start(bf16[16,48,768]{2,1,0:T(8,128)(2,1)} %get-tuple-element.296), channel_id=1, source_target_pairs={{0,1},{1,0},{2,3},{3,2},{4,5},{5,4},{6,7},{7,6},{8,9},{9,8},{10,11... | collective-permute-start | bytes 3538952 | tf_op jit(solution)/shard_map/ppermute | solution.py:713
  278.4 16.1 %collective-permute-start.21 = (bf16[2,2,96,768]{3,2,1,0:T(8,128)(2,1)}, bf16[2,2,96,768]{3,2,1,0:T(8,128)(2,1)S(1)}, u32[]{:S(2)}, u32[]{:S(2)}) collective-permute-start(bf16[2,2,96,768]{3,2,1,0:T(8,128)(2,1)} %fusion.15), channel_id=1, source_target_pairs={{0,2},{1,3},{2,0},{3,1},{4,6},{5,7},{6,4},{7,5},{8,10},{9,11},{10,... | collective-permute-start | bytes 1769480 | tf_op jit(solution)/shard_map/ppermute | solution.py:713
  279.9 15.4 %collective-permute-start.20 = (bf16[2,2,96,768]{3,2,0,1:T(8,128)(2,1)}, bf16[2,2,96,768]{3,2,0,1:T(8,128)(2,1)}, u32[]{:S(2)}, u32[]{:S(2)}) collective-permute-start(bf16[2,2,96,768]{3,2,0,1:T(8,128)(2,1)} %get-tuple-element.414), channel_id=1, source_target_pairs={{0,4},{1,5},{2,6},{3,7},{4,0},{5,1},{6,2},{7,3},{8,12},{9,13},{10,... | collective-permute-start | bytes 1769480 | tf_op jit(solution)/shard_map/ppermute | solution.py:713
  299.1 2.5 copy-start.9
  302.8 17.4 %collective-permute-start.27 = (bf16[16,40,768]{2,1,0:T(8,128)(2,1)}, bf16[16,40,768]{2,1,0:T(8,128)(2,1)}, u32[]{:S(2)}, u32[]{:S(2)}) collective-permute-start(bf16[16,40,768]{2,1,0:T(8,128)(2,1)} %get-tuple-element.322), channel_id=1, source_target_pairs={{0,1},{1,0},{2,3},{3,2},{4,5},{5,4},{6,7},{7,6},{8,9},{9,8},{10,11... | collective-permute-start | bytes 2949128 | tf_op jit(solution)/shard_map/ppermute | solution.py:713
  302.8 17.4 %collective-permute-start.28 = (bf16[16,32,768]{2,1,0:T(8,128)(2,1)}, bf16[16,32,768]{2,1,0:T(8,128)(2,1)}, u32[]{:S(2)}, u32[]{:S(2)}) collective-permute-start(bf16[16,32,768]{2,1,0:T(8,128)(2,1)} %get-tuple-element.324), channel_id=1, source_target_pairs={{0,1},{1,0},{2,3},{3,2},{4,5},{5,4},{6,7},{7,6},{8,9},{9,8},{10,11... | collective-permute-start | bytes 2359304 | tf_op jit(solution)/shard_map/ppermute | solution.py:713
  303.3 15.6 %collective-permute-start.26 = (bf16[2,2,2,48,768]{4,3,0,1,2:T(8,128)(2,1)}, bf16[2,2,2,48,768]{4,3,0,1,2:T(8,128)(2,1)}, u32[]{:S(2)}, u32[]{:S(2)}) collective-permute-start(bf16[2,2,2,48,768]{4,3,0,1,2:T(8,128)(2,1)} %get-tuple-element.410), channel_id=1, source_target_pairs={{0,4},{1,5},{2,6},{3,7},{4,0},{5,1},{6,2},{7,3},{8,12},{9,13},{10,... | collective-permute-start | bytes 1769480 | tf_op jit(solution)/shard_map/ppermute | solution.py:713
  304.6 15.3 %collective-permute-start.25 = (bf16[2,2,2,48,768]{4,3,0,1,2:T(8,128)(2,1)}, bf16[2,2,2,48,768]{4,3,0,1,2:T(8,128)(2,1)}, u32[]{:S(2)}, u32[]{:S(2)}) collective-permute-start(bf16[2,2,2,48,768]{4,3,0,1,2:T(8,128)(2,1)} %get-tuple-element.412), channel_id=1, source_target_pairs={{0,2},{1,3},{2,0},{3,1},{4,6},{5,7},{6,4},{7,5},{8,10},{9,11},{10,... | collective-permute-start | bytes 1769480 | tf_op jit(solution)/shard_map/ppermute | solution.py:713
  305.2 15.0 %collective-permute-start.24 = (bf16[2,192,768]{2,1,0:T(8,128)(2,1)}, bf16[2,192,768]{2,1,0:T(8,128)(2,1)}, u32[]{:S(2)}, u32[]{:S(2)}) collective-permute-start(bf16[2,192,768]{2,1,0:T(8,128)(2,1)} %fusion.16), channel_id=1, source_target_pairs={{0,8},{8,0},{16,24},{24,16},{1,9},{9,1},{17,25},{25,17},{2,10},{10... | collective-permute-start | bytes 1769480 | tf_op jit(solution)/shard_map/ppermute | solution.py:713
  324.0 3.0 copy-start.12
  325.5 19.1 %collective-permute-start.32 = (bf16[2,2,2,40,768]{4,3,0,1,2:T(8,128)(2,1)S(1)}, bf16[2,2,2,40,768]{4,3,0,1,2:T(8,128)(2,1)S(1)}, u32[]{:S(2)}, u32[]{:S(2)}) collective-permute-start(bf16[2,2,2,40,768]{4,3,0,1,2:T(8,128)(2,1)S(1)} %get-tuple-element.424), channel_id=1, source_target_pairs={{0,2},{1,3},{2,0},{3,1},{4,6},{5,7},{6,4},{7,5},{8,10},{9,11},{10,... | collective-permute-start | bytes 1474568 | tf_op jit(solution)/shard_map/ppermute | solution.py:713
  328.3 16.2 %collective-permute-start.33 = (bf16[2,2,2,32,768]{4,3,0,1,2:T(8,128)(2,1)S(1)}, bf16[2,2,2,32,768]{4,3,0,1,2:T(8,128)(2,1)S(1)}, u32[]{:S(2)}, u32[]{:S(2)}) collective-permute-start(bf16[2,2,2,32,768]{4,3,0,1,2:T(8,128)(2,1)S(1)} %get-tuple-element.426), channel_id=1, source_target_pairs={{0,4},{1,5},{2,6},{3,7},{4,0},{5,1},{6,2},{7,3},{8,12},{9,13},{10,... | collective-permute-start | bytes 1179656 | tf_op jit(solution)/shard_map/ppermute | solution.py:713
  329.1 14.4 %collective-permute-start.31 = (bf16[2,2,48,768]{3,2,0,1:T(8,128)(2,1)S(1)}, bf16[2,2,48,768]{3,2,0,1:T(8,128)(2,1)S(1)}, u32[]{:S(2)}, u32[]{:S(2)}) collective-permute-start(bf16[2,2,48,768]{3,2,0,1:T(8,128)(2,1)S(1)} %get-tuple-element.432), channel_id=1, source_target_pairs={{0,2},{1,3},{2,0},{3,1},{4,6},{5,7},{6,4},{7,5},{8,10},{9,11},{10,... | collective-permute-start | bytes 884744 | tf_op jit(solution)/shard_map/ppermute | solution.py:713
  329.5 14.5 %collective-permute-start.30 = (bf16[2,2,48,768]{3,2,0,1:T(8,128)(2,1)S(1)}, bf16[2,2,48,768]{3,2,0,1:T(8,128)(2,1)S(1)}, u32[]{:S(2)}, u32[]{:S(2)}) collective-permute-start(bf16[2,2,48,768]{3,2,0,1:T(8,128)(2,1)S(1)} %get-tuple-element.434), channel_id=1, source_target_pairs={{0,4},{1,5},{2,6},{3,7},{4,0},{5,1},{6,2},{7,3},{8,12},{9,13},{10,... | collective-permute-start | bytes 884744 | tf_op jit(solution)/shard_map/ppermute | solution.py:713
  331.0 13.5 %collective-permute-start.29 = (bf16[192,768]{1,0:T(8,128)(2,1)S(1)}, bf16[192,768]{1,0:T(8,128)(2,1)S(1)}, u32[]{:S(2)}, u32[]{:S(2)}) collective-permute-start(bf16[192,768]{1,0:T(8,128)(2,1)S(1)} %get-tuple-element.436), channel_id=1, source_target_pairs={{0,16},{8,24},{16,0},{24,8},{1,17},{9,25},{17,1},{25,9},{2,18},{10... | collective-permute-start | bytes 884744 | tf_op jit(solution)/shard_map/ppermute | solution.py:713
  344.8 8.6 %collective-permute-start.34 = (bf16[2,96,768]{2,1,0:T(8,128)(2,1)S(1)}, bf16[2,96,768]{2,1,0:T(8,128)(2,1)S(1)}, u32[]{:S(2)}, u32[]{:S(2)}) collective-permute-start(bf16[2,96,768]{2,1,0:T(8,128)(2,1)S(1)} %get-tuple-element.430), channel_id=1, source_target_pairs={{0,8},{8,0},{16,24},{24,16},{1,9},{9,1},{17,25},{25,17},{2,10},{10... | collective-permute-start | bytes 884744 | tf_op jit(solution)/shard_map/ppermute | solution.py:713
  345.0 7.6 %collective-permute-start.35 = (bf16[2,2,40,768]{3,2,0,1:T(8,128)(2,1)S(1)}, bf16[2,2,40,768]{3,2,0,1:T(8,128)(2,1)S(1)}, u32[]{:S(2)}, u32[]{:S(2)}) collective-permute-start(bf16[2,2,40,768]{3,2,0,1:T(8,128)(2,1)S(1)} %get-tuple-element.438), channel_id=1, source_target_pairs={{0,4},{1,5},{2,6},{3,7},{4,0},{5,1},{6,2},{7,3},{8,12},{9,13},{10,... | collective-permute-start | bytes 737288 | tf_op jit(solution)/shard_map/ppermute | solution.py:713
  346.2 5.7 %collective-permute-start.36 = (bf16[2,2,32,768]{3,2,0,1:T(8,128)(2,1)S(1)}, bf16[2,2,32,768]{3,2,0,1:T(8,128)(2,1)S(1)}, u32[]{:S(2)}, u32[]{:S(2)}) collective-permute-start(bf16[2,2,32,768]{3,2,0,1:T(8,128)(2,1)S(1)} %get-tuple-element.442), channel_id=1, source_target_pairs={{0,2},{1,3},{2,0},{3,1},{4,6},{5,7},{6,4},{7,5},{8,10},{9,11},{10,... | collective-permute-start | bytes 589832 | tf_op jit(solution)/shard_map/ppermute | solution.py:713
  353.8 9.3 %collective-permute-start.38 = (bf16[2,72,768]{2,1,0:T(8,128)(2,1)S(1)}, bf16[2,72,768]{2,1,0:T(8,128)(2,1)S(1)}, u32[]{:S(2)}, u32[]{:S(2)}) collective-permute-start(bf16[2,72,768]{2,1,0:T(8,128)(2,1)S(1)} %get-tuple-element.440), channel_id=1, source_target_pairs={{0,8},{8,0},{16,24},{24,16},{1,9},{9,1},{17,25},{25,17},{2,10},{10... | collective-permute-start | bytes 663560 | tf_op jit(solution)/shard_map/ppermute | solution.py:713
  354.7 7.0 %collective-permute-start.37 = (bf16[96,768]{1,0:T(8,128)(2,1)S(1)}, bf16[96,768]{1,0:T(8,128)(2,1)S(1)}, u32[]{:S(2)}, u32[]{:S(2)}) collective-permute-start(bf16[96,768]{1,0:T(8,128)(2,1)S(1)} %get-tuple-element.444), channel_id=1, source_target_pairs={{0,16},{8,24},{16,0},{24,8},{1,17},{9,25},{17,1},{25,9},{2,18},{10... | collective-permute-start | bytes 442376 | tf_op jit(solution)/shard_map/ppermute | solution.py:713
  363.1 6.9 %collective-permute-start.39 = (bf16[72,768]{1,0:T(8,128)(2,1)S(1)}, bf16[72,768]{1,0:T(8,128)(2,1)S(1)}, u32[]{:S(2)}, u32[]{:S(2)}) collective-permute-start(bf16[72,768]{1,0:T(8,128)(2,1)S(1)} %get-tuple-element.448), channel_id=1, source_target_pairs={{0,16},{8,24},{16,0},{24,8},{1,17},{9,25},{17,1},{25,9},{2,18},{10... | collective-permute-start | bytes 331784 | tf_op jit(solution)/shard_map/ppermute | solution.py:713
  370.0 15.0 %copy-start.20 = (pred[2]{0:T(512)(128)(4,1)S(1)}, pred[2]{0:T(512)(128)(4,1)}, u32[]{:S(2)}) copy-start(pred[2]{0:T(512)(128)(4,1)} %copy-done.19) | copy-start | bytes 10
  370.8 35.6 %copy-start.18 = (pred[2]{0:T(512)(128)(4,1)S(1)}, pred[2]{0:T(512)(128)(4,1)}, u32[]{:S(2)}) copy-start(pred[2]{0:T(512)(128)(4,1)} %copy-done.17) | copy-start | bytes 10
  370.9 14.1 %collective-permute-start.40 = (bf16[192,768]{1,0:T(8,128)(2,1)S(1)}, bf16[192,768]{1,0:T(8,128)(2,1)S(1)}, u32[]{:S(2)}, u32[]{:S(2)}) collective-permute-start(bf16[192,768]{1,0:T(8,128)(2,1)S(1)} %add_convert_fusion.16), channel_id=1, source_target_pairs={{0,16},{8,24},{16,0},{24,8},{1,17},{9,25},{17,1},{25,9},{2,18},{10... | collective-permute-start | bytes 884744 | tf_op jit(solution)/shard_map/ppermute | solution.py:713
  385.2 21.2 %collective-permute-start.41 = (bf16[2,192,768]{2,1,0:T(8,128)(2,1)S(1)}, bf16[2,192,768]{2,1,0:T(8,128)(2,1)S(1)}, u32[]{:S(2)}, u32[]{:S(2)}) collective-permute-start(bf16[2,192,768]{2,1,0:T(8,128)(2,1)S(1)} %broadcast_select_fusion.9), channel_id=1, source_target_pairs={{0,8},{8,0},{16,24},{24,16},{1,9},{9,1},{17,25},{25,17},{2,10},{10... | collective-permute-start | bytes 1769480 | tf_op jit(solution)/shard_map/ppermute | solution.py:713
  406.7 13.5 %collective-permute-start.43 = (bf16[2,2,96,768]{3,2,1,0:T(8,128)(2,1)S(1)}, bf16[2,2,96,768]{3,2,1,0:T(8,128)(2,1)S(1)}, u32[]{:S(2)}, u32[]{:S(2)}) collective-permute-start(bf16[2,2,96,768]{3,2,1,0:T(8,128)(2,1)S(1)} %get-tuple-element.428), channel_id=1, source_target_pairs={{0,2},{1,3},{2,0},{3,1},{4,6},{5,7},{6,4},{7,5},{8,10},{9,11},{10,... | collective-permute-start | bytes 1769480 | tf_op jit(solution)/shard_map/ppermute | solution.py:713
  410.6 9.9 %copy-start.16 = (pred[2]{0:T(512)(128)(4,1)S(1)}, pred[2]{0:T(512)(128)(4,1)}, u32[]{:S(2)}) copy-start(pred[2]{0:T(512)(128)(4,1)} %copy-done.15) | copy-start | bytes 10
  410.6 9.9 %collective-permute-start.42 = (bf16[2,2,96,768]{3,2,1,0:T(8,128)(2,1)S(1)}, bf16[2,2,96,768]{3,2,1,0:T(8,128)(2,1)S(1)}, u32[]{:S(2)}, u32[]{:S(2)}) collective-permute-start(bf16[2,2,96,768]{3,2,1,0:T(8,128)(2,1)S(1)} %get-tuple-element.429), channel_id=1, source_target_pairs={{0,4},{1,5},{2,6},{3,7},{4,0},{5,1},{6,2},{7,3},{8,12},{9,13},{10,... | collective-permute-start | bytes 1769480 | tf_op jit(solution)/shard_map/ppermute | solution.py:713
  420.7 41.5 %collective-permute-start.45 = (bf16[2,2,2,96,768]{4,3,2,1,0:T(8,128)(2,1)S(1)}, bf16[2,2,2,96,768]{4,3,2,1,0:T(8,128)(2,1)S(1)}, u32[]{:S(2)}, u32[]{:S(2)}) collective-permute-start(bf16[2,2,2,96,768]{4,3,2,1,0:T(8,128)(2,1)S(1)} %broadcast_select_fusion.2), channel_id=1, source_target_pairs={{0,4},{1,5},{2,6},{3,7},{4,0},{5,1},{6,2},{7,3},{8,12},{9,13},{10,... | collective-permute-start | bytes 3538952 | tf_op jit(solution)/shard_map/ppermute | solution.py:713
  422.0 41.6 %collective-permute-start.44 = (bf16[2,2,2,96,768]{4,3,2,1,0:T(8,128)(2,1)S(1)}, bf16[2,2,2,96,768]{4,3,2,1,0:T(8,128)(2,1)S(1)}, u32[]{:S(2)}, u32[]{:S(2)}) collective-permute-start(bf16[2,2,2,96,768]{4,3,2,1,0:T(8,128)(2,1)S(1)} %broadcast_select_fusion.4), channel_id=1, source_target_pairs={{0,2},{1,3},{2,0},{3,1},{4,6},{5,7},{6,4},{7,5},{8,10},{9,11},{10,... | collective-permute-start | bytes 3538952 | tf_op jit(solution)/shard_map/ppermute | solution.py:713
  462.5 2.8 copy-start.13
  462.5 2.8 copy-start.14
  463.9 8.3 %collective-permute-start.47 = (bf16[2,2,2,2,96,768]{5,4,3,2,1,0:T(8,128)(2,1)S(1)}, bf16[2,2,2,2,96,768]{5,4,3,2,1,0:T(8,128)(2,1)S(1)}, u32[]{:S(2)}, u32[]{:S(2)}) collective-permute-start(bf16[2,2,2,2,96,768]{5,4,3,2,1,0:T(8,128)(2,1)S(1)} %broadcast_select_fusion.1), channel_id=1, source_target_pairs={{0,1},{1,0},{2,3},{3,2},{4,5},{5,4},{6,7},{7,6},{8,9},{9,8},{10,11... | collective-permute-start | bytes 7077896 | tf_op jit(solution)/shard_map/ppermute | solution.py:713
  464.0 16.1 %collective-permute-start.46 = (bf16[2,2,2,2,96,768]{5,4,3,2,1,0:T(8,128)(2,1)S(1)}, bf16[2,2,2,2,96,768]{5,4,3,2,1,0:T(8,128)(2,1)}, u32[]{:S(2)}, u32[]{:S(2)}) collective-permute-start(bf16[2,2,2,2,96,768]{5,4,3,2,1,0:T(8,128)(2,1)S(1)} %broadcast_select_fusion), channel_id=1, source_target_pairs={{0,1},{1,0},{2,3},{3,2},{4,5},{5,4},{6,7},{7,6},{8,9},{9,8},{10,11... | collective-permute-start | bytes 7077896 | tf_op jit(solution)/shard_map/ppermute | solution.py:713
  (9 other events, 12.5 us)
Sparse Core Ops, SparseCore 0:
  30.7 103.3 all-gather.4
  371.0 101.1 all-gather.6

commit v5 on v4

--- a/solution.py
+++ b/solution.py
@@ -882,7 +882,7 @@
     img = Gather(w_img, far)
     attn = Gather(jnp.concatenate([w_query, w_key, w_value, w_out], 0), far)
     img.stage()
-    fence([img, attn])
+    (ff_shard,) = fence([img, attn], ff_shard)
     while img.order:
         img.stage()
         attn.stage()
@@ -1024,6 +1024,7 @@
         [ff], grad_query, grad_keys, grad_values, grad_slots, attn_sums
     )
     back = lax.all_to_all(grad_slots, axes, split_axis=0, concat_axis=0, tiled=True)
+    ff.stage()
     attn_parts = weight_grads(
         core,
         device_count,
@@ -1039,6 +1040,9 @@
     )
     attn = Sum(attn_parts, orders)
     (back,) = fence([ff, attn], back)
+    while len(ff.steps) > len(far):
+        ff.stage()
+        fence([ff])
     in_turn(ff, attn)
     small_rows = 40
     chunk = 8 * (-(-(feat + small_rows) // (8 * device_count)))
@@ -1059,12 +1063,17 @@
     img = Sum(img_parts, orders)
     fence([ff, attn, img])
     while ff.steps:
-        in_turn(ff, attn, img)
+        if len(ff.steps) > 1:
+            in_turn(ff)
+        else:
+            in_turn(ff, attn, img)
         fence([ff, attn, img])
+    ff = Gather(ff.total(), far)
+    in_turn(ff, img, attn)
+    fence([attn, img, ff])
     while img.steps:
         in_turn(attn, img)
-        fence([attn, img])
-    ff = Gather(ff.total(), far)
+        fence([attn, img, ff])
     rest = jnp.concatenate([attn.total(), img.total()], 0)
     rest_all = lax.all_gather(rest, axes, axis=0)
     fence([ff], rest)

time: 511 us -> 467 us (0.914)
  waiting for transfers between devices: 227 us -> 189 us
  other arithmetic: 32.1 us -> 24.6 us
    ppermute x48, waiting for transfers between devices: 218 us -> 183 us  [swap_bit(): return lax.ppermute(tensor, name, [(i, i ^ step) for i in range(size)])]
    all_to_all x1, waiting for transfers between devices: 9.33 us -> 0.01 us  [body(): lax.all_to_all(grad_slots, axes, split_axis=0, concat_axis=0, tiled=True)]
    convert_element_type x25, other arithmetic: 22.4 us -> 16.5 us  [add_low(): return (kept.astype(f32) + came.astype(f32)).astype(bf16)]
    all_gather x1, waiting for transfers between devices: 0.01 us -> 5.95 us  [body(): rest_all = lax.all_gather(rest, axes, axis=0)]
    ppermute x48, starting transfers between devices: 47.3 us -> 52.7 us  [swap_bit(): return lax.ppermute(tensor, name, [(i, i ^ step) for i in range(size)])]
  transfers between devices with their start and end apart: 52 -> 52, of which waited for: 37 -> 34; matrix products, arithmetic and copies ran while one was open for 4% -> 5% of each run, Pallas kernels for 19% -> 21%
where the time goes in v5:
time: 467 us; the launch traced here: 459 us
  waiting for transfers between devices  189 us (40%)
  Pallas kernels  156 us (33%)
  starting transfers between devices  61.2 us (13%)
  other arithmetic  24.6 us (5%)
  between operations  15.9 us (3%)
  local copies, waits for them, and re-layouts  11.8 us (3%)
    ppermute x48, waiting for transfers between devices, swap_bit(): return lax.ppermute(tensor, name, [(i, i ^ step) for i in range(size)])  183 us
    ppermute x48, starting transfers between devices, swap_bit(): return lax.ppermute(tensor, name, [(i, i ^ step) for i in range(size)])  52.7 us
    pallas_call x1, Pallas kernels, run_feed_forward(): pl.pallas_call(feed_forward, out_shape=shapes, grid_spec=pltpu.PrefetchSc...  41.7 us
    pallas_call x3, Pallas kernels, weight_grads(): pl.pallas_call(functools.partial(weight_grad_kernel, lhs_of, rhs_of, grou...  30.2 us
    pallas_call x1, Pallas kernels, run_attention_backward(): pl.pallas_call(functools.partial(attention_backward, *geometry), out_shap...  23.7 us
    pallas_call x1, Pallas kernels, run_attention_forward(): pl.pallas_call(functools.partial(attention_forward, *geometry), out_shape...  21.5 us
    convert_element_type x25, other arithmetic, add_low(): return (kept.astype(f32) + came.astype(f32)).astype(bf16)  16.5 us
    pallas_call x2, Pallas kernels, join_blocks(): pl.pallas_call(join_kernel, out_shape=jax.ShapeDtypeStruct(shape, f32), g...  13.1 us
  transfers between devices with their start and end apart: 52, of which 34 were waited for; matrix products, arithmetic and copies ran while one was open for 5% of the time, Pallas kernels for 21%

profile of v5, /device:TPU:0, one launch (start us, length us, event | category | flops | bytes accessed | tf_op | source)
XLA Modules:
  0.0 458.6 jit_solution(1685926544181886373)
XLA Ops:
  7.2 4.1 collective-permute-start
  12.3 1.6 pad_maximum_fusion
  14.8 1.7 collective-permute-done
  17.3 3.5 collective-permute-start.1
  20.7 5.1 %collective-permute-done.2 = bf16[96,768]{1,0:T(8,128)(2,1)S(1)} collective-permute-done((bf16[96,768]{1,0:T(8,128)(2,1)S(1)}, bf16[96,768]{1,0:T(8,128)(2,1)S(1)}, u32[]{:S(2)}, u32[]{:S(2)}) %collective-permute-start.2) | collective-permute-done | bytes 147488 | tf_op jit(solution)/shard_map/ppermute | solution.py:713
  30.6 2.8 collective-permute-done.4
  34.9 1.9 collective-permute-done.5
  37.0 1.6 collective-permute-start.7
  39.1 9.1 %collective-permute-done.7 = bf16[2,2,2,32,768]{4,3,2,1,0:T(8,128)(2,1)S(1)} collective-permute-done((bf16[2,2,2,32,768]{4,3,2,1,0:T(8,128)(2,1)S(1)}, bf16[2,2,2,32,768]{4,3,2,1,0:T(8,128)(2,1)S(1)}, u32[]{:S(2)}, u32[]{:S(2)}) %collective-permute-start.7) | collective-permute-done | bytes 393248 | tf_op jit(solution)/shard_map/ppermute | solution.py:713
  51.2 6.3 %collective-permute-done.9 = bf16[2,2,48,768]{3,2,1,0:T(8,128)(2,1)S(1)} collective-permute-done((bf16[2,2,48,768]{3,2,1,0:T(8,128)(2,1)S(1)}, bf16[2,2,48,768]{3,2,1,0:T(8,128)(2,1)S(1)}, u32[]{:S(2)}, u32[]{:S(2)}) %collective-permute-start.9) | collective-permute-done | bytes 294944 | tf_op jit(solution)/shard_map/ppermute | solution.py:713
  57.6 3.9 collective-permute-done.8
  61.7 7.8 %image_encode.1 = (f32[416,768]{1,0:T(8,128)}, bf16[512,768]{1,0:T(8,128)(2,1)}, bf16[32,64,768]{2,1,0:T(8,128)(2,1)}) custom-call(s32[1]{0:T(128)} %bitcast.2.core_ref, bf16[416,2048]{1,0:T(8,128)(2,1)} %x_ref.3, bf16[4,416]{1,0:T(4,128)(2,1)} %box_ref.3, bf16[4,768]{1,0:T(4,128)(2,1)} %wb_ref.1, f32[768]{0:T(1024)} %bi_ref.1, f32[768]{0:T(1024)} %gr_ref.3, ...), custom_call_target="tpu_custom_call" | custom-call | flops 1308622848 | bytes 9912320 | tf_op jit(solution)/shard_map/image_encode/pallas_call | solution.py:361
  69.5 3.9 all-to-all-start
  73.4 1.8 collective-permute-start.13
  76.6 32.2 %collective-permute-done.13 = bf16[2,2,2,48,768]{4,3,2,1,0:T(8,128)(2,1)S(1)} collective-permute-done((bf16[2,2,2,48,768]{4,3,2,1,0:T(8,128)(2,1)S(1)}, bf16[2,2,2,48,768]{4,3,2,1,0:T(8,128)(2,1)S(1)}, u32[]{:S(2)}, u32[]{:S(2)}) %collective-permute-start.13) | collective-permute-done | bytes 589856 | tf_op jit(solution)/shard_map/ppermute | solution.py:713
  111.4 2.0 collective-permute-done.14
  114.4 1.7 bitcast_select_fusion
  116.1 2.3 fusion.39
  118.4 21.5 %attention_forward.1 = (bf16[1024,768]{1,0:T(8,128)(2,1)}, bf16[1024,768]{1,0:T(8,128)(2,1)}, bf16[1024,768]{1,0:T(8,128)(2,1)}, bf16[1024,768]{1,0:T(8,128)(2,1...) custom-call(s32[4]{0:T(128)} %captions.3, ...), custom_call_target="tpu_custom_call" | custom-call | flops 8053063680 | bytes 20447232 | tf_op jit(solution)/shard_map/attention_forward/pallas_call | solution.py:395
  139.9 41.7 %feed_forward.1 = (bf16[1024,768]{1,0:T(8,128)(2,1)}, bf16[1024,3072]{1,0:T(8,128)(2,1)}, bf16[1024,768]{1,0:T(8,128)(2,1)}, bf16[1024,3072]{1,0:T(8,128)(2,1)},...) custom-call(s32[4]{0:T(128)} %captions.3, ...), custom_call_target="tpu_custom_call" | custom-call | flops 20535312384 | bytes 36175872 | tf_op jit(solution)/shard_map/feed_forward/pallas_call | solution.py:590
  181.7 9.4 %grad_w_down.1 = (bf16[16,96,768]{2,1,0:T(8,128)(2,1)}, bf16[16,96,768]{2,1,0:T(8,128)(2,1)}) custom-call(s32[1]{0:T(128)} %bitcast.2.core_ref, bf16[1024,3072]{1,0:T(8,128)(2,1)} %get-tuple-element.241.refs_0_, bf16[1024,768]{1,0:T(8,128)(2,1)} %get-tuple-element.242.refs_1_), custom_call_target="tpu_custom_call" | custom-call | flops 4831838208 | bytes 11010048 | tf_op jit(solution)/shard_map/grad_w_down/pallas_call | solution.py:673
  191.3 9.6 %grad_w_up.1 = (bf16[16,96,768]{2,1,0:T(8,128)(2,1)}, bf16[16,96,768]{2,1,0:T(8,128)(2,1)}) custom-call(s32[1]{0:T(128)} %bitcast.2.core_ref, bf16[1024,768]{1,0:T(8,128)(2,1)} %get-tuple-element.232.n_ref.refs_0_, bf16[1024,3072]{1,0:T(8,128)(2,1)} %get-tuple-element.245.refs_1_), custom_call_target="tpu_custom_call" | custom-call | flops 4831838208 | bytes 11010048 | tf_op jit(solution)/shard_map/grad_w_up/pallas_call | solution.py:673
  201.2 1.8 constant_dynamic-slice_fusion.1
  203.2 2.6 collective-permute-done.17
  205.8 1.6 fusion.3
  207.4 2.6 fusion.1
  210.0 2.0 collective-permute-start.19
  213.3 23.7 %attention_backward.1 = (bf16[1024,768]{1,0:T(8,128)(2,1)}, bf16[1024,768]{1,0:T(8,128)(2,1)}, bf16[1024,768]{1,0:T(8,128)(2,1)}, bf16[512,768]{1,0:T(8,128)(2,1...) custom-call(s32[4]{0:T(128)} %counts.5, s32[1]{0:T(128)S(6)} %copy.125.offset, ...), custom_call_target="tpu_custom_call" | custom-call | flops 10066329600 | bytes 22020096 | tf_op jit(solution)/shard_map/attention_backward/pallas_call | solution.py:622
  237.0 1.8 collective-permute-done.19
  238.8 1.6 collective-permute-done.18
  240.4 4.6 all-to-all-start.1
  245.0 2.0 fusion.15
  247.1 1.7 collective-permute-start.21
  248.8 2.4 fusion.8
  253.8 11.2 %grad_w_attn.1 = (bf16[16,48,768]{2,1,0:T(8,128)(2,1)}, bf16[16,48,768]{2,1,0:T(8,128)(2,1)}, bf16[16,48,768]{2,1,0:T(8,128)(2,1)}, bf16[16,48,768]{2,1,0:T(8,128)(2,1)}) custom-call(s32[1]{0:T(128)} %bitcast.2.core_ref, bf16[1024,768]{1,0:T(8,128)(2,1)} %get-tuple-element.262.refs_0_, bf16[1024,768]{1,0:T(8,128)(2,1)} %get-tuple-element.263.refs_1_, ...), custom_call_target="tpu_custom_call" | custom-call | flops 4831838208 | bytes 11010048 | tf_op jit(solution)/shard_map/grad_w_attn/pallas_call | solution.py:673
  265.0 3.9 collective-permute-done.21
  268.9 1.7 collective-permute-done.20
  274.4 1.6 collective-permute-start.22
  278.0 9.4 %image_backward.1 = (bf16[416,768]{1,0:T(8,128)(2,1)}, bf16[416,2048]{1,0:T(8,128)(2,1)}, bf16[16,40,768]{2,1,0:T(8,128)(2,1)}, bf16[16,32,768]{2,1,0:T(8,128)(2...) custom-call(s32[1]{0:T(128)} %bitcast.2.core_ref, bf16[416,2048]{1,0:T(8,128)(2,1)} %x_ref.3, ...), custom_call_target="tpu_custom_call" | custom-call | flops 2617245696 | bytes 10092544 | tf_op jit(solution)/shard_map/image_backward/pallas_call | solution.py:428
  287.4 2.5 collective-permute-done.22
  290.0 1.7 fusion.14
  291.7 1.7 fusion.12
  295.4 2.5 collective-permute-start.25
  297.9 13.2 %collective-permute-done.25 = bf16[192,768]{1,0:T(8,128)(2,1)S(1)} collective-permute-done((bf16[192,768]{1,0:T(8,128)(2,1)S(1)}, bf16[192,768]{1,0:T(8,128)(2,1)S(1)}, u32[]{:S(2)}, u32[]{:S(2)}) %collective-permute-start.25) | collective-permute-done | bytes 294944 | tf_op jit(solution)/shard_map/ppermute | solution.py:713
  317.6 8.6 %collective-permute-done.34 = bf16[192,768]{1,0:T(8,128)(2,1)S(1)} collective-permute-done((bf16[192,768]{1,0:T(8,128)(2,1)S(1)}, bf16[192,768]{1,0:T(8,128)(2,1)S(1)}, u32[]{:S(2)}, u32[]{:S(2)}) %collective-permute-start.34) | collective-permute-done | bytes 294944 | tf_op jit(solution)/shard_map/ppermute | solution.py:713
  326.3 5.9 %collective-permute-done.31 = bf16[2,2,48,768]{3,2,0,1:T(8,128)(2,1)S(1)} collective-permute-done((bf16[2,2,48,768]{3,2,0,1:T(8,128)(2,1)S(1)}, bf16[2,2,48,768]{3,2,0,1:T(8,128)(2,1)S(1)}, u32[]{:S(2)}, u32[]{:S(2)}) %collective-permute-start.31) | collective-permute-done | bytes 294944 | tf_op jit(solution)/shard_map/ppermute | solution.py:713
  332.5 2.7 collective-permute-start.35
  336.0 1.8 collective-permute-start.37
  337.8 3.9 collective-permute-done.37
  343.3 5.4 %collective-permute-done.38 = bf16[96,768]{1,0:T(8,128)(2,1)S(1)} collective-permute-done((bf16[96,768]{1,0:T(8,128)(2,1)S(1)}, bf16[96,768]{1,0:T(8,128)(2,1)S(1)}, u32[]{:S(2)}, u32[]{:S(2)}) %collective-permute-start.38) | collective-permute-done | bytes 147488 | tf_op jit(solution)/shard_map/ppermute | solution.py:713
  349.8 2.0 collective-permute-start.40
  351.8 4.9 %collective-permute-done.40 = bf16[72,768]{1,0:T(8,128)(2,1)S(1)} collective-permute-done((bf16[72,768]{1,0:T(8,128)(2,1)S(1)}, bf16[72,768]{1,0:T(8,128)(2,1)S(1)}, u32[]{:S(2)}, u32[]{:S(2)}) %collective-permute-start.40) | collective-permute-done | bytes 110624 | tf_op jit(solution)/shard_map/ppermute | solution.py:713
  358.2 10.6 %collective-permute-done.41 = bf16[2,192,768]{2,1,0:T(8,128)(2,1)S(1)} collective-permute-done((bf16[2,192,768]{2,1,0:T(8,128)(2,1)S(1)}, bf16[2,192,768]{2,1,0:T(8,128)(2,1)S(1)}, u32[]{:S(2)}, u32[]{:S(2)}) %collective-permute-start.41) | collective-permute-done | bytes 589856 | tf_op jit(solution)/shard_map/ppermute | solution.py:713
  369.0 1.7 collective-permute-start.43
  370.7 2.6 collective-permute-start.42
  373.3 8.8 %collective-permute-done.43 = bf16[2,2,96,768]{3,2,1,0:T(8,128)(2,1)S(1)} collective-permute-done((bf16[2,2,96,768]{3,2,1,0:T(8,128)(2,1)S(1)}, bf16[2,2,96,768]{3,2,1,0:T(8,128)(2,1)S(1)}, u32[]{:S(2)}, u32[]{:S(2)}) %collective-permute-start.43) | collective-permute-done | bytes 589856 | tf_op jit(solution)/shard_map/ppermute | solution.py:713
  382.2 2.2 collective-permute-done.42
  385.7 26.8 %collective-permute-done.45 = bf16[2,2,2,96,768]{4,3,2,1,0:T(8,128)(2,1)S(1)} collective-permute-done((bf16[2,2,2,96,768]{4,3,2,1,0:T(8,128)(2,1)S(1)}, bf16[2,2,2,96,768]{4,3,2,1,0:T(8,128)(2,1)S(1)}, u32[]{:S(2)}, u32[]{:S(2)}) %collective-permute-start.45) | collective-permute-done | bytes 1179680 | tf_op jit(solution)/shard_map/ppermute | solution.py:713
  412.8 2.5 collective-permute-done.44
  417.8 4.8 %collective-permute-done.47 = bf16[2,2,2,2,96,768]{5,4,3,2,1,0:T(8,128)(2,1)S(1)} collective-permute-done((bf16[2,2,2,2,96,768]{5,4,3,2,1,0:T(8,128)(2,1)S(1)}, bf16[2,2,2,2,96,768]{5,4,3,2,1,0:T(8,128)(2,1)S(1)}, u32[]{:S(2)}, u32[]{:S(2)}) %collective-permute-start.47) | collective-permute-done | bytes 2359328 | tf_op jit(solution)/shard_map/ppermute | solution.py:713
  424.0 6.6 %join_blocks.3 = f32[3072,768]{1,0:T(8,128)} custom-call(s32[1]{0:T(128)} %bitcast.2.core_ref, bf16[16,96,768]{2,1,0:T(8,128)(2,1)} %bitcast.129, bf16[16,96,768]{2,1,0:T(8,128)(2,1)} %bitcast.137), custom_call_target="tpu_custom_call" | custom-call | bytes 14155776 | tf_op jit(solution)/shard_map/join_blocks/pallas_call | solution.py:470
  430.6 6.5 %join_blocks.2 = f32[768,3072]{1,0:T(8,128)} custom-call(s32[1]{0:T(128)} %bitcast.2.core_ref, bf16[16,96,768]{2,1,0:T(8,128)(2,1)} %bitcast.128, bf16[16,96,768]{2,1,0:T(8,128)(2,1)} %bitcast.73.refs_1_), custom_call_target="tpu_custom_call" | custom-call | bytes 14155776 | tf_op jit(solution)/shard_map/join_blocks/pallas_call | solution.py:470
  437.1 5.9 %all-gather.7.cloned.1.call-done = bf16[5376,768]{1,0:T(8,128)(2,1)} async-done(((bf16[168,768]{1,0:T(8,128)(2,1)}), bf16[5376,768]{1,0:T(8,128)(2,1)}) %all-gather.7.cloned.1.call-update) | async-done | bytes 8257552 | tf_op jit(solution)/shard_map/all_gather | solution.py:1078
  443.1 8.2 %widen_rest.1 = (f32[768,768]{1,0:T(8,128)}, f32[768,768]{1,0:T(8,128)}, f32[768,768]{1,0:T(8,128)}, f32[768,768]{1,0:T(8,128)}, f32[2048,768]{1,0:T(8,128)}, /*...) custom-call(bf16[32,168,768]{2,1,0:T(8,128)(2,1)} %bitcast.130), custom_call_target="tpu_custom_call" | custom-call | bytes 24772608 | tf_op jit(solution)/shard_map/widen_rest/pallas_call | solution.py:534
  (166 shorter events, 47.2 us)
Async XLA Ops:
  7.2 9.3 %copy-start.11 = (bf16[64,768]{1,0:T(8,128)(2,1)S(1)}, bf16[64,768]{1,0:T(8,128)(2,1)}, u32[]{:S(2)}) copy-start(bf16[64,768]{1,0:T(8,128)(2,1)} %param.33) | copy-start | bytes 294916
  7.2 132.7 %all-gather.5.cloned.1.call-start = ((), (), s32[]{:S(2)}) async-start(), calls=%async_computation.2 | async-start | bytes 9732096 | tf_op jit(solution)/shard_map/all_gather | solution.py:890
  7.2 9.2 %collective-permute-start = (bf16[64,768]{1,0:T(8,128)(2,1)}, bf16[64,768]{1,0:T(8,128)(2,1)S(1)}, u32[]{:S(2)}, u32[]{:S(2)}) collective-permute-start(bf16[64,768]{1,0:T(8,128)(2,1)} %param.33), channel_id=1, source_target_pairs={{0,16},{8,24},{16,0},{24,8},{1,17},{9,25},{17,1},{25,9},{2,18},{10... | collective-permute-start | bytes 294920 | tf_op jit(solution)/shard_map/ppermute | solution.py:713
  14.8 11.2 %copy-start.14 = (pred[2]{0:T(512)(128)(4,1)}, pred[2]{0:T(512)(128)(4,1)S(1)}, u32[]{:S(2)}) copy-start(pred[2]{0:T(512)(128)(4,1)S(1)} %iota_compare_fusion.1) | copy-start | bytes 10
  16.6 9.3 %collective-permute-start.2 = (bf16[96,768]{1,0:T(8,128)(2,1)S(1)}, bf16[96,768]{1,0:T(8,128)(2,1)S(1)}, u32[]{:S(2)}, u32[]{:S(2)}) collective-permute-start(bf16[96,768]{1,0:T(8,128)(2,1)S(1)} %pad_maximum_fusion.2), channel_id=1, source_target_pairs={{0,16},{8,24},{16,0},{24,8},{1,17},{9,25},{17,1},{25,9},{2,18},{10... | collective-permute-start | bytes 442376 | tf_op jit(solution)/shard_map/ppermute | solution.py:713
  17.3 9.8 %collective-permute-start.1 = (bf16[2,64,768]{2,1,0:T(8,128)(2,1)S(1)}, bf16[2,64,768]{2,1,0:T(8,128)(2,1)S(1)}, u32[]{:S(2)}, u32[]{:S(2)}) collective-permute-start(bf16[2,64,768]{2,1,0:T(8,128)(2,1)S(1)} %broadcast_select_fusion.17), channel_id=1, source_target_pairs={{0,8},{8,0},{16,24},{24,16},{1,9},{9,1},{17,25},{25,17},{2,10},{10... | collective-permute-start | bytes 589832 | tf_op jit(solution)/shard_map/ppermute | solution.py:713
  27.3 6.1 %collective-permute-start.4 = (bf16[2,2,32,768]{3,2,1,0:T(8,128)(2,1)S(1)}, bf16[2,2,32,768]{3,2,1,0:T(8,128)(2,1)S(1)}, u32[]{:S(2)}, u32[]{:S(2)}) collective-permute-start(bf16[2,2,32,768]{3,2,1,0:T(8,128)(2,1)S(1)} %get-tuple-element.444), channel_id=1, source_target_pairs={{0,2},{1,3},{2,0},{3,1},{4,6},{5,7},{6,4},{7,5},{8,10},{9,11},{10,... | collective-permute-start | bytes 589832 | tf_op jit(solution)/shard_map/ppermute | solution.py:713
  28.9 8.0 %collective-permute-start.5 = (bf16[2,96,768]{2,1,0:T(8,128)(2,1)S(1)}, bf16[2,96,768]{2,1,0:T(8,128)(2,1)S(1)}, u32[]{:S(2)}, u32[]{:S(2)}) collective-permute-start(bf16[2,96,768]{2,1,0:T(8,128)(2,1)S(1)} %broadcast_select_fusion.16), channel_id=1, source_target_pairs={{0,8},{8,0},{16,24},{24,16},{1,9},{9,1},{17,25},{25,17},{2,10},{10... | collective-permute-start | bytes 884744 | tf_op jit(solution)/shard_map/ppermute | solution.py:713
  29.1 5.7 %collective-permute-start.3 = (bf16[2,2,32,768]{3,2,1,0:T(8,128)(2,1)S(1)}, bf16[2,2,32,768]{3,2,1,0:T(8,128)(2,1)S(1)}, u32[]{:S(2)}, u32[]{:S(2)}) collective-permute-start(bf16[2,2,32,768]{3,2,1,0:T(8,128)(2,1)S(1)} %get-tuple-element.445), channel_id=1, source_target_pairs={{0,4},{1,5},{2,6},{3,7},{4,0},{5,1},{6,2},{7,3},{8,12},{9,13},{10,... | collective-permute-start | bytes 589832 | tf_op jit(solution)/shard_map/ppermute | solution.py:713
  37.0 11.2 %collective-permute-start.7 = (bf16[2,2,2,32,768]{4,3,2,1,0:T(8,128)(2,1)S(1)}, bf16[2,2,2,32,768]{4,3,2,1,0:T(8,128)(2,1)S(1)}, u32[]{:S(2)}, u32[]{:S(2)}) collective-permute-start(bf16[2,2,2,32,768]{4,3,2,1,0:T(8,128)(2,1)S(1)} %broadcast_select_fusion.13), channel_id=1, source_target_pairs={{0,4},{1,5},{2,6},{3,7},{4,0},{5,1},{6,2},{7,3},{8,12},{9,13},{10,... | collective-permute-start | bytes 1179656 | tf_op jit(solution)/shard_map/ppermute | solution.py:713
  38.5 10.9 %collective-permute-start.6 = (bf16[2,2,2,32,768]{4,3,2,1,0:T(8,128)(2,1)S(1)}, bf16[2,2,2,32,768]{4,3,2,1,0:T(8,128)(2,1)S(1)}, u32[]{:S(2)}, u32[]{:S(2)}) collective-permute-start(bf16[2,2,2,32,768]{4,3,2,1,0:T(8,128)(2,1)S(1)} %broadcast_select_fusion.15), channel_id=1, source_target_pairs={{0,2},{1,3},{2,0},{3,1},{4,6},{5,7},{6,4},{7,5},{8,10},{9,11},{10,... | collective-permute-start | bytes 1179656 | tf_op jit(solution)/shard_map/ppermute | solution.py:713
  49.6 8.0 %copy-start.3 = (bf16[2,2,2,2,32,768]{5,4,3,2,1,0:T(8,128)(2,1)}, bf16[2,2,2,2,32,768]{5,4,3,2,1,0:T(8,128)(2,1)S(1)}, u32[]{:S(2)}) copy-start(bf16[2,2,2,2,32,768]{5,4,3,2,1,0:T(8,128)(2,1)S(1)} %broadcast_select_fusion.8) | copy-start | bytes 2359300
  49.6 7.9 %collective-permute-start.9 = (bf16[2,2,48,768]{3,2,1,0:T(8,128)(2,1)S(1)}, bf16[2,2,48,768]{3,2,1,0:T(8,128)(2,1)S(1)}, u32[]{:S(2)}, u32[]{:S(2)}) collective-permute-start(bf16[2,2,48,768]{3,2,1,0:T(8,128)(2,1)S(1)} %get-tuple-element.440), channel_id=1, source_target_pairs={{0,2},{1,3},{2,0},{3,1},{4,6},{5,7},{6,4},{7,5},{8,10},{9,11},{10,... | collective-permute-start | bytes 884744 | tf_op jit(solution)/shard_map/ppermute | solution.py:713
  50.2 11.4 %collective-permute-start.10 = (bf16[2,2,2,2,32,768]{5,4,3,2,1,0:T(8,128)(2,1)S(1)}, bf16[2,2,2,2,32,768]{5,4,3,2,1,0:T(8,128)(2,1)}, u32[]{:S(2)}, u32[]{:S(2)}) collective-permute-start(bf16[2,2,2,2,32,768]{5,4,3,2,1,0:T(8,128)(2,1)S(1)} %broadcast_select_fusion.8), channel_id=1, source_target_pairs={{0,1},{1,0},{2,3},{3,2},{4,5},{5,4},{6,7},{7,6},{8,9},{9,8},{10,11... | collective-permute-start | bytes 2359304 | tf_op jit(solution)/shard_map/ppermute | solution.py:713
  50.2 11.4 %collective-permute-start.11 = (bf16[2,2,2,2,32,768]{5,4,3,2,1,0:T(8,128)(2,1)S(1)}, bf16[2,2,2,2,32,768]{5,4,3,2,1,0:T(8,128)(2,1)}, u32[]{:S(2)}, u32[]{:S(2)}) collective-permute-start(bf16[2,2,2,2,32,768]{5,4,3,2,1,0:T(8,128)(2,1)S(1)} %broadcast_select_fusion.7), channel_id=1, source_target_pairs={{0,1},{1,0},{2,3},{3,2},{4,5},{5,4},{6,7},{7,6},{8,9},{9,8},{10,11... | collective-permute-start | bytes 2359304 | tf_op jit(solution)/shard_map/ppermute | solution.py:713
  50.7 10.8 %collective-permute-start.8 = (bf16[2,2,48,768]{3,2,1,0:T(8,128)(2,1)S(1)}, bf16[2,2,48,768]{3,2,1,0:T(8,128)(2,1)S(1)}, u32[]{:S(2)}, u32[]{:S(2)}) collective-permute-start(bf16[2,2,48,768]{3,2,1,0:T(8,128)(2,1)S(1)} %get-tuple-element.441), channel_id=1, source_target_pairs={{0,4},{1,5},{2,6},{3,7},{4,0},{5,1},{6,2},{7,3},{8,12},{9,13},{10,... | collective-permute-start | bytes 884744 | tf_op jit(solution)/shard_map/ppermute | solution.py:713
  69.5 40.1 %all-to-all-start = ((bf16[32,16,768]{2,1,0:T(8,128)(2,1)}), bf16[32,16,768]{2,1,0:T(8,128)(2,1)}, u32[]{:S(2)}, u32[]{:S(2)}) async-start(bf16[32,16,768]{2,1,0:T(8,128)(2,1)} %bitcast.151), calls=%async_computation | async-start | bytes 1572864 | tf_op jit(solution)/shard_map/all_to_all | solution.py:914
  73.4 35.4 %collective-permute-start.13 = (bf16[2,2,2,48,768]{4,3,2,1,0:T(8,128)(2,1)S(1)}, bf16[2,2,2,48,768]{4,3,2,1,0:T(8,128)(2,1)S(1)}, u32[]{:S(2)}, u32[]{:S(2)}) collective-permute-start(bf16[2,2,2,48,768]{4,3,2,1,0:T(8,128)(2,1)S(1)} %broadcast_select_fusion.10), channel_id=1, source_target_pairs={{0,4},{1,5},{2,6},{3,7},{4,0},{5,1},{6,2},{7,3},{8,12},{9,13},{10,... | collective-permute-start | bytes 1769480 | tf_op jit(solution)/shard_map/ppermute | solution.py:713
  75.2 34.2 %collective-permute-start.12 = (bf16[2,2,2,48,768]{4,3,2,1,0:T(8,128)(2,1)S(1)}, bf16[2,2,2,48,768]{4,3,2,1,0:T(8,128)(2,1)S(1)}, u32[]{:S(2)}, u32[]{:S(2)}) collective-permute-start(bf16[2,2,2,48,768]{4,3,2,1,0:T(8,128)(2,1)S(1)} %broadcast_select_fusion.12), channel_id=1, source_target_pairs={{0,2},{1,3},{2,0},{3,1},{4,6},{5,7},{6,4},{7,5},{8,10},{9,11},{10,... | collective-permute-start | bytes 1769480 | tf_op jit(solution)/shard_map/ppermute | solution.py:713
  109.5 3.8 collective-permute-start.14
  109.6 4.8 %collective-permute-start.15 = (bf16[2,2,2,2,48,768]{5,4,3,2,1,0:T(8,128)(2,1)S(1)}, bf16[2,2,2,2,48,768]{5,4,3,2,1,0:T(8,128)(2,1)}, u32[]{:S(2)}, u32[]{:S(2)}) collective-permute-start(bf16[2,2,2,2,48,768]{5,4,3,2,1,0:T(8,128)(2,1)S(1)} %broadcast_select_fusion.5), channel_id=1, source_target_pairs={{0,1},{1,0},{2,3},{3,2},{4,5},{5,4},{6,7},{7,6},{8,9},{9,8},{10,11... | collective-permute-start | bytes 3538952 | tf_op jit(solution)/shard_map/ppermute | solution.py:713
  191.1 11.9 %collective-permute-start.16 = (bf16[16,96,768]{2,1,0:T(8,128)(2,1)}, bf16[16,96,768]{2,1,0:T(8,128)(2,1)S(1)}, u32[]{:S(2)}, u32[]{:S(2)}) collective-permute-start(bf16[16,96,768]{2,1,0:T(8,128)(2,1)} %get-tuple-element.244), channel_id=1, source_target_pairs={{0,1},{1,0},{2,3},{3,2},{4,5},{5,4},{6,7},{7,6},{8,9},{9,8},{10,11... | collective-permute-start | bytes 7077896 | tf_op jit(solution)/shard_map/ppermute | solution.py:713
  200.8 4.9 %collective-permute-start.17 = (bf16[16,96,768]{2,1,0:T(8,128)(2,1)}, bf16[16,96,768]{2,1,0:T(8,128)(2,1)}, u32[]{:S(2)}, u32[]{:S(2)}) collective-permute-start(bf16[16,96,768]{2,1,0:T(8,128)(2,1)} %get-tuple-element.247), channel_id=1, source_target_pairs={{0,1},{1,0},{2,3},{3,2},{4,5},{5,4},{6,7},{7,6},{8,9},{9,8},{10,11... | collective-permute-start | bytes 7077896 | tf_op jit(solution)/shard_map/ppermute | solution.py:713
  203.0 2.8 copy-start.4
  210.0 28.8 %collective-permute-start.19 = (bf16[2,2,2,96,768]{4,3,0,1,2:T(8,128)(2,1)}, bf16[2,2,2,96,768]{4,3,0,1,2:T(8,128)(2,1)}, u32[]{:S(2)}, u32[]{:S(2)}) collective-permute-start(bf16[2,2,2,96,768]{4,3,0,1,2:T(8,128)(2,1)} %fusion.1), channel_id=1, source_target_pairs={{0,4},{1,5},{2,6},{3,7},{4,0},{5,1},{6,2},{7,3},{8,12},{9,13},{10,... | collective-permute-start | bytes 3538952 | tf_op jit(solution)/shard_map/ppermute | solution.py:713
  212.3 28.1 %collective-permute-start.18 = (bf16[2,2,2,96,768]{4,3,0,1,2:T(8,128)(2,1)S(1)}, bf16[2,2,2,96,768]{4,3,0,1,2:T(8,128)(2,1)}, u32[]{:S(2)}, u32[]{:S(2)}) collective-permute-start(bf16[2,2,2,96,768]{4,3,0,1,2:T(8,128)(2,1)S(1)} %fusion), channel_id=1, source_target_pairs={{0,2},{1,3},{2,0},{3,1},{4,6},{5,7},{6,4},{7,5},{8,10},{9,11},{10,... | collective-permute-start | bytes 3538952 | tf_op jit(solution)/shard_map/ppermute | solution.py:713
  240.4 30.2 %all-to-all-start.1 = ((bf16[32,16,768]{2,1,0:T(8,128)(2,1)}), bf16[32,16,768]{2,1,0:T(8,128)(2,1)}, u32[]{:S(2)}, u32[]{:S(2)}) async-start(bf16[32,16,768]{2,1,0:T(8,128)(2,1)} %bitcast.150), calls=%async_computation.1 | async-start | bytes 1572864 | tf_op jit(solution)/shard_map/all_to_all | solution.py:1026
  245.0 198.1 %all-gather.7.cloned.1.call-start = ((), (), s32[]{:S(2)}) async-start(), calls=%async_computation.3 | async-start | bytes 8515584 | tf_op jit(solution)/shard_map/all_gather | solution.py:1078
  247.1 21.8 %collective-permute-start.21 = (bf16[2,2,96,768]{3,2,1,0:T(8,128)(2,1)}, bf16[2,2,96,768]{3,2,1,0:T(8,128)(2,1)}, u32[]{:S(2)}, u32[]{:S(2)}) collective-permute-start(bf16[2,2,96,768]{3,2,1,0:T(8,128)(2,1)} %fusion.15), channel_id=1, source_target_pairs={{0,2},{1,3},{2,0},{3,1},{4,6},{5,7},{6,4},{7,5},{8,10},{9,11},{10,... | collective-permute-start | bytes 1769480 | tf_op jit(solution)/shard_map/ppermute | solution.py:713
  251.1 19.5 %collective-permute-start.20 = (bf16[2,2,96,768]{3,2,0,1:T(8,128)(2,1)}, bf16[2,2,96,768]{3,2,0,1:T(8,128)(2,1)}, u32[]{:S(2)}, u32[]{:S(2)}) collective-permute-start(bf16[2,2,96,768]{3,2,0,1:T(8,128)(2,1)} %get-tuple-element.408), channel_id=1, source_target_pairs={{0,4},{1,5},{2,6},{3,7},{4,0},{5,1},{6,2},{7,3},{8,12},{9,13},{10,... | collective-permute-start | bytes 1769480 | tf_op jit(solution)/shard_map/ppermute | solution.py:713
  272.9 3.6 copy-start.13
  273.9 16.0 %collective-permute-start.23 = (bf16[16,48,768]{2,1,0:T(8,128)(2,1)}, bf16[16,48,768]{2,1,0:T(8,128)(2,1)}, u32[]{:S(2)}, u32[]{:S(2)}) collective-permute-start(bf16[16,48,768]{2,1,0:T(8,128)(2,1)} %get-tuple-element.292), channel_id=1, source_target_pairs={{0,1},{1,0},{2,3},{3,2},{4,5},{5,4},{6,7},{7,6},{8,9},{9,8},{10,11... | collective-permute-start | bytes 3538952 | tf_op jit(solution)/shard_map/ppermute | solution.py:713
  273.9 16.0 %collective-permute-start.24 = (bf16[16,48,768]{2,1,0:T(8,128)(2,1)}, bf16[16,48,768]{2,1,0:T(8,128)(2,1)}, u32[]{:S(2)}, u32[]{:S(2)}) collective-permute-start(bf16[16,48,768]{2,1,0:T(8,128)(2,1)} %get-tuple-element.294), channel_id=1, source_target_pairs={{0,1},{1,0},{2,3},{3,2},{4,5},{5,4},{6,7},{7,6},{8,9},{9,8},{10,11... | collective-permute-start | bytes 3538952 | tf_op jit(solution)/shard_map/ppermute | solution.py:713
  274.4 15.4 %collective-permute-start.22 = (bf16[2,192,768]{2,1,0:T(8,128)(2,1)}, bf16[2,192,768]{2,1,0:T(8,128)(2,1)S(1)}, u32[]{:S(2)}, u32[]{:S(2)}) collective-permute-start(bf16[2,192,768]{2,1,0:T(8,128)(2,1)} %fusion.16), channel_id=1, source_target_pairs={{0,8},{8,0},{16,24},{24,16},{1,9},{9,1},{17,25},{25,17},{2,10},{10... | collective-permute-start | bytes 1769480 | tf_op jit(solution)/shard_map/ppermute | solution.py:713
  287.4 2.6 copy-start.7
  293.4 19.1 %copy-start.9 = (bf16[16,32,768]{2,1,0:T(8,128)(2,1)S(1)}, bf16[16,32,768]{2,1,0:T(8,128)(2,1)}, u32[]{:S(2)}) copy-start(bf16[16,32,768]{2,1,0:T(8,128)(2,1)} %get-tuple-element.317) | copy-start | bytes 2359300
  293.4 17.7 %collective-permute-start.28 = (bf16[16,40,768]{2,1,0:T(8,128)(2,1)S(1)}, bf16[16,40,768]{2,1,0:T(8,128)(2,1)S(1)}, u32[]{:S(2)}, u32[]{:S(2)}) collective-permute-start(bf16[16,40,768]{2,1,0:T(8,128)(2,1)S(1)} %copy-done.16), channel_id=1, source_target_pairs={{0,1},{1,0},{2,3},{3,2},{4,5},{5,4},{6,7},{7,6},{8,9},{9,8},{10,11... | collective-permute-start | bytes 2949128 | tf_op jit(solution)/shard_map/ppermute | solution.py:713
  293.5 17.6 %collective-permute-start.29 = (bf16[16,32,768]{2,1,0:T(8,128)(2,1)S(1)}, bf16[16,32,768]{2,1,0:T(8,128)(2,1)S(1)}, u32[]{:S(2)}, u32[]{:S(2)}) collective-permute-start(bf16[16,32,768]{2,1,0:T(8,128)(2,1)S(1)} %copy-done.17), channel_id=1, source_target_pairs={{0,1},{1,0},{2,3},{3,2},{4,5},{5,4},{6,7},{7,6},{8,9},{9,8},{10,11... | collective-permute-start | bytes 2359304 | tf_op jit(solution)/shard_map/ppermute | solution.py:713
  294.0 17.1 %collective-permute-start.27 = (bf16[2,2,2,48,768]{4,3,0,1,2:T(8,128)(2,1)S(1)}, bf16[2,2,2,48,768]{4,3,0,1,2:T(8,128)(2,1)S(1)}, u32[]{:S(2)}, u32[]{:S(2)}) collective-permute-start(bf16[2,2,2,48,768]{4,3,0,1,2:T(8,128)(2,1)S(1)} %get-tuple-element.404), channel_id=1, source_target_pairs={{0,4},{1,5},{2,6},{3,7},{4,0},{5,1},{6,2},{7,3},{8,12},{9,13},{10,... | collective-permute-start | bytes 1769480 | tf_op jit(solution)/shard_map/ppermute | solution.py:713
  294.8 16.3 %collective-permute-start.26 = (bf16[2,2,2,48,768]{4,3,0,1,2:T(8,128)(2,1)S(1)}, bf16[2,2,2,48,768]{4,3,0,1,2:T(8,128)(2,1)S(1)}, u32[]{:S(2)}, u32[]{:S(2)}) collective-permute-start(bf16[2,2,2,48,768]{4,3,0,1,2:T(8,128)(2,1)S(1)} %get-tuple-element.406), channel_id=1, source_target_pairs={{0,2},{1,3},{2,0},{3,1},{4,6},{5,7},{6,4},{7,5},{8,10},{9,11},{10,... | collective-permute-start | bytes 1769480 | tf_op jit(solution)/shard_map/ppermute | solution.py:713
  295.4 15.7 %collective-permute-start.25 = (bf16[192,768]{1,0:T(8,128)(2,1)S(1)}, bf16[192,768]{1,0:T(8,128)(2,1)S(1)}, u32[]{:S(2)}, u32[]{:S(2)}) collective-permute-start(bf16[192,768]{1,0:T(8,128)(2,1)S(1)} %get-tuple-element.430), channel_id=1, source_target_pairs={{0,16},{8,24},{16,0},{24,8},{1,17},{9,25},{17,1},{25,9},{2,18},{10... | collective-permute-start | bytes 884744 | tf_op jit(solution)/shard_map/ppermute | solution.py:713
  311.2 2.9 copy-start.8
  311.2 15.0 %collective-permute-start.34 = (bf16[192,768]{1,0:T(8,128)(2,1)S(1)}, bf16[192,768]{1,0:T(8,128)(2,1)S(1)}, u32[]{:S(2)}, u32[]{:S(2)}) collective-permute-start(bf16[192,768]{1,0:T(8,128)(2,1)S(1)} %add_convert_fusion.22), channel_id=1, source_target_pairs={{0,16},{8,24},{16,0},{24,8},{1,17},{9,25},{17,1},{25,9},{2,18},{10... | collective-permute-start | bytes 884744 | tf_op jit(solution)/shard_map/ppermute | solution.py:713
  312.7 19.5 %collective-permute-start.33 = (bf16[2,2,2,32,768]{4,3,0,1,2:T(8,128)(2,1)S(1)}, bf16[2,2,2,32,768]{4,3,0,1,2:T(8,128)(2,1)S(1)}, u32[]{:S(2)}, u32[]{:S(2)}) collective-permute-start(bf16[2,2,2,32,768]{4,3,0,1,2:T(8,128)(2,1)S(1)} %get-tuple-element.421), channel_id=1, source_target_pairs={{0,4},{1,5},{2,6},{3,7},{4,0},{5,1},{6,2},{7,3},{8,12},{9,13},{10,... | collective-permute-start | bytes 1179656 | tf_op jit(solution)/shard_map/ppermute | solution.py:713
  314.4 17.9 %collective-permute-start.32 = (bf16[2,2,2,40,768]{4,3,0,1,2:T(8,128)(2,1)S(1)}, bf16[2,2,2,40,768]{4,3,0,1,2:T(8,128)(2,1)S(1)}, u32[]{:S(2)}, u32[]{:S(2)}) collective-permute-start(bf16[2,2,2,40,768]{4,3,0,1,2:T(8,128)(2,1)S(1)} %get-tuple-element.419), channel_id=1, source_target_pairs={{0,2},{1,3},{2,0},{3,1},{4,6},{5,7},{6,4},{7,5},{8,10},{9,11},{10,... | collective-permute-start | bytes 1474568 | tf_op jit(solution)/shard_map/ppermute | solution.py:713
  315.1 11.1 %copy-start.15 = (pred[2]{0:T(512)(128)(4,1)S(1)}, pred[2]{0:T(512)(128)(4,1)}, u32[]{:S(2)}) copy-start(pred[2]{0:T(512)(128)(4,1)} %copy-done.14) | copy-start | bytes 10
  315.1 17.1 %collective-permute-start.31 = (bf16[2,2,48,768]{3,2,0,1:T(8,128)(2,1)S(1)}, bf16[2,2,48,768]{3,2,0,1:T(8,128)(2,1)S(1)}, u32[]{:S(2)}, u32[]{:S(2)}) collective-permute-start(bf16[2,2,48,768]{3,2,0,1:T(8,128)(2,1)S(1)} %get-tuple-element.426), channel_id=1, source_target_pairs={{0,2},{1,3},{2,0},{3,1},{4,6},{5,7},{6,4},{7,5},{8,10},{9,11},{10,... | collective-permute-start | bytes 884744 | tf_op jit(solution)/shard_map/ppermute | solution.py:713
  316.8 15.4 %collective-permute-start.30 = (bf16[2,2,48,768]{3,2,0,1:T(8,128)(2,1)S(1)}, bf16[2,2,48,768]{3,2,0,1:T(8,128)(2,1)S(1)}, u32[]{:S(2)}, u32[]{:S(2)}) collective-permute-start(bf16[2,2,48,768]{3,2,0,1:T(8,128)(2,1)S(1)} %get-tuple-element.428), channel_id=1, source_target_pairs={{0,4},{1,5},{2,6},{3,7},{4,0},{5,1},{6,2},{7,3},{8,12},{9,13},{10,... | collective-permute-start | bytes 884744 | tf_op jit(solution)/shard_map/ppermute | solution.py:713
  332.5 9.2 %collective-permute-start.35 = (bf16[2,96,768]{2,1,0:T(8,128)(2,1)S(1)}, bf16[2,96,768]{2,1,0:T(8,128)(2,1)S(1)}, u32[]{:S(2)}, u32[]{:S(2)}) collective-permute-start(bf16[2,96,768]{2,1,0:T(8,128)(2,1)S(1)} %get-tuple-element.424), channel_id=1, source_target_pairs={{0,8},{8,0},{16,24},{24,16},{1,9},{9,1},{17,25},{25,17},{2,10},{10... | collective-permute-start | bytes 884744 | tf_op jit(solution)/shard_map/ppermute | solution.py:713
  335.4 6.4 %collective-permute-start.36 = (bf16[2,2,40,768]{3,2,0,1:T(8,128)(2,1)S(1)}, bf16[2,2,40,768]{3,2,0,1:T(8,128)(2,1)S(1)}, u32[]{:S(2)}, u32[]{:S(2)}) collective-permute-start(bf16[2,2,40,768]{3,2,0,1:T(8,128)(2,1)S(1)} %get-tuple-element.432), channel_id=1, source_target_pairs={{0,4},{1,5},{2,6},{3,7},{4,0},{5,1},{6,2},{7,3},{8,12},{9,13},{10,... | collective-permute-start | bytes 737288 | tf_op jit(solution)/shard_map/ppermute | solution.py:713
  336.0 5.7 %collective-permute-start.37 = (bf16[2,2,32,768]{3,2,0,1:T(8,128)(2,1)S(1)}, bf16[2,2,32,768]{3,2,0,1:T(8,128)(2,1)S(1)}, u32[]{:S(2)}, u32[]{:S(2)}) collective-permute-start(bf16[2,2,32,768]{3,2,0,1:T(8,128)(2,1)S(1)} %get-tuple-element.436), channel_id=1, source_target_pairs={{0,2},{1,3},{2,0},{3,1},{4,6},{5,7},{6,4},{7,5},{8,10},{9,11},{10,... | collective-permute-start | bytes 589832 | tf_op jit(solution)/shard_map/ppermute | solution.py:713
  342.1 7.7 %collective-permute-start.39 = (bf16[2,72,768]{2,1,0:T(8,128)(2,1)S(1)}, bf16[2,72,768]{2,1,0:T(8,128)(2,1)S(1)}, u32[]{:S(2)}, u32[]{:S(2)}) collective-permute-start(bf16[2,72,768]{2,1,0:T(8,128)(2,1)S(1)} %get-tuple-element.434), channel_id=1, source_target_pairs={{0,8},{8,0},{16,24},{24,16},{1,9},{9,1},{17,25},{25,17},{2,10},{10... | collective-permute-start | bytes 663560 | tf_op jit(solution)/shard_map/ppermute | solution.py:713
  342.6 6.1 %collective-permute-start.38 = (bf16[96,768]{1,0:T(8,128)(2,1)S(1)}, bf16[96,768]{1,0:T(8,128)(2,1)S(1)}, u32[]{:S(2)}, u32[]{:S(2)}) collective-permute-start(bf16[96,768]{1,0:T(8,128)(2,1)S(1)} %get-tuple-element.438), channel_id=1, source_target_pairs={{0,16},{8,24},{16,0},{24,8},{1,17},{9,25},{17,1},{25,9},{2,18},{10... | collective-permute-start | bytes 442376 | tf_op jit(solution)/shard_map/ppermute | solution.py:713
  349.8 6.8 %collective-permute-start.40 = (bf16[72,768]{1,0:T(8,128)(2,1)S(1)}, bf16[72,768]{1,0:T(8,128)(2,1)S(1)}, u32[]{:S(2)}, u32[]{:S(2)}) collective-permute-start(bf16[72,768]{1,0:T(8,128)(2,1)S(1)} %get-tuple-element.442), channel_id=1, source_target_pairs={{0,16},{8,24},{16,0},{24,8},{1,17},{9,25},{17,1},{25,9},{2,18},{10... | collective-permute-start | bytes 331784 | tf_op jit(solution)/shard_map/ppermute | solution.py:713
  357.4 11.3 %collective-permute-start.41 = (bf16[2,192,768]{2,1,0:T(8,128)(2,1)S(1)}, bf16[2,192,768]{2,1,0:T(8,128)(2,1)S(1)}, u32[]{:S(2)}, u32[]{:S(2)}) collective-permute-start(bf16[2,192,768]{2,1,0:T(8,128)(2,1)S(1)} %broadcast_select_fusion.9), channel_id=1, source_target_pairs={{0,8},{8,0},{16,24},{24,16},{1,9},{9,1},{17,25},{25,17},{2,10},{10... | collective-permute-start | bytes 1769480 | tf_op jit(solution)/shard_map/ppermute | solution.py:713
  369.0 13.0 %collective-permute-start.43 = (bf16[2,2,96,768]{3,2,1,0:T(8,128)(2,1)S(1)}, bf16[2,2,96,768]{3,2,1,0:T(8,128)(2,1)S(1)}, u32[]{:S(2)}, u32[]{:S(2)}) collective-permute-start(bf16[2,2,96,768]{3,2,1,0:T(8,128)(2,1)S(1)} %get-tuple-element.422), channel_id=1, source_target_pairs={{0,2},{1,3},{2,0},{3,1},{4,6},{5,7},{6,4},{7,5},{8,10},{9,11},{10,... | collective-permute-start | bytes 1769480 | tf_op jit(solution)/shard_map/ppermute | solution.py:713
  370.7 13.7 %collective-permute-start.42 = (bf16[2,2,96,768]{3,2,1,0:T(8,128)(2,1)S(1)}, bf16[2,2,96,768]{3,2,1,0:T(8,128)(2,1)S(1)}, u32[]{:S(2)}, u32[]{:S(2)}) collective-permute-start(bf16[2,2,96,768]{3,2,1,0:T(8,128)(2,1)S(1)} %get-tuple-element.423), channel_id=1, source_target_pairs={{0,4},{1,5},{2,6},{3,7},{4,0},{5,1},{6,2},{7,3},{8,12},{9,13},{10,... | collective-permute-start | bytes 1769480 | tf_op jit(solution)/shard_map/ppermute | solution.py:713
  384.6 27.9 %collective-permute-start.45 = (bf16[2,2,2,96,768]{4,3,2,1,0:T(8,128)(2,1)S(1)}, bf16[2,2,2,96,768]{4,3,2,1,0:T(8,128)(2,1)S(1)}, u32[]{:S(2)}, u32[]{:S(2)}) collective-permute-start(bf16[2,2,2,96,768]{4,3,2,1,0:T(8,128)(2,1)S(1)} %broadcast_select_fusion.2), channel_id=1, source_target_pairs={{0,4},{1,5},{2,6},{3,7},{4,0},{5,1},{6,2},{7,3},{8,12},{9,13},{10,... | collective-permute-start | bytes 3538952 | tf_op jit(solution)/shard_map/ppermute | solution.py:713
  385.7 29.5 %collective-permute-start.44 = (bf16[2,2,2,96,768]{4,3,2,1,0:T(8,128)(2,1)S(1)}, bf16[2,2,2,96,768]{4,3,2,1,0:T(8,128)(2,1)S(1)}, u32[]{:S(2)}, u32[]{:S(2)}) collective-permute-start(bf16[2,2,2,96,768]{4,3,2,1,0:T(8,128)(2,1)S(1)} %broadcast_select_fusion.4), channel_id=1, source_target_pairs={{0,2},{1,3},{2,0},{3,1},{4,6},{5,7},{6,4},{7,5},{8,10},{9,11},{10,... | collective-permute-start | bytes 3538952 | tf_op jit(solution)/shard_map/ppermute | solution.py:713
  412.7 2.9 copy-start
  412.8 4.2 copy-start.10
  412.8 4.2 copy-start.12
  415.5 7.1 %collective-permute-start.47 = (bf16[2,2,2,2,96,768]{5,4,3,2,1,0:T(8,128)(2,1)S(1)}, bf16[2,2,2,2,96,768]{5,4,3,2,1,0:T(8,128)(2,1)S(1)}, u32[]{:S(2)}, u32[]{:S(2)}) collective-permute-start(bf16[2,2,2,2,96,768]{5,4,3,2,1,0:T(8,128)(2,1)S(1)} %broadcast_select_fusion.1), channel_id=1, source_target_pairs={{0,1},{1,0},{2,3},{3,2},{4,5},{5,4},{6,7},{7,6},{8,9},{9,8},{10,11... | collective-permute-start | bytes 7077896 | tf_op jit(solution)/shard_map/ppermute | solution.py:713
  415.6 15.0 %collective-permute-start.46 = (bf16[2,2,2,2,96,768]{5,4,3,2,1,0:T(8,128)(2,1)S(1)}, bf16[2,2,2,2,96,768]{5,4,3,2,1,0:T(8,128)(2,1)}, u32[]{:S(2)}, u32[]{:S(2)}) collective-permute-start(bf16[2,2,2,2,96,768]{5,4,3,2,1,0:T(8,128)(2,1)S(1)} %broadcast_select_fusion), channel_id=1, source_target_pairs={{0,1},{1,0},{2,3},{3,2},{4,5},{5,4},{6,7},{7,6},{8,9},{9,8},{10,11... | collective-permute-start | bytes 7077896 | tf_op jit(solution)/shard_map/ppermute | solution.py:713
  (6 other events, 9.9 us)
Sparse Core Ops, SparseCore 0:
  27.3 100.8 all-gather.4
  357.5 85.4 all-gather.6

commit v6 on v5

--- a/solution.py
+++ b/solution.py
@@ -895,7 +895,7 @@
             part.stage()
         fence([*img, attn])
     attn = attn.split(2 * cut, orders)
-    img_halves = [t for part in img for t in part.halves()]
+    img_halves = fence(attn, *[t for part in img for t in part.halves()])
     for part in attn:
         part.stage()
     device_count = lax.axis_size(axes)

time: 467 us -> 461 us (0.987)
  waiting for transfers between devices: 189 us -> 182 us
    ppermute x48, waiting for transfers between devices: 183 us -> 173 us  [swap_bit(): return lax.ppermute(tensor, name, [(i, i ^ step) for i in range(size)])]
    all_to_all x1, waiting for transfers between devices: 0.01 us -> 4.9 us  [body(): lax.all_to_all(encoded, axes, split_axis=0, concat_axis=0, tiled=True)]
  transfers between devices with their start and end apart: 52 -> 52, of which waited for: 34 -> 37; matrix products, arithmetic and copies ran while one was open for 5% -> 5% of each run, Pallas kernels for 21% -> 21%
where the time goes in v6:
time: 461 us; the launch traced here: 453 us
  waiting for transfers between devices  182 us (39%)
  Pallas kernels  156 us (34%)
  starting transfers between devices  61.1 us (13%)
  other arithmetic  24.7 us (5%)
  between operations  15.9 us (3%)
  local copies, waits for them, and re-layouts  12.5 us (3%)
    ppermute x48, waiting for transfers between devices, swap_bit(): return lax.ppermute(tensor, name, [(i, i ^ step) for i in range(size)])  173 us
    ppermute x48, starting transfers between devices, swap_bit(): return lax.ppermute(tensor, name, [(i, i ^ step) for i in range(size)])  53.3 us
    pallas_call x1, Pallas kernels, run_feed_forward(): pl.pallas_call(feed_forward, out_shape=shapes, grid_spec=pltpu.PrefetchSc...  41.7 us
    pallas_call x3, Pallas kernels, weight_grads(): pl.pallas_call(functools.partial(weight_grad_kernel, lhs_of, rhs_of, grou...  30.2 us
    pallas_call x1, Pallas kernels, run_attention_backward(): pl.pallas_call(functools.partial(attention_backward, *geometry), out_shap...  23.7 us
    pallas_call x1, Pallas kernels, run_attention_forward(): pl.pallas_call(functools.partial(attention_forward, *geometry), out_shape...  21.5 us
    convert_element_type x25, other arithmetic, add_low(): return (kept.astype(f32) + came.astype(f32)).astype(bf16)  16.4 us
    pallas_call x2, Pallas kernels, join_blocks(): pl.pallas_call(join_kernel, out_shape=jax.ShapeDtypeStruct(shape, f32), g...  13.1 us
  transfers between devices with their start and end apart: 52, of which 37 were waited for; matrix products, arithmetic and copies ran while one was open for 5% of the time, Pallas kernels for 21%

profile of v6, /device:TPU:0, one launch (start us, length us, event | category | flops | bytes accessed | tf_op | source)
XLA Modules:
  0.0 453.0 jit_solution(10588126690642037325)
XLA Ops:
  7.2 4.1 collective-permute-start
  12.3 1.6 pad_maximum_fusion
  14.8 1.7 collective-permute-done
  17.3 3.5 collective-permute-start.1
  20.7 5.1 %collective-permute-done.2 = bf16[96,768]{1,0:T(8,128)(2,1)S(1)} collective-permute-done((bf16[96,768]{1,0:T(8,128)(2,1)S(1)}, bf16[96,768]{1,0:T(8,128)(2,1)S(1)}, u32[]{:S(2)}, u32[]{:S(2)}) %collective-permute-start.2) | collective-permute-done | bytes 147488 | tf_op jit(solution)/shard_map/ppermute | solution.py:713
  30.6 2.8 collective-permute-done.4
  34.9 1.9 collective-permute-done.5
  37.0 1.6 collective-permute-start.7
  39.1 9.1 %collective-permute-done.7 = bf16[2,2,2,32,768]{4,3,2,1,0:T(8,128)(2,1)S(1)} collective-permute-done((bf16[2,2,2,32,768]{4,3,2,1,0:T(8,128)(2,1)S(1)}, bf16[2,2,2,32,768]{4,3,2,1,0:T(8,128)(2,1)S(1)}, u32[]{:S(2)}, u32[]{:S(2)}) %collective-permute-start.7) | collective-permute-done | bytes 393248 | tf_op jit(solution)/shard_map/ppermute | solution.py:713
  50.2 1.7 collective-permute-done.8
  54.1 7.7 %image_encode.1 = (f32[416,768]{1,0:T(8,128)}, bf16[512,768]{1,0:T(8,128)(2,1)}, bf16[32,64,768]{2,1,0:T(8,128)(2,1)}) custom-call(s32[1]{0:T(128)} %bitcast.6.core_ref, bf16[416,2048]{1,0:T(8,128)(2,1)} %x_ref.3, bf16[4,416]{1,0:T(4,128)(2,1)} %box_ref.3, bf16[4,768]{1,0:T(4,128)(2,1)} %wb_ref.1, f32[768]{0:T(1024)} %bi_ref.1, f32[768]{0:T(1024)} %gr_ref.3, ...), custom_call_target="tpu_custom_call" | custom-call | flops 1308622848 | bytes 9912320 | tf_op jit(solution)/shard_map/image_encode/pallas_call | solution.py:361
  61.8 4.4 collective-permute-done.11
  66.7 4.4 all-to-all-start
  71.1 1.8 collective-permute-start.13
  74.4 26.4 %collective-permute-done.13 = bf16[2,2,2,48,768]{4,3,2,1,0:T(8,128)(2,1)S(1)} collective-permute-done((bf16[2,2,2,48,768]{4,3,2,1,0:T(8,128)(2,1)S(1)}, bf16[2,2,2,48,768]{4,3,2,1,0:T(8,128)(2,1)S(1)}, u32[]{:S(2)}, u32[]{:S(2)}) %collective-permute-start.13) | collective-permute-done | bytes 589856 | tf_op jit(solution)/shard_map/ppermute | solution.py:713
  101.2 4.9 %all-to-all-done = bf16[32,16,768]{2,1,0:T(8,128)(2,1)} async-done(((bf16[32,16,768]{2,1,0:T(8,128)(2,1)}), bf16[32,16,768]{2,1,0:T(8,128)(2,1)}, u32[]{:S(2)}, u32[]{:S(2)}) %all-to-all-start) | async-done | bytes 786464 | tf_op jit(solution)/shard_map/all_to_all | solution.py:914
  107.9 2.1 collective-permute-done.14
  110.9 1.8 bitcast_select_fusion
  112.7 2.2 fusion.39
  115.0 21.5 %attention_forward.1 = (bf16[1024,768]{1,0:T(8,128)(2,1)}, bf16[1024,768]{1,0:T(8,128)(2,1)}, bf16[1024,768]{1,0:T(8,128)(2,1)}, bf16[1024,768]{1,0:T(8,128)(2,1...) custom-call(s32[4]{0:T(128)} %captions.3, ...), custom_call_target="tpu_custom_call" | custom-call | flops 8053063680 | bytes 20447232 | tf_op jit(solution)/shard_map/attention_forward/pallas_call | solution.py:395
  136.5 41.7 %feed_forward.1 = (bf16[1024,768]{1,0:T(8,128)(2,1)}, bf16[1024,3072]{1,0:T(8,128)(2,1)}, bf16[1024,768]{1,0:T(8,128)(2,1)}, bf16[1024,3072]{1,0:T(8,128)(2,1)},...) custom-call(s32[4]{0:T(128)} %captions.3, ...), custom_call_target="tpu_custom_call" | custom-call | flops 20535312384 | bytes 36175872 | tf_op jit(solution)/shard_map/feed_forward/pallas_call | solution.py:590
  178.2 9.4 %grad_w_down.1 = (bf16[16,96,768]{2,1,0:T(8,128)(2,1)}, bf16[16,96,768]{2,1,0:T(8,128)(2,1)}) custom-call(s32[1]{0:T(128)} %bitcast.6.core_ref, bf16[1024,3072]{1,0:T(8,128)(2,1)} %get-tuple-element.253.refs_0_, bf16[1024,768]{1,0:T(8,128)(2,1)} %get-tuple-element.254.refs_1_), custom_call_target="tpu_custom_call" | custom-call | flops 4831838208 | bytes 11010048 | tf_op jit(solution)/shard_map/grad_w_down/pallas_call | solution.py:673
  187.9 9.6 %grad_w_up.1 = (bf16[16,96,768]{2,1,0:T(8,128)(2,1)}, bf16[16,96,768]{2,1,0:T(8,128)(2,1)}) custom-call(s32[1]{0:T(128)} %bitcast.6.core_ref, bf16[1024,768]{1,0:T(8,128)(2,1)} %get-tuple-element.244.n_ref.refs_0_, bf16[1024,3072]{1,0:T(8,128)(2,1)} %get-tuple-element.257.refs_1_), custom_call_target="tpu_custom_call" | custom-call | flops 4831838208 | bytes 11010048 | tf_op jit(solution)/shard_map/grad_w_up/pallas_call | solution.py:673
  197.8 1.8 constant_dynamic-slice_fusion.1
  199.8 2.7 collective-permute-done.17
  202.4 1.6 fusion.3
  204.0 2.6 fusion.1
  209.0 23.7 %attention_backward.1 = (bf16[1024,768]{1,0:T(8,128)(2,1)}, bf16[1024,768]{1,0:T(8,128)(2,1)}, bf16[1024,768]{1,0:T(8,128)(2,1)}, bf16[512,768]{1,0:T(8,128)(2,1...) custom-call(s32[4]{0:T(128)} %counts.5, s32[1]{0:T(128)S(6)} %copy.125.offset, ...), custom_call_target="tpu_custom_call" | custom-call | flops 10066329600 | bytes 22020096 | tf_op jit(solution)/shard_map/attention_backward/pallas_call | solution.py:622
  232.7 2.3 collective-permute-done.19
  235.4 3.3 all-to-all-start.1
  238.8 2.0 fusion.15
  240.9 1.6 collective-permute-start.21
  242.4 2.4 fusion.8
  247.5 11.2 %grad_w_attn.1 = (bf16[16,48,768]{2,1,0:T(8,128)(2,1)}, bf16[16,48,768]{2,1,0:T(8,128)(2,1)}, bf16[16,48,768]{2,1,0:T(8,128)(2,1)}, bf16[16,48,768]{2,1,0:T(8,128)(2,1)}) custom-call(s32[1]{0:T(128)} %bitcast.6.core_ref, bf16[1024,768]{1,0:T(8,128)(2,1)} %get-tuple-element.274.refs_0_, bf16[1024,768]{1,0:T(8,128)(2,1)} %get-tuple-element.275.refs_1_, ...), custom_call_target="tpu_custom_call" | custom-call | flops 4831838208 | bytes 11010048 | tf_op jit(solution)/shard_map/grad_w_attn/pallas_call | solution.py:673
  258.8 3.8 collective-permute-done.21
  262.6 1.7 collective-permute-done.20
  268.8 1.6 collective-permute-start.22
  272.4 9.4 %image_backward.1 = (bf16[416,768]{1,0:T(8,128)(2,1)}, bf16[416,2048]{1,0:T(8,128)(2,1)}, bf16[16,40,768]{2,1,0:T(8,128)(2,1)}, bf16[16,32,768]{2,1,0:T(8,128)(2...) custom-call(s32[1]{0:T(128)} %bitcast.6.core_ref, bf16[416,2048]{1,0:T(8,128)(2,1)} %x_ref.3, ...), custom_call_target="tpu_custom_call" | custom-call | flops 2617245696 | bytes 10092544 | tf_op jit(solution)/shard_map/image_backward/pallas_call | solution.py:428
  281.8 2.5 collective-permute-done.22
  284.5 1.6 fusion.14
  286.1 1.7 fusion.12
  289.8 2.5 collective-permute-start.25
  292.3 13.2 %collective-permute-done.25 = bf16[192,768]{1,0:T(8,128)(2,1)S(1)} collective-permute-done((bf16[192,768]{1,0:T(8,128)(2,1)S(1)}, bf16[192,768]{1,0:T(8,128)(2,1)S(1)}, u32[]{:S(2)}, u32[]{:S(2)}) %collective-permute-start.25) | collective-permute-done | bytes 294944 | tf_op jit(solution)/shard_map/ppermute | solution.py:713
  311.9 8.6 %collective-permute-done.34 = bf16[192,768]{1,0:T(8,128)(2,1)S(1)} collective-permute-done((bf16[192,768]{1,0:T(8,128)(2,1)S(1)}, bf16[192,768]{1,0:T(8,128)(2,1)S(1)}, u32[]{:S(2)}, u32[]{:S(2)}) %collective-permute-start.34) | collective-permute-done | bytes 294944 | tf_op jit(solution)/shard_map/ppermute | solution.py:713
  320.7 5.9 %collective-permute-done.31 = bf16[2,2,48,768]{3,2,0,1:T(8,128)(2,1)S(1)} collective-permute-done((bf16[2,2,48,768]{3,2,0,1:T(8,128)(2,1)S(1)}, bf16[2,2,48,768]{3,2,0,1:T(8,128)(2,1)S(1)}, u32[]{:S(2)}, u32[]{:S(2)}) %collective-permute-start.31) | collective-permute-done | bytes 294944 | tf_op jit(solution)/shard_map/ppermute | solution.py:713
  326.9 3.0 collective-permute-start.35
  330.5 1.7 collective-permute-start.37
  332.2 4.0 collective-permute-done.37
  337.9 5.6 %collective-permute-done.38 = bf16[96,768]{1,0:T(8,128)(2,1)S(1)} collective-permute-done((bf16[96,768]{1,0:T(8,128)(2,1)S(1)}, bf16[96,768]{1,0:T(8,128)(2,1)S(1)}, u32[]{:S(2)}, u32[]{:S(2)}) %collective-permute-start.38) | collective-permute-done | bytes 147488 | tf_op jit(solution)/shard_map/ppermute | solution.py:713
  344.3 2.2 collective-permute-start.40
  346.5 3.5 collective-permute-done.40
  350.8 2.4 collective-permute-start.41
  353.1 10.1 %collective-permute-done.41 = bf16[2,192,768]{2,1,0:T(8,128)(2,1)S(1)} collective-permute-done((bf16[2,192,768]{2,1,0:T(8,128)(2,1)S(1)}, bf16[2,192,768]{2,1,0:T(8,128)(2,1)S(1)}, u32[]{:S(2)}, u32[]{:S(2)}) %collective-permute-start.41) | collective-permute-done | bytes 589856 | tf_op jit(solution)/shard_map/ppermute | solution.py:713
  363.6 1.7 collective-permute-start.43
  365.2 2.6 collective-permute-start.42
  367.8 8.9 %collective-permute-done.43 = bf16[2,2,96,768]{3,2,1,0:T(8,128)(2,1)S(1)} collective-permute-done((bf16[2,2,96,768]{3,2,1,0:T(8,128)(2,1)S(1)}, bf16[2,2,96,768]{3,2,1,0:T(8,128)(2,1)S(1)}, u32[]{:S(2)}, u32[]{:S(2)}) %collective-permute-start.43) | collective-permute-done | bytes 589856 | tf_op jit(solution)/shard_map/ppermute | solution.py:713
  376.9 2.1 collective-permute-done.42
  380.1 27.1 %collective-permute-done.45 = bf16[2,2,2,96,768]{4,3,2,1,0:T(8,128)(2,1)S(1)} collective-permute-done((bf16[2,2,2,96,768]{4,3,2,1,0:T(8,128)(2,1)S(1)}, bf16[2,2,2,96,768]{4,3,2,1,0:T(8,128)(2,1)S(1)}, u32[]{:S(2)}, u32[]{:S(2)}) %collective-permute-start.45) | collective-permute-done | bytes 1179680 | tf_op jit(solution)/shard_map/ppermute | solution.py:713
  407.4 3.3 collective-permute-done.44
  413.3 4.8 %collective-permute-done.47 = bf16[2,2,2,2,96,768]{5,4,3,2,1,0:T(8,128)(2,1)S(1)} collective-permute-done((bf16[2,2,2,2,96,768]{5,4,3,2,1,0:T(8,128)(2,1)S(1)}, bf16[2,2,2,2,96,768]{5,4,3,2,1,0:T(8,128)(2,1)S(1)}, u32[]{:S(2)}, u32[]{:S(2)}) %collective-permute-start.47) | collective-permute-done | bytes 2359328 | tf_op jit(solution)/shard_map/ppermute | solution.py:713
  419.5 6.5 %join_blocks.3 = f32[3072,768]{1,0:T(8,128)} custom-call(s32[1]{0:T(128)} %bitcast.6.core_ref, bf16[16,96,768]{2,1,0:T(8,128)(2,1)} %bitcast.129, bf16[16,96,768]{2,1,0:T(8,128)(2,1)} %bitcast.137), custom_call_target="tpu_custom_call" | custom-call | bytes 14155776 | tf_op jit(solution)/shard_map/join_blocks/pallas_call | solution.py:470
  426.0 6.6 %join_blocks.2 = f32[768,3072]{1,0:T(8,128)} custom-call(s32[1]{0:T(128)} %bitcast.6.core_ref, bf16[16,96,768]{2,1,0:T(8,128)(2,1)} %bitcast.128, bf16[16,96,768]{2,1,0:T(8,128)(2,1)} %bitcast.73.refs_1_), custom_call_target="tpu_custom_call" | custom-call | bytes 14155776 | tf_op jit(solution)/shard_map/join_blocks/pallas_call | solution.py:470
  432.6 4.8 %all-gather.7.cloned.1.call-done = bf16[5376,768]{1,0:T(8,128)(2,1)} async-done(((bf16[168,768]{1,0:T(8,128)(2,1)}), bf16[5376,768]{1,0:T(8,128)(2,1)}) %all-gather.7.cloned.1.call-update) | async-done | bytes 8257552 | tf_op jit(solution)/shard_map/all_gather | solution.py:1078
  437.4 8.2 %widen_rest.1 = (f32[768,768]{1,0:T(8,128)}, f32[768,768]{1,0:T(8,128)}, f32[768,768]{1,0:T(8,128)}, f32[768,768]{1,0:T(8,128)}, f32[2048,768]{1,0:T(8,128)}, /*...) custom-call(bf16[32,168,768]{2,1,0:T(8,128)(2,1)} %bitcast.130), custom_call_target="tpu_custom_call" | custom-call | bytes 24772608 | tf_op jit(solution)/shard_map/widen_rest/pallas_call | solution.py:534
  (174 shorter events, 49.2 us)
Async XLA Ops:
  7.2 9.3 %copy-start.15 = (bf16[64,768]{1,0:T(8,128)(2,1)S(1)}, bf16[64,768]{1,0:T(8,128)(2,1)}, u32[]{:S(2)}) copy-start(bf16[64,768]{1,0:T(8,128)(2,1)} %param.33) | copy-start | bytes 294916
  7.2 129.3 %all-gather.5.cloned.1.call-start = ((), (), s32[]{:S(2)}) async-start(), calls=%async_computation.2 | async-start | bytes 9732096 | tf_op jit(solution)/shard_map/all_gather | solution.py:890
  7.2 9.2 %collective-permute-start = (bf16[64,768]{1,0:T(8,128)(2,1)}, bf16[64,768]{1,0:T(8,128)(2,1)S(1)}, u32[]{:S(2)}, u32[]{:S(2)}) collective-permute-start(bf16[64,768]{1,0:T(8,128)(2,1)} %param.33), channel_id=1, source_target_pairs={{0,16},{8,24},{16,0},{24,8},{1,17},{9,25},{17,1},{25,9},{2,18},{10... | collective-permute-start | bytes 294920 | tf_op jit(solution)/shard_map/ppermute | solution.py:713
  14.8 11.2 %copy-start.18 = (pred[2]{0:T(512)(128)(4,1)}, pred[2]{0:T(512)(128)(4,1)S(1)}, u32[]{:S(2)}) copy-start(pred[2]{0:T(512)(128)(4,1)S(1)} %iota_compare_fusion.1) | copy-start | bytes 10
  16.6 9.3 %collective-permute-start.2 = (bf16[96,768]{1,0:T(8,128)(2,1)S(1)}, bf16[96,768]{1,0:T(8,128)(2,1)S(1)}, u32[]{:S(2)}, u32[]{:S(2)}) collective-permute-start(bf16[96,768]{1,0:T(8,128)(2,1)S(1)} %pad_maximum_fusion.2), channel_id=1, source_target_pairs={{0,16},{8,24},{16,0},{24,8},{1,17},{9,25},{17,1},{25,9},{2,18},{10... | collective-permute-start | bytes 442376 | tf_op jit(solution)/shard_map/ppermute | solution.py:713
  17.3 9.8 %collective-permute-start.1 = (bf16[2,64,768]{2,1,0:T(8,128)(2,1)S(1)}, bf16[2,64,768]{2,1,0:T(8,128)(2,1)S(1)}, u32[]{:S(2)}, u32[]{:S(2)}) collective-permute-start(bf16[2,64,768]{2,1,0:T(8,128)(2,1)S(1)} %broadcast_select_fusion.17), channel_id=1, source_target_pairs={{0,8},{8,0},{16,24},{24,16},{1,9},{9,1},{17,25},{25,17},{2,10},{10... | collective-permute-start | bytes 589832 | tf_op jit(solution)/shard_map/ppermute | solution.py:713
  27.3 6.1 %collective-permute-start.4 = (bf16[2,2,32,768]{3,2,1,0:T(8,128)(2,1)S(1)}, bf16[2,2,32,768]{3,2,1,0:T(8,128)(2,1)S(1)}, u32[]{:S(2)}, u32[]{:S(2)}) collective-permute-start(bf16[2,2,32,768]{3,2,1,0:T(8,128)(2,1)S(1)} %get-tuple-element.456), channel_id=1, source_target_pairs={{0,2},{1,3},{2,0},{3,1},{4,6},{5,7},{6,4},{7,5},{8,10},{9,11},{10,... | collective-permute-start | bytes 589832 | tf_op jit(solution)/shard_map/ppermute | solution.py:713
  28.9 8.0 %collective-permute-start.5 = (bf16[2,96,768]{2,1,0:T(8,128)(2,1)S(1)}, bf16[2,96,768]{2,1,0:T(8,128)(2,1)S(1)}, u32[]{:S(2)}, u32[]{:S(2)}) collective-permute-start(bf16[2,96,768]{2,1,0:T(8,128)(2,1)S(1)} %broadcast_select_fusion.16), channel_id=1, source_target_pairs={{0,8},{8,0},{16,24},{24,16},{1,9},{9,1},{17,25},{25,17},{2,10},{10... | collective-permute-start | bytes 884744 | tf_op jit(solution)/shard_map/ppermute | solution.py:713
  29.1 5.7 %collective-permute-start.3 = (bf16[2,2,32,768]{3,2,1,0:T(8,128)(2,1)S(1)}, bf16[2,2,32,768]{3,2,1,0:T(8,128)(2,1)S(1)}, u32[]{:S(2)}, u32[]{:S(2)}) collective-permute-start(bf16[2,2,32,768]{3,2,1,0:T(8,128)(2,1)S(1)} %get-tuple-element.457), channel_id=1, source_target_pairs={{0,4},{1,5},{2,6},{3,7},{4,0},{5,1},{6,2},{7,3},{8,12},{9,13},{10,... | collective-permute-start | bytes 589832 | tf_op jit(solution)/shard_map/ppermute | solution.py:713
  37.0 11.2 %collective-permute-start.7 = (bf16[2,2,2,32,768]{4,3,2,1,0:T(8,128)(2,1)S(1)}, bf16[2,2,2,32,768]{4,3,2,1,0:T(8,128)(2,1)S(1)}, u32[]{:S(2)}, u32[]{:S(2)}) collective-permute-start(bf16[2,2,2,32,768]{4,3,2,1,0:T(8,128)(2,1)S(1)} %broadcast_select_fusion.13), channel_id=1, source_target_pairs={{0,4},{1,5},{2,6},{3,7},{4,0},{5,1},{6,2},{7,3},{8,12},{9,13},{10,... | collective-permute-start | bytes 1179656 | tf_op jit(solution)/shard_map/ppermute | solution.py:713
  38.5 10.9 %collective-permute-start.6 = (bf16[2,2,2,32,768]{4,3,2,1,0:T(8,128)(2,1)S(1)}, bf16[2,2,2,32,768]{4,3,2,1,0:T(8,128)(2,1)S(1)}, u32[]{:S(2)}, u32[]{:S(2)}) collective-permute-start(bf16[2,2,2,32,768]{4,3,2,1,0:T(8,128)(2,1)S(1)} %broadcast_select_fusion.15), channel_id=1, source_target_pairs={{0,2},{1,3},{2,0},{3,1},{4,6},{5,7},{6,4},{7,5},{8,10},{9,11},{10,... | collective-permute-start | bytes 1179656 | tf_op jit(solution)/shard_map/ppermute | solution.py:713
  49.6 4.5 copy-start.3
  49.6 2.4 collective-permute-start.8
  49.7 3.4 collective-permute-start.9
  53.1 13.2 %collective-permute-start.11 = (bf16[2,2,48,768]{3,2,1,0:T(8,128)(2,1)S(1)}, bf16[2,2,48,768]{3,2,1,0:T(8,128)(2,1)S(1)}, u32[]{:S(2)}, u32[]{:S(2)}) collective-permute-start(bf16[2,2,48,768]{3,2,1,0:T(8,128)(2,1)S(1)} %get-tuple-element.232), channel_id=1, source_target_pairs={{0,2},{1,3},{2,0},{3,1},{4,6},{5,7},{6,4},{7,5},{8,10},{9,11},{10,... | collective-permute-start | bytes 884744 | tf_op jit(solution)/shard_map/ppermute | solution.py:713
  53.6 13.0 %collective-permute-start.10 = (bf16[2,2,48,768]{3,2,1,0:T(8,128)(2,1)S(1)}, bf16[2,2,48,768]{3,2,1,0:T(8,128)(2,1)S(1)}, u32[]{:S(2)}, u32[]{:S(2)}) collective-permute-start(bf16[2,2,48,768]{3,2,1,0:T(8,128)(2,1)S(1)} %get-tuple-element.231), channel_id=1, source_target_pairs={{0,4},{1,5},{2,6},{3,7},{4,0},{5,1},{6,2},{7,3},{8,12},{9,13},{10,... | collective-permute-start | bytes 884744 | tf_op jit(solution)/shard_map/ppermute | solution.py:713
  66.7 39.4 %all-to-all-start = ((bf16[32,16,768]{2,1,0:T(8,128)(2,1)}), bf16[32,16,768]{2,1,0:T(8,128)(2,1)}, u32[]{:S(2)}, u32[]{:S(2)}) async-start(bf16[32,16,768]{2,1,0:T(8,128)(2,1)} %bitcast.7), calls=%async_computation | async-start | bytes 1572864 | tf_op jit(solution)/shard_map/all_to_all | solution.py:914
  71.1 29.6 %collective-permute-start.13 = (bf16[2,2,2,48,768]{4,3,2,1,0:T(8,128)(2,1)S(1)}, bf16[2,2,2,48,768]{4,3,2,1,0:T(8,128)(2,1)S(1)}, u32[]{:S(2)}, u32[]{:S(2)}) collective-permute-start(bf16[2,2,2,48,768]{4,3,2,1,0:T(8,128)(2,1)S(1)} %broadcast_select_fusion.10), channel_id=1, source_target_pairs={{0,4},{1,5},{2,6},{3,7},{4,0},{5,1},{6,2},{7,3},{8,12},{9,13},{10,... | collective-permute-start | bytes 1769480 | tf_op jit(solution)/shard_map/ppermute | solution.py:713
  72.9 28.2 %collective-permute-start.12 = (bf16[2,2,2,48,768]{4,3,2,1,0:T(8,128)(2,1)S(1)}, bf16[2,2,2,48,768]{4,3,2,1,0:T(8,128)(2,1)S(1)}, u32[]{:S(2)}, u32[]{:S(2)}) collective-permute-start(bf16[2,2,2,48,768]{4,3,2,1,0:T(8,128)(2,1)S(1)} %broadcast_select_fusion.12), channel_id=1, source_target_pairs={{0,2},{1,3},{2,0},{3,1},{4,6},{5,7},{6,4},{7,5},{8,10},{9,11},{10,... | collective-permute-start | bytes 1769480 | tf_op jit(solution)/shard_map/ppermute | solution.py:713
  106.1 3.9 collective-permute-start.14
  106.2 4.7 %collective-permute-start.15 = (bf16[2,2,2,2,48,768]{5,4,3,2,1,0:T(8,128)(2,1)S(1)}, bf16[2,2,2,2,48,768]{5,4,3,2,1,0:T(8,128)(2,1)}, u32[]{:S(2)}, u32[]{:S(2)}) collective-permute-start(bf16[2,2,2,2,48,768]{5,4,3,2,1,0:T(8,128)(2,1)S(1)} %broadcast_select_fusion.5), channel_id=1, source_target_pairs={{0,1},{1,0},{2,3},{3,2},{4,5},{5,4},{6,7},{7,6},{8,9},{9,8},{10,11... | collective-permute-start | bytes 3538952 | tf_op jit(solution)/shard_map/ppermute | solution.py:713
  187.6 11.9 %collective-permute-start.16 = (bf16[16,96,768]{2,1,0:T(8,128)(2,1)}, bf16[16,96,768]{2,1,0:T(8,128)(2,1)S(1)}, u32[]{:S(2)}, u32[]{:S(2)}) collective-permute-start(bf16[16,96,768]{2,1,0:T(8,128)(2,1)} %get-tuple-element.256), channel_id=1, source_target_pairs={{0,1},{1,0},{2,3},{3,2},{4,5},{5,4},{6,7},{7,6},{8,9},{9,8},{10,11... | collective-permute-start | bytes 7077896 | tf_op jit(solution)/shard_map/ppermute | solution.py:713
  197.5 4.9 %collective-permute-start.17 = (bf16[16,96,768]{2,1,0:T(8,128)(2,1)}, bf16[16,96,768]{2,1,0:T(8,128)(2,1)}, u32[]{:S(2)}, u32[]{:S(2)}) collective-permute-start(bf16[16,96,768]{2,1,0:T(8,128)(2,1)} %get-tuple-element.259), channel_id=1, source_target_pairs={{0,1},{1,0},{2,3},{3,2},{4,5},{5,4},{6,7},{7,6},{8,9},{9,8},{10,11... | collective-permute-start | bytes 7077896 | tf_op jit(solution)/shard_map/ppermute | solution.py:713
  199.6 2.9 copy-start.4
  206.6 28.4 %collective-permute-start.19 = (bf16[2,2,2,96,768]{4,3,0,1,2:T(8,128)(2,1)}, bf16[2,2,2,96,768]{4,3,0,1,2:T(8,128)(2,1)}, u32[]{:S(2)}, u32[]{:S(2)}) collective-permute-start(bf16[2,2,2,96,768]{4,3,0,1,2:T(8,128)(2,1)} %fusion.1), channel_id=1, source_target_pairs={{0,4},{1,5},{2,6},{3,7},{4,0},{5,1},{6,2},{7,3},{8,12},{9,13},{10,... | collective-permute-start | bytes 3538952 | tf_op jit(solution)/shard_map/ppermute | solution.py:713
  207.4 28.0 %collective-permute-start.18 = (bf16[2,2,2,96,768]{4,3,0,1,2:T(8,128)(2,1)S(1)}, bf16[2,2,2,96,768]{4,3,0,1,2:T(8,128)(2,1)}, u32[]{:S(2)}, u32[]{:S(2)}) collective-permute-start(bf16[2,2,2,96,768]{4,3,0,1,2:T(8,128)(2,1)S(1)} %fusion), channel_id=1, source_target_pairs={{0,2},{1,3},{2,0},{3,1},{4,6},{5,7},{6,4},{7,5},{8,10},{9,11},{10,... | collective-permute-start | bytes 3538952 | tf_op jit(solution)/shard_map/ppermute | solution.py:713
  235.4 28.8 %all-to-all-start.1 = ((bf16[32,16,768]{2,1,0:T(8,128)(2,1)}), bf16[32,16,768]{2,1,0:T(8,128)(2,1)}, u32[]{:S(2)}, u32[]{:S(2)}) async-start(bf16[32,16,768]{2,1,0:T(8,128)(2,1)} %bitcast.150), calls=%async_computation.1 | async-start | bytes 1572864 | tf_op jit(solution)/shard_map/all_to_all | solution.py:1026
  238.8 198.6 %all-gather.7.cloned.1.call-start = ((), (), s32[]{:S(2)}) async-start(), calls=%async_computation.3 | async-start | bytes 8515584 | tf_op jit(solution)/shard_map/all_gather | solution.py:1078
  240.9 21.7 %collective-permute-start.21 = (bf16[2,2,96,768]{3,2,1,0:T(8,128)(2,1)}, bf16[2,2,96,768]{3,2,1,0:T(8,128)(2,1)}, u32[]{:S(2)}, u32[]{:S(2)}) collective-permute-start(bf16[2,2,96,768]{3,2,1,0:T(8,128)(2,1)} %fusion.15), channel_id=1, source_target_pairs={{0,2},{1,3},{2,0},{3,1},{4,6},{5,7},{6,4},{7,5},{8,10},{9,11},{10,... | collective-permute-start | bytes 1769480 | tf_op jit(solution)/shard_map/ppermute | solution.py:713
  244.8 19.5 %collective-permute-start.20 = (bf16[2,2,96,768]{3,2,0,1:T(8,128)(2,1)}, bf16[2,2,96,768]{3,2,0,1:T(8,128)(2,1)S(1)}, u32[]{:S(2)}, u32[]{:S(2)}) collective-permute-start(bf16[2,2,96,768]{3,2,0,1:T(8,128)(2,1)} %get-tuple-element.420), channel_id=1, source_target_pairs={{0,4},{1,5},{2,6},{3,7},{4,0},{5,1},{6,2},{7,3},{8,12},{9,13},{10,... | collective-permute-start | bytes 1769480 | tf_op jit(solution)/shard_map/ppermute | solution.py:713
  267.3 3.6 copy-start.17
  268.3 16.0 %collective-permute-start.23 = (bf16[16,48,768]{2,1,0:T(8,128)(2,1)}, bf16[16,48,768]{2,1,0:T(8,128)(2,1)}, u32[]{:S(2)}, u32[]{:S(2)}) collective-permute-start(bf16[16,48,768]{2,1,0:T(8,128)(2,1)} %get-tuple-element.304), channel_id=1, source_target_pairs={{0,1},{1,0},{2,3},{3,2},{4,5},{5,4},{6,7},{7,6},{8,9},{9,8},{10,11... | collective-permute-start | bytes 3538952 | tf_op jit(solution)/shard_map/ppermute | solution.py:713
  268.3 16.0 %collective-permute-start.24 = (bf16[16,48,768]{2,1,0:T(8,128)(2,1)}, bf16[16,48,768]{2,1,0:T(8,128)(2,1)}, u32[]{:S(2)}, u32[]{:S(2)}) collective-permute-start(bf16[16,48,768]{2,1,0:T(8,128)(2,1)} %get-tuple-element.306), channel_id=1, source_target_pairs={{0,1},{1,0},{2,3},{3,2},{4,5},{5,4},{6,7},{7,6},{8,9},{9,8},{10,11... | collective-permute-start | bytes 3538952 | tf_op jit(solution)/shard_map/ppermute | solution.py:713
  268.8 15.4 %collective-permute-start.22 = (bf16[2,192,768]{2,1,0:T(8,128)(2,1)}, bf16[2,192,768]{2,1,0:T(8,128)(2,1)S(1)}, u32[]{:S(2)}, u32[]{:S(2)}) collective-permute-start(bf16[2,192,768]{2,1,0:T(8,128)(2,1)} %fusion.16), channel_id=1, source_target_pairs={{0,8},{8,0},{16,24},{24,16},{1,9},{9,1},{17,25},{25,17},{2,10},{10... | collective-permute-start | bytes 1769480 | tf_op jit(solution)/shard_map/ppermute | solution.py:713
  281.8 2.6 copy-start.7
  287.8 19.0 %copy-start.9 = (bf16[16,32,768]{2,1,0:T(8,128)(2,1)S(1)}, bf16[16,32,768]{2,1,0:T(8,128)(2,1)}, u32[]{:S(2)}) copy-start(bf16[16,32,768]{2,1,0:T(8,128)(2,1)} %get-tuple-element.329) | copy-start | bytes 2359300
  287.8 17.7 %collective-permute-start.28 = (bf16[16,40,768]{2,1,0:T(8,128)(2,1)S(1)}, bf16[16,40,768]{2,1,0:T(8,128)(2,1)S(1)}, u32[]{:S(2)}, u32[]{:S(2)}) collective-permute-start(bf16[16,40,768]{2,1,0:T(8,128)(2,1)S(1)} %copy-done.20), channel_id=1, source_target_pairs={{0,1},{1,0},{2,3},{3,2},{4,5},{5,4},{6,7},{7,6},{8,9},{9,8},{10,11... | collective-permute-start | bytes 2949128 | tf_op jit(solution)/shard_map/ppermute | solution.py:713
  287.9 17.6 %collective-permute-start.29 = (bf16[16,32,768]{2,1,0:T(8,128)(2,1)S(1)}, bf16[16,32,768]{2,1,0:T(8,128)(2,1)S(1)}, u32[]{:S(2)}, u32[]{:S(2)}) collective-permute-start(bf16[16,32,768]{2,1,0:T(8,128)(2,1)S(1)} %copy-done.21), channel_id=1, source_target_pairs={{0,1},{1,0},{2,3},{3,2},{4,5},{5,4},{6,7},{7,6},{8,9},{9,8},{10,11... | collective-permute-start | bytes 2359304 | tf_op jit(solution)/shard_map/ppermute | solution.py:713
  288.4 17.1 %collective-permute-start.27 = (bf16[2,2,2,48,768]{4,3,0,1,2:T(8,128)(2,1)S(1)}, bf16[2,2,2,48,768]{4,3,0,1,2:T(8,128)(2,1)S(1)}, u32[]{:S(2)}, u32[]{:S(2)}) collective-permute-start(bf16[2,2,2,48,768]{4,3,0,1,2:T(8,128)(2,1)S(1)} %get-tuple-element.416), channel_id=1, source_target_pairs={{0,4},{1,5},{2,6},{3,7},{4,0},{5,1},{6,2},{7,3},{8,12},{9,13},{10,... | collective-permute-start | bytes 1769480 | tf_op jit(solution)/shard_map/ppermute | solution.py:713
  289.3 16.2 %collective-permute-start.26 = (bf16[2,2,2,48,768]{4,3,0,1,2:T(8,128)(2,1)S(1)}, bf16[2,2,2,48,768]{4,3,0,1,2:T(8,128)(2,1)S(1)}, u32[]{:S(2)}, u32[]{:S(2)}) collective-permute-start(bf16[2,2,2,48,768]{4,3,0,1,2:T(8,128)(2,1)S(1)} %get-tuple-element.418), channel_id=1, source_target_pairs={{0,2},{1,3},{2,0},{3,1},{4,6},{5,7},{6,4},{7,5},{8,10},{9,11},{10,... | collective-permute-start | bytes 1769480 | tf_op jit(solution)/shard_map/ppermute | solution.py:713
  289.8 15.7 %collective-permute-start.25 = (bf16[192,768]{1,0:T(8,128)(2,1)S(1)}, bf16[192,768]{1,0:T(8,128)(2,1)S(1)}, u32[]{:S(2)}, u32[]{:S(2)}) collective-permute-start(bf16[192,768]{1,0:T(8,128)(2,1)S(1)} %get-tuple-element.442), channel_id=1, source_target_pairs={{0,16},{8,24},{16,0},{24,8},{1,17},{9,25},{17,1},{25,9},{2,18},{10... | collective-permute-start | bytes 884744 | tf_op jit(solution)/shard_map/ppermute | solution.py:713
  305.6 2.9 copy-start.8
  305.6 15.0 %collective-permute-start.34 = (bf16[192,768]{1,0:T(8,128)(2,1)S(1)}, bf16[192,768]{1,0:T(8,128)(2,1)S(1)}, u32[]{:S(2)}, u32[]{:S(2)}) collective-permute-start(bf16[192,768]{1,0:T(8,128)(2,1)S(1)} %add_convert_fusion.22), channel_id=1, source_target_pairs={{0,16},{8,24},{16,0},{24,8},{1,17},{9,25},{17,1},{25,9},{2,18},{10... | collective-permute-start | bytes 884744 | tf_op jit(solution)/shard_map/ppermute | solution.py:713
  307.1 19.6 %collective-permute-start.33 = (bf16[2,2,2,32,768]{4,3,0,1,2:T(8,128)(2,1)S(1)}, bf16[2,2,2,32,768]{4,3,0,1,2:T(8,128)(2,1)S(1)}, u32[]{:S(2)}, u32[]{:S(2)}) collective-permute-start(bf16[2,2,2,32,768]{4,3,0,1,2:T(8,128)(2,1)S(1)} %get-tuple-element.433), channel_id=1, source_target_pairs={{0,4},{1,5},{2,6},{3,7},{4,0},{5,1},{6,2},{7,3},{8,12},{9,13},{10,... | collective-permute-start | bytes 1179656 | tf_op jit(solution)/shard_map/ppermute | solution.py:713
  308.7 17.9 %collective-permute-start.32 = (bf16[2,2,2,40,768]{4,3,0,1,2:T(8,128)(2,1)S(1)}, bf16[2,2,2,40,768]{4,3,0,1,2:T(8,128)(2,1)S(1)}, u32[]{:S(2)}, u32[]{:S(2)}) collective-permute-start(bf16[2,2,2,40,768]{4,3,0,1,2:T(8,128)(2,1)S(1)} %get-tuple-element.431), channel_id=1, source_target_pairs={{0,2},{1,3},{2,0},{3,1},{4,6},{5,7},{6,4},{7,5},{8,10},{9,11},{10,... | collective-permute-start | bytes 1474568 | tf_op jit(solution)/shard_map/ppermute | solution.py:713
  309.5 11.1 %copy-start.19 = (pred[2]{0:T(512)(128)(4,1)S(1)}, pred[2]{0:T(512)(128)(4,1)}, u32[]{:S(2)}) copy-start(pred[2]{0:T(512)(128)(4,1)} %copy-done.18) | copy-start | bytes 10
  309.5 17.1 %collective-permute-start.31 = (bf16[2,2,48,768]{3,2,0,1:T(8,128)(2,1)S(1)}, bf16[2,2,48,768]{3,2,0,1:T(8,128)(2,1)S(1)}, u32[]{:S(2)}, u32[]{:S(2)}) collective-permute-start(bf16[2,2,48,768]{3,2,0,1:T(8,128)(2,1)S(1)} %get-tuple-element.438), channel_id=1, source_target_pairs={{0,2},{1,3},{2,0},{3,1},{4,6},{5,7},{6,4},{7,5},{8,10},{9,11},{10,... | collective-permute-start | bytes 884744 | tf_op jit(solution)/shard_map/ppermute | solution.py:713
  311.2 15.4 %collective-permute-start.30 = (bf16[2,2,48,768]{3,2,0,1:T(8,128)(2,1)S(1)}, bf16[2,2,48,768]{3,2,0,1:T(8,128)(2,1)S(1)}, u32[]{:S(2)}, u32[]{:S(2)}) collective-permute-start(bf16[2,2,48,768]{3,2,0,1:T(8,128)(2,1)S(1)} %get-tuple-element.440), channel_id=1, source_target_pairs={{0,4},{1,5},{2,6},{3,7},{4,0},{5,1},{6,2},{7,3},{8,12},{9,13},{10,... | collective-permute-start | bytes 884744 | tf_op jit(solution)/shard_map/ppermute | solution.py:713
  326.9 9.4 %collective-permute-start.35 = (bf16[2,96,768]{2,1,0:T(8,128)(2,1)S(1)}, bf16[2,96,768]{2,1,0:T(8,128)(2,1)S(1)}, u32[]{:S(2)}, u32[]{:S(2)}) collective-permute-start(bf16[2,96,768]{2,1,0:T(8,128)(2,1)S(1)} %get-tuple-element.436), channel_id=1, source_target_pairs={{0,8},{8,0},{16,24},{24,16},{1,9},{9,1},{17,25},{25,17},{2,10},{10... | collective-permute-start | bytes 884744 | tf_op jit(solution)/shard_map/ppermute | solution.py:713
  330.0 6.3 %collective-permute-start.36 = (bf16[2,2,40,768]{3,2,0,1:T(8,128)(2,1)S(1)}, bf16[2,2,40,768]{3,2,0,1:T(8,128)(2,1)S(1)}, u32[]{:S(2)}, u32[]{:S(2)}) collective-permute-start(bf16[2,2,40,768]{3,2,0,1:T(8,128)(2,1)S(1)} %get-tuple-element.444), channel_id=1, source_target_pairs={{0,4},{1,5},{2,6},{3,7},{4,0},{5,1},{6,2},{7,3},{8,12},{9,13},{10,... | collective-permute-start | bytes 737288 | tf_op jit(solution)/shard_map/ppermute | solution.py:713
  330.5 5.7 %collective-permute-start.37 = (bf16[2,2,32,768]{3,2,0,1:T(8,128)(2,1)S(1)}, bf16[2,2,32,768]{3,2,0,1:T(8,128)(2,1)S(1)}, u32[]{:S(2)}, u32[]{:S(2)}) collective-permute-start(bf16[2,2,32,768]{3,2,0,1:T(8,128)(2,1)S(1)} %get-tuple-element.448), channel_id=1, source_target_pairs={{0,2},{1,3},{2,0},{3,1},{4,6},{5,7},{6,4},{7,5},{8,10},{9,11},{10,... | collective-permute-start | bytes 589832 | tf_op jit(solution)/shard_map/ppermute | solution.py:713
  336.6 7.6 %collective-permute-start.39 = (bf16[2,72,768]{2,1,0:T(8,128)(2,1)S(1)}, bf16[2,72,768]{2,1,0:T(8,128)(2,1)S(1)}, u32[]{:S(2)}, u32[]{:S(2)}) collective-permute-start(bf16[2,72,768]{2,1,0:T(8,128)(2,1)S(1)} %get-tuple-element.446), channel_id=1, source_target_pairs={{0,8},{8,0},{16,24},{24,16},{1,9},{9,1},{17,25},{25,17},{2,10},{10... | collective-permute-start | bytes 663560 | tf_op jit(solution)/shard_map/ppermute | solution.py:713
  337.3 6.2 %collective-permute-start.38 = (bf16[96,768]{1,0:T(8,128)(2,1)S(1)}, bf16[96,768]{1,0:T(8,128)(2,1)S(1)}, u32[]{:S(2)}, u32[]{:S(2)}) collective-permute-start(bf16[96,768]{1,0:T(8,128)(2,1)S(1)} %get-tuple-element.450), channel_id=1, source_target_pairs={{0,16},{8,24},{16,0},{24,8},{1,17},{9,25},{17,1},{25,9},{2,18},{10... | collective-permute-start | bytes 442376 | tf_op jit(solution)/shard_map/ppermute | solution.py:713
  344.3 5.7 %collective-permute-start.40 = (bf16[72,768]{1,0:T(8,128)(2,1)S(1)}, bf16[72,768]{1,0:T(8,128)(2,1)S(1)}, u32[]{:S(2)}, u32[]{:S(2)}) collective-permute-start(bf16[72,768]{1,0:T(8,128)(2,1)S(1)} %get-tuple-element.454), channel_id=1, source_target_pairs={{0,16},{8,24},{16,0},{24,8},{1,17},{9,25},{17,1},{25,9},{2,18},{10... | collective-permute-start | bytes 331784 | tf_op jit(solution)/shard_map/ppermute | solution.py:713
  350.8 12.5 %collective-permute-start.41 = (bf16[2,192,768]{2,1,0:T(8,128)(2,1)S(1)}, bf16[2,192,768]{2,1,0:T(8,128)(2,1)S(1)}, u32[]{:S(2)}, u32[]{:S(2)}) collective-permute-start(bf16[2,192,768]{2,1,0:T(8,128)(2,1)S(1)} %broadcast_select_fusion.9), channel_id=1, source_target_pairs={{0,8},{8,0},{16,24},{24,16},{1,9},{9,1},{17,25},{25,17},{2,10},{10... | collective-permute-start | bytes 1769480 | tf_op jit(solution)/shard_map/ppermute | solution.py:713
  363.6 13.1 %collective-permute-start.43 = (bf16[2,2,96,768]{3,2,1,0:T(8,128)(2,1)S(1)}, bf16[2,2,96,768]{3,2,1,0:T(8,128)(2,1)S(1)}, u32[]{:S(2)}, u32[]{:S(2)}) collective-permute-start(bf16[2,2,96,768]{3,2,1,0:T(8,128)(2,1)S(1)} %get-tuple-element.434), channel_id=1, source_target_pairs={{0,2},{1,3},{2,0},{3,1},{4,6},{5,7},{6,4},{7,5},{8,10},{9,11},{10,... | collective-permute-start | bytes 1769480 | tf_op jit(solution)/shard_map/ppermute | solution.py:713
  365.2 13.7 %collective-permute-start.42 = (bf16[2,2,96,768]{3,2,1,0:T(8,128)(2,1)S(1)}, bf16[2,2,96,768]{3,2,1,0:T(8,128)(2,1)S(1)}, u32[]{:S(2)}, u32[]{:S(2)}) collective-permute-start(bf16[2,2,96,768]{3,2,1,0:T(8,128)(2,1)S(1)} %get-tuple-element.435), channel_id=1, source_target_pairs={{0,4},{1,5},{2,6},{3,7},{4,0},{5,1},{6,2},{7,3},{8,12},{9,13},{10,... | collective-permute-start | bytes 1769480 | tf_op jit(solution)/shard_map/ppermute | solution.py:713
  379.1 28.0 %collective-permute-start.45 = (bf16[2,2,2,96,768]{4,3,2,1,0:T(8,128)(2,1)S(1)}, bf16[2,2,2,96,768]{4,3,2,1,0:T(8,128)(2,1)S(1)}, u32[]{:S(2)}, u32[]{:S(2)}) collective-permute-start(bf16[2,2,2,96,768]{4,3,2,1,0:T(8,128)(2,1)S(1)} %broadcast_select_fusion.2), channel_id=1, source_target_pairs={{0,4},{1,5},{2,6},{3,7},{4,0},{5,1},{6,2},{7,3},{8,12},{9,13},{10,... | collective-permute-start | bytes 3538952 | tf_op jit(solution)/shard_map/ppermute | solution.py:713
  379.8 30.9 %collective-permute-start.44 = (bf16[2,2,2,96,768]{4,3,2,1,0:T(8,128)(2,1)S(1)}, bf16[2,2,2,96,768]{4,3,2,1,0:T(8,128)(2,1)S(1)}, u32[]{:S(2)}, u32[]{:S(2)}) collective-permute-start(bf16[2,2,2,96,768]{4,3,2,1,0:T(8,128)(2,1)S(1)} %broadcast_select_fusion.4), channel_id=1, source_target_pairs={{0,2},{1,3},{2,0},{3,1},{4,6},{5,7},{6,4},{7,5},{8,10},{9,11},{10,... | collective-permute-start | bytes 3538952 | tf_op jit(solution)/shard_map/ppermute | solution.py:713
  407.4 3.7 copy-start
  407.4 5.0 %copy-start.12 = (bf16[416,768]{1,0:T(8,128)(2,1)S(1)}, bf16[416,768]{1,0:T(8,128)(2,1)}, u32[]{:S(2)}) copy-start(bf16[416,768]{1,0:T(8,128)(2,1)} %get-tuple-element.290) | copy-start | bytes 1916932
  407.4 5.0 %copy-start.16 = (bf16[4,768]{1,0:T(4,128)(2,1)S(1)}, bf16[4,768]{1,0:T(4,128)(2,1)}, u32[]{:S(2)}) copy-start(bf16[4,768]{1,0:T(4,128)(2,1)} %wb_ref.1) | copy-start | bytes 18436
  411.0 7.1 %collective-permute-start.47 = (bf16[2,2,2,2,96,768]{5,4,3,2,1,0:T(8,128)(2,1)S(1)}, bf16[2,2,2,2,96,768]{5,4,3,2,1,0:T(8,128)(2,1)S(1)}, u32[]{:S(2)}, u32[]{:S(2)}) collective-permute-start(bf16[2,2,2,2,96,768]{5,4,3,2,1,0:T(8,128)(2,1)S(1)} %broadcast_select_fusion.1), channel_id=1, source_target_pairs={{0,1},{1,0},{2,3},{3,2},{4,5},{5,4},{6,7},{7,6},{8,9},{9,8},{10,11... | collective-permute-start | bytes 7077896 | tf_op jit(solution)/shard_map/ppermute | solution.py:713
  411.1 14.9 %collective-permute-start.46 = (bf16[2,2,2,2,96,768]{5,4,3,2,1,0:T(8,128)(2,1)S(1)}, bf16[2,2,2,2,96,768]{5,4,3,2,1,0:T(8,128)(2,1)}, u32[]{:S(2)}, u32[]{:S(2)}) collective-permute-start(bf16[2,2,2,2,96,768]{5,4,3,2,1,0:T(8,128)(2,1)S(1)} %broadcast_select_fusion), channel_id=1, source_target_pairs={{0,1},{1,0},{2,3},{3,2},{4,5},{5,4},{6,7},{7,6},{8,9},{9,8},{10,11... | collective-permute-start | bytes 7077896 | tf_op jit(solution)/shard_map/ppermute | solution.py:713
  (10 other events, 14.9 us)
Sparse Core Ops, SparseCore 0:
  27.3 98.6 all-gather.4
  350.9 86.4 all-gather.6

commit v7 on v6

--- a/solution.py
+++ b/solution.py
@@ -154,8 +154,8 @@
 
 def image_backward(
     pad, sent, core_ref,
-    x_ref, box_ref, wi_ref, pre_ref, back_ref, gr_ref, sums_ref, attn_sums_ref, bu_ref,
-    gp_ref, gx_ref, *outs,
+    x_ref, box_ref, pre_ref, back_ref, gr_ref, sums_ref, attn_sums_ref, bu_ref,
+    gp_ref, *outs,
 ):
     *outs, acc_ref = outs
     rows, feat = x_ref.shape
@@ -184,7 +184,6 @@
                 rows_here = ref.shape[1]
                 ref[i] = acc_ref[pl.ds(pl.multiple_of(at, 8), rows_here), :].astype(bf16)
                 at = at + rows_here
-    gx_ref[...] = nt(gp, wi_ref[...]).astype(bf16)
 
 
 def feed_forward(
@@ -252,7 +251,8 @@
         cols = slice(j, j + step)
         gg = (nt(gdo, down_rows(j)) * d_ref[:, cols]).astype(bf16)
         gg_ref[:, cols] = gg
-        bu_sum_ref[:, cols] += jnp.sum(gg.astype(f32), 0, keepdims=True)
+        at = j // step
+        bu_sum_ref[at : at + 1, :] += jnp.sum(gg.astype(f32), 0, keepdims=True)
         first = first + nt(gg, wu_ref[j // step])
     normed, inverse = norm_parts(mixed_ref[...])
     add(3, first * normed)
@@ -416,7 +416,7 @@
     )
 
 
-def run_image_backward(geometry, chunk, core, x, boxes, wi, pre, back, gr, sums, attn_sums, bu):
+def run_image_backward(geometry, chunk, core, x, boxes, pre, back, gr, sums, attn_sums, bu):
     pad, sent, devices = geometry
     rows, feat = x.shape
     d = pre.shape[1]
@@ -424,28 +424,27 @@
     parts = [
         jax.ShapeDtypeStruct((devices // 2, r, d), bf16) for r in (first, chunk - first) * 2
     ]
-    operands = (x, boxes, wi, pre, back, gr, sums, attn_sums, bu)
-    gp, gx, *out = pl.pallas_call(
+    operands = (x, boxes, pre, back, gr, sums, attn_sums, bu)
+    gp, *out = pl.pallas_call(
         functools.partial(image_backward, pad, sent),
         out_shape=[
             jax.ShapeDtypeStruct((rows, d), bf16),
-            jax.ShapeDtypeStruct((rows, feat), bf16),
             *parts,
         ],
         grid_spec=pltpu.PrefetchScalarGridSpec(
             num_scalar_prefetch=1,
             grid=(1,),
             in_specs=[whole(o.shape) for o in operands],
-            out_specs=[whole((rows, d)), whole((rows, feat))] + [whole(p.shape) for p in parts],
+            out_specs=[whole((rows, d))] + [whole(p.shape) for p in parts],
             scratch_shapes=[pltpu.VMEM((devices * chunk, d), f32)],
         ),
         compiler_params=pltpu.CompilerParams(
             dimension_semantics=("arbitrary",), vmem_limit_bytes=LIMIT
         ),
-        cost_estimate=cost(4 * rows * d * feat, x.size * 4 + wi.size * 2 + devices * chunk * d * 2),
+        cost_estimate=cost(2 * rows * d * feat, x.size * 2 + devices * chunk * d * 2),
         name="image_backward",
     )(core, *operands)
-    return gp, gx, list(zip(out[:2], out[2:]))
+    return gp, list(zip(out[:2], out[2:]))
 
 
 def join_kernel(core_ref, *refs):
@@ -585,7 +584,7 @@
         jax.ShapeDtypeStruct((total, d), bf16),
         jax.ShapeDtypeStruct((total, d), bf16),
         jax.ShapeDtypeStruct((8, d), f32),
-        jax.ShapeDtypeStruct((1, ff), f32),
+        jax.ShapeDtypeStruct((blocks, d), f32),
     ]
     return pl.pallas_call(
         feed_forward,
@@ -596,7 +595,7 @@
             in_specs=[row, row, row, part(down, 0)]
             + ups
             + [whole((d, d)), whole((ff,)), vec, vec, vec, vec],
-            out_specs=[row, wide, row, wide, row, row, row, still((8, d)), still((1, ff))],
+            out_specs=[row, wide, row, wide, row, row, row, still((8, d)), still((blocks, d))],
             scratch_shapes=[pltpu.VMEM((L, ff), f32), pltpu.VMEM((blocks, d, d), bf16)],
         ),
         compiler_params=pltpu.CompilerParams(
@@ -734,19 +733,23 @@
         self.value = (away, kept)
         self.fresh = True
 
+    def prepare(self):
+        bit = self.order[0]
+        axis = self.layout.index(bit)
+        mine = my_bit(bit)
+        self.value = tuple(
+            add_low(*[lax.dynamic_index_in_dim(t, i, axis, keepdims=False) for t in self.value])
+            for i in (1 - mine, mine)
+        )
+        self.fresh = True
+
     def stage(self):
+        if not self.fresh:
+            self.prepare()
+        self.fresh = False
         bit = self.order.pop(0)
-        axis = self.layout.index(bit)
         self.layout.remove(bit)
-        if self.fresh:
-            away, kept = self.value
-            self.fresh = False
-        else:
-            mine = my_bit(bit)
-            away, kept = [
-                add_low(*[lax.dynamic_index_in_dim(t, i, axis, keepdims=False) for t in self.value])
-                for i in (1 - mine, mine)
-            ]
+        away, kept = self.value
         shape = (2,) * len(self.layout) + kept.shape[-2:]
         self.value = (kept.reshape(shape), swap_bit(away, bit).reshape(shape))
         return away
@@ -826,6 +829,10 @@
 
     def run(self):
         return [mover.stage() for mover in self.movers]
+
+    def prepare(self):
+        for mover in self.movers:
+            mover.prepare()
 
     def merge(self):
         first = self.movers[0]
@@ -1044,29 +1051,31 @@
         ff.stage()
         fence([ff])
     in_turn(ff, attn)
+    attn.prepare()
     small_rows = 40
     chunk = 8 * (-(-(feat + small_rows) // (8 * device_count)))
-    grad_pre, grad_feats, img_parts = run_image_backward(
+    grad_pre, img_parts = run_image_backward(
         geometry,
         chunk,
         core,
         region_feats,
         boxes,
-        img_full,
         pre_norm,
         back,
         g_reg,
         sums,
         attn_sums,
-        grad_b_up.reshape(ff_blocks, model_width),
+        grad_b_up,
     )
     img = Sum(img_parts, orders)
+    img.stage()
     fence([ff, attn, img])
     while ff.steps:
         if len(ff.steps) > 1:
             in_turn(ff)
         else:
-            in_turn(ff, attn, img)
+            in_turn(ff, attn)
+            img.prepare()
         fence([ff, attn, img])
     ff = Gather(ff.total(), far)
     in_turn(ff, img, attn)
@@ -1076,7 +1085,7 @@
         fence([attn, img, ff])
     rest = jnp.concatenate([attn.total(), img.total()], 0)
     rest_all = lax.all_gather(rest, axes, axis=0)
-    fence([ff], rest)
+    _, grad_pre = fence([ff], rest, grad_pre)
     while ff.order:
         ff.stage()
         fence([ff])
@@ -1090,6 +1099,7 @@
         core, down_halves, (ff_blocks * model_width, model_width), (1, 0)
     )
     grad_w_up = join_blocks(core, up_halves, (model_width, ff_blocks * model_width), (0, 1))
+    grad_feats = jnp.einsum("rb,ab->ra", grad_pre, img_full, preferred_element_type=f32).astype(bf16)
     grad_boxes = jnp.einsum("cd,rd->cr", w_box, grad_pre, preferred_element_type=f32).astype(bf16)
     (
         grad_w_query,

time: 461 us -> 456 us (0.989)
    convert_element_type x25 -> x27, other arithmetic: 16.4 us -> 14.8 us  [add_low(): return (kept.astype(f32) + came.astype(f32)).astype(bf16)]
  transfers between devices with their start and end apart: 52 -> 52, of which waited for: 37 -> 35; matrix products, arithmetic and copies ran while one was open for 5% -> 6% of each run, Pallas kernels for 21% -> 21%
where the time goes in v7:
time: 456 us; the launch traced here: 447 us
  waiting for transfers between devices  181 us (40%)
  Pallas kernels  154 us (34%)
  starting transfers between devices  56.6 us (12%)
  other arithmetic  22.2 us (5%)
  between operations  15.9 us (3%)
  local copies, waits for them, and re-layouts  14.1 us (3%)
    ppermute x48, waiting for transfers between devices, swap_bit(): return lax.ppermute(tensor, name, [(i, i ^ step) for i in range(size)])  173 us
    ppermute x48, starting transfers between devices, swap_bit(): return lax.ppermute(tensor, name, [(i, i ^ step) for i in range(size)])  49.6 us
    pallas_call x1, Pallas kernels, run_feed_forward(): pl.pallas_call(feed_forward, out_shape=shapes, grid_spec=pltpu.PrefetchSc...  41.7 us
    pallas_call x3, Pallas kernels, weight_grads(): pl.pallas_call(functools.partial(weight_grad_kernel, lhs_of, rhs_of, grou...  30.2 us
    pallas_call x1, Pallas kernels, run_attention_backward(): pl.pallas_call(functools.partial(attention_backward, *geometry), out_shap...  23.7 us
    pallas_call x1, Pallas kernels, run_attention_forward(): pl.pallas_call(functools.partial(attention_forward, *geometry), out_shape...  21.5 us
    convert_element_type x27, other arithmetic, add_low(): return (kept.astype(f32) + came.astype(f32)).astype(bf16)  14.8 us
    pallas_call x2, Pallas kernels, join_blocks(): pl.pallas_call(join_kernel, out_shape=jax.ShapeDtypeStruct(shape, f32), g...  13.1 us
  transfers between devices with their start and end apart: 52, of which 35 were waited for; matrix products, arithmetic and copies ran while one was open for 6% of the time, Pallas kernels for 21%

profile of v7, /device:TPU:0, one launch (start us, length us, event | category | flops | bytes accessed | tf_op | source)
XLA Modules:
  0.0 447.2 jit_solution(2382143395312452444)
XLA Ops:
  7.2 4.1 collective-permute-start
  12.3 1.6 pad_maximum_fusion
  14.8 1.7 collective-permute-done
  17.3 3.5 collective-permute-start.1
  20.7 5.1 %collective-permute-done.2 = bf16[96,768]{1,0:T(8,128)(2,1)S(1)} collective-permute-done((bf16[96,768]{1,0:T(8,128)(2,1)S(1)}, bf16[96,768]{1,0:T(8,128)(2,1)S(1)}, u32[]{:S(2)}, u32[]{:S(2)}) %collective-permute-start.2) | collective-permute-done | bytes 147488 | tf_op jit(solution)/shard_map/ppermute | solution.py:712
  27.3 1.6 collective-permute-start.4
  29.1 1.5 collective-permute-start.3
  30.6 2.8 collective-permute-done.4
  34.9 1.9 collective-permute-done.5
  37.0 1.6 collective-permute-start.7
  39.1 9.1 %collective-permute-done.7 = bf16[2,2,2,32,768]{4,3,2,1,0:T(8,128)(2,1)S(1)} collective-permute-done((bf16[2,2,2,32,768]{4,3,2,1,0:T(8,128)(2,1)S(1)}, bf16[2,2,2,32,768]{4,3,2,1,0:T(8,128)(2,1)S(1)}, u32[]{:S(2)}, u32[]{:S(2)}) %collective-permute-start.7) | collective-permute-done | bytes 393248 | tf_op jit(solution)/shard_map/ppermute | solution.py:712
  50.2 1.7 collective-permute-done.8
  55.0 8.0 %image_encode.1 = (f32[416,768]{1,0:T(8,128)}, bf16[512,768]{1,0:T(8,128)(2,1)}, bf16[32,64,768]{2,1,0:T(8,128)(2,1)}) custom-call(s32[1]{0:T(128)} %bitcast.6.core_ref, bf16[416,2048]{1,0:T(8,128)(2,1)} %x_ref.3, bf16[4,416]{1,0:T(4,128)(2,1)} %box_ref.3, bf16[4,768]{1,0:T(4,128)(2,1)} %wb_ref.1, f32[768]{0:T(1024)} %bi_ref.1, f32[768]{0:T(1024)} %gr_ref.3, ...), custom_call_target="tpu_custom_call" | custom-call | flops 1308622848 | bytes 9912320 | tf_op jit(solution)/shard_map/image_encode/pallas_call | solution.py:361
  63.0 5.1 %collective-permute-done.11 = bf16[2,2,48,768]{3,2,1,0:T(8,128)(2,1)S(1)} collective-permute-done((bf16[2,2,48,768]{3,2,1,0:T(8,128)(2,1)S(1)}, bf16[2,2,48,768]{3,2,1,0:T(8,128)(2,1)S(1)}, u32[]{:S(2)}, u32[]{:S(2)}) %collective-permute-start.11) | collective-permute-done | bytes 294944 | tf_op jit(solution)/shard_map/ppermute | solution.py:712
  68.4 3.6 all-to-all-start
  72.0 1.8 collective-permute-start.13
  75.2 26.4 %collective-permute-done.13 = bf16[2,2,2,48,768]{4,3,2,1,0:T(8,128)(2,1)S(1)} collective-permute-done((bf16[2,2,2,48,768]{4,3,2,1,0:T(8,128)(2,1)S(1)}, bf16[2,2,2,48,768]{4,3,2,1,0:T(8,128)(2,1)S(1)}, u32[]{:S(2)}, u32[]{:S(2)}) %collective-permute-start.13) | collective-permute-done | bytes 589856 | tf_op jit(solution)/shard_map/ppermute | solution.py:712
  102.1 4.9 %all-to-all-done = bf16[32,16,768]{2,1,0:T(8,128)(2,1)} async-done(((bf16[32,16,768]{2,1,0:T(8,128)(2,1)}), bf16[32,16,768]{2,1,0:T(8,128)(2,1)}, u32[]{:S(2)}, u32[]{:S(2)}) %all-to-all-start) | async-done | bytes 786464 | tf_op jit(solution)/shard_map/all_to_all | solution.py:921
  108.8 2.1 collective-permute-done.14
  111.8 1.7 bitcast_select_fusion
  113.5 2.2 fusion.39
  115.7 21.5 %attention_forward.1 = (bf16[1024,768]{1,0:T(8,128)(2,1)}, bf16[1024,768]{1,0:T(8,128)(2,1)}, bf16[1024,768]{1,0:T(8,128)(2,1)}, bf16[1024,768]{1,0:T(8,128)(2,1...) custom-call(s32[4]{0:T(128)} %captions.3, ...), custom_call_target="tpu_custom_call" | custom-call | flops 8053063680 | bytes 20447232 | tf_op jit(solution)/shard_map/attention_forward/pallas_call | solution.py:395
  137.3 41.7 %feed_forward.1 = (bf16[1024,768]{1,0:T(8,128)(2,1)}, bf16[1024,3072]{1,0:T(8,128)(2,1)}, bf16[1024,768]{1,0:T(8,128)(2,1)}, bf16[1024,3072]{1,0:T(8,128)(2,1)},...) custom-call(s32[4]{0:T(128)} %captions.3, ...), custom_call_target="tpu_custom_call" | custom-call | flops 20535312384 | bytes 36175872 | tf_op jit(solution)/shard_map/feed_forward/pallas_call | solution.py:589
  179.0 9.4 %grad_w_down.1 = (bf16[16,96,768]{2,1,0:T(8,128)(2,1)}, bf16[16,96,768]{2,1,0:T(8,128)(2,1)}) custom-call(s32[1]{0:T(128)} %bitcast.6.core_ref, bf16[1024,3072]{1,0:T(8,128)(2,1)} %get-tuple-element.249.refs_0_, bf16[1024,768]{1,0:T(8,128)(2,1)} %get-tuple-element.250.refs_1_), custom_call_target="tpu_custom_call" | custom-call | flops 4831838208 | bytes 11010048 | tf_op jit(solution)/shard_map/grad_w_down/pallas_call | solution.py:672
  188.7 9.6 %grad_w_up.1 = (bf16[16,96,768]{2,1,0:T(8,128)(2,1)}, bf16[16,96,768]{2,1,0:T(8,128)(2,1)}) custom-call(s32[1]{0:T(128)} %bitcast.6.core_ref, bf16[1024,768]{1,0:T(8,128)(2,1)} %get-tuple-element.240.n_ref.refs_0_, bf16[1024,3072]{1,0:T(8,128)(2,1)} %get-tuple-element.253.refs_1_), custom_call_target="tpu_custom_call" | custom-call | flops 4831838208 | bytes 11010048 | tf_op jit(solution)/shard_map/grad_w_up/pallas_call | solution.py:672
  198.6 1.8 constant_dynamic-slice_fusion.9
  200.5 2.7 collective-permute-done.17
  203.2 1.6 fusion.3
  204.8 2.6 fusion.1
  209.9 23.7 %attention_backward.1 = (bf16[1024,768]{1,0:T(8,128)(2,1)}, bf16[1024,768]{1,0:T(8,128)(2,1)}, bf16[1024,768]{1,0:T(8,128)(2,1)}, bf16[512,768]{1,0:T(8,128)(2,1...) custom-call(s32[4]{0:T(128)} %counts.5, s32[1]{0:T(128)S(6)} %copy.133.offset, ...), custom_call_target="tpu_custom_call" | custom-call | flops 10066329600 | bytes 22020096 | tf_op jit(solution)/shard_map/attention_backward/pallas_call | solution.py:621
  233.6 2.3 collective-permute-done.19
  236.3 3.3 all-to-all-start.1
  239.7 2.0 fusion.15
  241.7 1.6 collective-permute-start.21
  243.3 2.4 fusion.8
  248.3 11.2 %grad_w_attn.1 = (bf16[16,48,768]{2,1,0:T(8,128)(2,1)}, bf16[16,48,768]{2,1,0:T(8,128)(2,1)}, bf16[16,48,768]{2,1,0:T(8,128)(2,1)}, bf16[16,48,768]{2,1,0:T(8,128)(2,1)}) custom-call(s32[1]{0:T(128)} %bitcast.6.core_ref, bf16[1024,768]{1,0:T(8,128)(2,1)} %get-tuple-element.268.refs_0_, bf16[1024,768]{1,0:T(8,128)(2,1)} %get-tuple-element.269.refs_1_, ...), custom_call_target="tpu_custom_call" | custom-call | flops 4831838208 | bytes 11010048 | tf_op jit(solution)/shard_map/grad_w_attn/pallas_call | solution.py:672
  259.6 3.8 collective-permute-done.21
  263.4 1.8 collective-permute-done.20
  268.5 1.6 collective-permute-start.22
  270.4 7.2 %image_backward.1 = (bf16[416,768]{1,0:T(8,128)(2,1)}, bf16[16,40,768]{2,1,0:T(8,128)(2,1)}, bf16[16,32,768]{2,1,0:T(8,128)(2,1)}, bf16[16,40,768]{2,1,0:T(8,128)(2,1)}, bf16[16,32,768]{2,1,0:T(8,128)(2,1)}) custom-call(s32[1]{0:T(128)} %bitcast.6.core_ref, bf16[416,2048]{1,0:T(8,128)(2,1)} %x_ref.3, bf16[4,416]{1,0:T(4,128)(2,1)} %box_ref.3, ...), custom_call_target="tpu_custom_call" | custom-call | flops 1308622848 | bytes 5242880 | tf_op jit(solution)/shard_map/image_backward/pallas_call | solution.py:428
  282.2 2.3 collective-permute-done.22
  287.2 2.5 collective-permute-start.27
  290.2 12.5 %collective-permute-done.27 = bf16[192,768]{1,0:T(8,128)(2,1)S(1)} collective-permute-done((bf16[192,768]{1,0:T(8,128)(2,1)S(1)}, bf16[192,768]{1,0:T(8,128)(2,1)S(1)}, u32[]{:S(2)}, u32[]{:S(2)}) %collective-permute-start.27) | collective-permute-done | bytes 294944 | tf_op jit(solution)/shard_map/ppermute | solution.py:712
  308.3 9.6 %collective-permute-done.34 = bf16[192,768]{1,0:T(8,128)(2,1)S(1)} collective-permute-done((bf16[192,768]{1,0:T(8,128)(2,1)S(1)}, bf16[192,768]{1,0:T(8,128)(2,1)S(1)}, u32[]{:S(2)}, u32[]{:S(2)}) %collective-permute-start.34) | collective-permute-done | bytes 294944 | tf_op jit(solution)/shard_map/ppermute | solution.py:712
  318.0 3.5 collective-permute-done.31
  321.8 3.1 collective-permute-start.35
  325.0 1.8 collective-permute-start.36
  326.9 1.7 collective-permute-start.37
  328.5 4.1 collective-permute-done.37
  333.6 8.3 %collective-permute-done.38 = bf16[96,768]{1,0:T(8,128)(2,1)S(1)} collective-permute-done((bf16[96,768]{1,0:T(8,128)(2,1)S(1)}, bf16[96,768]{1,0:T(8,128)(2,1)S(1)}, u32[]{:S(2)}, u32[]{:S(2)}) %collective-permute-start.38) | collective-permute-done | bytes 147488 | tf_op jit(solution)/shard_map/ppermute | solution.py:712
  342.2 6.0 %collective-permute-done.40 = bf16[72,768]{1,0:T(8,128)(2,1)S(1)} collective-permute-done((bf16[72,768]{1,0:T(8,128)(2,1)S(1)}, bf16[72,768]{1,0:T(8,128)(2,1)S(1)}, u32[]{:S(2)}, u32[]{:S(2)}) %collective-permute-start.40) | collective-permute-done | bytes 110624 | tf_op jit(solution)/shard_map/ppermute | solution.py:712
  349.0 13.0 %collective-permute-done.41 = bf16[2,192,768]{2,1,0:T(8,128)(2,1)S(1)} collective-permute-done((bf16[2,192,768]{2,1,0:T(8,128)(2,1)S(1)}, bf16[2,192,768]{2,1,0:T(8,128)(2,1)S(1)}, u32[]{:S(2)}, u32[]{:S(2)}) %collective-permute-start.41) | collective-permute-done | bytes 589856 | tf_op jit(solution)/shard_map/ppermute | solution.py:712
  363.5 1.7 collective-permute-start.42
  365.2 9.6 %collective-permute-done.43 = bf16[2,2,96,768]{3,2,1,0:T(8,128)(2,1)S(1)} collective-permute-done((bf16[2,2,96,768]{3,2,1,0:T(8,128)(2,1)S(1)}, bf16[2,2,96,768]{3,2,1,0:T(8,128)(2,1)S(1)}, u32[]{:S(2)}, u32[]{:S(2)}) %collective-permute-start.43) | collective-permute-done | bytes 589856 | tf_op jit(solution)/shard_map/ppermute | solution.py:712
  375.0 4.8 %collective-permute-done.42 = bf16[2,2,96,768]{3,2,1,0:T(8,128)(2,1)S(1)} collective-permute-done((bf16[2,2,96,768]{3,2,1,0:T(8,128)(2,1)S(1)}, bf16[2,2,96,768]{3,2,1,0:T(8,128)(2,1)S(1)}, u32[]{:S(2)}, u32[]{:S(2)}) %collective-permute-start.42) | collective-permute-done | bytes 589856 | tf_op jit(solution)/shard_map/ppermute | solution.py:712
  379.9 2.5 collective-permute-start.45
  382.5 19.9 %collective-permute-done.45 = bf16[2,2,2,96,768]{4,3,2,1,0:T(8,128)(2,1)S(1)} collective-permute-done((bf16[2,2,2,96,768]{4,3,2,1,0:T(8,128)(2,1)S(1)}, bf16[2,2,2,96,768]{4,3,2,1,0:T(8,128)(2,1)S(1)}, u32[]{:S(2)}, u32[]{:S(2)}) %collective-permute-start.45) | collective-permute-done | bytes 1179680 | tf_op jit(solution)/shard_map/ppermute | solution.py:712
  402.6 3.7 collective-permute-done.44
  408.0 2.7 convolution_convert_fusion
  410.7 2.9 collective-permute-done.47
  415.0 6.5 %join_blocks.3 = f32[3072,768]{1,0:T(8,128)} custom-call(s32[1]{0:T(128)} %bitcast.6.core_ref, bf16[16,96,768]{2,1,0:T(8,128)(2,1)} %bitcast.131, bf16[16,96,768]{2,1,0:T(8,128)(2,1)} %bitcast.139), custom_call_target="tpu_custom_call" | custom-call | bytes 14155776 | tf_op jit(solution)/shard_map/join_blocks/pallas_call | solution.py:469
  421.5 6.5 %join_blocks.2 = f32[768,3072]{1,0:T(8,128)} custom-call(s32[1]{0:T(128)} %bitcast.6.core_ref, bf16[16,96,768]{2,1,0:T(8,128)(2,1)} %bitcast.130, bf16[16,96,768]{2,1,0:T(8,128)(2,1)} %bitcast.73.refs_1_), custom_call_target="tpu_custom_call" | custom-call | bytes 14155776 | tf_op jit(solution)/shard_map/join_blocks/pallas_call | solution.py:469
  428.1 3.6 all-gather.7.cloned.1.call-done
  431.7 8.2 %widen_rest.1 = (f32[768,768]{1,0:T(8,128)}, f32[768,768]{1,0:T(8,128)}, f32[768,768]{1,0:T(8,128)}, f32[768,768]{1,0:T(8,128)}, f32[2048,768]{1,0:T(8,128)}, /*...) custom-call(bf16[32,168,768]{2,1,0:T(8,128)(2,1)} %bitcast.132), custom_call_target="tpu_custom_call" | custom-call | bytes 24772608 | tf_op jit(solution)/shard_map/widen_rest/pallas_call | solution.py:533
  (170 shorter events, 46.6 us)
Async XLA Ops:
  7.2 9.3 %copy-start.13 = (bf16[64,768]{1,0:T(8,128)(2,1)S(1)}, bf16[64,768]{1,0:T(8,128)(2,1)}, u32[]{:S(2)}) copy-start(bf16[64,768]{1,0:T(8,128)(2,1)} %param.33) | copy-start | bytes 294916
  7.2 130.1 %all-gather.5.cloned.1.call-start = ((), (), s32[]{:S(2)}) async-start(), calls=%async_computation.2 | async-start | bytes 9732096 | tf_op jit(solution)/shard_map/all_gather | solution.py:897
  7.2 9.2 %collective-permute-start = (bf16[64,768]{1,0:T(8,128)(2,1)}, bf16[64,768]{1,0:T(8,128)(2,1)S(1)}, u32[]{:S(2)}, u32[]{:S(2)}) collective-permute-start(bf16[64,768]{1,0:T(8,128)(2,1)} %param.33), channel_id=1, source_target_pairs={{0,16},{8,24},{16,0},{24,8},{1,17},{9,25},{17,1},{25,9},{2,18},{10... | collective-permute-start | bytes 294920 | tf_op jit(solution)/shard_map/ppermute | solution.py:712
  14.8 11.2 %copy-start.15 = (pred[2]{0:T(512)(128)(4,1)}, pred[2]{0:T(512)(128)(4,1)S(1)}, u32[]{:S(2)}) copy-start(pred[2]{0:T(512)(128)(4,1)S(1)} %iota_compare_fusion.1) | copy-start | bytes 10
  16.6 9.3 %collective-permute-start.2 = (bf16[96,768]{1,0:T(8,128)(2,1)S(1)}, bf16[96,768]{1,0:T(8,128)(2,1)S(1)}, u32[]{:S(2)}, u32[]{:S(2)}) collective-permute-start(bf16[96,768]{1,0:T(8,128)(2,1)S(1)} %pad_maximum_fusion.2), channel_id=1, source_target_pairs={{0,16},{8,24},{16,0},{24,8},{1,17},{9,25},{17,1},{25,9},{2,18},{10... | collective-permute-start | bytes 442376 | tf_op jit(solution)/shard_map/ppermute | solution.py:712
  17.3 9.8 %collective-permute-start.1 = (bf16[2,64,768]{2,1,0:T(8,128)(2,1)S(1)}, bf16[2,64,768]{2,1,0:T(8,128)(2,1)S(1)}, u32[]{:S(2)}, u32[]{:S(2)}) collective-permute-start(bf16[2,64,768]{2,1,0:T(8,128)(2,1)S(1)} %broadcast_select_fusion.17), channel_id=1, source_target_pairs={{0,8},{8,0},{16,24},{24,16},{1,9},{9,1},{17,25},{25,17},{2,10},{10... | collective-permute-start | bytes 589832 | tf_op jit(solution)/shard_map/ppermute | solution.py:712
  27.3 6.1 %collective-permute-start.4 = (bf16[2,2,32,768]{3,2,1,0:T(8,128)(2,1)S(1)}, bf16[2,2,32,768]{3,2,1,0:T(8,128)(2,1)S(1)}, u32[]{:S(2)}, u32[]{:S(2)}) collective-permute-start(bf16[2,2,32,768]{3,2,1,0:T(8,128)(2,1)S(1)} %get-tuple-element.452), channel_id=1, source_target_pairs={{0,2},{1,3},{2,0},{3,1},{4,6},{5,7},{6,4},{7,5},{8,10},{9,11},{10,... | collective-permute-start | bytes 589832 | tf_op jit(solution)/shard_map/ppermute | solution.py:712
  28.9 8.0 %collective-permute-start.5 = (bf16[2,96,768]{2,1,0:T(8,128)(2,1)S(1)}, bf16[2,96,768]{2,1,0:T(8,128)(2,1)S(1)}, u32[]{:S(2)}, u32[]{:S(2)}) collective-permute-start(bf16[2,96,768]{2,1,0:T(8,128)(2,1)S(1)} %broadcast_select_fusion.16), channel_id=1, source_target_pairs={{0,8},{8,0},{16,24},{24,16},{1,9},{9,1},{17,25},{25,17},{2,10},{10... | collective-permute-start | bytes 884744 | tf_op jit(solution)/shard_map/ppermute | solution.py:712
  29.1 5.7 %collective-permute-start.3 = (bf16[2,2,32,768]{3,2,1,0:T(8,128)(2,1)S(1)}, bf16[2,2,32,768]{3,2,1,0:T(8,128)(2,1)S(1)}, u32[]{:S(2)}, u32[]{:S(2)}) collective-permute-start(bf16[2,2,32,768]{3,2,1,0:T(8,128)(2,1)S(1)} %get-tuple-element.453), channel_id=1, source_target_pairs={{0,4},{1,5},{2,6},{3,7},{4,0},{5,1},{6,2},{7,3},{8,12},{9,13},{10,... | collective-permute-start | bytes 589832 | tf_op jit(solution)/shard_map/ppermute | solution.py:712
  37.0 11.2 %collective-permute-start.7 = (bf16[2,2,2,32,768]{4,3,2,1,0:T(8,128)(2,1)S(1)}, bf16[2,2,2,32,768]{4,3,2,1,0:T(8,128)(2,1)S(1)}, u32[]{:S(2)}, u32[]{:S(2)}) collective-permute-start(bf16[2,2,2,32,768]{4,3,2,1,0:T(8,128)(2,1)S(1)} %broadcast_select_fusion.13), channel_id=1, source_target_pairs={{0,4},{1,5},{2,6},{3,7},{4,0},{5,1},{6,2},{7,3},{8,12},{9,13},{10,... | collective-permute-start | bytes 1179656 | tf_op jit(solution)/shard_map/ppermute | solution.py:712
  38.5 10.9 %collective-permute-start.6 = (bf16[2,2,2,32,768]{4,3,2,1,0:T(8,128)(2,1)S(1)}, bf16[2,2,2,32,768]{4,3,2,1,0:T(8,128)(2,1)S(1)}, u32[]{:S(2)}, u32[]{:S(2)}) collective-permute-start(bf16[2,2,2,32,768]{4,3,2,1,0:T(8,128)(2,1)S(1)} %broadcast_select_fusion.15), channel_id=1, source_target_pairs={{0,2},{1,3},{2,0},{3,1},{4,6},{5,7},{6,4},{7,5},{8,10},{9,11},{10,... | collective-permute-start | bytes 1179656 | tf_op jit(solution)/shard_map/ppermute | solution.py:712
  49.6 5.4 %copy-start.3 = (bf16[2,2,2,2,32,768]{5,4,3,2,1,0:T(8,128)(2,1)}, bf16[2,2,2,2,32,768]{5,4,3,2,1,0:T(8,128)(2,1)S(1)}, u32[]{:S(2)}) copy-start(bf16[2,2,2,2,32,768]{5,4,3,2,1,0:T(8,128)(2,1)S(1)} %broadcast_select_fusion.8) | copy-start | bytes 2359300
  49.6 2.4 collective-permute-start.8
  49.7 3.4 collective-permute-start.9
  51.9 3.0 copy-start.10
  53.9 14.2 %collective-permute-start.11 = (bf16[2,2,48,768]{3,2,1,0:T(8,128)(2,1)S(1)}, bf16[2,2,48,768]{3,2,1,0:T(8,128)(2,1)S(1)}, u32[]{:S(2)}, u32[]{:S(2)}) collective-permute-start(bf16[2,2,48,768]{3,2,1,0:T(8,128)(2,1)S(1)} %get-tuple-element.228), channel_id=1, source_target_pairs={{0,2},{1,3},{2,0},{3,1},{4,6},{5,7},{6,4},{7,5},{8,10},{9,11},{10,... | collective-permute-start | bytes 884744 | tf_op jit(solution)/shard_map/ppermute | solution.py:712
  54.5 13.8 %collective-permute-start.10 = (bf16[2,2,48,768]{3,2,1,0:T(8,128)(2,1)S(1)}, bf16[2,2,48,768]{3,2,1,0:T(8,128)(2,1)S(1)}, u32[]{:S(2)}, u32[]{:S(2)}) collective-permute-start(bf16[2,2,48,768]{3,2,1,0:T(8,128)(2,1)S(1)} %get-tuple-element.227), channel_id=1, source_target_pairs={{0,4},{1,5},{2,6},{3,7},{4,0},{5,1},{6,2},{7,3},{8,12},{9,13},{10,... | collective-permute-start | bytes 884744 | tf_op jit(solution)/shard_map/ppermute | solution.py:712
  68.4 38.7 %all-to-all-start = ((bf16[32,16,768]{2,1,0:T(8,128)(2,1)}), bf16[32,16,768]{2,1,0:T(8,128)(2,1)}, u32[]{:S(2)}, u32[]{:S(2)}) async-start(bf16[32,16,768]{2,1,0:T(8,128)(2,1)} %bitcast.7), calls=%async_computation | async-start | bytes 1572864 | tf_op jit(solution)/shard_map/all_to_all | solution.py:921
  72.0 29.6 %collective-permute-start.13 = (bf16[2,2,2,48,768]{4,3,2,1,0:T(8,128)(2,1)S(1)}, bf16[2,2,2,48,768]{4,3,2,1,0:T(8,128)(2,1)S(1)}, u32[]{:S(2)}, u32[]{:S(2)}) collective-permute-start(bf16[2,2,2,48,768]{4,3,2,1,0:T(8,128)(2,1)S(1)} %broadcast_select_fusion.10), channel_id=1, source_target_pairs={{0,4},{1,5},{2,6},{3,7},{4,0},{5,1},{6,2},{7,3},{8,12},{9,13},{10,... | collective-permute-start | bytes 1769480 | tf_op jit(solution)/shard_map/ppermute | solution.py:712
  73.8 28.2 %collective-permute-start.12 = (bf16[2,2,2,48,768]{4,3,2,1,0:T(8,128)(2,1)S(1)}, bf16[2,2,2,48,768]{4,3,2,1,0:T(8,128)(2,1)S(1)}, u32[]{:S(2)}, u32[]{:S(2)}) collective-permute-start(bf16[2,2,2,48,768]{4,3,2,1,0:T(8,128)(2,1)S(1)} %broadcast_select_fusion.12), channel_id=1, source_target_pairs={{0,2},{1,3},{2,0},{3,1},{4,6},{5,7},{6,4},{7,5},{8,10},{9,11},{10,... | collective-permute-start | bytes 1769480 | tf_op jit(solution)/shard_map/ppermute | solution.py:712
  107.0 3.9 collective-permute-start.14
  107.1 4.7 %collective-permute-start.15 = (bf16[2,2,2,2,48,768]{5,4,3,2,1,0:T(8,128)(2,1)S(1)}, bf16[2,2,2,2,48,768]{5,4,3,2,1,0:T(8,128)(2,1)}, u32[]{:S(2)}, u32[]{:S(2)}) collective-permute-start(bf16[2,2,2,2,48,768]{5,4,3,2,1,0:T(8,128)(2,1)S(1)} %broadcast_select_fusion.5), channel_id=1, source_target_pairs={{0,1},{1,0},{2,3},{3,2},{4,5},{5,4},{6,7},{7,6},{8,9},{9,8},{10,11... | collective-permute-start | bytes 3538952 | tf_op jit(solution)/shard_map/ppermute | solution.py:712
  188.4 11.9 %collective-permute-start.16 = (bf16[16,96,768]{2,1,0:T(8,128)(2,1)}, bf16[16,96,768]{2,1,0:T(8,128)(2,1)S(1)}, u32[]{:S(2)}, u32[]{:S(2)}) collective-permute-start(bf16[16,96,768]{2,1,0:T(8,128)(2,1)} %get-tuple-element.252), channel_id=1, source_target_pairs={{0,1},{1,0},{2,3},{3,2},{4,5},{5,4},{6,7},{7,6},{8,9},{9,8},{10,11... | collective-permute-start | bytes 7077896 | tf_op jit(solution)/shard_map/ppermute | solution.py:712
  198.3 4.9 %collective-permute-start.17 = (bf16[16,96,768]{2,1,0:T(8,128)(2,1)}, bf16[16,96,768]{2,1,0:T(8,128)(2,1)}, u32[]{:S(2)}, u32[]{:S(2)}) collective-permute-start(bf16[16,96,768]{2,1,0:T(8,128)(2,1)} %get-tuple-element.255), channel_id=1, source_target_pairs={{0,1},{1,0},{2,3},{3,2},{4,5},{5,4},{6,7},{7,6},{8,9},{9,8},{10,11... | collective-permute-start | bytes 7077896 | tf_op jit(solution)/shard_map/ppermute | solution.py:712
  207.4 28.4 %collective-permute-start.19 = (bf16[2,2,2,96,768]{4,3,0,1,2:T(8,128)(2,1)}, bf16[2,2,2,96,768]{4,3,0,1,2:T(8,128)(2,1)}, u32[]{:S(2)}, u32[]{:S(2)}) collective-permute-start(bf16[2,2,2,96,768]{4,3,0,1,2:T(8,128)(2,1)} %fusion.1), channel_id=1, source_target_pairs={{0,4},{1,5},{2,6},{3,7},{4,0},{5,1},{6,2},{7,3},{8,12},{9,13},{10,... | collective-permute-start | bytes 3538952 | tf_op jit(solution)/shard_map/ppermute | solution.py:712
  208.2 28.1 %collective-permute-start.18 = (bf16[2,2,2,96,768]{4,3,0,1,2:T(8,128)(2,1)S(1)}, bf16[2,2,2,96,768]{4,3,0,1,2:T(8,128)(2,1)}, u32[]{:S(2)}, u32[]{:S(2)}) collective-permute-start(bf16[2,2,2,96,768]{4,3,0,1,2:T(8,128)(2,1)S(1)} %fusion), channel_id=1, source_target_pairs={{0,2},{1,3},{2,0},{3,1},{4,6},{5,7},{6,4},{7,5},{8,10},{9,11},{10,... | collective-permute-start | bytes 3538952 | tf_op jit(solution)/shard_map/ppermute | solution.py:712
  236.3 28.9 %all-to-all-start.1 = ((bf16[32,16,768]{2,1,0:T(8,128)(2,1)}), bf16[32,16,768]{2,1,0:T(8,128)(2,1)}, u32[]{:S(2)}, u32[]{:S(2)}) async-start(bf16[32,16,768]{2,1,0:T(8,128)(2,1)} %bitcast.153), calls=%async_computation.1 | async-start | bytes 1572864 | tf_op jit(solution)/shard_map/all_to_all | solution.py:1033
  239.6 192.1 %all-gather.7.cloned.1.call-start = ((), (), s32[]{:S(2)}) async-start(), calls=%async_computation.3 | async-start | bytes 8515584 | tf_op jit(solution)/shard_map/all_gather | solution.py:1087
  241.7 21.7 %collective-permute-start.21 = (bf16[2,2,96,768]{3,2,1,0:T(8,128)(2,1)}, bf16[2,2,96,768]{3,2,1,0:T(8,128)(2,1)}, u32[]{:S(2)}, u32[]{:S(2)}) collective-permute-start(bf16[2,2,96,768]{3,2,1,0:T(8,128)(2,1)} %fusion.15), channel_id=1, source_target_pairs={{0,2},{1,3},{2,0},{3,1},{4,6},{5,7},{6,4},{7,5},{8,10},{9,11},{10,... | collective-permute-start | bytes 1769480 | tf_op jit(solution)/shard_map/ppermute | solution.py:712
  245.6 19.6 %collective-permute-start.20 = (bf16[2,2,96,768]{3,2,0,1:T(8,128)(2,1)}, bf16[2,2,96,768]{3,2,0,1:T(8,128)(2,1)}, u32[]{:S(2)}, u32[]{:S(2)}) collective-permute-start(bf16[2,2,96,768]{3,2,0,1:T(8,128)(2,1)} %get-tuple-element.408), channel_id=1, source_target_pairs={{0,4},{1,5},{2,6},{3,7},{4,0},{5,1},{6,2},{7,3},{8,12},{9,13},{10,... | collective-permute-start | bytes 1769480 | tf_op jit(solution)/shard_map/ppermute | solution.py:712
  268.5 11.7 %collective-permute-start.24 = (bf16[16,48,768]{2,1,0:T(8,128)(2,1)}, bf16[16,48,768]{2,1,0:T(8,128)(2,1)S(1)}, u32[]{:S(2)}, u32[]{:S(2)}) collective-permute-start(bf16[16,48,768]{2,1,0:T(8,128)(2,1)} %get-tuple-element.294), channel_id=1, source_target_pairs={{0,1},{1,0},{2,3},{3,2},{4,5},{5,4},{6,7},{7,6},{8,9},{9,8},{10,11... | collective-permute-start | bytes 3538952 | tf_op jit(solution)/shard_map/ppermute | solution.py:712
  268.5 16.1 %collective-permute-start.22 = (bf16[2,192,768]{2,1,0:T(8,128)(2,1)}, bf16[2,192,768]{2,1,0:T(8,128)(2,1)}, u32[]{:S(2)}, u32[]{:S(2)}) collective-permute-start(bf16[2,192,768]{2,1,0:T(8,128)(2,1)} %fusion.16), channel_id=1, source_target_pairs={{0,8},{8,0},{16,24},{24,16},{1,9},{9,1},{17,25},{25,17},{2,10},{10... | collective-permute-start | bytes 1769480 | tf_op jit(solution)/shard_map/ppermute | solution.py:712
  270.1 10.4 %collective-permute-start.23 = (bf16[16,48,768]{2,1,0:T(8,128)(2,1)}, bf16[16,48,768]{2,1,0:T(8,128)(2,1)}, u32[]{:S(2)}, u32[]{:S(2)}) collective-permute-start(bf16[16,48,768]{2,1,0:T(8,128)(2,1)} %get-tuple-element.292), channel_id=1, source_target_pairs={{0,1},{1,0},{2,3},{3,2},{4,5},{5,4},{6,7},{7,6},{8,9},{9,8},{10,11... | collective-permute-start | bytes 3538952 | tf_op jit(solution)/shard_map/ppermute | solution.py:712
  277.5 7.0 %collective-permute-start.25 = (bf16[16,40,768]{2,1,0:T(8,128)(2,1)}, bf16[16,40,768]{2,1,0:T(8,128)(2,1)S(1)}, u32[]{:S(2)}, u32[]{:S(2)}) collective-permute-start(bf16[16,40,768]{2,1,0:T(8,128)(2,1)} %get-tuple-element.301), channel_id=1, source_target_pairs={{0,1},{1,0},{2,3},{3,2},{4,5},{5,4},{6,7},{7,6},{8,9},{9,8},{10,11... | collective-permute-start | bytes 2949128 | tf_op jit(solution)/shard_map/ppermute | solution.py:712
  277.8 6.7 %collective-permute-start.26 = (bf16[16,32,768]{2,1,0:T(8,128)(2,1)}, bf16[16,32,768]{2,1,0:T(8,128)(2,1)S(1)}, u32[]{:S(2)}, u32[]{:S(2)}) collective-permute-start(bf16[16,32,768]{2,1,0:T(8,128)(2,1)} %get-tuple-element.303), channel_id=1, source_target_pairs={{0,1},{1,0},{2,3},{3,2},{4,5},{5,4},{6,7},{7,6},{8,9},{9,8},{10,11... | collective-permute-start | bytes 2359304 | tf_op jit(solution)/shard_map/ppermute | solution.py:712
  282.2 7.5 %copy-start.9 = (bf16[16,32,768]{2,1,0:T(8,128)(2,1)S(1)}, bf16[16,32,768]{2,1,0:T(8,128)(2,1)}, u32[]{:S(2)}) copy-start(bf16[16,32,768]{2,1,0:T(8,128)(2,1)} %get-tuple-element.302) | copy-start | bytes 2359300
  285.8 4.2 copy-start.8
  285.8 16.9 %collective-permute-start.28 = (bf16[2,2,2,48,768]{4,3,0,1,2:T(8,128)(2,1)S(1)}, bf16[2,2,2,48,768]{4,3,0,1,2:T(8,128)(2,1)S(1)}, u32[]{:S(2)}, u32[]{:S(2)}) collective-permute-start(bf16[2,2,2,48,768]{4,3,0,1,2:T(8,128)(2,1)S(1)} %fusion.11), channel_id=1, source_target_pairs={{0,2},{1,3},{2,0},{3,1},{4,6},{5,7},{6,4},{7,5},{8,10},{9,11},{10,... | collective-permute-start | bytes 1769480 | tf_op jit(solution)/shard_map/ppermute | solution.py:712
  286.2 16.5 %collective-permute-start.29 = (bf16[2,2,2,48,768]{4,3,0,1,2:T(8,128)(2,1)S(1)}, bf16[2,2,2,48,768]{4,3,0,1,2:T(8,128)(2,1)S(1)}, u32[]{:S(2)}, u32[]{:S(2)}) collective-permute-start(bf16[2,2,2,48,768]{4,3,0,1,2:T(8,128)(2,1)S(1)} %fusion.13), channel_id=1, source_target_pairs={{0,4},{1,5},{2,6},{3,7},{4,0},{5,1},{6,2},{7,3},{8,12},{9,13},{10,... | collective-permute-start | bytes 1769480 | tf_op jit(solution)/shard_map/ppermute | solution.py:712
  287.2 15.4 %collective-permute-start.27 = (bf16[192,768]{1,0:T(8,128)(2,1)S(1)}, bf16[192,768]{1,0:T(8,128)(2,1)S(1)}, u32[]{:S(2)}, u32[]{:S(2)}) collective-permute-start(bf16[192,768]{1,0:T(8,128)(2,1)S(1)} %get-tuple-element.430), channel_id=1, source_target_pairs={{0,16},{8,24},{16,0},{24,8},{1,17},{9,25},{17,1},{25,9},{2,18},{10... | collective-permute-start | bytes 884744 | tf_op jit(solution)/shard_map/ppermute | solution.py:712
  302.8 15.1 %collective-permute-start.34 = (bf16[192,768]{1,0:T(8,128)(2,1)S(1)}, bf16[192,768]{1,0:T(8,128)(2,1)S(1)}, u32[]{:S(2)}, u32[]{:S(2)}) collective-permute-start(bf16[192,768]{1,0:T(8,128)(2,1)S(1)} %add_convert_fusion.22), channel_id=1, source_target_pairs={{0,16},{8,24},{16,0},{24,8},{1,17},{9,25},{17,1},{25,9},{2,18},{10... | collective-permute-start | bytes 884744 | tf_op jit(solution)/shard_map/ppermute | solution.py:712
  303.8 17.7 %collective-permute-start.32 = (bf16[2,2,2,40,768]{4,3,0,1,2:T(8,128)(2,1)S(1)}, bf16[2,2,2,40,768]{4,3,0,1,2:T(8,128)(2,1)S(1)}, u32[]{:S(2)}, u32[]{:S(2)}) collective-permute-start(bf16[2,2,2,40,768]{4,3,0,1,2:T(8,128)(2,1)S(1)} %get-tuple-element.330), channel_id=1, source_target_pairs={{0,2},{1,3},{2,0},{3,1},{4,6},{5,7},{6,4},{7,5},{8,10},{9,11},{10,... | collective-permute-start | bytes 1474568 | tf_op jit(solution)/shard_map/ppermute | solution.py:712
  305.2 16.3 %collective-permute-start.33 = (bf16[2,2,2,32,768]{4,3,0,1,2:T(8,128)(2,1)S(1)}, bf16[2,2,2,32,768]{4,3,0,1,2:T(8,128)(2,1)S(1)}, u32[]{:S(2)}, u32[]{:S(2)}) collective-permute-start(bf16[2,2,2,32,768]{4,3,0,1,2:T(8,128)(2,1)S(1)} %get-tuple-element.331), channel_id=1, source_target_pairs={{0,4},{1,5},{2,6},{3,7},{4,0},{5,1},{6,2},{7,3},{8,12},{9,13},{10,... | collective-permute-start | bytes 1179656 | tf_op jit(solution)/shard_map/ppermute | solution.py:712
  306.1 11.8 %copy-start.16 = (pred[2]{0:T(512)(128)(4,1)S(1)}, pred[2]{0:T(512)(128)(4,1)}, u32[]{:S(2)}) copy-start(pred[2]{0:T(512)(128)(4,1)} %copy-done.15) | copy-start | bytes 10
  306.1 15.4 %collective-permute-start.31 = (bf16[2,2,48,768]{3,2,0,1:T(8,128)(2,1)S(1)}, bf16[2,2,48,768]{3,2,0,1:T(8,128)(2,1)S(1)}, u32[]{:S(2)}, u32[]{:S(2)}) collective-permute-start(bf16[2,2,48,768]{3,2,0,1:T(8,128)(2,1)S(1)} %get-tuple-element.426), channel_id=1, source_target_pairs={{0,2},{1,3},{2,0},{3,1},{4,6},{5,7},{6,4},{7,5},{8,10},{9,11},{10,... | collective-permute-start | bytes 884744 | tf_op jit(solution)/shard_map/ppermute | solution.py:712
  306.9 14.6 %collective-permute-start.30 = (bf16[2,2,48,768]{3,2,0,1:T(8,128)(2,1)S(1)}, bf16[2,2,48,768]{3,2,0,1:T(8,128)(2,1)S(1)}, u32[]{:S(2)}, u32[]{:S(2)}) collective-permute-start(bf16[2,2,48,768]{3,2,0,1:T(8,128)(2,1)S(1)} %get-tuple-element.428), channel_id=1, source_target_pairs={{0,4},{1,5},{2,6},{3,7},{4,0},{5,1},{6,2},{7,3},{8,12},{9,13},{10,... | collective-permute-start | bytes 884744 | tf_op jit(solution)/shard_map/ppermute | solution.py:712
  321.8 10.8 %collective-permute-start.35 = (bf16[2,96,768]{2,1,0:T(8,128)(2,1)S(1)}, bf16[2,96,768]{2,1,0:T(8,128)(2,1)S(1)}, u32[]{:S(2)}, u32[]{:S(2)}) collective-permute-start(bf16[2,96,768]{2,1,0:T(8,128)(2,1)S(1)} %get-tuple-element.424), channel_id=1, source_target_pairs={{0,8},{8,0},{16,24},{24,16},{1,9},{9,1},{17,25},{25,17},{2,10},{10... | collective-permute-start | bytes 884744 | tf_op jit(solution)/shard_map/ppermute | solution.py:712
  325.0 7.6 %collective-permute-start.36 = (bf16[2,2,40,768]{3,2,0,1:T(8,128)(2,1)S(1)}, bf16[2,2,40,768]{3,2,0,1:T(8,128)(2,1)S(1)}, u32[]{:S(2)}, u32[]{:S(2)}) collective-permute-start(bf16[2,2,40,768]{3,2,0,1:T(8,128)(2,1)S(1)} %get-tuple-element.440), channel_id=1, source_target_pairs={{0,4},{1,5},{2,6},{3,7},{4,0},{5,1},{6,2},{7,3},{8,12},{9,13},{10,... | collective-permute-start | bytes 737288 | tf_op jit(solution)/shard_map/ppermute | solution.py:712
  326.9 5.7 %collective-permute-start.37 = (bf16[2,2,32,768]{3,2,0,1:T(8,128)(2,1)S(1)}, bf16[2,2,32,768]{3,2,0,1:T(8,128)(2,1)S(1)}, u32[]{:S(2)}, u32[]{:S(2)}) collective-permute-start(bf16[2,2,32,768]{3,2,0,1:T(8,128)(2,1)S(1)} %get-tuple-element.444), channel_id=1, source_target_pairs={{0,2},{1,3},{2,0},{3,1},{4,6},{5,7},{6,4},{7,5},{8,10},{9,11},{10,... | collective-permute-start | bytes 589832 | tf_op jit(solution)/shard_map/ppermute | solution.py:712
  332.9 9.0 %collective-permute-start.39 = (bf16[2,72,768]{2,1,0:T(8,128)(2,1)S(1)}, bf16[2,72,768]{2,1,0:T(8,128)(2,1)S(1)}, u32[]{:S(2)}, u32[]{:S(2)}) collective-permute-start(bf16[2,72,768]{2,1,0:T(8,128)(2,1)S(1)} %get-tuple-element.442), channel_id=1, source_target_pairs={{0,8},{8,0},{16,24},{24,16},{1,9},{9,1},{17,25},{25,17},{2,10},{10... | collective-permute-start | bytes 663560 | tf_op jit(solution)/shard_map/ppermute | solution.py:712
  333.0 8.9 %collective-permute-start.38 = (bf16[96,768]{1,0:T(8,128)(2,1)S(1)}, bf16[96,768]{1,0:T(8,128)(2,1)S(1)}, u32[]{:S(2)}, u32[]{:S(2)}) collective-permute-start(bf16[96,768]{1,0:T(8,128)(2,1)S(1)} %get-tuple-element.446), channel_id=1, source_target_pairs={{0,16},{8,24},{16,0},{24,8},{1,17},{9,25},{17,1},{25,9},{2,18},{10... | collective-permute-start | bytes 442376 | tf_op jit(solution)/shard_map/ppermute | solution.py:712
  342.0 6.2 %collective-permute-start.40 = (bf16[72,768]{1,0:T(8,128)(2,1)S(1)}, bf16[72,768]{1,0:T(8,128)(2,1)S(1)}, u32[]{:S(2)}, u32[]{:S(2)}) collective-permute-start(bf16[72,768]{1,0:T(8,128)(2,1)S(1)} %get-tuple-element.450), channel_id=1, source_target_pairs={{0,16},{8,24},{16,0},{24,8},{1,17},{9,25},{17,1},{25,9},{2,18},{10... | collective-permute-start | bytes 331784 | tf_op jit(solution)/shard_map/ppermute | solution.py:712
  349.0 13.1 %collective-permute-start.41 = (bf16[2,192,768]{2,1,0:T(8,128)(2,1)S(1)}, bf16[2,192,768]{2,1,0:T(8,128)(2,1)S(1)}, u32[]{:S(2)}, u32[]{:S(2)}) collective-permute-start(bf16[2,192,768]{2,1,0:T(8,128)(2,1)S(1)} %broadcast_select_fusion.9), channel_id=1, source_target_pairs={{0,8},{8,0},{16,24},{24,16},{1,9},{9,1},{17,25},{25,17},{2,10},{10... | collective-permute-start | bytes 1769480 | tf_op jit(solution)/shard_map/ppermute | solution.py:712
  362.3 12.5 %collective-permute-start.43 = (bf16[2,2,96,768]{3,2,1,0:T(8,128)(2,1)S(1)}, bf16[2,2,96,768]{3,2,1,0:T(8,128)(2,1)S(1)}, u32[]{:S(2)}, u32[]{:S(2)}) collective-permute-start(bf16[2,2,96,768]{3,2,1,0:T(8,128)(2,1)S(1)} %get-tuple-element.422), channel_id=1, source_target_pairs={{0,2},{1,3},{2,0},{3,1},{4,6},{5,7},{6,4},{7,5},{8,10},{9,11},{10,... | collective-permute-start | bytes 1769480 | tf_op jit(solution)/shard_map/ppermute | solution.py:712
  363.5 16.3 %collective-permute-start.42 = (bf16[2,2,96,768]{3,2,1,0:T(8,128)(2,1)S(1)}, bf16[2,2,96,768]{3,2,1,0:T(8,128)(2,1)S(1)}, u32[]{:S(2)}, u32[]{:S(2)}) collective-permute-start(bf16[2,2,96,768]{3,2,1,0:T(8,128)(2,1)S(1)} %get-tuple-element.423), channel_id=1, source_target_pairs={{0,4},{1,5},{2,6},{3,7},{4,0},{5,1},{6,2},{7,3},{8,12},{9,13},{10,... | collective-permute-start | bytes 1769480 | tf_op jit(solution)/shard_map/ppermute | solution.py:712
  379.9 22.4 %collective-permute-start.45 = (bf16[2,2,2,96,768]{4,3,2,1,0:T(8,128)(2,1)S(1)}, bf16[2,2,2,96,768]{4,3,2,1,0:T(8,128)(2,1)S(1)}, u32[]{:S(2)}, u32[]{:S(2)}) collective-permute-start(bf16[2,2,2,96,768]{4,3,2,1,0:T(8,128)(2,1)S(1)} %broadcast_select_fusion.2), channel_id=1, source_target_pairs={{0,4},{1,5},{2,6},{3,7},{4,0},{5,1},{6,2},{7,3},{8,12},{9,13},{10,... | collective-permute-start | bytes 3538952 | tf_op jit(solution)/shard_map/ppermute | solution.py:712
  382.5 23.8 %collective-permute-start.44 = (bf16[2,2,2,96,768]{4,3,2,1,0:T(8,128)(2,1)S(1)}, bf16[2,2,2,96,768]{4,3,2,1,0:T(8,128)(2,1)S(1)}, u32[]{:S(2)}, u32[]{:S(2)}) collective-permute-start(bf16[2,2,2,96,768]{4,3,2,1,0:T(8,128)(2,1)S(1)} %broadcast_select_fusion.4), channel_id=1, source_target_pairs={{0,2},{1,3},{2,0},{3,1},{4,6},{5,7},{6,4},{7,5},{8,10},{9,11},{10,... | collective-permute-start | bytes 3538952 | tf_op jit(solution)/shard_map/ppermute | solution.py:712
  402.6 4.0 copy-start
  402.6 4.5 %copy-start.12 = (bf16[416,768]{1,0:T(8,128)(2,1)S(1)}, bf16[416,768]{1,0:T(8,128)(2,1)}, u32[]{:S(2)}) copy-start(bf16[416,768]{1,0:T(8,128)(2,1)} %get-tuple-element.383) | copy-start | bytes 1916932
  402.6 4.5 %copy-start.14 = (bf16[4,768]{1,0:T(4,128)(2,1)S(1)}, bf16[4,768]{1,0:T(4,128)(2,1)}, u32[]{:S(2)}) copy-start(bf16[4,768]{1,0:T(4,128)(2,1)} %wb_ref.1) | copy-start | bytes 18436
  402.6 5.4 %copy-start.17 = (bf16[32,64,768]{2,1,0:T(8,128)(2,1)S(1)}, bf16[32,64,768]{2,1,0:T(8,128)(2,1)}, u32[]{:S(2)}) copy-start(bf16[32,64,768]{2,1,0:T(8,128)(2,1)} %get-tuple-element.384) | copy-start | bytes 9437188
  406.5 4.2 copy-start.1
  406.5 7.1 %collective-permute-start.47 = (bf16[2,2,2,2,96,768]{5,4,3,2,1,0:T(8,128)(2,1)S(1)}, bf16[2,2,2,2,96,768]{5,4,3,2,1,0:T(8,128)(2,1)S(1)}, u32[]{:S(2)}, u32[]{:S(2)}) collective-permute-start(bf16[2,2,2,2,96,768]{5,4,3,2,1,0:T(8,128)(2,1)S(1)} %broadcast_select_fusion.1), channel_id=1, source_target_pairs={{0,1},{1,0},{2,3},{3,2},{4,5},{5,4},{6,7},{7,6},{8,9},{9,8},{10,11... | collective-permute-start | bytes 7077896 | tf_op jit(solution)/shard_map/ppermute | solution.py:712
  406.6 14.9 %collective-permute-start.46 = (bf16[2,2,2,2,96,768]{5,4,3,2,1,0:T(8,128)(2,1)S(1)}, bf16[2,2,2,2,96,768]{5,4,3,2,1,0:T(8,128)(2,1)}, u32[]{:S(2)}, u32[]{:S(2)}) collective-permute-start(bf16[2,2,2,2,96,768]{5,4,3,2,1,0:T(8,128)(2,1)S(1)} %broadcast_select_fusion), channel_id=1, source_target_pairs={{0,1},{1,0},{2,3},{3,2},{4,5},{5,4},{6,7},{7,6},{8,9},{9,8},{10,11... | collective-permute-start | bytes 7077896 | tf_op jit(solution)/shard_map/ppermute | solution.py:712
  (6 other events, 9.6 us)
Sparse Core Ops, SparseCore 0:
  27.3 99.4 all-gather.4
  349.1 82.5 all-gather.6

commit v8 on v7

--- a/solution.py
+++ b/solution.py
@@ -894,13 +894,14 @@
         img.stage()
         attn.stage()
         (ff_shard,) = fence([img, attn], ff_shard)
-    ff_weights = lax.all_gather(ff_shard, axes, axis=0)
     img = img.split(w_img.shape[0] // 2, orders)
     attn.stage()
-    for _ in range(middle):
+    for step in range(middle):
         for part in img:
             part.stage()
-        fence([*img, attn])
+        (ff_shard,) = fence([*img, attn], ff_shard)
+        if step == 0:
+            ff_weights = lax.all_gather(ff_shard, axes, axis=0)
     attn = attn.split(2 * cut, orders)
     img_halves = fence(attn, *[t for part in img for t in part.halves()])
     for part in attn:

time: 456 us -> 451 us (0.989)
  waiting for transfers between devices: 181 us -> 175 us
    ppermute x48, waiting for transfers between devices: 173 us -> 167 us  [swap_bit(): return lax.ppermute(tensor, name, [(i, i ^ step) for i in range(size)])]
  transfers between devices with their start and end apart: 52 -> 52, of which waited for: 35 -> 37; matrix products, arithmetic and copies ran while one was open for 6% -> 6% of each run, Pallas kernels for 21% -> 21%
where the time goes in v8:
time: 451 us; the launch traced here: 442 us
  waiting for transfers between devices  175 us (39%)
  Pallas kernels  153 us (34%)
  starting transfers between devices  58.3 us (13%)
  other arithmetic  22.2 us (5%)
  between operations  15.8 us (4%)
  local copies, waits for them, and re-layouts  14.1 us (3%)
    ppermute x48, waiting for transfers between devices, swap_bit(): return lax.ppermute(tensor, name, [(i, i ^ step) for i in range(size)])  167 us
    ppermute x48, starting transfers between devices, swap_bit(): return lax.ppermute(tensor, name, [(i, i ^ step) for i in range(size)])  49.8 us
    pallas_call x1, Pallas kernels, run_feed_forward(): pl.pallas_call(feed_forward, out_shape=shapes, grid_spec=pltpu.PrefetchSc...  41.7 us
    pallas_call x3, Pallas kernels, weight_grads(): pl.pallas_call(functools.partial(weight_grad_kernel, lhs_of, rhs_of, grou...  30.2 us
    pallas_call x1, Pallas kernels, run_attention_backward(): pl.pallas_call(functools.partial(attention_backward, *geometry), out_shap...  23.7 us
    pallas_call x1, Pallas kernels, run_attention_forward(): pl.pallas_call(functools.partial(attention_forward, *geometry), out_shape...  21.5 us
    convert_element_type x27, other arithmetic, add_low(): return (kept.astype(f32) + came.astype(f32)).astype(bf16)  14.8 us
    pallas_call x2, Pallas kernels, join_blocks(): pl.pallas_call(join_kernel, out_shape=jax.ShapeDtypeStruct(shape, f32), g...  13.2 us
  transfers between devices with their start and end apart: 52, of which 37 were waited for; matrix products, arithmetic and copies ran while one was open for 6% of the time, Pallas kernels for 21%

profile of v8, /device:TPU:0, one launch (start us, length us, event | category | flops | bytes accessed | tf_op | source)
XLA Modules:
  0.0 442.3 jit_solution(13613205171459999507)
XLA Ops:
  7.2 4.1 collective-permute-start
  12.3 1.6 pad_maximum_fusion
  14.8 1.7 collective-permute-done
  17.3 3.5 collective-permute-start.1
  20.7 5.1 %collective-permute-done.2 = bf16[96,768]{1,0:T(8,128)(2,1)S(1)} collective-permute-done((bf16[96,768]{1,0:T(8,128)(2,1)S(1)}, bf16[96,768]{1,0:T(8,128)(2,1)S(1)}, u32[]{:S(2)}, u32[]{:S(2)}) %collective-permute-start.2) | collective-permute-done | bytes 147488 | tf_op jit(solution)/shard_map/ppermute | solution.py:712
  27.2 1.6 collective-permute-start.4
  29.1 1.5 collective-permute-start.3
  30.6 2.8 collective-permute-done.4
  34.8 1.9 collective-permute-done.5
  36.9 1.6 collective-permute-start.7
  39.0 7.0 %collective-permute-done.7 = bf16[2,2,2,32,768]{4,3,2,1,0:T(8,128)(2,1)S(1)} collective-permute-done((bf16[2,2,2,32,768]{4,3,2,1,0:T(8,128)(2,1)S(1)}, bf16[2,2,2,32,768]{4,3,2,1,0:T(8,128)(2,1)S(1)}, u32[]{:S(2)}, u32[]{:S(2)}) %collective-permute-start.7) | collective-permute-done | bytes 393248 | tf_op jit(solution)/shard_map/ppermute | solution.py:712
  48.1 1.7 collective-permute-done.8
  52.8 7.7 %image_encode.1 = (f32[416,768]{1,0:T(8,128)}, bf16[512,768]{1,0:T(8,128)(2,1)}, bf16[32,64,768]{2,1,0:T(8,128)(2,1)}) custom-call(s32[1]{0:T(128)} %bitcast.6.core_ref, bf16[416,2048]{1,0:T(8,128)(2,1)} %x_ref.3, bf16[4,416]{1,0:T(4,128)(2,1)} %box_ref.3, bf16[4,768]{1,0:T(4,128)(2,1)} %wb_ref.1, f32[768]{0:T(1024)} %bi_ref.1, f32[768]{0:T(1024)} %gr_ref.3, ...), custom_call_target="tpu_custom_call" | custom-call | flops 1308622848 | bytes 9912320 | tf_op jit(solution)/shard_map/image_encode/pallas_call | solution.py:361
  61.2 5.1 %all-to-all-start = ((bf16[32,16,768]{2,1,0:T(8,128)(2,1)}), bf16[32,16,768]{2,1,0:T(8,128)(2,1)}, u32[]{:S(2)}, u32[]{:S(2)}) async-start(bf16[32,16,768]{2,1,0:T(8,128)(2,1)} %bitcast.7), calls=%async_computation | async-start | bytes 1572864 | tf_op jit(solution)/shard_map/all_to_all | solution.py:922
  66.3 1.8 collective-permute-start.13
  69.5 20.7 %collective-permute-done.13 = bf16[2,2,2,48,768]{4,3,2,1,0:T(8,128)(2,1)S(1)} collective-permute-done((bf16[2,2,2,48,768]{4,3,2,1,0:T(8,128)(2,1)S(1)}, bf16[2,2,2,48,768]{4,3,2,1,0:T(8,128)(2,1)S(1)}, u32[]{:S(2)}, u32[]{:S(2)}) %collective-permute-start.13) | collective-permute-done | bytes 589856 | tf_op jit(solution)/shard_map/ppermute | solution.py:712
  90.3 4.6 %collective-permute-done.12 = bf16[2,2,2,48,768]{4,3,2,1,0:T(8,128)(2,1)S(1)} collective-permute-done((bf16[2,2,2,48,768]{4,3,2,1,0:T(8,128)(2,1)S(1)}, bf16[2,2,2,48,768]{4,3,2,1,0:T(8,128)(2,1)S(1)}, u32[]{:S(2)}, u32[]{:S(2)}) %collective-permute-start.12) | collective-permute-done | bytes 589856 | tf_op jit(solution)/shard_map/ppermute | solution.py:712
  98.2 2.7 collective-permute-done.14
  102.4 1.7 bitcast_select_fusion
  104.1 2.2 fusion.39
  106.4 21.5 %attention_forward.1 = (bf16[1024,768]{1,0:T(8,128)(2,1)}, bf16[1024,768]{1,0:T(8,128)(2,1)}, bf16[1024,768]{1,0:T(8,128)(2,1)}, bf16[1024,768]{1,0:T(8,128)(2,1...) custom-call(s32[4]{0:T(128)} %captions.3, ...), custom_call_target="tpu_custom_call" | custom-call | flops 8053063680 | bytes 20447232 | tf_op jit(solution)/shard_map/attention_forward/pallas_call | solution.py:395
  127.9 3.6 all-gather.5.cloned.1.call-done
  131.5 41.7 %feed_forward.1 = (bf16[1024,768]{1,0:T(8,128)(2,1)}, bf16[1024,3072]{1,0:T(8,128)(2,1)}, bf16[1024,768]{1,0:T(8,128)(2,1)}, bf16[1024,3072]{1,0:T(8,128)(2,1)},...) custom-call(s32[4]{0:T(128)} %captions.3, ...), custom_call_target="tpu_custom_call" | custom-call | flops 20535312384 | bytes 36175872 | tf_op jit(solution)/shard_map/feed_forward/pallas_call | solution.py:589
  173.2 9.4 %grad_w_down.1 = (bf16[16,96,768]{2,1,0:T(8,128)(2,1)}, bf16[16,96,768]{2,1,0:T(8,128)(2,1)}) custom-call(s32[1]{0:T(128)} %bitcast.6.core_ref, bf16[1024,3072]{1,0:T(8,128)(2,1)} %get-tuple-element.251.refs_0_, bf16[1024,768]{1,0:T(8,128)(2,1)} %get-tuple-element.252.refs_1_), custom_call_target="tpu_custom_call" | custom-call | flops 4831838208 | bytes 11010048 | tf_op jit(solution)/shard_map/grad_w_down/pallas_call | solution.py:672
  182.8 9.6 %grad_w_up.1 = (bf16[16,96,768]{2,1,0:T(8,128)(2,1)}, bf16[16,96,768]{2,1,0:T(8,128)(2,1)}) custom-call(s32[1]{0:T(128)} %bitcast.6.core_ref, bf16[1024,768]{1,0:T(8,128)(2,1)} %get-tuple-element.243.n_ref.refs_0_, bf16[1024,3072]{1,0:T(8,128)(2,1)} %get-tuple-element.255.refs_1_), custom_call_target="tpu_custom_call" | custom-call | flops 4831838208 | bytes 11010048 | tf_op jit(solution)/shard_map/grad_w_up/pallas_call | solution.py:672
  192.7 1.8 constant_dynamic-slice_fusion.9
  194.7 2.6 collective-permute-done.17
  197.4 1.6 fusion.3
  199.0 2.6 fusion.1
  204.3 23.7 %attention_backward.1 = (bf16[1024,768]{1,0:T(8,128)(2,1)}, bf16[1024,768]{1,0:T(8,128)(2,1)}, bf16[1024,768]{1,0:T(8,128)(2,1)}, bf16[512,768]{1,0:T(8,128)(2,1...) custom-call(s32[4]{0:T(128)} %counts.5, s32[1]{0:T(128)S(6)} %copy.133.offset, ...), custom_call_target="tpu_custom_call" | custom-call | flops 10066329600 | bytes 22020096 | tf_op jit(solution)/shard_map/attention_backward/pallas_call | solution.py:621
  228.0 2.0 collective-permute-done.19
  231.4 3.3 all-to-all-start.1
  234.8 2.0 fusion.15
  236.8 1.6 collective-permute-start.21
  238.4 2.4 fusion.8
  243.4 11.2 %grad_w_attn.1 = (bf16[16,48,768]{2,1,0:T(8,128)(2,1)}, bf16[16,48,768]{2,1,0:T(8,128)(2,1)}, bf16[16,48,768]{2,1,0:T(8,128)(2,1)}, bf16[16,48,768]{2,1,0:T(8,128)(2,1)}) custom-call(s32[1]{0:T(128)} %bitcast.6.core_ref, bf16[1024,768]{1,0:T(8,128)(2,1)} %get-tuple-element.270.refs_0_, bf16[1024,768]{1,0:T(8,128)(2,1)} %get-tuple-element.271.refs_1_, ...), custom_call_target="tpu_custom_call" | custom-call | flops 4831838208 | bytes 11010048 | tf_op jit(solution)/shard_map/grad_w_attn/pallas_call | solution.py:672
  254.7 3.9 collective-permute-done.21
  258.5 1.8 collective-permute-done.20
  263.6 1.6 collective-permute-start.22
  265.4 7.2 %image_backward.1 = (bf16[416,768]{1,0:T(8,128)(2,1)}, bf16[16,40,768]{2,1,0:T(8,128)(2,1)}, bf16[16,32,768]{2,1,0:T(8,128)(2,1)}, bf16[16,40,768]{2,1,0:T(8,128)(2,1)}, bf16[16,32,768]{2,1,0:T(8,128)(2,1)}) custom-call(s32[1]{0:T(128)} %bitcast.6.core_ref, bf16[416,2048]{1,0:T(8,128)(2,1)} %x_ref.3, bf16[4,416]{1,0:T(4,128)(2,1)} %box_ref.3, ...), custom_call_target="tpu_custom_call" | custom-call | flops 1308622848 | bytes 5242880 | tf_op jit(solution)/shard_map/image_backward/pallas_call | solution.py:428
  277.3 2.3 collective-permute-done.22
  282.3 2.5 collective-permute-start.27
  285.3 12.5 %collective-permute-done.27 = bf16[192,768]{1,0:T(8,128)(2,1)S(1)} collective-permute-done((bf16[192,768]{1,0:T(8,128)(2,1)S(1)}, bf16[192,768]{1,0:T(8,128)(2,1)S(1)}, u32[]{:S(2)}, u32[]{:S(2)}) %collective-permute-start.27) | collective-permute-done | bytes 294944 | tf_op jit(solution)/shard_map/ppermute | solution.py:712
  303.3 9.6 %collective-permute-done.34 = bf16[192,768]{1,0:T(8,128)(2,1)S(1)} collective-permute-done((bf16[192,768]{1,0:T(8,128)(2,1)S(1)}, bf16[192,768]{1,0:T(8,128)(2,1)S(1)}, u32[]{:S(2)}, u32[]{:S(2)}) %collective-permute-start.34) | collective-permute-done | bytes 294944 | tf_op jit(solution)/shard_map/ppermute | solution.py:712
  313.1 3.5 collective-permute-done.31
  316.9 3.1 collective-permute-start.35
  320.1 1.8 collective-permute-start.36
  321.9 1.7 collective-permute-start.37
  323.6 4.1 collective-permute-done.37
  328.7 8.3 %collective-permute-done.38 = bf16[96,768]{1,0:T(8,128)(2,1)S(1)} collective-permute-done((bf16[96,768]{1,0:T(8,128)(2,1)S(1)}, bf16[96,768]{1,0:T(8,128)(2,1)S(1)}, u32[]{:S(2)}, u32[]{:S(2)}) %collective-permute-start.38) | collective-permute-done | bytes 147488 | tf_op jit(solution)/shard_map/ppermute | solution.py:712
  337.3 6.0 %collective-permute-done.40 = bf16[72,768]{1,0:T(8,128)(2,1)S(1)} collective-permute-done((bf16[72,768]{1,0:T(8,128)(2,1)S(1)}, bf16[72,768]{1,0:T(8,128)(2,1)S(1)}, u32[]{:S(2)}, u32[]{:S(2)}) %collective-permute-start.40) | collective-permute-done | bytes 110624 | tf_op jit(solution)/shard_map/ppermute | solution.py:712
  344.1 13.0 %collective-permute-done.41 = bf16[2,192,768]{2,1,0:T(8,128)(2,1)S(1)} collective-permute-done((bf16[2,192,768]{2,1,0:T(8,128)(2,1)S(1)}, bf16[2,192,768]{2,1,0:T(8,128)(2,1)S(1)}, u32[]{:S(2)}, u32[]{:S(2)}) %collective-permute-start.41) | collective-permute-done | bytes 589856 | tf_op jit(solution)/shard_map/ppermute | solution.py:712
  357.4 1.7 collective-permute-start.43
  360.3 9.7 %collective-permute-done.43 = bf16[2,2,96,768]{3,2,1,0:T(8,128)(2,1)S(1)} collective-permute-done((bf16[2,2,96,768]{3,2,1,0:T(8,128)(2,1)S(1)}, bf16[2,2,96,768]{3,2,1,0:T(8,128)(2,1)S(1)}, u32[]{:S(2)}, u32[]{:S(2)}) %collective-permute-start.43) | collective-permute-done | bytes 589856 | tf_op jit(solution)/shard_map/ppermute | solution.py:712
  370.1 4.7 %collective-permute-done.42 = bf16[2,2,96,768]{3,2,1,0:T(8,128)(2,1)S(1)} collective-permute-done((bf16[2,2,96,768]{3,2,1,0:T(8,128)(2,1)S(1)}, bf16[2,2,96,768]{3,2,1,0:T(8,128)(2,1)S(1)}, u32[]{:S(2)}, u32[]{:S(2)}) %collective-permute-start.42) | collective-permute-done | bytes 589856 | tf_op jit(solution)/shard_map/ppermute | solution.py:712
  375.0 2.5 collective-permute-start.45
  377.6 20.4 %collective-permute-done.45 = bf16[2,2,2,96,768]{4,3,2,1,0:T(8,128)(2,1)S(1)} collective-permute-done((bf16[2,2,2,96,768]{4,3,2,1,0:T(8,128)(2,1)S(1)}, bf16[2,2,2,96,768]{4,3,2,1,0:T(8,128)(2,1)S(1)}, u32[]{:S(2)}, u32[]{:S(2)}) %collective-permute-start.45) | collective-permute-done | bytes 1179680 | tf_op jit(solution)/shard_map/ppermute | solution.py:712
  398.2 3.8 collective-permute-done.44
  403.8 2.7 convolution_convert_fusion
  406.5 2.9 collective-permute-done.47
  410.8 6.5 %join_blocks.3 = f32[3072,768]{1,0:T(8,128)} custom-call(s32[1]{0:T(128)} %bitcast.6.core_ref, bf16[16,96,768]{2,1,0:T(8,128)(2,1)} %bitcast.131, bf16[16,96,768]{2,1,0:T(8,128)(2,1)} %bitcast.139), custom_call_target="tpu_custom_call" | custom-call | bytes 14155776 | tf_op jit(solution)/shard_map/join_blocks/pallas_call | solution.py:469
  417.3 6.7 %join_blocks.2 = f32[768,3072]{1,0:T(8,128)} custom-call(s32[1]{0:T(128)} %bitcast.6.core_ref, bf16[16,96,768]{2,1,0:T(8,128)(2,1)} %bitcast.130, bf16[16,96,768]{2,1,0:T(8,128)(2,1)} %bitcast.73.refs_1_), custom_call_target="tpu_custom_call" | custom-call | bytes 14155776 | tf_op jit(solution)/shard_map/join_blocks/pallas_call | solution.py:469
  424.0 2.7 all-gather.7.cloned.1.call-done
  426.7 8.2 %widen_rest.1 = (f32[768,768]{1,0:T(8,128)}, f32[768,768]{1,0:T(8,128)}, f32[768,768]{1,0:T(8,128)}, f32[768,768]{1,0:T(8,128)}, f32[2048,768]{1,0:T(8,128)}, /*...) custom-call(bf16[32,168,768]{2,1,0:T(8,128)(2,1)} %bitcast.132), custom_call_target="tpu_custom_call" | custom-call | bytes 24772608 | tf_op jit(solution)/shard_map/widen_rest/pallas_call | solution.py:533
  (170 shorter events, 50.0 us)
Async XLA Ops:
  7.2 9.3 %copy-start.13 = (bf16[64,768]{1,0:T(8,128)(2,1)S(1)}, bf16[64,768]{1,0:T(8,128)(2,1)}, u32[]{:S(2)}) copy-start(bf16[64,768]{1,0:T(8,128)(2,1)} %param.33) | copy-start | bytes 294916
  7.2 124.3 %all-gather.5.cloned.1.call-start = ((), (), s32[]{:S(2)}) async-start(), calls=%async_computation.2 | async-start | bytes 9732096 | tf_op jit(solution)/shard_map/all_gather | solution.py:904
  7.2 9.2 %collective-permute-start = (bf16[64,768]{1,0:T(8,128)(2,1)}, bf16[64,768]{1,0:T(8,128)(2,1)S(1)}, u32[]{:S(2)}, u32[]{:S(2)}) collective-permute-start(bf16[64,768]{1,0:T(8,128)(2,1)} %param.33), channel_id=1, source_target_pairs={{0,16},{8,24},{16,0},{24,8},{1,17},{9,25},{17,1},{25,9},{2,18},{10... | collective-permute-start | bytes 294920 | tf_op jit(solution)/shard_map/ppermute | solution.py:712
  14.8 12.5 %copy-start.15 = (pred[2]{0:T(512)(128)(4,1)}, pred[2]{0:T(512)(128)(4,1)S(1)}, u32[]{:S(2)}) copy-start(pred[2]{0:T(512)(128)(4,1)S(1)} %iota_compare_fusion.1) | copy-start | bytes 10
  16.6 9.3 %collective-permute-start.2 = (bf16[96,768]{1,0:T(8,128)(2,1)S(1)}, bf16[96,768]{1,0:T(8,128)(2,1)S(1)}, u32[]{:S(2)}, u32[]{:S(2)}) collective-permute-start(bf16[96,768]{1,0:T(8,128)(2,1)S(1)} %pad_maximum_fusion.2), channel_id=1, source_target_pairs={{0,16},{8,24},{16,0},{24,8},{1,17},{9,25},{17,1},{25,9},{2,18},{10... | collective-permute-start | bytes 442376 | tf_op jit(solution)/shard_map/ppermute | solution.py:712
  17.3 9.8 %collective-permute-start.1 = (bf16[2,64,768]{2,1,0:T(8,128)(2,1)S(1)}, bf16[2,64,768]{2,1,0:T(8,128)(2,1)S(1)}, u32[]{:S(2)}, u32[]{:S(2)}) collective-permute-start(bf16[2,64,768]{2,1,0:T(8,128)(2,1)S(1)} %broadcast_select_fusion.17), channel_id=1, source_target_pairs={{0,8},{8,0},{16,24},{24,16},{1,9},{9,1},{17,25},{25,17},{2,10},{10... | collective-permute-start | bytes 589832 | tf_op jit(solution)/shard_map/ppermute | solution.py:712
  27.2 6.1 %collective-permute-start.4 = (bf16[2,2,32,768]{3,2,1,0:T(8,128)(2,1)S(1)}, bf16[2,2,32,768]{3,2,1,0:T(8,128)(2,1)S(1)}, u32[]{:S(2)}, u32[]{:S(2)}) collective-permute-start(bf16[2,2,32,768]{3,2,1,0:T(8,128)(2,1)S(1)} %get-tuple-element.454), channel_id=1, source_target_pairs={{0,2},{1,3},{2,0},{3,1},{4,6},{5,7},{6,4},{7,5},{8,10},{9,11},{10,... | collective-permute-start | bytes 589832 | tf_op jit(solution)/shard_map/ppermute | solution.py:712
  28.8 8.0 %collective-permute-start.5 = (bf16[2,96,768]{2,1,0:T(8,128)(2,1)S(1)}, bf16[2,96,768]{2,1,0:T(8,128)(2,1)S(1)}, u32[]{:S(2)}, u32[]{:S(2)}) collective-permute-start(bf16[2,96,768]{2,1,0:T(8,128)(2,1)S(1)} %broadcast_select_fusion.16), channel_id=1, source_target_pairs={{0,8},{8,0},{16,24},{24,16},{1,9},{9,1},{17,25},{25,17},{2,10},{10... | collective-permute-start | bytes 884744 | tf_op jit(solution)/shard_map/ppermute | solution.py:712
  29.1 5.7 %collective-permute-start.3 = (bf16[2,2,32,768]{3,2,1,0:T(8,128)(2,1)S(1)}, bf16[2,2,32,768]{3,2,1,0:T(8,128)(2,1)S(1)}, u32[]{:S(2)}, u32[]{:S(2)}) collective-permute-start(bf16[2,2,32,768]{3,2,1,0:T(8,128)(2,1)S(1)} %get-tuple-element.455), channel_id=1, source_target_pairs={{0,4},{1,5},{2,6},{3,7},{4,0},{5,1},{6,2},{7,3},{8,12},{9,13},{10,... | collective-permute-start | bytes 589832 | tf_op jit(solution)/shard_map/ppermute | solution.py:712
  36.9 9.1 %collective-permute-start.7 = (bf16[2,2,2,32,768]{4,3,2,1,0:T(8,128)(2,1)S(1)}, bf16[2,2,2,32,768]{4,3,2,1,0:T(8,128)(2,1)S(1)}, u32[]{:S(2)}, u32[]{:S(2)}) collective-permute-start(bf16[2,2,2,32,768]{4,3,2,1,0:T(8,128)(2,1)S(1)} %broadcast_select_fusion.13), channel_id=1, source_target_pairs={{0,4},{1,5},{2,6},{3,7},{4,0},{5,1},{6,2},{7,3},{8,12},{9,13},{10,... | collective-permute-start | bytes 1179656 | tf_op jit(solution)/shard_map/ppermute | solution.py:712
  38.5 8.8 %collective-permute-start.6 = (bf16[2,2,2,32,768]{4,3,2,1,0:T(8,128)(2,1)S(1)}, bf16[2,2,2,32,768]{4,3,2,1,0:T(8,128)(2,1)S(1)}, u32[]{:S(2)}, u32[]{:S(2)}) collective-permute-start(bf16[2,2,2,32,768]{4,3,2,1,0:T(8,128)(2,1)S(1)} %broadcast_select_fusion.15), channel_id=1, source_target_pairs={{0,2},{1,3},{2,0},{3,1},{4,6},{5,7},{6,4},{7,5},{8,10},{9,11},{10,... | collective-permute-start | bytes 1179656 | tf_op jit(solution)/shard_map/ppermute | solution.py:712
  47.4 5.4 %copy-start.3 = (bf16[2,2,2,2,32,768]{5,4,3,2,1,0:T(8,128)(2,1)}, bf16[2,2,2,2,32,768]{5,4,3,2,1,0:T(8,128)(2,1)S(1)}, u32[]{:S(2)}) copy-start(bf16[2,2,2,2,32,768]{5,4,3,2,1,0:T(8,128)(2,1)S(1)} %broadcast_select_fusion.8) | copy-start | bytes 2359300
  47.4 2.4 collective-permute-start.8
  47.5 3.4 collective-permute-start.9
  51.8 9.0 %collective-permute-start.11 = (bf16[2,2,48,768]{3,2,1,0:T(8,128)(2,1)S(1)}, bf16[2,2,48,768]{3,2,1,0:T(8,128)(2,1)S(1)}, u32[]{:S(2)}, u32[]{:S(2)}) collective-permute-start(bf16[2,2,48,768]{3,2,1,0:T(8,128)(2,1)S(1)} %get-tuple-element.231), channel_id=1, source_target_pairs={{0,2},{1,3},{2,0},{3,1},{4,6},{5,7},{6,4},{7,5},{8,10},{9,11},{10,... | collective-permute-start | bytes 884744 | tf_op jit(solution)/shard_map/ppermute | solution.py:712
  52.3 8.8 %collective-permute-start.10 = (bf16[2,2,48,768]{3,2,1,0:T(8,128)(2,1)S(1)}, bf16[2,2,48,768]{3,2,1,0:T(8,128)(2,1)S(1)}, u32[]{:S(2)}, u32[]{:S(2)}) collective-permute-start(bf16[2,2,48,768]{3,2,1,0:T(8,128)(2,1)S(1)} %get-tuple-element.230), channel_id=1, source_target_pairs={{0,4},{1,5},{2,6},{3,7},{4,0},{5,1},{6,2},{7,3},{8,12},{9,13},{10,... | collective-permute-start | bytes 884744 | tf_op jit(solution)/shard_map/ppermute | solution.py:712
  61.2 35.2 %all-to-all-start = ((bf16[32,16,768]{2,1,0:T(8,128)(2,1)}), bf16[32,16,768]{2,1,0:T(8,128)(2,1)}, u32[]{:S(2)}, u32[]{:S(2)}) async-start(bf16[32,16,768]{2,1,0:T(8,128)(2,1)} %bitcast.7), calls=%async_computation | async-start | bytes 1572864 | tf_op jit(solution)/shard_map/all_to_all | solution.py:922
  66.3 23.9 %collective-permute-start.13 = (bf16[2,2,2,48,768]{4,3,2,1,0:T(8,128)(2,1)S(1)}, bf16[2,2,2,48,768]{4,3,2,1,0:T(8,128)(2,1)S(1)}, u32[]{:S(2)}, u32[]{:S(2)}) collective-permute-start(bf16[2,2,2,48,768]{4,3,2,1,0:T(8,128)(2,1)S(1)} %broadcast_select_fusion.10), channel_id=1, source_target_pairs={{0,4},{1,5},{2,6},{3,7},{4,0},{5,1},{6,2},{7,3},{8,12},{9,13},{10,... | collective-permute-start | bytes 1769480 | tf_op jit(solution)/shard_map/ppermute | solution.py:712
  68.1 26.9 %collective-permute-start.12 = (bf16[2,2,2,48,768]{4,3,2,1,0:T(8,128)(2,1)S(1)}, bf16[2,2,2,48,768]{4,3,2,1,0:T(8,128)(2,1)S(1)}, u32[]{:S(2)}, u32[]{:S(2)}) collective-permute-start(bf16[2,2,2,48,768]{4,3,2,1,0:T(8,128)(2,1)S(1)} %broadcast_select_fusion.12), channel_id=1, source_target_pairs={{0,2},{1,3},{2,0},{3,1},{4,6},{5,7},{6,4},{7,5},{8,10},{9,11},{10,... | collective-permute-start | bytes 1769480 | tf_op jit(solution)/shard_map/ppermute | solution.py:712
  96.5 4.5 %collective-permute-start.14 = (bf16[2,2,2,2,48,768]{5,4,3,2,1,0:T(8,128)(2,1)S(1)}, bf16[2,2,2,2,48,768]{5,4,3,2,1,0:T(8,128)(2,1)S(1)}, u32[]{:S(2)}, u32[]{:S(2)}) collective-permute-start(bf16[2,2,2,2,48,768]{5,4,3,2,1,0:T(8,128)(2,1)S(1)} %broadcast_select_fusion.6), channel_id=1, source_target_pairs={{0,1},{1,0},{2,3},{3,2},{4,5},{5,4},{6,7},{7,6},{8,9},{9,8},{10,11... | collective-permute-start | bytes 3538952 | tf_op jit(solution)/shard_map/ppermute | solution.py:712
  96.5 6.0 %collective-permute-start.15 = (bf16[2,2,2,2,48,768]{5,4,3,2,1,0:T(8,128)(2,1)S(1)}, bf16[2,2,2,2,48,768]{5,4,3,2,1,0:T(8,128)(2,1)}, u32[]{:S(2)}, u32[]{:S(2)}) collective-permute-start(bf16[2,2,2,2,48,768]{5,4,3,2,1,0:T(8,128)(2,1)S(1)} %broadcast_select_fusion.5), channel_id=1, source_target_pairs={{0,1},{1,0},{2,3},{3,2},{4,5},{5,4},{6,7},{7,6},{8,9},{9,8},{10,11... | collective-permute-start | bytes 3538952 | tf_op jit(solution)/shard_map/ppermute | solution.py:712
  182.6 11.9 %collective-permute-start.16 = (bf16[16,96,768]{2,1,0:T(8,128)(2,1)}, bf16[16,96,768]{2,1,0:T(8,128)(2,1)S(1)}, u32[]{:S(2)}, u32[]{:S(2)}) collective-permute-start(bf16[16,96,768]{2,1,0:T(8,128)(2,1)} %get-tuple-element.254), channel_id=1, source_target_pairs={{0,1},{1,0},{2,3},{3,2},{4,5},{5,4},{6,7},{7,6},{8,9},{9,8},{10,11... | collective-permute-start | bytes 7077896 | tf_op jit(solution)/shard_map/ppermute | solution.py:712
  192.4 4.9 %collective-permute-start.17 = (bf16[16,96,768]{2,1,0:T(8,128)(2,1)}, bf16[16,96,768]{2,1,0:T(8,128)(2,1)}, u32[]{:S(2)}, u32[]{:S(2)}) collective-permute-start(bf16[16,96,768]{2,1,0:T(8,128)(2,1)} %get-tuple-element.257), channel_id=1, source_target_pairs={{0,1},{1,0},{2,3},{3,2},{4,5},{5,4},{6,7},{7,6},{8,9},{9,8},{10,11... | collective-permute-start | bytes 7077896 | tf_op jit(solution)/shard_map/ppermute | solution.py:712
  194.5 2.8 copy-start.4
  201.6 28.4 %collective-permute-start.19 = (bf16[2,2,2,96,768]{4,3,0,1,2:T(8,128)(2,1)}, bf16[2,2,2,96,768]{4,3,0,1,2:T(8,128)(2,1)}, u32[]{:S(2)}, u32[]{:S(2)}) collective-permute-start(bf16[2,2,2,96,768]{4,3,0,1,2:T(8,128)(2,1)} %fusion.1), channel_id=1, source_target_pairs={{0,4},{1,5},{2,6},{3,7},{4,0},{5,1},{6,2},{7,3},{8,12},{9,13},{10,... | collective-permute-start | bytes 3538952 | tf_op jit(solution)/shard_map/ppermute | solution.py:712
  203.4 28.0 %collective-permute-start.18 = (bf16[2,2,2,96,768]{4,3,0,1,2:T(8,128)(2,1)S(1)}, bf16[2,2,2,96,768]{4,3,0,1,2:T(8,128)(2,1)}, u32[]{:S(2)}, u32[]{:S(2)}) collective-permute-start(bf16[2,2,2,96,768]{4,3,0,1,2:T(8,128)(2,1)S(1)} %fusion), channel_id=1, source_target_pairs={{0,2},{1,3},{2,0},{3,1},{4,6},{5,7},{6,4},{7,5},{8,10},{9,11},{10,... | collective-permute-start | bytes 3538952 | tf_op jit(solution)/shard_map/ppermute | solution.py:712
  231.4 28.9 %all-to-all-start.1 = ((bf16[32,16,768]{2,1,0:T(8,128)(2,1)}), bf16[32,16,768]{2,1,0:T(8,128)(2,1)}, u32[]{:S(2)}, u32[]{:S(2)}) async-start(bf16[32,16,768]{2,1,0:T(8,128)(2,1)} %bitcast.153), calls=%async_computation.1 | async-start | bytes 1572864 | tf_op jit(solution)/shard_map/all_to_all | solution.py:1034
  234.7 192.0 %all-gather.7.cloned.1.call-start = ((), (), s32[]{:S(2)}) async-start(), calls=%async_computation.3 | async-start | bytes 8515584 | tf_op jit(solution)/shard_map/all_gather | solution.py:1088
  236.8 21.7 %collective-permute-start.21 = (bf16[2,2,96,768]{3,2,1,0:T(8,128)(2,1)}, bf16[2,2,96,768]{3,2,1,0:T(8,128)(2,1)}, u32[]{:S(2)}, u32[]{:S(2)}) collective-permute-start(bf16[2,2,96,768]{3,2,1,0:T(8,128)(2,1)} %fusion.15), channel_id=1, source_target_pairs={{0,2},{1,3},{2,0},{3,1},{4,6},{5,7},{6,4},{7,5},{8,10},{9,11},{10,... | collective-permute-start | bytes 1769480 | tf_op jit(solution)/shard_map/ppermute | solution.py:712
  240.8 19.6 %collective-permute-start.20 = (bf16[2,2,96,768]{3,2,0,1:T(8,128)(2,1)}, bf16[2,2,96,768]{3,2,0,1:T(8,128)(2,1)}, u32[]{:S(2)}, u32[]{:S(2)}) collective-permute-start(bf16[2,2,96,768]{3,2,0,1:T(8,128)(2,1)} %get-tuple-element.410), channel_id=1, source_target_pairs={{0,4},{1,5},{2,6},{3,7},{4,0},{5,1},{6,2},{7,3},{8,12},{9,13},{10,... | collective-permute-start | bytes 1769480 | tf_op jit(solution)/shard_map/ppermute | solution.py:712
  263.6 11.7 %collective-permute-start.24 = (bf16[16,48,768]{2,1,0:T(8,128)(2,1)}, bf16[16,48,768]{2,1,0:T(8,128)(2,1)S(1)}, u32[]{:S(2)}, u32[]{:S(2)}) collective-permute-start(bf16[16,48,768]{2,1,0:T(8,128)(2,1)} %get-tuple-element.296), channel_id=1, source_target_pairs={{0,1},{1,0},{2,3},{3,2},{4,5},{5,4},{6,7},{7,6},{8,9},{9,8},{10,11... | collective-permute-start | bytes 3538952 | tf_op jit(solution)/shard_map/ppermute | solution.py:712
  263.6 16.1 %collective-permute-start.22 = (bf16[2,192,768]{2,1,0:T(8,128)(2,1)}, bf16[2,192,768]{2,1,0:T(8,128)(2,1)}, u32[]{:S(2)}, u32[]{:S(2)}) collective-permute-start(bf16[2,192,768]{2,1,0:T(8,128)(2,1)} %fusion.16), channel_id=1, source_target_pairs={{0,8},{8,0},{16,24},{24,16},{1,9},{9,1},{17,25},{25,17},{2,10},{10... | collective-permute-start | bytes 1769480 | tf_op jit(solution)/shard_map/ppermute | solution.py:712
  265.2 10.4 %collective-permute-start.23 = (bf16[16,48,768]{2,1,0:T(8,128)(2,1)}, bf16[16,48,768]{2,1,0:T(8,128)(2,1)}, u32[]{:S(2)}, u32[]{:S(2)}) collective-permute-start(bf16[16,48,768]{2,1,0:T(8,128)(2,1)} %get-tuple-element.294), channel_id=1, source_target_pairs={{0,1},{1,0},{2,3},{3,2},{4,5},{5,4},{6,7},{7,6},{8,9},{9,8},{10,11... | collective-permute-start | bytes 3538952 | tf_op jit(solution)/shard_map/ppermute | solution.py:712
  272.6 7.0 %collective-permute-start.25 = (bf16[16,40,768]{2,1,0:T(8,128)(2,1)}, bf16[16,40,768]{2,1,0:T(8,128)(2,1)S(1)}, u32[]{:S(2)}, u32[]{:S(2)}) collective-permute-start(bf16[16,40,768]{2,1,0:T(8,128)(2,1)} %get-tuple-element.303), channel_id=1, source_target_pairs={{0,1},{1,0},{2,3},{3,2},{4,5},{5,4},{6,7},{7,6},{8,9},{9,8},{10,11... | collective-permute-start | bytes 2949128 | tf_op jit(solution)/shard_map/ppermute | solution.py:712
  272.9 6.7 %collective-permute-start.26 = (bf16[16,32,768]{2,1,0:T(8,128)(2,1)}, bf16[16,32,768]{2,1,0:T(8,128)(2,1)S(1)}, u32[]{:S(2)}, u32[]{:S(2)}) collective-permute-start(bf16[16,32,768]{2,1,0:T(8,128)(2,1)} %get-tuple-element.305), channel_id=1, source_target_pairs={{0,1},{1,0},{2,3},{3,2},{4,5},{5,4},{6,7},{7,6},{8,9},{9,8},{10,11... | collective-permute-start | bytes 2359304 | tf_op jit(solution)/shard_map/ppermute | solution.py:712
  277.3 7.5 %copy-start.9 = (bf16[16,32,768]{2,1,0:T(8,128)(2,1)S(1)}, bf16[16,32,768]{2,1,0:T(8,128)(2,1)}, u32[]{:S(2)}) copy-start(bf16[16,32,768]{2,1,0:T(8,128)(2,1)} %get-tuple-element.304) | copy-start | bytes 2359300
  280.8 4.2 copy-start.8
  280.9 16.9 %collective-permute-start.28 = (bf16[2,2,2,48,768]{4,3,0,1,2:T(8,128)(2,1)S(1)}, bf16[2,2,2,48,768]{4,3,0,1,2:T(8,128)(2,1)S(1)}, u32[]{:S(2)}, u32[]{:S(2)}) collective-permute-start(bf16[2,2,2,48,768]{4,3,0,1,2:T(8,128)(2,1)S(1)} %fusion.11), channel_id=1, source_target_pairs={{0,2},{1,3},{2,0},{3,1},{4,6},{5,7},{6,4},{7,5},{8,10},{9,11},{10,... | collective-permute-start | bytes 1769480 | tf_op jit(solution)/shard_map/ppermute | solution.py:712
  281.3 16.5 %collective-permute-start.29 = (bf16[2,2,2,48,768]{4,3,0,1,2:T(8,128)(2,1)S(1)}, bf16[2,2,2,48,768]{4,3,0,1,2:T(8,128)(2,1)S(1)}, u32[]{:S(2)}, u32[]{:S(2)}) collective-permute-start(bf16[2,2,2,48,768]{4,3,0,1,2:T(8,128)(2,1)S(1)} %fusion.13), channel_id=1, source_target_pairs={{0,4},{1,5},{2,6},{3,7},{4,0},{5,1},{6,2},{7,3},{8,12},{9,13},{10,... | collective-permute-start | bytes 1769480 | tf_op jit(solution)/shard_map/ppermute | solution.py:712
  282.3 15.4 %collective-permute-start.27 = (bf16[192,768]{1,0:T(8,128)(2,1)S(1)}, bf16[192,768]{1,0:T(8,128)(2,1)S(1)}, u32[]{:S(2)}, u32[]{:S(2)}) collective-permute-start(bf16[192,768]{1,0:T(8,128)(2,1)S(1)} %get-tuple-element.432), channel_id=1, source_target_pairs={{0,16},{8,24},{16,0},{24,8},{1,17},{9,25},{17,1},{25,9},{2,18},{10... | collective-permute-start | bytes 884744 | tf_op jit(solution)/shard_map/ppermute | solution.py:712
  297.9 15.1 %collective-permute-start.34 = (bf16[192,768]{1,0:T(8,128)(2,1)S(1)}, bf16[192,768]{1,0:T(8,128)(2,1)S(1)}, u32[]{:S(2)}, u32[]{:S(2)}) collective-permute-start(bf16[192,768]{1,0:T(8,128)(2,1)S(1)} %add_convert_fusion.22), channel_id=1, source_target_pairs={{0,16},{8,24},{16,0},{24,8},{1,17},{9,25},{17,1},{25,9},{2,18},{10... | collective-permute-start | bytes 884744 | tf_op jit(solution)/shard_map/ppermute | solution.py:712
  298.9 17.7 %collective-permute-start.32 = (bf16[2,2,2,40,768]{4,3,0,1,2:T(8,128)(2,1)S(1)}, bf16[2,2,2,40,768]{4,3,0,1,2:T(8,128)(2,1)S(1)}, u32[]{:S(2)}, u32[]{:S(2)}) collective-permute-start(bf16[2,2,2,40,768]{4,3,0,1,2:T(8,128)(2,1)S(1)} %get-tuple-element.332), channel_id=1, source_target_pairs={{0,2},{1,3},{2,0},{3,1},{4,6},{5,7},{6,4},{7,5},{8,10},{9,11},{10,... | collective-permute-start | bytes 1474568 | tf_op jit(solution)/shard_map/ppermute | solution.py:712
  300.3 16.3 %collective-permute-start.33 = (bf16[2,2,2,32,768]{4,3,0,1,2:T(8,128)(2,1)S(1)}, bf16[2,2,2,32,768]{4,3,0,1,2:T(8,128)(2,1)S(1)}, u32[]{:S(2)}, u32[]{:S(2)}) collective-permute-start(bf16[2,2,2,32,768]{4,3,0,1,2:T(8,128)(2,1)S(1)} %get-tuple-element.333), channel_id=1, source_target_pairs={{0,4},{1,5},{2,6},{3,7},{4,0},{5,1},{6,2},{7,3},{8,12},{9,13},{10,... | collective-permute-start | bytes 1179656 | tf_op jit(solution)/shard_map/ppermute | solution.py:712
  301.2 11.8 %copy-start.16 = (pred[2]{0:T(512)(128)(4,1)S(1)}, pred[2]{0:T(512)(128)(4,1)}, u32[]{:S(2)}) copy-start(pred[2]{0:T(512)(128)(4,1)} %copy-done.15) | copy-start | bytes 10
  301.2 15.4 %collective-permute-start.31 = (bf16[2,2,48,768]{3,2,0,1:T(8,128)(2,1)S(1)}, bf16[2,2,48,768]{3,2,0,1:T(8,128)(2,1)S(1)}, u32[]{:S(2)}, u32[]{:S(2)}) collective-permute-start(bf16[2,2,48,768]{3,2,0,1:T(8,128)(2,1)S(1)} %get-tuple-element.428), channel_id=1, source_target_pairs={{0,2},{1,3},{2,0},{3,1},{4,6},{5,7},{6,4},{7,5},{8,10},{9,11},{10,... | collective-permute-start | bytes 884744 | tf_op jit(solution)/shard_map/ppermute | solution.py:712
  302.0 14.6 %collective-permute-start.30 = (bf16[2,2,48,768]{3,2,0,1:T(8,128)(2,1)S(1)}, bf16[2,2,48,768]{3,2,0,1:T(8,128)(2,1)S(1)}, u32[]{:S(2)}, u32[]{:S(2)}) collective-permute-start(bf16[2,2,48,768]{3,2,0,1:T(8,128)(2,1)S(1)} %get-tuple-element.430), channel_id=1, source_target_pairs={{0,4},{1,5},{2,6},{3,7},{4,0},{5,1},{6,2},{7,3},{8,12},{9,13},{10,... | collective-permute-start | bytes 884744 | tf_op jit(solution)/shard_map/ppermute | solution.py:712
  316.9 10.8 %collective-permute-start.35 = (bf16[2,96,768]{2,1,0:T(8,128)(2,1)S(1)}, bf16[2,96,768]{2,1,0:T(8,128)(2,1)S(1)}, u32[]{:S(2)}, u32[]{:S(2)}) collective-permute-start(bf16[2,96,768]{2,1,0:T(8,128)(2,1)S(1)} %get-tuple-element.426), channel_id=1, source_target_pairs={{0,8},{8,0},{16,24},{24,16},{1,9},{9,1},{17,25},{25,17},{2,10},{10... | collective-permute-start | bytes 884744 | tf_op jit(solution)/shard_map/ppermute | solution.py:712
  320.1 7.6 %collective-permute-start.36 = (bf16[2,2,40,768]{3,2,0,1:T(8,128)(2,1)S(1)}, bf16[2,2,40,768]{3,2,0,1:T(8,128)(2,1)S(1)}, u32[]{:S(2)}, u32[]{:S(2)}) collective-permute-start(bf16[2,2,40,768]{3,2,0,1:T(8,128)(2,1)S(1)} %get-tuple-element.442), channel_id=1, source_target_pairs={{0,4},{1,5},{2,6},{3,7},{4,0},{5,1},{6,2},{7,3},{8,12},{9,13},{10,... | collective-permute-start | bytes 737288 | tf_op jit(solution)/shard_map/ppermute | solution.py:712
  321.9 5.7 %collective-permute-start.37 = (bf16[2,2,32,768]{3,2,0,1:T(8,128)(2,1)S(1)}, bf16[2,2,32,768]{3,2,0,1:T(8,128)(2,1)S(1)}, u32[]{:S(2)}, u32[]{:S(2)}) collective-permute-start(bf16[2,2,32,768]{3,2,0,1:T(8,128)(2,1)S(1)} %get-tuple-element.446), channel_id=1, source_target_pairs={{0,2},{1,3},{2,0},{3,1},{4,6},{5,7},{6,4},{7,5},{8,10},{9,11},{10,... | collective-permute-start | bytes 589832 | tf_op jit(solution)/shard_map/ppermute | solution.py:712
  328.0 9.0 %collective-permute-start.39 = (bf16[2,72,768]{2,1,0:T(8,128)(2,1)S(1)}, bf16[2,72,768]{2,1,0:T(8,128)(2,1)S(1)}, u32[]{:S(2)}, u32[]{:S(2)}) collective-permute-start(bf16[2,72,768]{2,1,0:T(8,128)(2,1)S(1)} %get-tuple-element.444), channel_id=1, source_target_pairs={{0,8},{8,0},{16,24},{24,16},{1,9},{9,1},{17,25},{25,17},{2,10},{10... | collective-permute-start | bytes 663560 | tf_op jit(solution)/shard_map/ppermute | solution.py:712
  328.1 8.9 %collective-permute-start.38 = (bf16[96,768]{1,0:T(8,128)(2,1)S(1)}, bf16[96,768]{1,0:T(8,128)(2,1)S(1)}, u32[]{:S(2)}, u32[]{:S(2)}) collective-permute-start(bf16[96,768]{1,0:T(8,128)(2,1)S(1)} %get-tuple-element.448), channel_id=1, source_target_pairs={{0,16},{8,24},{16,0},{24,8},{1,17},{9,25},{17,1},{25,9},{2,18},{10... | collective-permute-start | bytes 442376 | tf_op jit(solution)/shard_map/ppermute | solution.py:712
  337.1 6.2 %collective-permute-start.40 = (bf16[72,768]{1,0:T(8,128)(2,1)S(1)}, bf16[72,768]{1,0:T(8,128)(2,1)S(1)}, u32[]{:S(2)}, u32[]{:S(2)}) collective-permute-start(bf16[72,768]{1,0:T(8,128)(2,1)S(1)} %get-tuple-element.452), channel_id=1, source_target_pairs={{0,16},{8,24},{16,0},{24,8},{1,17},{9,25},{17,1},{25,9},{2,18},{10... | collective-permute-start | bytes 331784 | tf_op jit(solution)/shard_map/ppermute | solution.py:712
  344.1 13.1 %collective-permute-start.41 = (bf16[2,192,768]{2,1,0:T(8,128)(2,1)S(1)}, bf16[2,192,768]{2,1,0:T(8,128)(2,1)S(1)}, u32[]{:S(2)}, u32[]{:S(2)}) collective-permute-start(bf16[2,192,768]{2,1,0:T(8,128)(2,1)S(1)} %broadcast_select_fusion.9), channel_id=1, source_target_pairs={{0,8},{8,0},{16,24},{24,16},{1,9},{9,1},{17,25},{25,17},{2,10},{10... | collective-permute-start | bytes 1769480 | tf_op jit(solution)/shard_map/ppermute | solution.py:712
  357.4 12.6 %collective-permute-start.43 = (bf16[2,2,96,768]{3,2,1,0:T(8,128)(2,1)S(1)}, bf16[2,2,96,768]{3,2,1,0:T(8,128)(2,1)S(1)}, u32[]{:S(2)}, u32[]{:S(2)}) collective-permute-start(bf16[2,2,96,768]{3,2,1,0:T(8,128)(2,1)S(1)} %get-tuple-element.424), channel_id=1, source_target_pairs={{0,2},{1,3},{2,0},{3,1},{4,6},{5,7},{6,4},{7,5},{8,10},{9,11},{10,... | collective-permute-start | bytes 1769480 | tf_op jit(solution)/shard_map/ppermute | solution.py:712
  359.1 15.8 %collective-permute-start.42 = (bf16[2,2,96,768]{3,2,1,0:T(8,128)(2,1)S(1)}, bf16[2,2,96,768]{3,2,1,0:T(8,128)(2,1)S(1)}, u32[]{:S(2)}, u32[]{:S(2)}) collective-permute-start(bf16[2,2,96,768]{3,2,1,0:T(8,128)(2,1)S(1)} %get-tuple-element.425), channel_id=1, source_target_pairs={{0,4},{1,5},{2,6},{3,7},{4,0},{5,1},{6,2},{7,3},{8,12},{9,13},{10,... | collective-permute-start | bytes 1769480 | tf_op jit(solution)/shard_map/ppermute | solution.py:712
  375.0 22.9 %collective-permute-start.45 = (bf16[2,2,2,96,768]{4,3,2,1,0:T(8,128)(2,1)S(1)}, bf16[2,2,2,96,768]{4,3,2,1,0:T(8,128)(2,1)S(1)}, u32[]{:S(2)}, u32[]{:S(2)}) collective-permute-start(bf16[2,2,2,96,768]{4,3,2,1,0:T(8,128)(2,1)S(1)} %broadcast_select_fusion.2), channel_id=1, source_target_pairs={{0,4},{1,5},{2,6},{3,7},{4,0},{5,1},{6,2},{7,3},{8,12},{9,13},{10,... | collective-permute-start | bytes 3538952 | tf_op jit(solution)/shard_map/ppermute | solution.py:712
  377.6 24.5 %collective-permute-start.44 = (bf16[2,2,2,96,768]{4,3,2,1,0:T(8,128)(2,1)S(1)}, bf16[2,2,2,96,768]{4,3,2,1,0:T(8,128)(2,1)S(1)}, u32[]{:S(2)}, u32[]{:S(2)}) collective-permute-start(bf16[2,2,2,96,768]{4,3,2,1,0:T(8,128)(2,1)S(1)} %broadcast_select_fusion.4), channel_id=1, source_target_pairs={{0,2},{1,3},{2,0},{3,1},{4,6},{5,7},{6,4},{7,5},{8,10},{9,11},{10,... | collective-permute-start | bytes 3538952 | tf_op jit(solution)/shard_map/ppermute | solution.py:712
  398.2 4.2 copy-start
  398.2 4.7 %copy-start.12 = (bf16[416,768]{1,0:T(8,128)(2,1)S(1)}, bf16[416,768]{1,0:T(8,128)(2,1)}, u32[]{:S(2)}) copy-start(bf16[416,768]{1,0:T(8,128)(2,1)} %get-tuple-element.385) | copy-start | bytes 1916932
  398.2 4.7 %copy-start.14 = (bf16[4,768]{1,0:T(4,128)(2,1)S(1)}, bf16[4,768]{1,0:T(4,128)(2,1)}, u32[]{:S(2)}) copy-start(bf16[4,768]{1,0:T(4,128)(2,1)} %wb_ref.1) | copy-start | bytes 18436
  398.2 5.6 %copy-start.17 = (bf16[32,64,768]{2,1,0:T(8,128)(2,1)S(1)}, bf16[32,64,768]{2,1,0:T(8,128)(2,1)}, u32[]{:S(2)}) copy-start(bf16[32,64,768]{2,1,0:T(8,128)(2,1)} %get-tuple-element.386) | copy-start | bytes 9437188
  402.3 4.2 copy-start.1
  402.3 7.1 %collective-permute-start.47 = (bf16[2,2,2,2,96,768]{5,4,3,2,1,0:T(8,128)(2,1)S(1)}, bf16[2,2,2,2,96,768]{5,4,3,2,1,0:T(8,128)(2,1)S(1)}, u32[]{:S(2)}, u32[]{:S(2)}) collective-permute-start(bf16[2,2,2,2,96,768]{5,4,3,2,1,0:T(8,128)(2,1)S(1)} %broadcast_select_fusion.1), channel_id=1, source_target_pairs={{0,1},{1,0},{2,3},{3,2},{4,5},{5,4},{6,7},{7,6},{8,9},{9,8},{10,11... | collective-permute-start | bytes 7077896 | tf_op jit(solution)/shard_map/ppermute | solution.py:712
  402.4 14.9 %collective-permute-start.46 = (bf16[2,2,2,2,96,768]{5,4,3,2,1,0:T(8,128)(2,1)S(1)}, bf16[2,2,2,2,96,768]{5,4,3,2,1,0:T(8,128)(2,1)}, u32[]{:S(2)}, u32[]{:S(2)}) collective-permute-start(bf16[2,2,2,2,96,768]{5,4,3,2,1,0:T(8,128)(2,1)S(1)} %broadcast_select_fusion), channel_id=1, source_target_pairs={{0,1},{1,0},{2,3},{3,2},{4,5},{5,4},{6,7},{7,6},{8,9},{9,8},{10,11... | collective-permute-start | bytes 7077896 | tf_op jit(solution)/shard_map/ppermute | solution.py:712
  (6 other events, 7.8 us)
Sparse Core Ops, SparseCore 0:
  37.0 94.3 all-gather.4
  344.2 82.5 all-gather.6
